TPU v7x, 32 devices: a whole 2x2x4 slice. The times are simulated.
32 devices in a mesh: day: 2 (over y), tm: 4 (over z), sta: 4 (over x, core).
Axes of the slice: x: 2, y: 2, z: 4, core: 2. Of those that a mesh axis runs over, the one named last changes fastest.
Arguments:
- traces: bfloat16 [2048, 24576], P('sta', ('day', 'tm')), parts along dimension 1, may hold values from -12 to 12
- offsets: int32 [24], P(('day', 'tm')), parts along dimension 0, may hold values from 0 to 3072, as said below
- pair_first: int32 [2048], P('sta'), may hold values from 0 to 511
- pair_slot: int32 [2048], P('sta'), may hold values from 0 to 127, as said below
- send_rows: int32 [4, 128], P('sta'), may hold values from 0 to 511, as said below
Outputs:
- correlations: float32 [2048, 2048], P(('day', 'tm'), 'sta'), parts along dimension 0
There are 2 independent parts, one for each index of `day`. A program takes and returns all parts, laid end to end along the dimension named above; an argument that names none is the same for every part. Nothing has to cross between parts.
Inputs may be any that keep to these rules, and one draw needn't show every extreme that they name: offsets[t * 3 + w] lies between w * 1024 and (w + 1) * 1024. For a pair owned by group g whose src = pair_slot // 32 lies two or more groups from g around the cycle of 4 groups (neither g - 1, g nor g + 1 modulo 4), pair_slot mod 32 is below 8. The 32 entries send_rows[s, g * 32 .. (g + 1) * 32 - 1] are distinct.
All inputs are finite; a program needn't handle non-finite values.
Results may differ from a plain program's by a relative error of at most 0.0039.
Values may be sent and summed in bfloat16 or wider, within the bound.
No kernel may reach another device: no remote copies, remote signals or barrier semaphores. Data moves between devices by JAX's collectives and lax.ppermute only.
A program may use at most 64 MiB of HBM per device.

v0:
```python
import math

import jax
import jax.numpy as jnp
from jax import lax
from jax.sharding import PartitionSpec as P

WIN = 2048
NF = 512
NL = 1024


FLOOR = 0.1


def shifted(block, axis, distance):
    devices = range(lax.axis_size(axis))
    route = [(i - distance, i) for i in devices if i - distance in devices]
    return lax.ppermute(block, axis, route)


def taper_table(length):
    sample_index = jnp.arange(length, dtype=jnp.float32)
    return 0.5 - 0.5 * jnp.cos(2.0 * math.pi * sample_index / length)


def dft_table(length, bin_count):
    sample_index = jnp.arange(length, dtype=jnp.int32)[:, None]
    bin_index = jnp.arange(bin_count, dtype=jnp.int32)[None, :] + 1
    angles = (sample_index * bin_index % length).astype(jnp.float32) * (2.0 * math.pi / length)
    return jnp.concatenate([jnp.cos(angles), -jnp.sin(angles)], axis=1).astype(jnp.bfloat16)


def lag_table(lag_count, length, bin_count):
    lag_shift = jnp.arange(lag_count, dtype=jnp.int32)[:, None] - lag_count // 2
    bin_index = jnp.arange(bin_count, dtype=jnp.int32)[None, :] + 1
    angles = (lag_shift * bin_index % length).astype(jnp.float32) * (2.0 * math.pi / length)
    return jnp.concatenate([jnp.cos(angles), -jnp.sin(angles)], axis=1)


def segments(block_data, starts, length):

    def take_one(start_at):
        return lax.dynamic_slice_in_dim(block_data, start_at, length, axis=1)

    pieces = jax.vmap(take_one)(starts)
    values = pieces.astype(jnp.float32)
    centred = values - jnp.mean(values, axis=2, keepdims=True)
    return (centred * taper_table(length)).astype(jnp.bfloat16)


def whiten(spectrum, bin_count):
    real_part = spectrum[..., :bin_count]
    imag_part = spectrum[..., bin_count:]
    amplitude = jnp.sqrt(real_part * real_part + imag_part * imag_part + 1e-06)
    padded = jnp.pad(amplitude, [(0, 0)] * (amplitude.ndim - 1) + [(2, 2)])
    smooth = (
        padded[..., 0:bin_count]
        + padded[..., 1 : bin_count + 1]
        + padded[..., 2 : bin_count + 2]
        + padded[..., 3 : bin_count + 3]
        + padded[..., 4 : bin_count + 4]
    ) / 5.0
    inverse = 1.0 / jnp.maximum(smooth, FLOOR)
    return (spectrum * jnp.concatenate([inverse, inverse], axis=-1)).astype(jnp.bfloat16)


def cross_terms(first_spec, second_spec, bin_count):
    first_real = first_spec[..., :bin_count].astype(jnp.float32)
    first_imag = first_spec[..., bin_count:].astype(jnp.float32)
    second_real = second_spec[..., :bin_count].astype(jnp.float32)
    second_imag = second_spec[..., bin_count:].astype(jnp.float32)
    return jnp.concatenate(
        [
            first_real * second_real + first_imag * second_imag,
            first_imag * second_real - first_real * second_imag,
        ],
        axis=-1,
    )


def on_device(traces, offsets, pair_first, pair_slot, send_rows):
    stations = traces.shape[0]
    windows = offsets.shape[0]
    time_devices = lax.axis_size("tm")
    next_rim = shifted(traces[:, :WIN], "tm", -1)
    block_data = jnp.concatenate([traces, next_rim], axis=1)
    segment = segments(block_data, offsets, WIN)
    spectrum = jnp.dot(
        segment.reshape(windows * stations, WIN),
        dft_table(WIN, NF),
        preferred_element_type=jnp.float32,
    ) * (1.0 / math.sqrt(WIN))
    whitened = whiten(spectrum.reshape(windows, stations, 2 * NF), NF)
    row_list = send_rows[0]
    outgoing = jnp.take(whitened, row_list, axis=1)
    incoming = lax.all_to_all(outgoing, "sta", split_axis=1, concat_axis=1, tiled=True)

    def add_window(window, running):
        first_spec = jnp.take(whitened[window], pair_first, axis=0)
        second_spec = jnp.take(incoming[window], pair_slot, axis=0)
        return running + cross_terms(first_spec, second_spec, NF)

    cross_sum = lax.fori_loop(
        0, windows, add_window, jnp.zeros((pair_first.shape[0], 2 * NF), jnp.float32)
    )
    lag_rows = lag_table(NL, WIN, NF)
    scaling = 1.0 / math.sqrt(NF * windows * time_devices)
    stacked = lax.psum_scatter(
        lax.dot_general(
            lag_rows,
            cross_sum,
            (((1,), (1,)), ((), ())),
            precision=lax.Precision.HIGHEST,
            preferred_element_type=jnp.float32,
        ),
        "tm",
        scatter_dimension=0,
        tiled=True,
    )
    return stacked * scaling


def solution(mesh):
    in_specs = (P("sta", ("day", "tm")), P(("day", "tm")), P("sta"), P("sta"), P("sta", None))
    out_specs = P(("day", "tm"), "sta")
    return jax.shard_map(
        on_device, mesh=mesh, in_specs=in_specs, out_specs=out_specs, check_vma=False
    )
```

profile of v0, /device:TPU:0, one launch (start us, length us, event | category | flops | bytes accessed | tf_op | source)
XLA Modules:
  0.0 256.5 jit_solution(7347927885232624078)
XLA Ops:
  6.5 3.3 %slice.50 = bf16[512,2048]{1,0:T(8,128)(2,1)} slice(bf16[512,3072]{1,0:T(8,128)(2,1)} %param.7), slice={[0:512], [0:2048]} | slice | bytes 4194304 | tf_op jit(solution)/shard_map/slice | solution.py:86
  11.3 18.3 %cosine_convert_fusion = (bf16[2048,512]{1,0:T(8,128)(2,1)}, bf16[2048,512]{1,0:T(8,128)(2,1)}) fusion(s32[512]{0:T(512)S(1)} %iota_add_fusion.1), kind=kLoop, calls=%fused_computation.61 | loop fusion | flops 17825792 | bytes 4196352 | tf_op jit(solution)/shard_map/convert.1
  29.6 31.2 %collective-permute-done = bf16[512,2048]{1,0:T(8,128)(2,1)} collective-permute-done((bf16[512,2048]{1,0:T(8,128)(2,1)}, bf16[512,2048]{1,0:T(8,128)(2,1)}, u32[]{:S(2)}, u32[]{:S(2)}) %collective-permute-start) | collective-permute-done | bytes 2097184 | tf_op jit(solution)/shard_map/ppermute | solution.py:19
  60.8 4.3 %pad_maximum_fusion = bf16[512,5120]{1,0:T(8,128)(2,1)} fusion(bf16[512,2048]{1,0:T(8,128)(2,1)} %collective-permute-done, bf16[512,3072]{1,0:T(8,128)(2,1)S(1)} %copy-done.2), kind=kLoop, calls=%fused_computation.32 | loop fusion | flops 10485760 | bytes 10485760 | tf_op jit(solution)/shard_map/concatenate | solution.py:87
  65.1 16.4 %while.15 = (s32[]{:T(128)}, bf16[512,5120]{1,0:T(8,128)(2,1)}, s32[3,2]{0,1:T(2,128)S(1)}, bf16[3,512,2048]{2,1,0:T(8,128)(2,1)}, s32[]{:T(128)}) while((s32[]{:T(128)}, bf16[512,5120]{1,0:T(8,128)(2,1)}, s32[3,2]{0,1:T(2,128)S(1)}, bf16[3,512,2048]{2,1,0:T(8,128)(2,1)}, s32[]{:T(128)}) %tuple.52), condition=%wide.while_cond, body=%wide.while_body.sunk | while | flops 2 | bytes 4195417 | solution.py:44
  65.7 4.9 %bitcast_dynamic-update-slice_fusion.2 = bf16[3,512,2048]{2,1,0:T(8,128)(2,1)} fusion(bf16[3,512,2048]{2,1,0:T(8,128)(2,1)} %get-tuple-element.256, s32[]{:T(128)} %get-tuple-element.253, bf16[512,5120]{1,0:T(8,128)(2,1)} %get-tuple-element.259, s32[]{:T(128)} %bitcast.39), kind=kLoop, calls=%fused_computation.3.clone.1 | loop fusion | bytes 4195328 | tf_op jit(solution)/shard_map/vmap()/gather
  71.1 4.9 %bitcast_dynamic-update-slice_fusion.2 = bf16[3,512,2048]{2,1,0:T(8,128)(2,1)} fusion(bf16[3,512,2048]{2,1,0:T(8,128)(2,1)} %get-tuple-element.256, s32[]{:T(128)} %get-tuple-element.253, bf16[512,5120]{1,0:T(8,128)(2,1)} %get-tuple-element.259, s32[]{:T(128)} %bitcast.39), kind=kLoop, calls=%fused_computation.3.clone.1 | loop fusion | bytes 4195328 | tf_op jit(solution)/shard_map/vmap()/gather
  76.6 4.8 %bitcast_dynamic-update-slice_fusion.2 = bf16[3,512,2048]{2,1,0:T(8,128)(2,1)} fusion(bf16[3,512,2048]{2,1,0:T(8,128)(2,1)} %get-tuple-element.256, s32[]{:T(128)} %get-tuple-element.253, bf16[512,5120]{1,0:T(8,128)(2,1)} %get-tuple-element.259, s32[]{:T(128)} %bitcast.39), kind=kLoop, calls=%fused_computation.3.clone.1 | loop fusion | bytes 4195328 | tf_op jit(solution)/shard_map/vmap()/gather
  81.4 3.7 %convert_reduce_fusion = f32[3,512]{1,0:T(4,128)S(1)} fusion(bf16[3,512,2048]{2,1,0:T(8,128)(2,1)} %get-tuple-element.122), kind=kLoop, calls=%fused_computation.68 | loop fusion | flops 6289920 | bytes 6297600 | tf_op jit(solution)/shard_map/reduce_sum | solution.py:48
  85.2 4.4 %fusion.3 = bf16[1536,2048]{1,0:T(8,128)(2,1)S(1)} fusion(f32[2048]{0:T(1024)S(1)} %multiply_subtract_fusion, f32[1536]{0:T(1024)S(1)} %div.28, bf16[3,512,2048]{2,1,0:T(8,128)(2,1)} %get-tuple-element.122), kind=kLoop, calls=%fused_computation.26 | loop fusion | flops 12582912 | bytes 12597248 | tf_op jit(solution)/shard_map/convert_element_type | solution.py:49
  89.6 9.0 %convolution_multiply_fusion = f32[1536,1024]{1,0:T(8,128)} fusion(bf16[1536,2048]{1,0:T(8,128)(2,1)S(1)} %fusion.3, bf16[2048,512]{1,0:T(8,128)(2,1)S(1)} %copy-done.4, bf16[2048,512]{1,0:T(8,128)(2,1)S(1)} %copy-done.3), kind=kOutput, calls=%fused_computation.37 | convolution fusion | flops 6452412416 | bytes 16777216 | tf_op jit(solution)/shard_map/dot_general | solution.py:89
  98.6 7.1 %copy.8 = f32[3,512,1024]{2,0,1:T(4,128)S(1)} copy(f32[3,512,1024]{2,1,0:T(8,128)} %bitcast.46) | data formatting | bytes 12582912 | tf_op jit(solution)/shard_map/reshape | solution.py:94
  105.7 4.4 %fusion.17 = f32[3,512,512]{2,0,1:T(4,128)} fusion(f32[3,512,1024]{2,0,1:T(4,128)S(1)} %copy.8), kind=kLoop, calls=%fused_computation.51 | loop fusion | flops 3145728 | bytes 9437184 | tf_op jit(solution)/shard_map/sqrt | solution.py:55
  110.1 16.7 %fusion.11 = f32[3,512,512]{2,0,1:T(4,128)S(1)} fusion(f32[3,512,512]{2,0,1:T(4,128)} %fusion.17), kind=kLoop, calls=%fused_computation.44 | loop fusion | flops 5505024 | bytes 6291456 | tf_op jit(solution)/shard_map/div | solution.py:64
  126.8 12.6 %fusion.4 = bf16[3,512,1024]{2,0,1:T(4,128)(2,1)} fusion(f32[3,512,512]{2,0,1:T(4,128)S(1)} %fusion.11, f32[3,512,1024]{2,1,0:T(8,128)S(1)} %bitcast.47), kind=kLoop, calls=%fused_computation.28 | loop fusion | flops 4718592 | bytes 12582912 | tf_op jit(solution)/shard_map/convert_element_type | solution.py:65
  139.5 3.6 %gather_fusion.2 = bf16[128,3,1024]{2,1,0:T(4,128)(2,1)S(1)} fusion(bf16[3,512,1024]{2,0,1:T(4,128)(2,1)} %fusion.4, s32[1024]{0:T(1024)S(1)} %pad_clamp_fusion.2), kind=kCustom, calls=%fused_computation.2 | custom fusion | bytes 1573376 | tf_op jit(solution)/shard_map/jit(_take)/gather | solution.py:96
  144.7 3.5 %all-to-all-start = ((bf16[3,128,1024]{2,0,1:T(4,128)(2,1)}), bf16[3,128,1024]{2,0,1:T(4,128)(2,1)S(1)}, u32[]{:S(2)}, u32[]{:S(2)}) async-start(bf16[3,128,1024]{2,0,1:T(4,128)(2,1)} %select_bitcast_fusion), calls=%async_computation | async-start | bytes 2097152 | tf_op jit(solution)/shard_map/all_to_all | solution.py:97
  148.3 9.8 %fusion.31 = (f32[1024,512]{1,0:T(8,128)}, f32[1024,512]{1,0:T(8,128)}) fusion(s32[512]{0:T(512)S(1)} %iota_add_fusion.1, s32[1024]{0:T(1024)S(1)} %iota_add_fusion), kind=kLoop, calls=%fused_computation.76 | loop fusion | flops 7864320 | bytes 4200448 | tf_op jit(solution)/shard_map/cos | solution.py:38
  158.0 2.9 %copy.9 = bf16[3,512,1024]{2,1,0:T(8,128)(2,1)} copy(bf16[3,512,1024]{2,0,1:T(4,128)(2,1)S(1)} %copy-done.1) | data formatting | bytes 6291456
  163.8 30.4 %while.16 = (s32[]{:T(128)}, f32[512,1024]{1,0:T(8,128)}, s32[512]{0:T(512)S(1)}, bf16[3,512,1024]{2,1,0:T(8,128)(2,1)}, s32[512]{0:T(512)S(1)}, /*index=5*/bf16[3,128,1024]{2,1,0:T(8,128)(2,1)}, s32[]{:T(128)}, s32[]{:T(128)}) while((s32[]{:T(128)}, f32[512,1024]{1,0:T(8,128)}, s32[512]{0:T(512)S(1)}, ...), condition=%wide.region_2.3_spmd.clone, body=%wide.region_1.2_spmd.clone.sunk | while | flops 5254147 | bytes 21526632 | solution.py:104
  165.1 2.1 gather_fusion.1
  168.4 2.1 gather_fusion
  171.0 1.9 maximum_add_fusion.2
  174.2 2.1 gather_fusion.1
  177.4 2.1 gather_fusion
  180.0 3.5 %maximum_add_fusion.2 = f32[512,1024]{1,0:T(8,128)} fusion(f32[512,512]{1,0:T(8,128)S(1)} %get-tuple-element.246, f32[512,512]{1,0:T(8,128)S(1)} %get-tuple-element.247, f32[512,1024]{1,0:T(8,128)} %get-tuple-element.272, pred[]{:T(512)S(6)} %compare.9), kind=kLoop, calls=%fused_computation.5.clone.1 | loop fusion | flops 1572864 | bytes 6291457 | tf_op jit(solution)/shard_map/while/body/eval_jaxpr/add | solution.py:102
  184.8 2.1 gather_fusion.1
  188.1 2.1 gather_fusion
  190.7 3.5 %maximum_add_fusion.2 = f32[512,1024]{1,0:T(8,128)} fusion(f32[512,512]{1,0:T(8,128)S(1)} %get-tuple-element.246, f32[512,512]{1,0:T(8,128)S(1)} %get-tuple-element.247, f32[512,1024]{1,0:T(8,128)} %get-tuple-element.272, pred[]{:T(512)S(6)} %compare.9), kind=kLoop, calls=%fused_computation.5.clone.1 | loop fusion | flops 1572864 | bytes 6291457 | tf_op jit(solution)/shard_map/while/body/eval_jaxpr/add | solution.py:102
  194.2 10.3 %fusion.18 = f32[1024,512]{1,0:T(8,128)} fusion(f32[512,1024]{1,0:T(8,128)} %get-tuple-element.114, f32[1024,512]{1,0:T(8,128)} %get-tuple-element.175, f32[1024,512]{1,0:T(8,128)} %get-tuple-element.174), kind=kOutput, calls=%fused_computation.53 | convolution fusion | flops 6443499520 | bytes 8388608 | tf_op jit(solution)/shard_map/dot_general | solution.py:110
  204.5 43.3 %reduce-scatter.2.cloned.1.call-done = f32[256,512]{1,0:T(8,128)} async-done(((f32[1024,512]{1,0:T(8,128)}), f32[256,512]{1,0:T(8,128)}) %reduce-scatter.2.cloned.1.call-update) | async-done | bytes 524304 | tf_op jit(solution)/shard_map/reduce_scatter | solution.py:109
  247.8 1.9 broadcast_multiply_fusion
  (72 shorter events, 16.6 us)
Async XLA Ops:
  6.5 54.2 %copy-start.2 = (bf16[512,3072]{1,0:T(8,128)(2,1)S(1)}, bf16[512,3072]{1,0:T(8,128)(2,1)}, u32[]{:S(2)}) copy-start(bf16[512,3072]{1,0:T(8,128)(2,1)} %param.7) | copy-start | bytes 9437188
  6.5 4.6 %copy-start.7 = (s32[3]{0:T(128)S(1)}, s32[3]{0:T(128)}, u32[]{:S(2)}) copy-start(s32[3]{0:T(128)} %param.8) | copy-start | bytes 40
  6.5 4.7 %copy-start.8 = (s32[1,128]{1,0:T(1,128)S(1)}, s32[1,128]{1,0:T(1,128)}, u32[]{:S(2)}) copy-start(s32[1,128]{1,0:T(1,128)} %param.11) | copy-start | bytes 1540
  9.9 50.9 %collective-permute-start = (bf16[512,2048]{1,0:T(8,128)(2,1)}, bf16[512,2048]{1,0:T(8,128)(2,1)}, u32[]{:S(2)}, u32[]{:S(2)}) collective-permute-start(bf16[512,2048]{1,0:T(8,128)(2,1)} %slice.50), channel_id=1, source_target_pairs={{4,0},{8,4},{12,8},{5,1},{9,5},{13,9},{6,2},{10,6},{14,10},{7,3},{... | collective-permute-start | bytes 6291464 | tf_op jit(solution)/shard_map/ppermute | solution.py:19
  85.1 4.5 %copy-start.3 = (bf16[2048,512]{1,0:T(8,128)(2,1)S(1)}, bf16[2048,512]{1,0:T(8,128)(2,1)}, u32[]{:S(2)}) copy-start(bf16[2048,512]{1,0:T(8,128)(2,1)} %get-tuple-element.176) | copy-start | bytes 6291460
  85.1 4.5 %copy-start.4 = (bf16[2048,512]{1,0:T(8,128)(2,1)S(1)}, bf16[2048,512]{1,0:T(8,128)(2,1)}, u32[]{:S(2)}) copy-start(bf16[2048,512]{1,0:T(8,128)(2,1)} %get-tuple-element.177) | copy-start | bytes 6291460
  110.1 16.7 %copy-start = (f32[1536,1024]{1,0:T(8,128)S(1)}, f32[1536,1024]{1,0:T(8,128)}, u32[]{:S(2)}) copy-start(f32[1536,1024]{1,0:T(8,128)} %convolution_multiply_fusion) | copy-start | bytes 18874372
  144.7 17.9 %all-to-all-start = ((bf16[3,128,1024]{2,0,1:T(4,128)(2,1)}), bf16[3,128,1024]{2,0,1:T(4,128)(2,1)S(1)}, u32[]{:S(2)}, u32[]{:S(2)}) async-start(bf16[3,128,1024]{2,0,1:T(4,128)(2,1)} %select_bitcast_fusion), calls=%async_computation | async-start | bytes 2097152 | tf_op jit(solution)/shard_map/all_to_all | solution.py:97
  148.2 99.6 %reduce-scatter.2.cloned.1.call-start = ((), (), s32[]{:S(2)}) async-start(), calls=%async_computation.2 | async-start | bytes 2621440 | tf_op jit(solution)/shard_map/reduce_scatter | solution.py:109
  148.2 9.8 %copy-start.1 = (bf16[3,512,1024]{2,0,1:T(4,128)(2,1)S(1)}, bf16[3,512,1024]{2,0,1:T(4,128)(2,1)}, u32[]{:S(2)}) copy-start(bf16[3,512,1024]{2,0,1:T(4,128)(2,1)} %fusion.4) | copy-start | bytes 9437188
  158.0 5.7 %copy-start.5 = (s32[512]{0:T(512)S(1)}, s32[512]{0:T(512)}, u32[]{:S(2)}) copy-start(s32[512]{0:T(512)} %param.9) | copy-start | bytes 6148
  158.0 5.7 %copy-start.6 = (s32[512]{0:T(512)S(1)}, s32[512]{0:T(512)}, u32[]{:S(2)}) copy-start(s32[512]{0:T(512)} %param.10) | copy-start | bytes 6148
Sparse Core Ops, SparseCore 0:
  204.6 43.1 reduce-scatter.1
where the time goes:
time: 257 us; the launch traced here: 256 us
  other arithmetic  88.7 us (35%)
  waiting for transfers between devices  76.1 us (30%)
  local copies, waits for them, and re-layouts  53.7 us (21%)
  matrix products  19.3 us (8%)
  between operations  13.6 us (5%)
  starting transfers between devices  4.84 us (2%)
    reduce_scatter x1, waiting for transfers between devices, on_device(): lax.psum_scatter(lax.dot_general(lag_rows, cross_sum, (((1,), (1,)), ((),...  43.3 us
    ppermute x1, waiting for transfers between devices, shifted(): return lax.ppermute(block, axis, route)  31.2 us
    another operation x1, other arithmetic  18.3 us
    div x1, other arithmetic, whiten(): inverse = 1.0 / jnp.maximum(smooth, FLOOR)  16.7 us
    gather x9, local copies, waits for them, and re-layouts  16.4 us
    convert_element_type x1, other arithmetic, whiten(): (spectrum * jnp.concatenate([inverse, inverse], axis=-1)).astype(jnp.bflo...  12.6 us
    dot_general x1, matrix products, on_device(): lax.dot_general(lag_rows, cross_sum, (((1,), (1,)), ((), ())), precision=...  10.3 us
    cos x1, other arithmetic, lag_table(): return jnp.concatenate([jnp.cos(angles), -jnp.sin(angles)], axis=1)  9.78 us
  transfers between devices with their start and end apart: 3, of which 3 were waited for; matrix products, arithmetic and copies ran while one was open for 12% of the time, Pallas kernels for 0%

commit v1 on v0

v1 whole, which is shorter than its diff:
```python
import functools
import math

import jax
import jax.numpy as jnp
from jax import lax
from jax.experimental import pallas as pl
from jax.experimental.pallas import tpu as pltpu
from jax.sharding import PartitionSpec as P

WIN = 2048
NF = 512
NL = 1024
FLOOR = 0.1
STEP = 1024
HALF = 1024
CAP_FAR = 8
LANES = 128
CHUNKS = WIN // LANES
HC = CHUNKS // 2
QB = NF // 2
ROOT = 1.0 / math.sqrt(WIN)
F32 = jnp.float32
BF16 = jnp.bfloat16
ROWS = 16
VMEM = pl.BlockSpec(memory_space=pltpu.VMEM)
SMEM = pl.BlockSpec(memory_space=pltpu.SMEM)
PARAMS = pltpu.CompilerParams(vmem_limit_bytes=56 << 20)


def shape(dims, dtype):
    return jax.ShapeDtypeStruct(dims, dtype)


def small_tables():
    step = jnp.arange(32, dtype=jnp.int32)[:, None]
    half = jnp.arange(QB, dtype=jnp.int32)
    freq = jnp.concatenate([2 * half + 1, 2 * half + 2])[None, :]
    steps = jnp.concatenate([32 * step, step], axis=0)
    angles = (steps * freq % WIN).astype(F32) * (2.0 * math.pi / WIN)
    return jnp.cos(angles), jnp.sin(angles)


def taper_row():
    index = jnp.arange(WIN, dtype=F32)
    return (0.5 - 0.5 * jnp.cos(2.0 * math.pi * index / WIN))[None, :]


def fill_tables(cos_ref, sin_ref, odd_ref, even_ref):
    def block(a, carry):
        ca = cos_ref[pl.ds(a, 1), :]
        sa = sin_ref[pl.ds(a, 1), :]
        cb = cos_ref[32:64, :]
        sb = sin_ref[32:64, :]
        c = (ca * cb - sa * sb).astype(BF16)
        s = (-(sa * cb + ca * sb)).astype(BF16)
        rows = pl.ds(pl.multiple_of(a * 32, 32), 32)
        odd_ref[rows, :QB] = c[:, :QB]
        odd_ref[rows, QB:] = s[:, :QB]
        even_ref[rows, :QB] = c[:, QB:]
        even_ref[rows, QB:] = s[:, QB:]
        return carry

    lax.fori_loop(0, HALF // 32, block, 0)


def prepare(pick, start, count, taper_ref, turned_ref, even_ref, odd_ref):
    q = start // LANES
    s = start % LANES
    shift = (LANES - s) % LANES
    for c in range(CHUNKS):
        j = (c - q + CHUNKS) % CHUNKS
        turned_ref[:, c * LANES : (c + 1) * LANES] = taper_ref[
            :, pl.ds(pl.multiple_of(j * LANES, LANES), LANES)
        ]
    keep = lax.broadcasted_iota(jnp.int32, (ROWS, LANES), 1) < LANES - s

    def group(i, carry):
        rows = pl.ds(pl.multiple_of(i * ROWS, ROWS), ROWS)
        raw = [pick(rows, c) for c in range(CHUNKS)]
        total = raw[0]
        for c in range(1, CHUNKS):
            total = total + raw[c]
        mean = jnp.sum(total, axis=1, keepdims=True) * (1.0 / WIN)
        rolled = [pltpu.roll(r - mean, shift, 1) for r in raw]
        seg = []
        for c in range(CHUNKS):
            y = jnp.where(keep, rolled[c], rolled[(c + 1) % CHUNKS])
            seg.append((y * turned_ref[:, c * LANES : (c + 1) * LANES]).astype(BF16))
        for c in range(HC):
            j = (c - q + CHUNKS) % CHUNKS
            sign = jnp.where(j < HC, 1.0, -1.0).astype(F32)
            low = seg[c].astype(F32)
            high = seg[c + HC].astype(F32)
            lanes = pl.ds(pl.multiple_of((j % HC) * LANES, LANES), LANES)
            even_ref[rows, lanes] = (low + high).astype(BF16)
            odd_ref[rows, lanes] = ((low - high) * sign).astype(BF16)
        return carry

    lax.fori_loop(0, count // ROWS, group, 0)


def whiten_rows(spec_ref, count, live, out_ref, first_row):
    lane = lax.broadcasted_iota(jnp.int32, (ROWS, QB), 1)
    not_first = lane > 0
    not_last = lane < QB - 1

    def up(x):
        return jnp.where(not_first, pltpu.roll(x, 1, 1), 0.0)

    def down(x):
        return jnp.where(not_last, pltpu.roll(x, QB - 1, 1), 0.0)

    def group(i, carry):
        rows = pl.ds(pl.multiple_of(i * ROWS, ROWS), ROWS)
        o_re = spec_ref[rows, 0:QB] * ROOT
        o_im = spec_ref[rows, QB : 2 * QB] * ROOT
        e_re = spec_ref[rows, 2 * QB : 3 * QB] * ROOT
        e_im = spec_ref[rows, 3 * QB :] * ROOT
        odd = jnp.sqrt(o_re * o_re + o_im * o_im + 1e-06)
        even = jnp.sqrt(e_re * e_re + e_im * e_im + 1e-06)
        both = odd + even
        smooth_odd = (up(both) + both + down(odd)) / 5.0
        smooth_even = (up(even) + both + down(both)) / 5.0
        inv_odd = live / jnp.maximum(smooth_odd, FLOOR)
        inv_even = live / jnp.maximum(smooth_even, FLOOR)
        to = pl.ds(pl.multiple_of(first_row + i * ROWS, ROWS), ROWS)
        out_ref[to, 0:QB] = (o_re * inv_odd).astype(BF16)
        out_ref[to, QB : 2 * QB] = (e_re * inv_even).astype(BF16)
        out_ref[to, 2 * QB : 3 * QB] = (o_im * inv_odd).astype(BF16)
        out_ref[to, 3 * QB :] = (e_im * inv_even).astype(BF16)
        return carry

    lax.fori_loop(0, count // ROWS, group, 0)


def window(pick, start, live, count, taper_ref, turned, even, odd, t_odd, t_even, spec, out_ref, first_row):
    prepare(pick, start, count, taper_ref, turned, even, odd)
    spec[:, : 2 * QB] = jnp.dot(odd[...], t_odd[...], preferred_element_type=F32)
    spec[:, 2 * QB :] = jnp.dot(even[...], t_even[...], preferred_element_type=F32)
    whiten_rows(spec, count, live, out_ref, first_row)


def slots(c):
    return c * LANES + lax.broadcasted_iota(jnp.int32, (ROWS, LANES), 1)


def part(ref, offset, rows, c):
    return ref[rows, offset + c * LANES : offset + (c + 1) * LANES].astype(F32)


def shifted_rows(ref, first):
    def get(rows, offset, c):
        at = pl.ds(pl.multiple_of(rows.start + first, ROWS), ROWS)
        return part(ref, offset, at, c)

    return get


def choose(sel, spectra, out_refs):
    results = []
    for index, spectrum in zip(sel, spectra):
        count = index.shape[0]
        stations = sum(s.shape[0] for s in spectrum)
        hot = (lax.broadcasted_iota(jnp.int32, (count, stations), 1) == index[...]).astype(F32).astype(BF16)
        total = None
        at = 0
        for piece in spectrum:
            term = jnp.dot(hot[:, at : at + piece.shape[0]], piece[...], preferred_element_type=F32)
            total = term if total is None else total + term
            at += piece.shape[0]
        results.append(total)
    return results


def write_chosen(results, near_count, cap, refs):
    for i in range(near_count):
        for w in range(2):
            refs[i][w * cap : (w + 1) * cap, :] = results[w][i * cap : (i + 1) * cap].astype(BF16)
    base = near_count * cap
    for i in range(near_count, len(refs)):
        at = base + (i - near_count) * 2 * CAP_FAR
        refs[i][...] = (
            results[0][at : at + 2 * CAP_FAR] + results[1][at : at + 2 * CAP_FAR]
        ).astype(BF16)


def scratches(count):
    return [
        pltpu.VMEM((1, WIN), F32),
        pltpu.VMEM((count, HALF), BF16),
        pltpu.VMEM((count, HALF), BF16),
        pltpu.VMEM((count, 2 * NF), F32),
    ]


def local_kernel(near_count, cap, block, scal, main, cos_t, sin_t, taper, sel0, sel1, *rest):
    t_odd, t_even, white0, white3 = rest[:4]
    sends = rest[4:-4]
    turned, even, odd, spec = rest[-4:]
    fill_tables(cos_t, sin_t, t_odd, t_even)
    stations = main.shape[0]
    first_start = scal[0]
    last_start = scal[2] - 2 * STEP
    last_live = scal[4].astype(F32)
    for first in range(0, stations, block):
        get = shifted_rows(main, first)

        def pick0(rows, c):
            if c >= HC:
                return get(rows, HALF, c - HC)
            return jnp.where(slots(c) >= first_start, get(rows, 0, c), get(rows, 2 * HALF, c))

        def pick3(rows, c):
            if c >= HC:
                return jnp.zeros((ROWS, LANES), F32)
            return jnp.where(slots(c) >= last_start, get(rows, 2 * HALF, c), 0.0)

        rest_args = (block, taper, turned, even, odd, t_odd, t_even, spec)
        window(pick0, first_start, 1.0, *rest_args, white0, first)
        window(pick3, last_start, last_live, *rest_args, white3, first)
    results = choose((sel0, sel1), ((white0,), (white3,)), sends)
    write_chosen(results, near_count, cap, sends)


def rim_kernel(first, near_count, cap, earlier, last, scal, main, rim, tail, taper, t_odd, t_even, *rest):
    sel0, sel1 = rest[:2]
    before = rest[2 : 2 + 2 * earlier]
    rest = rest[2 + 2 * earlier :]
    white1, white2 = rest[:2]
    sends = rest[2:-4]
    turned, even, odd, spec = rest[-4:]
    count = rim.shape[0]
    start1 = scal[1]
    start2 = scal[3] - 2 * STEP
    live2 = scal[5].astype(F32)
    get = shifted_rows(main, first)

    def pick1(rows, c):
        if c < HC:
            return get(rows, 2 * HALF, c)
        return jnp.where(slots(c) >= start1, get(rows, HALF, c - HC), part(rim, 0, rows, c - HC))

    def pick2(rows, c):
        if c >= HC:
            return get(rows, 0, c - HC)
        return jnp.where(slots(c) >= start2, part(tail, 0, rows, c), get(rows, HALF, c))

    rest_args = (count, taper, turned, even, odd, t_odd, t_even, spec)
    window(pick1, lax.rem(start1, WIN), 1.0, *rest_args, white1, 0)
    window(pick2, start2, live2, *rest_args, white2, 0)
    if last:
        spectra1 = tuple(before[0::2]) + (white1,)
        spectra2 = tuple(before[1::2]) + (white2,)
        results = choose((sel0, sel1), (spectra1, spectra2), sends)
        write_chosen(results, near_count, cap, sends)


def add_pairs(near_count, cap, pieces, first_col, slot_cols, groups, incoming, cross):
    pairs = first_col.shape[0]
    width = incoming.shape[0]
    block = min(pairs, 256)
    for w in range(2):
        for i in range(near_count):
            incoming[i * cap : (i + 1) * cap, :] = pieces[i][w * cap : (w + 1) * cap, :]
        if w == 0:
            at = near_count * cap
            for i in range(near_count, len(pieces)):
                incoming[at : at + 2 * CAP_FAR, :] = pieces[i][...]
                at += 2 * CAP_FAR
            if at < width:
                incoming[at:, :] = jnp.zeros((width - at, 2 * NF), BF16)
        spectrum = groups[w]
        for p in range(0, pairs, block):
            col = first_col[p : p + block, :]
            first = None
            at = 0
            for piece in spectrum:
                n = piece.shape[0]
                hot = (lax.broadcasted_iota(jnp.int32, (block, n), 1) + at == col).astype(F32).astype(BF16)
                term = jnp.dot(hot, piece[...], preferred_element_type=F32)
                first = term if first is None else first + term
                at += n
            hot = (
                lax.broadcasted_iota(jnp.int32, (block, width), 1) == slot_cols[w][p : p + block, :]
            ).astype(F32).astype(BF16)
            second = jnp.dot(hot, incoming[...], preferred_element_type=F32)
            a_i, b_i = first[:, :NF], first[:, NF:]
            a_j, b_j = second[:, :NF], second[:, NF:]
            cross[p : p + block, :NF] += a_i * a_j + b_i * b_j
            cross[p : p + block, NF:] += b_i * a_j - a_i * b_j


def early_kernel(near_count, cap, n_pieces, first_col, slot0, slot1, white0, white3, *rest):
    pieces = rest[:n_pieces]
    cross, incoming = rest[n_pieces:]
    cross[...] = jnp.zeros_like(cross)
    add_pairs(near_count, cap, pieces, first_col, (slot0, slot1), ((white0,), (white3,)), incoming, cross)


def late_kernel(near_count, cap, n_pieces, n_white, n_dest, scale, scal, first_col, slot0, slot1, early, t_odd, t_even, *rest):
    whites = rest[: 2 * n_white]
    pieces = rest[2 * n_white : 2 * n_white + n_pieces]
    rest = rest[2 * n_white + n_pieces :]
    own = rest[0]
    outs = rest[1:n_dest]
    incoming, cross, x_odd, x_even = rest[n_dest:]
    cross[...] = early[...]
    add_pairs(
        near_count, cap, pieces, first_col, (slot0, slot1), (whites[0::2], whites[1::2]), incoming, cross
    )
    lane = lax.broadcasted_iota(jnp.int32, (1, QB), 1)
    s = jnp.where(lane % 2 == 0, scale, -scale).astype(F32)
    x_odd[:, :QB] = (cross[:, NF : NF + QB] * s).astype(BF16)
    x_odd[:, QB:] = (cross[:, :QB] * -s).astype(BF16)
    x_even[:, :QB] = (cross[:, QB:NF] * -s).astype(BF16)
    x_even[:, QB:] = (cross[:, NF + QB :] * -s).astype(BF16)
    rows = own.shape[0]
    me = scal[6]
    dims = (((1,), (1,)), ((), ()))
    for d in list(range(1, n_dest)) + [0]:
        at = pl.ds(pl.multiple_of(lax.rem(me + d, n_dest) * rows, rows), rows)
        value = lax.dot_general(t_odd[at, :], x_odd[...], dims, preferred_element_type=F32)
        value = value + lax.dot_general(t_even[at, :], x_even[...], dims, preferred_element_type=F32)
        if d == 0:
            own[...] = value
        else:
            outs[d - 1][...] = value.astype(BF16)


def cost(flops, moved):
    return pl.CostEstimate(flops=int(flops), bytes_accessed=int(moved), transcendentals=0)


def on_device(traces, offsets, pair_first, pair_slot, send_rows):
    stations, block_len = traces.shape
    n_tm = lax.axis_size("tm")
    n_sta = lax.axis_size("sta")
    windows = offsets.shape[0]
    pairs = pair_first.shape[0]
    cap = send_rows.shape[1] // n_sta
    t = lax.axis_index("tm")
    g = lax.axis_index("sta")

    n_chunks = 2
    rows = stations // n_chunks
    down = [(i + 1, i) for i in range(n_tm - 1)]
    back = [(i, i + 1) for i in range(n_tm - 1)]
    rims, tails = [], []
    for i in range(n_chunks):
        piece = traces[i * rows : (i + 1) * rows]
        rims.append(lax.ppermute(piece[:, :HALF], "tm", down))
        tails.append(lax.ppermute(piece[:, block_len - HALF :], "tm", back))
    before = lax.ppermute(offsets, "tm", back)
    has_before = (t > 0).astype(jnp.int32)
    is_last = (t == n_tm - 1).astype(jnp.int32)
    last_before = jnp.where(t > 0, before[2], 2 * STEP)
    early_scal = jnp.stack([offsets[0], offsets[1], offsets[2], offsets[2], is_last, is_last, t])
    scal = jnp.stack([offsets[0], offsets[1], offsets[2], last_before, is_last, has_before, t])

    near = [0, 1, n_sta - 1] if n_sta > 2 else list(range(n_sta))
    far = [d for d in range(n_sta) if d not in near]
    table = send_rows[0].reshape(n_sta, cap)
    near_rows = [lax.dynamic_index_in_dim(table, lax.rem(g + d, n_sta), keepdims=False) for d in near]
    far_rows = [
        lax.dynamic_index_in_dim(table, lax.rem(g + d, n_sta), keepdims=False)[:CAP_FAR] for d in far
    ]
    none = jnp.full((CAP_FAR,), -1, jnp.int32)
    sel0 = jnp.concatenate(near_rows + [x for r in far_rows for x in (r, none)])[:, None]
    sel1 = jnp.concatenate(near_rows + [x for r in far_rows for x in (none, r)])[:, None]
    n_sel = sel0.shape[0]

    distance = lax.rem(g - pair_slot // cap + n_sta, n_sta)
    inside = pair_slot % cap
    place = jnp.zeros_like(pair_slot)
    stride = jnp.zeros_like(pair_slot)
    for i, d in enumerate(near):
        place = jnp.where(distance == d, i * cap + inside, place)
    for i, d in enumerate(far):
        base = len(near) * cap + i * 2 * CAP_FAR
        place = jnp.where(distance == d, base + inside, place)
        stride = jnp.where(distance == d, CAP_FAR, stride)
    slot0 = place[:, None]
    slot1 = (place + stride)[:, None]
    first_col = pair_first[:, None]
    width = -(-n_sel // LANES) * LANES

    cos_t, sin_t = small_tables()
    taper = taper_row()
    buffers = [shape((2 * cap, 2 * NF), BF16)] * len(near) + [shape((2 * CAP_FAR, 2 * NF), BF16)] * len(far)
    dft_flops = 2 * 2 * HALF * 2 * QB * 2
    spectrum = shape((stations, 2 * NF), BF16)
    local = pl.pallas_call(
        functools.partial(local_kernel, len(near), cap, rows),
        out_shape=[shape((HALF, 2 * QB), BF16)] * 2 + [spectrum] * 2 + buffers,
        in_specs=[SMEM] + [VMEM] * 6,
        out_specs=[VMEM] * (4 + len(buffers)),
        scratch_shapes=scratches(rows),
        compiler_params=PARAMS,
        cost_estimate=cost(dft_flops * stations, 8 << 20),
        name="local_windows",
    )(early_scal, traces, cos_t, sin_t, taper, sel0, sel1)
    t_odd, t_even, white0, white3 = local[:4]

    def exchange(pieces):
        got = []
        for d, piece in zip(near + far, pieces):
            if d == 0:
                got.append(piece)
            else:
                route = [(i, (i + d) % n_sta) for i in range(n_sta)]
                got.append(lax.ppermute(piece, "sta", route))
        return got

    early_in = exchange(local[4:])
    early = pl.pallas_call(
        functools.partial(early_kernel, len(near), cap, len(buffers)),
        out_shape=shape((pairs, 2 * NF), F32),
        in_specs=[VMEM] * (5 + len(buffers)),
        out_specs=VMEM,
        scratch_shapes=[pltpu.VMEM((width, 2 * NF), BF16)],
        compiler_params=PARAMS,
        cost_estimate=cost(2 * 2 * pairs * (stations + width) * 2 * NF, 4 << 20),
        name="early_pairs",
    )(first_col, slot0, slot1, white0, white3, *early_in)

    whites = []
    late_out = None
    for i in range(n_chunks):
        last = i == n_chunks - 1
        chunk = shape((rows, 2 * NF), BF16)
        result = pl.pallas_call(
            functools.partial(rim_kernel, i * rows, len(near), cap, i, last),
            out_shape=[chunk] * 2 + (buffers if last else []),
            in_specs=[SMEM] + [VMEM] * (8 + 2 * i),
            out_specs=[VMEM] * (2 + (len(buffers) if last else 0)),
            scratch_shapes=scratches(rows),
            compiler_params=PARAMS,
            cost_estimate=cost(dft_flops * rows, 4 << 20),
            name="rim_windows_%d" % i,
        )(scal, traces, rims[i], tails[i], taper, t_odd, t_even, sel0, sel1, *whites)
        whites = whites + list(result[:2])
        late_out = result[2:]
    late_in = exchange(late_out)

    lag_rows = NL // n_tm
    scale = 1.0 / math.sqrt(NF * windows * n_tm)
    result = pl.pallas_call(
        functools.partial(late_kernel, len(near), cap, len(buffers), n_chunks, n_tm, scale),
        out_shape=[shape((lag_rows, pairs), F32)] + [shape((lag_rows, pairs), BF16)] * (n_tm - 1),
        in_specs=[SMEM] + [VMEM] * (6 + 2 * n_chunks + len(buffers)),
        out_specs=[VMEM] * n_tm,
        scratch_shapes=[
            pltpu.VMEM((width, 2 * NF), BF16),
            pltpu.VMEM((pairs, 2 * NF), F32),
            pltpu.VMEM((pairs, NF), BF16),
            pltpu.VMEM((pairs, NF), BF16),
        ],
        compiler_params=PARAMS,
        cost_estimate=cost(2 * 2 * pairs * (stations + width) * 2 * NF + 2 * NL * pairs * 2 * NF, 6 << 20),
        name="late_pairs",
    )(scal, first_col, slot0, slot1, early, t_odd, t_even, *whites, *late_in)

    total = result[0]
    for d in range(1, n_tm):
        route = [(i, (i + d) % n_tm) for i in range(n_tm)]
        total = total + lax.ppermute(result[d], "tm", route).astype(F32)
    return total


def solution(mesh):
    in_specs = (P("sta", ("day", "tm")), P(("day", "tm")), P("sta"), P("sta"), P("sta", None))
    out_specs = P(("day", "tm"), "sta")
    return jax.shard_map(
        on_device, mesh=mesh, in_specs=in_specs, out_specs=out_specs, check_vma=False
    )
```

time: 257 us -> 140 us (0.54)
  other arithmetic: 88.7 us -> 4.88 us
  Pallas kernels: 0 us -> 72.5 us
  waiting for transfers between devices: 76.1 us -> 21 us
  local copies, waits for them, and re-layouts: 53.7 us -> 13.1 us
  starting transfers between devices: 4.84 us -> 27.3 us
  matrix products: 19.3 us -> 0 us
  between operations: 13.6 us -> 0.81 us
    pallas_call x0 -> x5, Pallas kernels: none -> 72.5 us  [the longest x2 31.7 us: on_device(): pl.pallas_call(functools.partial(rim_kernel, i * rows, len(near), cap, i,...]
    reduce_scatter x1 -> x0, waiting for transfers between devices: 43.3 us -> none  [on_device(): lax.psum_scatter(lax.dot_general(lag_rows, cross_sum, (((1,), (1,)), ((),...]
    gather x16 -> x0, local copies, waits for them, and re-layouts: 32.3 us -> none
    ppermute x1 -> x14, starting transfers between devices: 1.28 us -> 27.3 us  [the longest x2 9.16 us: on_device(): tails.append(lax.ppermute(piece[:, block_len - HALF:], 'tm', back))]
    dot_general x2 -> x0, matrix products: 19.3 us -> none  [the longest x1 10.3 us: on_device(): lax.dot_general(lag_rows, cross_sum, (((1,), (1,)), ((), ())), precision=...]
    another operation x1 -> x0, other arithmetic: 18.3 us -> none
    convert_element_type x2 -> x0, other arithmetic: 17.1 us -> none  [the longest x1 12.6 us: whiten(): (spectrum * jnp.concatenate([inverse, inverse], axis=-1)).astype(jnp.bflo...]
    div x2 -> x0, other arithmetic: 16.7 us -> none  [the longest x1 16.7 us: whiten(): inverse = 1.0 / jnp.maximum(smooth, FLOOR)]
  transfers between devices with their start and end apart: 3 -> 14, of which waited for: 3 -> 2; matrix products, arithmetic and copies ran while one was open for 12% -> 10% of each run, Pallas kernels for 0% -> 47%
where the time goes in v1:
time: 140 us
  Pallas kernels  72.5 us (52%)
  starting transfers between devices  27.3 us (20%)
  waiting for transfers between devices  21 us (15%)
  local copies, waits for them, and re-layouts  13.1 us (9%)
  other arithmetic  4.88 us (3%)
    pallas_call x2, Pallas kernels, on_device(): pl.pallas_call(functools.partial(rim_kernel, i * rows, len(near), cap, i,...  31.7 us
    pallas_call x1, Pallas kernels, on_device(): pl.pallas_call(functools.partial(local_kernel, len(near), cap, rows), out...  27.8 us
    ppermute x3, waiting for transfers between devices, on_device(): total = total + lax.ppermute(result[d], 'tm', route).astype(F32)  21 us
    ppermute x2, starting transfers between devices, on_device(): tails.append(lax.ppermute(piece[:, block_len - HALF:], 'tm', back))  9.16 us
    pallas_call x1, Pallas kernels, on_device(): pl.pallas_call(functools.partial(late_kernel, len(near), cap, len(buffers...  7.51 us
    ppermute x6, starting transfers between devices, exchange(): got.append(lax.ppermute(piece, 'sta', route))  5.81 us
    pallas_call x1, Pallas kernels, on_device(): pl.pallas_call(functools.partial(early_kernel, len(near), cap, len(buffer...  5.51 us
    ppermute x1, starting transfers between devices, on_device(): before = lax.ppermute(offsets, 'tm', back)  5.08 us
  transfers between devices with their start and end apart: 14, of which 2 were waited for; matrix products, arithmetic and copies ran while one was open for 10% of the time, Pallas kernels for 47%

profile of v1, /device:TPU:0, one launch (start us, length us, event | category | flops | bytes accessed | tf_op | source)
XLA Modules:
  0.0 139.6 jit_solution(881709421334653942)
XLA Ops:
  0.0 5.1 %collective-permute-start = (s32[3]{0:T(128)}, s32[3]{0:T(128)S(1)}, u32[]{:S(2)}, u32[]{:S(2)}) collective-permute-start(s32[3]{0:T(128)} %param.6), channel_id=1, source_target_pairs={{0,4},{4,8},{8,12},{1,5},{5,9},{9,13},{2,6},{6,10},{10,14},{3,7},{... | collective-permute-start | bytes 44 | tf_op jit(solution)/shard_map/ppermute | solution.py:354
  5.1 2.7 %fusion.14 = (bf16[256,1024]{1,0:T(8,128)(2,1)S(1)}, bf16[256,1024]{1,0:T(8,128)(2,1)S(1)}, bf16[256,1024]{1,0:T(8,128)(2,1)}, bf16[256,1024]{1,0:T(8,128)(2,1)}) fusion(bf16[512,3072]{1,0:T(8,128)(2,1)} %main.5), kind=kLoop, calls=%fused_computation.42 | loop fusion | bytes 4194304 | tf_op jit(solution)/shard_map/slice | solution.py:353
  7.8 1.3 collective-permute-start.4
  9.0 4.6 %collective-permute-start.5 = (bf16[256,1024]{1,0:T(8,128)(2,1)}, bf16[256,1024]{1,0:T(8,128)(2,1)S(1)}, u32[]{:S(2)}, u32[]{:S(2)}) collective-permute-start(bf16[256,1024]{1,0:T(8,128)(2,1)} %get-tuple-element.49), channel_id=1, source_target_pairs={{0,4},{4,8},{8,12},{1,5},{5,9},{9,13},{2,6},{6,10},{10,14},{3,7},{... | collective-permute-start | bytes 1572872 | tf_op jit(solution)/shard_map/ppermute | solution.py:353
  13.6 1.3 collective-permute-start.6
  14.9 4.6 %collective-permute-start.7 = (bf16[256,1024]{1,0:T(8,128)(2,1)S(1)}, bf16[256,1024]{1,0:T(8,128)(2,1)S(1)}, u32[]{:S(2)}, u32[]{:S(2)}) collective-permute-start(bf16[256,1024]{1,0:T(8,128)(2,1)S(1)} %get-tuple-element.47), channel_id=1, source_target_pairs={{0,4},{4,8},{8,12},{1,5},{5,9},{9,13},{2,6},{6,10},{10,14},{3,7},{... | collective-permute-start | bytes 1572872 | tf_op jit(solution)/shard_map/ppermute | solution.py:353
  20.1 0.6 reduce.3
  21.0 1.3 fusion.3
  23.1 0.7 copy.12.sel0.rest_0_
  23.9 0.7 copy.13.sel1.rest_1_
  24.6 1.3 stack.34.scal
  25.9 0.8 multiply_subtract_fusion.taper
  26.7 27.8 %local_windows.1 = (bf16[1024,512]{1,0:T(8,128)(2,1)}, bf16[1024,512]{1,0:T(8,128)(2,1)}, bf16[512,1024]{1,0:T(8,128)(2,1)}, bf16[512,1024]{1,0:T(8,128)(2,1)}, ...) custom-call(s32[7]{0:T(128)} %stack.34.scal, ...), custom_call_target="tpu_custom_call" | custom-call | flops 2147483648 | bytes 8388608 | tf_op jit(solution)/shard_map/local_windows/pallas_call | solution.py:393
  55.7 0.7 stack.33.scal
  56.4 1.7 %collective-permute-start.2 = (bf16[64,1024]{1,0:T(8,128)(2,1)}, bf16[64,1024]{1,0:T(8,128)(2,1)S(1)}, u32[]{:S(2)}, u32[]{:S(2)}) collective-permute-start(bf16[64,1024]{1,0:T(8,128)(2,1)} %get-tuple-element.29), channel_id=1, source_target_pairs={{0,3},{1,0},{2,1},{3,2},{4,7},{5,4},{6,5},{7,6},{8,11},{9,8},{10,9... | collective-permute-start | bytes 393224 | tf_op jit(solution)/shard_map/ppermute | solution.py:412
  58.1 1.5 %collective-permute-start.3 = (bf16[16,1024]{1,0:T(8,128)(2,1)}, bf16[16,1024]{1,0:T(8,128)(2,1)S(1)}, u32[]{:S(2)}, u32[]{:S(2)}) collective-permute-start(bf16[16,1024]{1,0:T(8,128)(2,1)} %get-tuple-element.30), channel_id=1, source_target_pairs={{0,2},{1,3},{2,0},{3,1},{4,6},{5,7},{6,4},{7,5},{8,10},{9,11},{10,... | collective-permute-start | bytes 98312 | tf_op jit(solution)/shard_map/ppermute | solution.py:412
  59.6 15.5 %rim_windows_0.1 = (bf16[256,1024]{1,0:T(8,128)(2,1)}, bf16[256,1024]{1,0:T(8,128)(2,1)}) custom-call(s32[7]{0:T(128)} %stack.33.scal, bf16[512,3072]{1,0:T(8,128)(2,1)} %main.5, bf16[256,1024]{1,0:T(8,128)(2,1)} %copy-done.2, bf16[256,1024]{1,0:T(8,128)(2,1)} %copy-done.3, f32[1,2048]{1,0:T(1,128)} %multiply_subtract_fusion.taper, ...), custom_call_target="tpu_custom_call" | custom-call | flops 1073741824 | bytes 4194304 | tf_op jit(solution)/shard_map/rim_windows_0/pallas_call | solution.py:432
  75.2 0.8 copy-done
  76.1 16.2 %rim_windows_1.1 = (bf16[256,1024]{1,0:T(8,128)(2,1)}, bf16[256,1024]{1,0:T(8,128)(2,1)}, bf16[64,1024]{1,0:T(8,128)(2,1)}, bf16[64,1024]{1,0:T(8,128)(2,1)}, bf...) custom-call(s32[7]{0:T(128)} %stack.33.scal, bf16[512,3072]{1,0:T(8,128)(2,1)} %main.5, bf16[256,1024]{1,0:T(8,128)(2,1)} %copy-done, ...), custom_call_target="tpu_custom_call" | custom-call | flops 1073741824 | bytes 4194304 | tf_op jit(solution)/shard_map/rim_windows_1/pallas_call | solution.py:432
  92.4 1.7 %collective-permute-start.9 = (bf16[64,1024]{1,0:T(8,128)(2,1)}, bf16[64,1024]{1,0:T(8,128)(2,1)S(1)}, u32[]{:S(2)}, u32[]{:S(2)}) collective-permute-start(bf16[64,1024]{1,0:T(8,128)(2,1)} %get-tuple-element.39), channel_id=1, source_target_pairs={{0,3},{1,0},{2,1},{3,2},{4,7},{5,4},{6,5},{7,6},{8,11},{9,8},{10,9... | collective-permute-start | bytes 393224 | tf_op jit(solution)/shard_map/ppermute | solution.py:412
  94.1 0.9 copy.21.first_col
  95.0 0.9 copy.22.slot0
  95.9 0.9 copy.23.slot1
  96.7 0.8 collective-permute-start.10
  98.2 5.5 %early_pairs.1.early = f32[512,1024]{1,0:T(8,128)} custom-call(s32[512,1]{1,0:T(8,128)} %copy.21.first_col, s32[512,1]{1,0:T(8,128)} %copy.22.slot0, s32[512,1]{1,0:T(8,128)} %copy.23.slot1, bf16[512,1024]{1,0:T(8,128)(2,1)} %get-tuple-element.25.white0, bf16[512,1024]{1,0:T(8,128)(2,1)} %get-tuple-element.26.white3, ...), custom_call_target="tpu_custom_call" | custom-call | flops 1342177280 | bytes 4194304 | tf_op jit(solution)/shard_map/early_pairs/pallas_call | solution.py:416
  104.5 7.5 %late_pairs.1 = (f32[256,512]{1,0:T(8,128)}, bf16[256,512]{1,0:T(8,128)(2,1)}, bf16[256,512]{1,0:T(8,128)(2,1)}, bf16[256,512]{1,0:T(8,128)(2,1)}) custom-call(s32[7]{0:T(128)} %stack.33.scal, s32[512,1]{1,0:T(8,128)} %copy.21.first_col, s32[512,1]{1,0:T(8,128)} %copy.22.slot0, s32[512,1]{1,0:T(8,128)} %copy.23.slot1, f32[512,1024]{1,0:T(8,128)} %early_pairs.1.early, ...), custom_call_target="tpu_custom_call" | custom-call | flops 2415919104 | bytes 6291456 | tf_op jit(solution)/shard_map/late_pairs/pallas_call | solution.py:448
  112.0 1.5 %collective-permute-start.13 = (bf16[256,512]{1,0:T(8,128)(2,1)}, bf16[256,512]{1,0:T(8,128)(2,1)S(1)}, u32[]{:S(2)}, u32[]{:S(2)}) collective-permute-start(bf16[256,512]{1,0:T(8,128)(2,1)} %get-tuple-element.44), channel_id=1, source_target_pairs={{0,12},{4,0},{8,4},{12,8},{1,13},{5,1},{9,5},{13,9},{2,14},{6,2},{... | collective-permute-start | bytes 786440 | tf_op jit(solution)/shard_map/ppermute | solution.py:467
  113.5 1.6 %collective-permute-start.12 = (bf16[256,512]{1,0:T(8,128)(2,1)}, bf16[256,512]{1,0:T(8,128)(2,1)S(1)}, u32[]{:S(2)}, u32[]{:S(2)}) collective-permute-start(bf16[256,512]{1,0:T(8,128)(2,1)} %get-tuple-element.43), channel_id=1, source_target_pairs={{0,8},{4,12},{8,0},{12,4},{1,9},{5,13},{9,1},{13,5},{2,10},{6,14},... | collective-permute-start | bytes 786440 | tf_op jit(solution)/shard_map/ppermute | solution.py:467
  115.0 1.6 %collective-permute-start.11 = (bf16[256,512]{1,0:T(8,128)(2,1)}, bf16[256,512]{1,0:T(8,128)(2,1)S(1)}, u32[]{:S(2)}, u32[]{:S(2)}) collective-permute-start(bf16[256,512]{1,0:T(8,128)(2,1)} %get-tuple-element.42), channel_id=1, source_target_pairs={{0,4},{4,8},{8,12},{12,0},{1,5},{5,9},{9,13},{13,1},{2,6},{6,10},{... | collective-permute-start | bytes 786440 | tf_op jit(solution)/shard_map/ppermute | solution.py:467
  116.7 3.9 %collective-permute-done.13 = bf16[256,512]{1,0:T(8,128)(2,1)S(1)} collective-permute-done((bf16[256,512]{1,0:T(8,128)(2,1)}, bf16[256,512]{1,0:T(8,128)(2,1)S(1)}, u32[]{:S(2)}, u32[]{:S(2)}) %collective-permute-start.13) | collective-permute-done | bytes 262176 | tf_op jit(solution)/shard_map/ppermute | solution.py:467
  120.6 17.1 %collective-permute-done.12 = bf16[256,512]{1,0:T(8,128)(2,1)S(1)} collective-permute-done((bf16[256,512]{1,0:T(8,128)(2,1)}, bf16[256,512]{1,0:T(8,128)(2,1)S(1)}, u32[]{:S(2)}, u32[]{:S(2)}) %collective-permute-start.12) | collective-permute-done | bytes 262176 | tf_op jit(solution)/shard_map/ppermute | solution.py:467
  137.6 2.0 %convert_add_fusion = f32[256,512]{1,0:T(8,128)} fusion(bf16[256,512]{1,0:T(8,128)(2,1)S(1)} %collective-permute-done.13, bf16[256,512]{1,0:T(8,128)(2,1)S(1)} %collective-permute-done.12, f32[256,512]{1,0:T(8,128)} %get-tuple-element.41, bf16[256,512]{1,0:T(8,128)(2,1)S(1)} %collective-permute-done.11), kind=kLoop, calls=%fused_computation | loop fusion | flops 786432 | bytes 1835008 | tf_op jit(solution)/shard_map/add | solution.py:467
  (56 shorter events, 3.9 us)
Async XLA Ops:
  0.0 22.3 %copy-start.9 = (s32[3]{0:T(128)S(1)}, s32[3]{0:T(128)}, u32[]{:S(2)}) copy-start(s32[3]{0:T(128)} %param.6) | copy-start | bytes 40
  0.0 20.1 %copy-start.13 = (s32[1,128]{1,0:T(1,128)S(1)}, s32[1,128]{1,0:T(1,128)}, u32[]{:S(2)}) copy-start(s32[1,128]{1,0:T(1,128)} %param.9) | copy-start | bytes 1540
  0.0 54.5 %collective-permute-start = (s32[3]{0:T(128)}, s32[3]{0:T(128)S(1)}, u32[]{:S(2)}, u32[]{:S(2)}) collective-permute-start(s32[3]{0:T(128)} %param.6), channel_id=1, source_target_pairs={{0,4},{4,8},{8,12},{1,5},{5,9},{9,13},{2,6},{6,10},{10,14},{3,7},{... | collective-permute-start | bytes 44 | tf_op jit(solution)/shard_map/ppermute | solution.py:354
  7.8 48.7 %collective-permute-start.4 = (bf16[256,1024]{1,0:T(8,128)(2,1)}, bf16[256,1024]{1,0:T(8,128)(2,1)S(1)}, u32[]{:S(2)}, u32[]{:S(2)}) collective-permute-start(bf16[256,1024]{1,0:T(8,128)(2,1)} %get-tuple-element.50), channel_id=1, source_target_pairs={{4,0},{8,4},{12,8},{5,1},{9,5},{13,9},{6,2},{10,6},{14,10},{7,3},{... | collective-permute-start | bytes 1572872 | tf_op jit(solution)/shard_map/ppermute | solution.py:352
  9.0 49.1 %collective-permute-start.5 = (bf16[256,1024]{1,0:T(8,128)(2,1)}, bf16[256,1024]{1,0:T(8,128)(2,1)S(1)}, u32[]{:S(2)}, u32[]{:S(2)}) collective-permute-start(bf16[256,1024]{1,0:T(8,128)(2,1)} %get-tuple-element.49), channel_id=1, source_target_pairs={{0,4},{4,8},{8,12},{1,5},{5,9},{9,13},{2,6},{6,10},{10,14},{3,7},{... | collective-permute-start | bytes 1572872 | tf_op jit(solution)/shard_map/ppermute | solution.py:353
  13.6 61.5 %collective-permute-start.6 = (bf16[256,1024]{1,0:T(8,128)(2,1)S(1)}, bf16[256,1024]{1,0:T(8,128)(2,1)S(1)}, u32[]{:S(2)}, u32[]{:S(2)}) collective-permute-start(bf16[256,1024]{1,0:T(8,128)(2,1)S(1)} %get-tuple-element.48), channel_id=1, source_target_pairs={{4,0},{8,4},{12,8},{5,1},{9,5},{13,9},{6,2},{10,6},{14,10},{7,3},{... | collective-permute-start | bytes 1572872 | tf_op jit(solution)/shard_map/ppermute | solution.py:352
  14.9 60.2 %collective-permute-start.7 = (bf16[256,1024]{1,0:T(8,128)(2,1)S(1)}, bf16[256,1024]{1,0:T(8,128)(2,1)S(1)}, u32[]{:S(2)}, u32[]{:S(2)}) collective-permute-start(bf16[256,1024]{1,0:T(8,128)(2,1)S(1)} %get-tuple-element.47), channel_id=1, source_target_pairs={{0,4},{4,8},{8,12},{1,5},{5,9},{9,13},{2,6},{6,10},{10,14},{3,7},{... | collective-permute-start | bytes 1572872 | tf_op jit(solution)/shard_map/ppermute | solution.py:353
  54.5 43.0 %collective-permute-start.1 = (bf16[64,1024]{1,0:T(8,128)(2,1)}, bf16[64,1024]{1,0:T(8,128)(2,1)S(1)}, u32[]{:S(2)}, u32[]{:S(2)}) collective-permute-start(bf16[64,1024]{1,0:T(8,128)(2,1)} %get-tuple-element.28), channel_id=1, source_target_pairs={{0,1},{1,2},{2,3},{3,0},{4,5},{5,6},{6,7},{7,4},{8,9},{9,10},{10,1... | collective-permute-start | bytes 393224 | tf_op jit(solution)/shard_map/ppermute | solution.py:412
  56.4 3.2 %copy-start.2 = (bf16[256,1024]{1,0:T(8,128)(2,1)}, bf16[256,1024]{1,0:T(8,128)(2,1)S(1)}, u32[]{:S(2)}) copy-start(bf16[256,1024]{1,0:T(8,128)(2,1)S(1)} %collective-permute-done.4.rim) | copy-start | bytes 1572868
  56.4 41.1 %collective-permute-start.2 = (bf16[64,1024]{1,0:T(8,128)(2,1)}, bf16[64,1024]{1,0:T(8,128)(2,1)S(1)}, u32[]{:S(2)}, u32[]{:S(2)}) collective-permute-start(bf16[64,1024]{1,0:T(8,128)(2,1)} %get-tuple-element.29), channel_id=1, source_target_pairs={{0,3},{1,0},{2,1},{3,2},{4,7},{5,4},{6,5},{7,6},{8,11},{9,8},{10,9... | collective-permute-start | bytes 393224 | tf_op jit(solution)/shard_map/ppermute | solution.py:412
  58.1 1.5 %copy-start.3 = (bf16[256,1024]{1,0:T(8,128)(2,1)}, bf16[256,1024]{1,0:T(8,128)(2,1)S(1)}, u32[]{:S(2)}) copy-start(bf16[256,1024]{1,0:T(8,128)(2,1)S(1)} %collective-permute-done.5.tail) | copy-start | bytes 1572868
  58.1 38.6 %collective-permute-start.3 = (bf16[16,1024]{1,0:T(8,128)(2,1)}, bf16[16,1024]{1,0:T(8,128)(2,1)S(1)}, u32[]{:S(2)}, u32[]{:S(2)}) collective-permute-start(bf16[16,1024]{1,0:T(8,128)(2,1)} %get-tuple-element.30), channel_id=1, source_target_pairs={{0,2},{1,3},{2,0},{3,1},{4,6},{5,7},{6,4},{7,5},{8,10},{9,11},{10,... | collective-permute-start | bytes 98312 | tf_op jit(solution)/shard_map/ppermute | solution.py:412
  75.1 0.8 copy-start
  75.2 1.0 copy-start.1
  76.1 18.0 %copy-start.8 = (s32[512]{0:T(512)S(1)}, s32[512]{0:T(512)}, u32[]{:S(2)}) copy-start(s32[512]{0:T(512)} %param.8) | copy-start | bytes 6148
  76.1 18.0 %copy-start.7 = (s32[512]{0:T(512)S(1)}, s32[512]{0:T(512)}, u32[]{:S(2)}) copy-start(s32[512]{0:T(512)} %param.7) | copy-start | bytes 6148
  92.4 11.4 %collective-permute-start.8 = (bf16[64,1024]{1,0:T(8,128)(2,1)}, bf16[64,1024]{1,0:T(8,128)(2,1)S(1)}, u32[]{:S(2)}, u32[]{:S(2)}) collective-permute-start(bf16[64,1024]{1,0:T(8,128)(2,1)} %get-tuple-element.38), channel_id=1, source_target_pairs={{0,1},{1,2},{2,3},{3,0},{4,5},{5,6},{6,7},{7,4},{8,9},{9,10},{10,1... | collective-permute-start | bytes 393224 | tf_op jit(solution)/shard_map/ppermute | solution.py:412
  92.4 11.4 %collective-permute-start.9 = (bf16[64,1024]{1,0:T(8,128)(2,1)}, bf16[64,1024]{1,0:T(8,128)(2,1)S(1)}, u32[]{:S(2)}, u32[]{:S(2)}) collective-permute-start(bf16[64,1024]{1,0:T(8,128)(2,1)} %get-tuple-element.39), channel_id=1, source_target_pairs={{0,3},{1,0},{2,1},{3,2},{4,7},{5,4},{6,5},{7,6},{8,11},{9,8},{10,9... | collective-permute-start | bytes 393224 | tf_op jit(solution)/shard_map/ppermute | solution.py:412
  96.7 0.8 copy-start.6
  96.7 7.0 %collective-permute-start.10 = (bf16[16,1024]{1,0:T(8,128)(2,1)}, bf16[16,1024]{1,0:T(8,128)(2,1)S(1)}, u32[]{:S(2)}, u32[]{:S(2)}) collective-permute-start(bf16[16,1024]{1,0:T(8,128)(2,1)} %get-tuple-element.40), channel_id=1, source_target_pairs={{0,2},{1,3},{2,0},{3,1},{4,6},{5,7},{6,4},{7,5},{8,10},{9,11},{10,... | collective-permute-start | bytes 98312 | tf_op jit(solution)/shard_map/ppermute | solution.py:412
  97.5 0.7 copy-start.4
  97.5 0.7 copy-start.5
  103.7 0.6 copy-start.12
  103.8 0.7 copy-start.10
  103.8 0.7 copy-start.11
  112.0 8.6 %collective-permute-start.13 = (bf16[256,512]{1,0:T(8,128)(2,1)}, bf16[256,512]{1,0:T(8,128)(2,1)S(1)}, u32[]{:S(2)}, u32[]{:S(2)}) collective-permute-start(bf16[256,512]{1,0:T(8,128)(2,1)} %get-tuple-element.44), channel_id=1, source_target_pairs={{0,12},{4,0},{8,4},{12,8},{1,13},{5,1},{9,5},{13,9},{2,14},{6,2},{... | collective-permute-start | bytes 786440 | tf_op jit(solution)/shard_map/ppermute | solution.py:467
  113.5 24.2 %collective-permute-start.12 = (bf16[256,512]{1,0:T(8,128)(2,1)}, bf16[256,512]{1,0:T(8,128)(2,1)S(1)}, u32[]{:S(2)}, u32[]{:S(2)}) collective-permute-start(bf16[256,512]{1,0:T(8,128)(2,1)} %get-tuple-element.43), channel_id=1, source_target_pairs={{0,8},{4,12},{8,0},{12,4},{1,9},{5,13},{9,1},{13,5},{2,10},{6,14},... | collective-permute-start | bytes 786440 | tf_op jit(solution)/shard_map/ppermute | solution.py:467
  115.0 22.6 %collective-permute-start.11 = (bf16[256,512]{1,0:T(8,128)(2,1)}, bf16[256,512]{1,0:T(8,128)(2,1)S(1)}, u32[]{:S(2)}, u32[]{:S(2)}) collective-permute-start(bf16[256,512]{1,0:T(8,128)(2,1)} %get-tuple-element.42), channel_id=1, source_target_pairs={{0,4},{4,8},{8,12},{12,0},{1,5},{5,9},{9,13},{13,1},{2,6},{6,10},{... | collective-permute-start | bytes 786440 | tf_op jit(solution)/shard_map/ppermute | solution.py:467

commit v2 on v1

v2 whole, which is shorter than its diff:
```python
import functools
import math

import jax
import jax.numpy as jnp
import numpy as np
from jax import lax
from jax.experimental import pallas as pl
from jax.experimental.pallas import tpu as pltpu
from jax.sharding import PartitionSpec as P

WIN = 2048
NF = 512
NL = 1024
FLOOR = 0.1
STEP = 1024
HALF = 1024
CAP_FAR = 8
LANES = 128
CHUNKS = WIN // LANES
HC = CHUNKS // 2
QB = NF // 2
ROOT = 1.0 / math.sqrt(WIN)
F32 = jnp.float32
BF16 = jnp.bfloat16
ROWS = 16
UNIT = 512
UNROLL = 2
VMEM = pl.BlockSpec(memory_space=pltpu.VMEM)
SMEM = pl.BlockSpec(memory_space=pltpu.SMEM)


def small_tables():
    step = np.arange(32)[:, None]
    half = np.arange(QB)
    freq = np.concatenate([2 * half + 1, 2 * half + 2])[None, :]
    angles = np.concatenate([32 * step, step], axis=0) * freq % WIN * (2.0 * np.pi / WIN)
    return np.cos(angles).astype(np.float32), np.sin(angles).astype(np.float32)


def taper_row():
    index = np.arange(WIN)
    return (0.5 - 0.5 * np.cos(2.0 * np.pi * index / WIN)).astype(np.float32)[None, :]


def fill_tables(cos_ref, sin_ref, odd_ref, even_ref):
    def block(a, carry):
        ca = cos_ref[pl.ds(a, 1), :]
        sa = sin_ref[pl.ds(a, 1), :]
        cb = cos_ref[32:64, :]
        sb = sin_ref[32:64, :]
        c = (ca * cb - sa * sb).astype(BF16)
        s = (-(sa * cb + ca * sb)).astype(BF16)
        rows = pl.ds(pl.multiple_of(a * 32, 32), 32)
        odd_ref[rows, :QB] = c[:, :QB]
        odd_ref[rows, QB:] = s[:, :QB]
        even_ref[rows, :QB] = c[:, QB:]
        even_ref[rows, QB:] = s[:, QB:]
        return carry

    lax.fori_loop(0, HALF // 32, block, 0)


def prepare(pick, start, count, to, taper_ref, scratch):
    turned_ref, rolled_ref, sums_ref, even_ref, odd_ref = scratch[:5]
    q = start // LANES
    s = start % LANES
    shift = (LANES - s) % LANES
    spots, signs = [], []
    for c in range(CHUNKS):
        j = (c - q + CHUNKS) % CHUNKS
        turned_ref[:, c * LANES : (c + 1) * LANES] = taper_ref[
            :, pl.ds(pl.multiple_of(j * LANES, LANES), LANES)
        ]
        if c < HC:
            spots.append(j % HC)
            signs.append(jnp.where(j < HC, 1.0, -1.0).astype(F32))
    keep = lax.broadcasted_iota(jnp.int32, (ROWS, LANES), 1) < LANES - s

    def turn(i, carry):
        rows = pl.ds(pl.multiple_of(i * ROWS, ROWS), ROWS)
        rolled = [pltpu.roll(pick(rows, c).astype(F32), shift, 1) for c in range(CHUNKS)]
        turned = [jnp.where(keep, rolled[c], rolled[(c + 1) % CHUNKS]) for c in range(CHUNKS)]
        for c in range(CHUNKS):
            rolled_ref[c, rows, :] = turned[c].astype(BF16)
        while len(turned) > 1:
            turned = [turned[2 * k] + turned[2 * k + 1] for k in range(len(turned) // 2)]
        sums_ref[rows, :] = turned[0]
        return carry

    lax.fori_loop(0, count // ROWS, turn, 0, unroll=UNROLL)

    def fold(i, carry):
        rows = pl.ds(pl.multiple_of(i * ROWS, ROWS), ROWS)
        put = pl.ds(pl.multiple_of(to + i * ROWS, ROWS), ROWS)
        mean = jnp.sum(sums_ref[rows, :], axis=1, keepdims=True) * (1.0 / WIN)
        for c in range(HC):
            low = rolled_ref[c, rows, :].astype(F32)
            high = rolled_ref[c + HC, rows, :].astype(F32)
            low = ((low - mean) * turned_ref[:, c * LANES : (c + 1) * LANES]).astype(BF16)
            high = (high - mean) * turned_ref[:, (c + HC) * LANES : (c + HC + 1) * LANES]
            high = high.astype(BF16)
            even_ref[spots[c], put, :] = low + high
            odd_ref[spots[c], put, :] = (low - high) * signs[c].astype(BF16)
        return carry

    lax.fori_loop(0, count // ROWS, fold, 0, unroll=UNROLL)


def transform(t_odd, t_even, scratch):
    even_ref, odd_ref, spec = scratch[3:6]
    odd = jnp.concatenate([odd_ref[c] for c in range(HC)], axis=1)
    spec[:, : 2 * QB] = jnp.dot(odd, t_odd[...], preferred_element_type=F32)
    even = jnp.concatenate([even_ref[c] for c in range(HC)], axis=1)
    spec[:, 2 * QB :] = jnp.dot(even, t_even[...], preferred_element_type=F32)


def whiten_rows(first_row, count, live, out_ref, scratch):
    spec_ref = scratch[5]
    lane = lax.broadcasted_iota(jnp.int32, (ROWS, QB), 1)
    not_first = lane > 0
    not_last = lane < QB - 1
    numerator = live * (5.0 * ROOT)

    def up(x):
        return jnp.where(not_first, pltpu.roll(x, 1, 1), 0.0)

    def down(x):
        return jnp.where(not_last, pltpu.roll(x, QB - 1, 1), 0.0)

    def amplitude(re, im):
        power = (re * re + im * im) * (1.0 / WIN) + 1e-06
        return power * lax.rsqrt(power)

    def group(i, carry):
        rows = pl.ds(pl.multiple_of(first_row + i * ROWS, ROWS), ROWS)
        o_re = spec_ref[rows, 0:QB]
        o_im = spec_ref[rows, QB : 2 * QB]
        e_re = spec_ref[rows, 2 * QB : 3 * QB]
        e_im = spec_ref[rows, 3 * QB :]
        odd = amplitude(o_re, o_im)
        even = amplitude(e_re, e_im)
        both = odd + even
        inv_odd = numerator / jnp.maximum(up(both) + both + down(odd), 5.0 * FLOOR)
        inv_even = numerator / jnp.maximum(up(even) + both + down(both), 5.0 * FLOOR)
        to = pl.ds(pl.multiple_of(i * ROWS, ROWS), ROWS)
        out_ref[to, 0:QB] = (o_re * inv_odd).astype(BF16)
        out_ref[to, QB : 2 * QB] = (e_re * inv_even).astype(BF16)
        out_ref[to, 2 * QB : 3 * QB] = (o_im * inv_odd).astype(BF16)
        out_ref[to, 3 * QB :] = (e_im * inv_even).astype(BF16)
        return carry

    lax.fori_loop(0, count // ROWS, group, 0, unroll=2)


def slots(c):
    return c * LANES + lax.broadcasted_iota(jnp.int32, (ROWS, LANES), 1)


def part(ref, offset, rows, c):
    return ref[rows, offset + c * LANES : offset + (c + 1) * LANES].astype(F32)


def shifted_rows(ref, first):
    def get(rows, offset, c):
        at = pl.ds(pl.multiple_of(rows.start + first, ROWS), ROWS)
        return part(ref, offset, at, c)

    return get


def column(row):
    n = row.shape[1]
    return jnp.transpose(jnp.broadcast_to(row.astype(F32), (LANES, n)))


def one_hot(col, width, first=0):
    pieces = []
    for at in range(0, width, LANES):
        lane = lax.broadcasted_iota(jnp.int32, col.shape, 1) + (first + at)
        pieces.append(jnp.where(lane.astype(F32) == col, 1.0, 0.0).astype(BF16))
    hot = pieces[0] if len(pieces) == 1 else jnp.concatenate(pieces, axis=1)
    return hot[:, :width]


def lookup(col, spectra):
    total = None
    at = 0
    for piece in spectra:
        n = piece.shape[0]
        term = jnp.dot(one_hot(col, n, at), piece[...], preferred_element_type=F32)
        total = term if total is None else total + term
        at += n
    return total


def write_rows(send_rows, spectra, near, far, n_sta, cap, refs):
    g = lax.axis_index("sta")
    lane = lax.broadcasted_iota(jnp.int32, (1, n_sta * cap), 1)
    col = column(send_rows[...])
    hots = one_hot(col, sum(p.shape[0] for p in spectra[0]))
    for w in range(2):
        result = None
        at = 0
        for piece in spectra[w]:
            n = piece.shape[0]
            term = jnp.dot(hots[:, at : at + n], piece[...], preferred_element_type=F32)
            result = term if result is None else result + term
            at += n
        refs[-1][w] = result.astype(BF16)
    rows = refs[-1]
    for ref, d in zip(refs, near + far):
        first = pl.multiple_of(lax.rem(g + d, n_sta) * cap, cap)
        for w in range(2):
            if d in far:
                ref[w * ROWS : (w + 1) * ROWS, :] = rows[w, pl.ds(first, ROWS), :]
            else:
                ref[w * cap : (w + 1) * cap, :] = rows[w, pl.ds(first, cap), :]


def scratches(n_sta, cap):
    return [
        pltpu.VMEM((1, WIN), F32),
        pltpu.VMEM((CHUNKS, UNIT, LANES), BF16),
        pltpu.VMEM((UNIT, LANES), F32),
        pltpu.VMEM((HC, UNIT, LANES), BF16),
        pltpu.VMEM((HC, UNIT, LANES), BF16),
        pltpu.VMEM((UNIT, 2 * NF), F32),
        pltpu.VMEM((2, n_sta * cap, 2 * NF), BF16),
    ]


def local_kernel(groups, offsets, main, cos_t, sin_t, taper, send_rows, *rest):
    t_odd, t_even, white0, white3 = rest[:4]
    scratch = rest[-7:]
    sends = rest[4:-7] + (scratch[6],)
    fill_tables(cos_t, sin_t, t_odd, t_even)
    start0 = offsets[0]
    start3 = offsets[2] - 2 * STEP
    live3 = jnp.where(lax.axis_index("tm") == lax.axis_size("tm") - 1, 1.0, 0.0).astype(F32)
    stations = main.shape[0]
    for first in range(0, stations, UNIT):
        count = min(UNIT, stations - first)
        get = shifted_rows(main, first)

        def pick0(rows, c):
            if c >= HC:
                return get(rows, HALF, c - HC)
            return jnp.where(slots(c) >= start0, get(rows, 0, c), get(rows, 2 * HALF, c))

        def pick3(rows, c):
            if c >= HC:
                return jnp.zeros((ROWS, LANES), F32)
            return jnp.where(slots(c) >= start3, get(rows, 2 * HALF, c), 0.0)

        for pick, start, live, white in ((pick0, start0, 1.0, white0), (pick3, start3, live3, white3)):
            prepare(pick, start, count, 0, taper, scratch)
            transform(t_odd, t_even, scratch)
            whiten_rows(0, count, live, white.at[first : first + count], scratch)
    write_rows(send_rows, ((white0,), (white3,)), *groups, sends)


def rim_kernel(groups, first, earlier, last, offsets, before, main, rim, tail, taper, t_odd, t_even, send_rows, *rest):
    older = rest[: 2 * earlier]
    white1, white2 = rest[2 * earlier : 2 * earlier + 2]
    scratch = rest[-7:]
    sends = rest[2 * earlier + 2 : -7] + (scratch[6],)
    count = rim.shape[0]
    t = lax.axis_index("tm")
    start1 = offsets[1]
    start2 = jnp.where(t > 0, before[2] - 2 * STEP, 0)
    live2 = jnp.where(t > 0, 1.0, 0.0).astype(F32)
    get = shifted_rows(main, first)

    def pick1(rows, c):
        if c < HC:
            return get(rows, 2 * HALF, c)
        return jnp.where(slots(c) >= start1, get(rows, HALF, c - HC), part(rim, 0, rows, c - HC))

    def pick2(rows, c):
        if c >= HC:
            return get(rows, 0, c - HC)
        return jnp.where(slots(c) >= start2, part(tail, 0, rows, c), get(rows, HALF, c))

    prepare(pick1, lax.rem(start1, WIN), count, 0, taper, scratch)
    prepare(pick2, start2, count, count, taper, scratch)
    transform(t_odd, t_even, scratch)
    whiten_rows(0, count, 1.0, white1, scratch)
    whiten_rows(count, count, live2, white2, scratch)
    if last:
        write_rows(send_rows, (older[0::2] + (white1,), older[1::2] + (white2,)), *groups, sends)


def add_pairs(groups, pieces, pair_first, pair_slot, spectra, incoming, cross):
    near, far, n_sta, cap = groups
    pairs = pair_first.shape[1]
    width = incoming.shape[1]
    for w in range(2):
        at = 0
        for i, d in enumerate(near + far):
            n = ROWS if d in far else cap
            incoming[w, at : at + n, :] = pieces[i][w * n : (w + 1) * n, :]
            at += n
        if at < width:
            incoming[w, at:, :] = jnp.zeros((width - at, 2 * NF), BF16)
    g = lax.axis_index("sta")
    slot = pair_slot[...]
    distance = (g - slot // cap + n_sta) % n_sta
    place = jnp.zeros_like(slot)
    at = 0
    for d in near + far:
        place = jnp.where(distance == d, at + slot % cap, place)
        at += ROWS if d in far else cap
    first_col = column(pair_first[...])
    slot_col = column(place)
    block = min(pairs, 256)
    for p in range(0, pairs, block):
        hot = one_hot(slot_col[p : p + block], width)
        for w in range(2):
            first = lookup(first_col[p : p + block], spectra[w])
            second = jnp.dot(hot, incoming[w], preferred_element_type=F32)
            a_i, b_i = first[:, :NF], first[:, NF:]
            a_j, b_j = second[:, :NF], second[:, NF:]
            cross[p : p + block, :NF] += a_i * a_j + b_i * b_j
            cross[p : p + block, NF:] += b_i * a_j - a_i * b_j


def early_kernel(groups, n_pieces, pair_first, pair_slot, white0, white3, *rest):
    pieces = rest[:n_pieces]
    cross, incoming = rest[n_pieces:]
    cross[...] = jnp.zeros_like(cross)
    add_pairs(groups, pieces, pair_first, pair_slot, ((white0,), (white3,)), incoming, cross)


def late_kernel(groups, n_pieces, n_white, n_dest, scale, pair_first, pair_slot, early, t_odd, t_even, *rest):
    whites = rest[: 2 * n_white]
    pieces = rest[2 * n_white : 2 * n_white + n_pieces]
    rest = rest[2 * n_white + n_pieces :]
    own = rest[0]
    outs = rest[1:n_dest]
    incoming, cross, x_odd, x_even = rest[n_dest:]
    cross[...] = early[...]
    add_pairs(groups, pieces, pair_first, pair_slot, (whites[0::2], whites[1::2]), incoming, cross)
    lane = lax.broadcasted_iota(jnp.int32, (1, QB), 1)
    s = jnp.where(lane % 2 == 0, scale, -scale).astype(F32)
    x_odd[:, :QB] = (cross[:, NF : NF + QB] * s).astype(BF16)
    x_odd[:, QB:] = (cross[:, :QB] * -s).astype(BF16)
    x_even[:, :QB] = (cross[:, QB:NF] * -s).astype(BF16)
    x_even[:, QB:] = (cross[:, NF + QB :] * -s).astype(BF16)
    rows = own.shape[0]
    me = lax.axis_index("tm")
    dims = (((1,), (1,)), ((), ()))
    for d in list(range(1, n_dest)) + [0]:
        at = pl.ds(pl.multiple_of(lax.rem(me + d, n_dest) * rows, rows), rows)
        value = lax.dot_general(t_odd[at, :], x_odd[...], dims, preferred_element_type=F32)
        value = value + lax.dot_general(t_even[at, :], x_even[...], dims, preferred_element_type=F32)
        if d == 0:
            own[...] = value
        else:
            outs[d - 1][...] = value.astype(BF16)


def in_vmem(*arrays):
    return [pltpu.with_memory_space_constraint(a, pltpu.VMEM) for a in arrays]


def params(mib):
    return pltpu.CompilerParams(vmem_limit_bytes=mib << 20)


def cost(flops, moved):
    return pl.CostEstimate(flops=int(flops), bytes_accessed=int(moved), transcendentals=0)


def on_device(traces, offsets, pair_first, pair_slot, send_rows):
    stations, block_len = traces.shape
    n_tm = lax.axis_size("tm")
    n_sta = lax.axis_size("sta")
    windows = offsets.shape[0]
    pairs = pair_first.shape[0]
    cap = send_rows.shape[1] // n_sta

    n_chunks = 2
    rows = stations // n_chunks
    down = [(i + 1, i) for i in range(n_tm - 1)]
    back = [(i, i + 1) for i in range(n_tm - 1)]
    rims, tails = [], []
    for i in range(n_chunks):
        piece = traces[i * rows : (i + 1) * rows]
        rims.append(lax.ppermute(piece[:, :HALF], "tm", down))
        tails.append(lax.ppermute(piece[:, block_len - HALF :], "tm", back))
    before = lax.ppermute(offsets, "tm", back)

    near = [0, 1, n_sta - 1] if n_sta > 2 else list(range(n_sta))
    far = [d for d in range(n_sta) if d not in near]
    groups = (near, far, n_sta, cap)
    width = -(-(len(near) * cap + len(far) * ROWS) // LANES) * LANES
    first_row, slot_row = pair_first[None, :], pair_slot[None, :]
    cos_t, sin_t = (jnp.asarray(x) for x in small_tables())
    taper = jnp.asarray(taper_row())
    main, = in_vmem(traces)

    buffers = [pltpu.VMEM((2 * (ROWS if d in far else cap), 2 * NF), BF16) for d in near + far]
    dft_flops = 2 * 2 * HALF * 2 * QB * 2
    spectrum = pltpu.VMEM((stations, 2 * NF), BF16)
    table = pltpu.VMEM((HALF, 2 * QB), BF16)
    local = pl.pallas_call(
        functools.partial(local_kernel, groups),
        out_shape=[table] * 2 + [spectrum] * 2 + buffers,
        in_specs=[SMEM] + [VMEM] * 5,
        out_specs=[VMEM] * (4 + len(buffers)),
        scratch_shapes=scratches(n_sta, cap),
        compiler_params=params(14),
        cost_estimate=cost(dft_flops * stations, 8 << 20),
        name="local_windows",
    )(offsets, main, cos_t, sin_t, taper, send_rows)
    t_odd, t_even, white0, white3 = local[:4]

    def exchange(pieces):
        got = []
        for d, piece in zip(near + far, pieces):
            if d == 0:
                got.append(piece)
            else:
                route = [(i, (i + d) % n_sta) for i in range(n_sta)]
                got.append(lax.ppermute(piece, "sta", route))
        return got

    early_in = exchange(local[4:])
    early = pl.pallas_call(
        functools.partial(early_kernel, groups, len(buffers)),
        out_shape=pltpu.VMEM((pairs, 2 * NF), F32),
        in_specs=[VMEM] * (4 + len(buffers)),
        out_specs=VMEM,
        scratch_shapes=[pltpu.VMEM((2, width, 2 * NF), BF16)],
        compiler_params=params(12),
        cost_estimate=cost(2 * 2 * pairs * (stations + width) * 2 * NF, 4 << 20),
        name="early_pairs",
    )(first_row, slot_row, *in_vmem(white0, white3, *early_in))

    whites = []
    late_out = None
    for i in range(n_chunks):
        last = i == n_chunks - 1
        chunk = pltpu.VMEM((rows, 2 * NF), BF16)
        result = pl.pallas_call(
            functools.partial(rim_kernel, groups, i * rows, i, last),
            out_shape=[chunk] * 2 + (buffers if last else []),
            in_specs=[SMEM] * 2 + [VMEM] * (7 + 2 * i),
            out_specs=[VMEM] * (2 + (len(buffers) if last else 0)),
            scratch_shapes=scratches(n_sta, cap),
            compiler_params=params(14),
            cost_estimate=cost(dft_flops * rows, 4 << 20),
            name="rim_windows_%d" % i,
        )(offsets, before, *in_vmem(main, rims[i], tails[i]), taper, *in_vmem(t_odd, t_even), send_rows, *in_vmem(*whites))
        whites = whites + list(result[:2])
        late_out = result[2:]
    late_in = exchange(late_out)

    lag_rows = NL // n_tm
    scale = 1.0 / math.sqrt(NF * windows * n_tm)
    result = pl.pallas_call(
        functools.partial(late_kernel, groups, len(buffers), n_chunks, n_tm, scale),
        out_shape=[pltpu.VMEM((lag_rows, pairs), F32)] + [pltpu.VMEM((lag_rows, pairs), BF16)] * (n_tm - 1),
        in_specs=[VMEM] * (5 + 2 * n_chunks + len(buffers)),
        out_specs=[VMEM] * n_tm,
        scratch_shapes=[
            pltpu.VMEM((2, width, 2 * NF), BF16),
            pltpu.VMEM((pairs, 2 * NF), F32),
            pltpu.VMEM((pairs, NF), BF16),
            pltpu.VMEM((pairs, NF), BF16),
        ],
        compiler_params=params(14),
        cost_estimate=cost(2 * 2 * pairs * (stations + width) * 2 * NF + 2 * NL * pairs * 2 * NF, 6 << 20),
        name="late_pairs",
    )(first_row, slot_row, *in_vmem(early, t_odd, t_even, *whites, *late_in))

    total = result[0]
    for d in range(1, n_tm):
        route = [(i, (i + d) % n_tm) for i in range(n_tm)]
        total = total + lax.ppermute(result[d], "tm", route).astype(F32)
    return total


def solution(mesh):
    in_specs = (P("sta", ("day", "tm")), P(("day", "tm")), P("sta"), P("sta"), P("sta", None))
    out_specs = P(("day", "tm"), "sta")
    return jax.shard_map(
        on_device, mesh=mesh, in_specs=in_specs, out_specs=out_specs, check_vma=False
    )
```

time: 140 us -> 91.7 us (0.66)
  Pallas kernels: 72.5 us -> 38.4 us
  local copies, waits for them, and re-layouts: 13.1 us -> 1.88 us
  other arithmetic: 4.88 us -> 0.93 us
  waiting for transfers between devices: 21 us -> 24.6 us
  starting transfers between devices: 27.3 us -> 25.4 us
    pallas_call x5, Pallas kernels: 72.5 us -> 38.4 us  [the longest x2 16.2 us: on_device(): pl.pallas_call(functools.partial(rim_kernel, groups, i * rows, i, last),...]
    broadcast_in_dim x5 -> x0, local copies, waits for them, and re-layouts: 4.07 us -> none  [the longest x1 0.88 us: on_device(): slot0 = place[:, None]]
    unnamed x29 -> x16, local copies, waits for them, and re-layouts: 2.93 us -> 0.04 us
    ppermute x6, waiting for transfers between devices: 0.02 us -> 2.5 us  [exchange(): got.append(lax.ppermute(piece, 'sta', route))]
    another operation x4 -> x0, local copies, waits for them, and re-layouts: 2.06 us -> none  [the longest x1 1.31 us: on_device(): jnp.stack([offsets[0], offsets[1], offsets[2], offsets[2], is_last, is_la...]
    ppermute x3, starting transfers between devices: 4.67 us -> 3.18 us  [on_device(): total = total + lax.ppermute(result[d], 'tm', route).astype(F32)]
  transfers between devices with their start and end apart: 14 -> 14, of which waited for: 2 -> 3; matrix products, arithmetic and copies ran while one was open for 10% -> 0% of each run, Pallas kernels for 47% -> 38%
where the time goes in v2:
time: 91.7 us; the launch traced here: 91.5 us
  Pallas kernels  38.4 us (42%)
  starting transfers between devices  25.4 us (28%)
  waiting for transfers between devices  24.6 us (27%)
  local copies, waits for them, and re-layouts  1.88 us (2%)
  other arithmetic  0.93 us (1%)
    ppermute x3, waiting for transfers between devices, on_device(): total = total + lax.ppermute(result[d], 'tm', route).astype(F32)  22.1 us
    pallas_call x2, Pallas kernels, on_device(): pl.pallas_call(functools.partial(rim_kernel, groups, i * rows, i, last),...  16.2 us
    pallas_call x1, Pallas kernels, on_device(): pl.pallas_call(functools.partial(local_kernel, groups), out_shape=[table]...  16 us
    ppermute x2, starting transfers between devices, on_device(): tails.append(lax.ppermute(piece[:, block_len - HALF:], 'tm', back))  10.2 us
    ppermute x6, starting transfers between devices, exchange(): got.append(lax.ppermute(piece, 'sta', route))  5.61 us
    ppermute x1, starting transfers between devices, on_device(): before = lax.ppermute(offsets, 'tm', back)  3.86 us
    pallas_call x1, Pallas kernels, on_device(): pl.pallas_call(functools.partial(late_kernel, groups, len(buffers), n_chu...  3.83 us
    ppermute x3, starting transfers between devices, on_device(): total = total + lax.ppermute(result[d], 'tm', route).astype(F32)  3.18 us
  transfers between devices with their start and end apart: 14, of which 3 were waited for; matrix products, arithmetic and copies ran while one was open for 0% of the time, Pallas kernels for 38%

profile of v2, /device:TPU:0, one launch (start us, length us, event | category | flops | bytes accessed | tf_op | source)
XLA Modules:
  0.0 91.5 jit_solution(4256369014627822722)
XLA Ops:
  0.0 1.8 %fusion = (bf16[256,1024]{1,0:T(8,128)(2,1)S(1)}, bf16[256,1024]{1,0:T(8,128)(2,1)S(1)}, bf16[256,1024]{1,0:T(8,128)(2,1)S(1)}, bf16[256,1024]{1,0:T(8,128)(2,1)S(1)}) fusion(bf16[512,3072]{1,0:T(8,128)(2,1)} %main.5), kind=kLoop, calls=%fused_computation.1 | loop fusion | bytes 4194304 | tf_op jit(solution)/shard_map/slice | solution.py:391
  1.9 1.3 %collective-permute-start.4 = (bf16[256,1024]{1,0:T(8,128)(2,1)S(1)}, bf16[256,1024]{1,0:T(8,128)(2,1)S(1)}, u32[]{:S(2)}, u32[]{:S(2)}) collective-permute-start(bf16[256,1024]{1,0:T(8,128)(2,1)S(1)} %get-tuple-element.48), channel_id=1, source_target_pairs={{4,0},{8,4},{12,8},{5,1},{9,5},{13,9},{6,2},{10,6},{14,10},{7,3},{... | collective-permute-start | bytes 1572872 | tf_op jit(solution)/shard_map/ppermute | solution.py:390
  3.2 5.6 %collective-permute-start.5 = (bf16[256,1024]{1,0:T(8,128)(2,1)S(1)}, bf16[256,1024]{1,0:T(8,128)(2,1)S(1)}, u32[]{:S(2)}, u32[]{:S(2)}) collective-permute-start(bf16[256,1024]{1,0:T(8,128)(2,1)S(1)} %get-tuple-element.47), channel_id=1, source_target_pairs={{0,4},{4,8},{8,12},{1,5},{5,9},{9,13},{2,6},{6,10},{10,14},{3,7},{... | collective-permute-start | bytes 1572872 | tf_op jit(solution)/shard_map/ppermute | solution.py:391
  8.8 1.3 %collective-permute-start.6 = (bf16[256,1024]{1,0:T(8,128)(2,1)S(1)}, bf16[256,1024]{1,0:T(8,128)(2,1)S(1)}, u32[]{:S(2)}, u32[]{:S(2)}) collective-permute-start(bf16[256,1024]{1,0:T(8,128)(2,1)S(1)} %get-tuple-element.46), channel_id=1, source_target_pairs={{4,0},{8,4},{12,8},{5,1},{9,5},{13,9},{6,2},{10,6},{14,10},{7,3},{... | collective-permute-start | bytes 1572872 | tf_op jit(solution)/shard_map/ppermute | solution.py:390
  10.1 4.6 %collective-permute-start.7 = (bf16[256,1024]{1,0:T(8,128)(2,1)S(1)}, bf16[256,1024]{1,0:T(8,128)(2,1)S(1)}, u32[]{:S(2)}, u32[]{:S(2)}) collective-permute-start(bf16[256,1024]{1,0:T(8,128)(2,1)S(1)} %get-tuple-element.45), channel_id=1, source_target_pairs={{0,4},{4,8},{8,12},{1,5},{5,9},{9,13},{2,6},{6,10},{10,14},{3,7},{... | collective-permute-start | bytes 1572872 | tf_op jit(solution)/shard_map/ppermute | solution.py:391
  14.7 3.9 %collective-permute-start.3 = (s32[3]{0:T(128)S(1)}, s32[3]{0:T(128)S(1)}, u32[]{:S(2)}, u32[]{:S(2)}) collective-permute-start(s32[3]{0:T(128)S(1)} %copy-done.2), channel_id=1, source_target_pairs={{0,4},{4,8},{8,12},{1,5},{5,9},{9,13},{2,6},{6,10},{10,14},{3,7},{... | collective-permute-start | bytes 44 | tf_op jit(solution)/shard_map/ppermute | solution.py:392
  18.6 16.0 %local_windows.1 = (bf16[1024,512]{1,0:T(8,128)(2,1)S(1)}, bf16[1024,512]{1,0:T(8,128)(2,1)S(1)}, bf16[512,1024]{1,0:T(8,128)(2,1)S(1)}, bf16[512,1024]{1,0:T(8,...) custom-call(s32[3]{0:T(128)S(1)} %copy-done.2, ...), custom_call_target="tpu_custom_call" | custom-call | flops 2147483648 | bytes 8388608 | tf_op jit(solution)/shard_map/local_windows/pallas_call | solution.py:407
  34.6 0.0 collective-permute-done.3.before
  34.6 0.1 collective-permute-start
  34.7 0.0 collective-permute-done.4.rim
  34.7 1.7 %collective-permute-start.1 = (bf16[64,1024]{1,0:T(8,128)(2,1)S(1)}, bf16[64,1024]{1,0:T(8,128)(2,1)S(1)}, u32[]{:S(2)}, u32[]{:S(2)}) collective-permute-start(bf16[64,1024]{1,0:T(8,128)(2,1)S(1)} %get-tuple-element.29), channel_id=1, source_target_pairs={{0,3},{1,0},{2,1},{3,2},{4,7},{5,4},{6,5},{7,6},{8,11},{9,8},{10,9... | collective-permute-start | bytes 393224 | tf_op jit(solution)/shard_map/ppermute | solution.py:426
  36.5 0.0 collective-permute-done.5.tail
  36.5 1.5 %collective-permute-start.2 = (bf16[32,1024]{1,0:T(8,128)(2,1)S(1)}, bf16[32,1024]{1,0:T(8,128)(2,1)S(1)}, u32[]{:S(2)}, u32[]{:S(2)}) collective-permute-start(bf16[32,1024]{1,0:T(8,128)(2,1)S(1)} %get-tuple-element.30), channel_id=1, source_target_pairs={{0,2},{1,3},{2,0},{3,1},{4,6},{5,7},{6,4},{7,5},{8,10},{9,11},{10,... | collective-permute-start | bytes 196616 | tf_op jit(solution)/shard_map/ppermute | solution.py:426
  38.0 7.8 %rim_windows_0.1 = (bf16[256,1024]{1,0:T(8,128)(2,1)S(1)}, bf16[256,1024]{1,0:T(8,128)(2,1)S(1)}) custom-call(s32[3]{0:T(128)S(1)} %copy-done.2, s32[3]{0:T(128)S(1)} %collective-permute-done.3.before, bf16[512,3072]{1,0:T(8,128)(2,1)S(1)} %copy-done, bf16[256,1024]{1,0:T(8,128)(2,1)S(1)} %collective-permute-done.4.rim, ...), custom_call_target="tpu_custom_call" | custom-call | flops 1073741824 | bytes 4194304 | tf_op jit(solution)/shard_map/rim_windows_0/pallas_call | solution.py:446
  45.8 0.0 collective-permute-done.7.tail
  45.8 0.0 copy-start.4
  45.8 0.0 copy-start.5
  45.8 8.4 %rim_windows_1.1 = (bf16[256,1024]{1,0:T(8,128)(2,1)S(1)}, bf16[256,1024]{1,0:T(8,128)(2,1)S(1)}, bf16[64,1024]{1,0:T(8,128)(2,1)S(1)}, bf16[64,1024]{1,0:T(8,12...) custom-call(s32[3]{0:T(128)S(1)} %copy-done.2, s32[3]{0:T(128)S(1)} %collective-permute-done.3.before, ...), custom_call_target="tpu_custom_call" | custom-call | flops 1073741824 | bytes 4194304 | tf_op jit(solution)/shard_map/rim_windows_1/pallas_call | solution.py:446
  54.2 0.1 collective-permute-start.8
  54.2 1.7 %collective-permute-start.9 = (bf16[64,1024]{1,0:T(8,128)(2,1)S(1)}, bf16[64,1024]{1,0:T(8,128)(2,1)S(1)}, u32[]{:S(2)}, u32[]{:S(2)}) collective-permute-start(bf16[64,1024]{1,0:T(8,128)(2,1)S(1)} %get-tuple-element.39), channel_id=1, source_target_pairs={{0,3},{1,0},{2,1},{3,2},{4,7},{5,4},{6,5},{7,6},{8,11},{9,8},{10,9... | collective-permute-start | bytes 393224 | tf_op jit(solution)/shard_map/ppermute | solution.py:426
  56.0 0.0 collective-permute-done.2.rest_3_
  56.0 0.5 collective-permute-start.10
  56.5 0.0 collective-permute-done.rest_1_
  56.5 2.4 %early_pairs.1.early = f32[512,1024]{1,0:T(8,128)S(1)} custom-call(s32[1,512]{1,0:T(1,128)S(1)} %bitcast.2, s32[1,512]{1,0:T(1,128)S(1)} %bitcast.4, bf16[512,1024]{1,0:T(8,128)(2,1)S(1)} %get-tuple-element.25.white0, bf16[512,1024]{1,0:T(8,128)(2,1)S(1)} %get-tuple-element.26.white3, bf16[64,1024]{1,0:T(8,128)(2,1)S(1)} %get-tuple-element.27.rest_0_, ...), custom_call_target="tpu_custom_call" | custom-call | flops 1342177280 | bytes 4194304 | tf_op jit(solution)/shard_map/early_pairs/pallas_call | solution.py:430
  58.9 2.5 %collective-permute-done.10.rest_7_ = bf16[32,1024]{1,0:T(8,128)(2,1)S(1)} collective-permute-done((bf16[32,1024]{1,0:T(8,128)(2,1)S(1)}, bf16[32,1024]{1,0:T(8,128)(2,1)S(1)}, u32[]{:S(2)}, u32[]{:S(2)}) %collective-permute-start.10) | collective-permute-done | bytes 65568 | tf_op jit(solution)/shard_map/ppermute | solution.py:426
  61.4 3.8 %late_pairs.1 = (f32[256,512]{1,0:T(8,128)S(1)}, bf16[256,512]{1,0:T(8,128)(2,1)S(1)}, bf16[256,512]{1,0:T(8,128)(2,1)S(1)}, bf16[256,512]{1,0:T(8,128)(2,1)S(1)}) custom-call(s32[1,512]{1,0:T(1,128)S(1)} %bitcast.3, s32[1,512]{1,0:T(1,128)S(1)} %bitcast.5, f32[512,1024]{1,0:T(8,128)S(1)} %early_pairs.1.early, ...), custom_call_target="tpu_custom_call" | custom-call | flops 2415919104 | bytes 6291456 | tf_op jit(solution)/shard_map/late_pairs/pallas_call | solution.py:462
  65.3 1.3 %collective-permute-start.13 = (bf16[256,512]{1,0:T(8,128)(2,1)S(1)}, bf16[256,512]{1,0:T(8,128)(2,1)S(1)}, u32[]{:S(2)}, u32[]{:S(2)}) collective-permute-start(bf16[256,512]{1,0:T(8,128)(2,1)S(1)} %get-tuple-element.44), channel_id=1, source_target_pairs={{0,12},{4,0},{8,4},{12,8},{1,13},{5,1},{9,5},{13,9},{2,14},{6,2},{... | collective-permute-start | bytes 786440 | tf_op jit(solution)/shard_map/ppermute | solution.py:481
  66.6 1.8 %collective-permute-start.12 = (bf16[256,512]{1,0:T(8,128)(2,1)S(1)}, bf16[256,512]{1,0:T(8,128)(2,1)S(1)}, u32[]{:S(2)}, u32[]{:S(2)}) collective-permute-start(bf16[256,512]{1,0:T(8,128)(2,1)S(1)} %get-tuple-element.43), channel_id=1, source_target_pairs={{0,8},{4,12},{8,0},{12,4},{1,9},{5,13},{9,1},{13,5},{2,10},{6,14},... | collective-permute-start | bytes 786440 | tf_op jit(solution)/shard_map/ppermute | solution.py:481
  68.4 0.0 collective-permute-start.11
  68.4 4.9 %collective-permute-done.13 = bf16[256,512]{1,0:T(8,128)(2,1)S(1)} collective-permute-done((bf16[256,512]{1,0:T(8,128)(2,1)S(1)}, bf16[256,512]{1,0:T(8,128)(2,1)S(1)}, u32[]{:S(2)}, u32[]{:S(2)}) %collective-permute-start.13) | collective-permute-done | bytes 262176 | tf_op jit(solution)/shard_map/ppermute | solution.py:481
  73.4 17.2 %collective-permute-done.12 = bf16[256,512]{1,0:T(8,128)(2,1)S(1)} collective-permute-done((bf16[256,512]{1,0:T(8,128)(2,1)S(1)}, bf16[256,512]{1,0:T(8,128)(2,1)S(1)}, u32[]{:S(2)}, u32[]{:S(2)}) %collective-permute-start.12) | collective-permute-done | bytes 262176 | tf_op jit(solution)/shard_map/ppermute | solution.py:481
  90.6 0.9 %convert_add_fusion = f32[256,512]{1,0:T(8,128)} fusion(bf16[256,512]{1,0:T(8,128)(2,1)S(1)} %collective-permute-done.13, bf16[256,512]{1,0:T(8,128)(2,1)S(1)} %collective-permute-done.12, f32[256,512]{1,0:T(8,128)S(1)} %get-tuple-element.41, bf16[256,512]{1,0:T(8,128)(2,1)S(1)} %collective-permute-done.11), kind=kLoop, calls=%fused_computation | loop fusion | flops 786432 | bytes 1835008 | tf_op jit(solution)/shard_map/add | solution.py:481
  (19 shorter events, 0.0 us)
Async XLA Ops:
  0.0 18.6 %copy-start.6 = (f32[64,512]{1,0:T(8,128)S(1)}, f32[64,512]{1,0:T(8,128)}, u32[]{:S(2)}) copy-start(f32[64,512]{1,0:T(8,128)} %constant.6.clone.cos_t) | copy-start | bytes 393220
  0.0 18.6 %copy-start.7 = (f32[64,512]{1,0:T(8,128)S(1)}, f32[64,512]{1,0:T(8,128)}, u32[]{:S(2)}) copy-start(f32[64,512]{1,0:T(8,128)} %constant.7.clone.sin_t) | copy-start | bytes 393220
  0.0 18.6 %copy-start.1 = (f32[1,2048]{1,0:T(1,128)S(1)}, f32[1,2048]{1,0:T(1,128)}, u32[]{:S(2)}) copy-start(f32[1,2048]{1,0:T(1,128)} %constant.8.clone.taper) | copy-start | bytes 24580
  0.0 18.6 %copy-start = (bf16[512,3072]{1,0:T(8,128)(2,1)S(1)}, bf16[512,3072]{1,0:T(8,128)(2,1)}, u32[]{:S(2)}) copy-start(bf16[512,3072]{1,0:T(8,128)(2,1)} %main.5) | copy-start | bytes 9437188
  0.0 14.7 %copy-start.2 = (s32[3]{0:T(128)S(1)}, s32[3]{0:T(128)}, u32[]{:S(2)}) copy-start(s32[3]{0:T(128)} %offsets.5) | copy-start | bytes 40
  0.0 18.6 %copy-start.3 = (s32[1,128]{1,0:T(1,128)S(1)}, s32[1,128]{1,0:T(1,128)}, u32[]{:S(2)}) copy-start(s32[1,128]{1,0:T(1,128)} %send_rows.5) | copy-start | bytes 1540
  1.9 32.8 %collective-permute-start.4 = (bf16[256,1024]{1,0:T(8,128)(2,1)S(1)}, bf16[256,1024]{1,0:T(8,128)(2,1)S(1)}, u32[]{:S(2)}, u32[]{:S(2)}) collective-permute-start(bf16[256,1024]{1,0:T(8,128)(2,1)S(1)} %get-tuple-element.48), channel_id=1, source_target_pairs={{4,0},{8,4},{12,8},{5,1},{9,5},{13,9},{6,2},{10,6},{14,10},{7,3},{... | collective-permute-start | bytes 1572872 | tf_op jit(solution)/shard_map/ppermute | solution.py:390
  3.2 33.3 %collective-permute-start.5 = (bf16[256,1024]{1,0:T(8,128)(2,1)S(1)}, bf16[256,1024]{1,0:T(8,128)(2,1)S(1)}, u32[]{:S(2)}, u32[]{:S(2)}) collective-permute-start(bf16[256,1024]{1,0:T(8,128)(2,1)S(1)} %get-tuple-element.47), channel_id=1, source_target_pairs={{0,4},{4,8},{8,12},{1,5},{5,9},{9,13},{2,6},{6,10},{10,14},{3,7},{... | collective-permute-start | bytes 1572872 | tf_op jit(solution)/shard_map/ppermute | solution.py:391
  8.8 37.0 %collective-permute-start.6 = (bf16[256,1024]{1,0:T(8,128)(2,1)S(1)}, bf16[256,1024]{1,0:T(8,128)(2,1)S(1)}, u32[]{:S(2)}, u32[]{:S(2)}) collective-permute-start(bf16[256,1024]{1,0:T(8,128)(2,1)S(1)} %get-tuple-element.46), channel_id=1, source_target_pairs={{4,0},{8,4},{12,8},{5,1},{9,5},{13,9},{6,2},{10,6},{14,10},{7,3},{... | collective-permute-start | bytes 1572872 | tf_op jit(solution)/shard_map/ppermute | solution.py:390
  10.1 35.7 %collective-permute-start.7 = (bf16[256,1024]{1,0:T(8,128)(2,1)S(1)}, bf16[256,1024]{1,0:T(8,128)(2,1)S(1)}, u32[]{:S(2)}, u32[]{:S(2)}) collective-permute-start(bf16[256,1024]{1,0:T(8,128)(2,1)S(1)} %get-tuple-element.45), channel_id=1, source_target_pairs={{0,4},{4,8},{8,12},{1,5},{5,9},{9,13},{2,6},{6,10},{10,14},{3,7},{... | collective-permute-start | bytes 1572872 | tf_op jit(solution)/shard_map/ppermute | solution.py:391
  14.7 19.9 %collective-permute-start.3 = (s32[3]{0:T(128)S(1)}, s32[3]{0:T(128)S(1)}, u32[]{:S(2)}, u32[]{:S(2)}) collective-permute-start(s32[3]{0:T(128)S(1)} %copy-done.2), channel_id=1, source_target_pairs={{0,4},{4,8},{8,12},{1,5},{5,9},{9,13},{2,6},{6,10},{10,14},{3,7},{... | collective-permute-start | bytes 44 | tf_op jit(solution)/shard_map/ppermute | solution.py:392
  34.6 21.9 %collective-permute-start = (bf16[64,1024]{1,0:T(8,128)(2,1)S(1)}, bf16[64,1024]{1,0:T(8,128)(2,1)S(1)}, u32[]{:S(2)}, u32[]{:S(2)}) collective-permute-start(bf16[64,1024]{1,0:T(8,128)(2,1)S(1)} %get-tuple-element.28), channel_id=1, source_target_pairs={{0,1},{1,2},{2,3},{3,0},{4,5},{5,6},{6,7},{7,4},{8,9},{9,10},{10,1... | collective-permute-start | bytes 393224 | tf_op jit(solution)/shard_map/ppermute | solution.py:426
  34.7 21.8 %collective-permute-start.1 = (bf16[64,1024]{1,0:T(8,128)(2,1)S(1)}, bf16[64,1024]{1,0:T(8,128)(2,1)S(1)}, u32[]{:S(2)}, u32[]{:S(2)}) collective-permute-start(bf16[64,1024]{1,0:T(8,128)(2,1)S(1)} %get-tuple-element.29), channel_id=1, source_target_pairs={{0,3},{1,0},{2,1},{3,2},{4,7},{5,4},{6,5},{7,6},{8,11},{9,8},{10,9... | collective-permute-start | bytes 393224 | tf_op jit(solution)/shard_map/ppermute | solution.py:426
  36.5 19.5 %collective-permute-start.2 = (bf16[32,1024]{1,0:T(8,128)(2,1)S(1)}, bf16[32,1024]{1,0:T(8,128)(2,1)S(1)}, u32[]{:S(2)}, u32[]{:S(2)}) collective-permute-start(bf16[32,1024]{1,0:T(8,128)(2,1)S(1)} %get-tuple-element.30), channel_id=1, source_target_pairs={{0,2},{1,3},{2,0},{3,1},{4,6},{5,7},{6,4},{7,5},{8,10},{9,11},{10,... | collective-permute-start | bytes 196616 | tf_op jit(solution)/shard_map/ppermute | solution.py:426
  45.8 10.7 %copy-start.4 = (s32[512]{0:T(512)S(1)}, s32[512]{0:T(512)}, u32[]{:S(2)}) copy-start(s32[512]{0:T(512)} %param.10) | copy-start | bytes 6148
  45.8 10.7 %copy-start.5 = (s32[512]{0:T(512)S(1)}, s32[512]{0:T(512)}, u32[]{:S(2)}) copy-start(s32[512]{0:T(512)} %param.11) | copy-start | bytes 6148
  54.2 7.3 %collective-permute-start.8 = (bf16[64,1024]{1,0:T(8,128)(2,1)S(1)}, bf16[64,1024]{1,0:T(8,128)(2,1)S(1)}, u32[]{:S(2)}, u32[]{:S(2)}) collective-permute-start(bf16[64,1024]{1,0:T(8,128)(2,1)S(1)} %get-tuple-element.38), channel_id=1, source_target_pairs={{0,1},{1,2},{2,3},{3,0},{4,5},{5,6},{6,7},{7,4},{8,9},{9,10},{10,1... | collective-permute-start | bytes 393224 | tf_op jit(solution)/shard_map/ppermute | solution.py:426
  54.2 7.2 %collective-permute-start.9 = (bf16[64,1024]{1,0:T(8,128)(2,1)S(1)}, bf16[64,1024]{1,0:T(8,128)(2,1)S(1)}, u32[]{:S(2)}, u32[]{:S(2)}) collective-permute-start(bf16[64,1024]{1,0:T(8,128)(2,1)S(1)} %get-tuple-element.39), channel_id=1, source_target_pairs={{0,3},{1,0},{2,1},{3,2},{4,7},{5,4},{6,5},{7,6},{8,11},{9,8},{10,9... | collective-permute-start | bytes 393224 | tf_op jit(solution)/shard_map/ppermute | solution.py:426
  56.0 5.5 %collective-permute-start.10 = (bf16[32,1024]{1,0:T(8,128)(2,1)S(1)}, bf16[32,1024]{1,0:T(8,128)(2,1)S(1)}, u32[]{:S(2)}, u32[]{:S(2)}) collective-permute-start(bf16[32,1024]{1,0:T(8,128)(2,1)S(1)} %get-tuple-element.40), channel_id=1, source_target_pairs={{0,2},{1,3},{2,0},{3,1},{4,6},{5,7},{6,4},{7,5},{8,10},{9,11},{10,... | collective-permute-start | bytes 196616 | tf_op jit(solution)/shard_map/ppermute | solution.py:426
  65.3 8.1 %collective-permute-start.13 = (bf16[256,512]{1,0:T(8,128)(2,1)S(1)}, bf16[256,512]{1,0:T(8,128)(2,1)S(1)}, u32[]{:S(2)}, u32[]{:S(2)}) collective-permute-start(bf16[256,512]{1,0:T(8,128)(2,1)S(1)} %get-tuple-element.44), channel_id=1, source_target_pairs={{0,12},{4,0},{8,4},{12,8},{1,13},{5,1},{9,5},{13,9},{2,14},{6,2},{... | collective-permute-start | bytes 786440 | tf_op jit(solution)/shard_map/ppermute | solution.py:481
  66.6 24.0 %collective-permute-start.12 = (bf16[256,512]{1,0:T(8,128)(2,1)S(1)}, bf16[256,512]{1,0:T(8,128)(2,1)S(1)}, u32[]{:S(2)}, u32[]{:S(2)}) collective-permute-start(bf16[256,512]{1,0:T(8,128)(2,1)S(1)} %get-tuple-element.43), channel_id=1, source_target_pairs={{0,8},{4,12},{8,0},{12,4},{1,9},{5,13},{9,1},{13,5},{2,10},{6,14},... | collective-permute-start | bytes 786440 | tf_op jit(solution)/shard_map/ppermute | solution.py:481
  68.4 22.1 %collective-permute-start.11 = (bf16[256,512]{1,0:T(8,128)(2,1)S(1)}, bf16[256,512]{1,0:T(8,128)(2,1)S(1)}, u32[]{:S(2)}, u32[]{:S(2)}) collective-permute-start(bf16[256,512]{1,0:T(8,128)(2,1)S(1)} %get-tuple-element.42), channel_id=1, source_target_pairs={{0,4},{4,8},{8,12},{12,0},{1,5},{5,9},{9,13},{13,1},{2,6},{6,10},{... | collective-permute-start | bytes 786440 | tf_op jit(solution)/shard_map/ppermute | solution.py:481

commit v3 on v2

--- a/solution.py
+++ b/solution.py
@@ -25,7 +25,9 @@
 BF16 = jnp.bfloat16
 ROWS = 16
 UNIT = 512
-UNROLL = 2
+TURN_UNROLL = 4
+FOLD_UNROLL = 4
+WHITEN_UNROLL = 8
 VMEM = pl.BlockSpec(memory_space=pltpu.VMEM)
 SMEM = pl.BlockSpec(memory_space=pltpu.SMEM)
 
@@ -82,21 +84,29 @@
         rolled = [pltpu.roll(pick(rows, c).astype(F32), shift, 1) for c in range(CHUNKS)]
         turned = [jnp.where(keep, rolled[c], rolled[(c + 1) % CHUNKS]) for c in range(CHUNKS)]
         for c in range(CHUNKS):
-            rolled_ref[c, rows, :] = turned[c].astype(BF16)
+            rolled_ref[c, rows, :] = turned[c]
         while len(turned) > 1:
             turned = [turned[2 * k] + turned[2 * k + 1] for k in range(len(turned) // 2)]
         sums_ref[rows, :] = turned[0]
         return carry
 
-    lax.fori_loop(0, count // ROWS, turn, 0, unroll=UNROLL)
+    lax.fori_loop(0, count // ROWS, turn, 0, unroll=TURN_UNROLL)
+
+    def average(i, carry):
+        rows = pl.ds(pl.multiple_of(i * 8 * ROWS, ROWS), 8 * ROWS)
+        mean = jnp.sum(sums_ref[rows, :], axis=1, keepdims=True) * (1.0 / WIN)
+        sums_ref[rows, :] = jnp.broadcast_to(mean, (8 * ROWS, LANES))
+        return carry
+
+    lax.fori_loop(0, count // (8 * ROWS), average, 0)
 
     def fold(i, carry):
         rows = pl.ds(pl.multiple_of(i * ROWS, ROWS), ROWS)
         put = pl.ds(pl.multiple_of(to + i * ROWS, ROWS), ROWS)
-        mean = jnp.sum(sums_ref[rows, :], axis=1, keepdims=True) * (1.0 / WIN)
+        mean = sums_ref[rows, :]
         for c in range(HC):
-            low = rolled_ref[c, rows, :].astype(F32)
-            high = rolled_ref[c + HC, rows, :].astype(F32)
+            low = rolled_ref[c, rows, :]
+            high = rolled_ref[c + HC, rows, :]
             low = ((low - mean) * turned_ref[:, c * LANES : (c + 1) * LANES]).astype(BF16)
             high = (high - mean) * turned_ref[:, (c + HC) * LANES : (c + HC + 1) * LANES]
             high = high.astype(BF16)
@@ -104,7 +114,7 @@
             odd_ref[spots[c], put, :] = (low - high) * signs[c].astype(BF16)
         return carry
 
-    lax.fori_loop(0, count // ROWS, fold, 0, unroll=UNROLL)
+    lax.fori_loop(0, count // ROWS, fold, 0, unroll=FOLD_UNROLL)
 
 
 def transform(t_odd, t_even, scratch):
@@ -150,7 +160,7 @@
         out_ref[to, 3 * QB :] = (e_im * inv_even).astype(BF16)
         return carry
 
-    lax.fori_loop(0, count // ROWS, group, 0, unroll=2)
+    lax.fori_loop(0, count // ROWS, group, 0, unroll=WHITEN_UNROLL)
 
 
 def slots(c):
@@ -221,7 +231,7 @@
 def scratches(n_sta, cap):
     return [
         pltpu.VMEM((1, WIN), F32),
-        pltpu.VMEM((CHUNKS, UNIT, LANES), BF16),
+        pltpu.VMEM((CHUNKS, UNIT, LANES), F32),
         pltpu.VMEM((UNIT, LANES), F32),
         pltpu.VMEM((HC, UNIT, LANES), BF16),
         pltpu.VMEM((HC, UNIT, LANES), BF16),
@@ -260,35 +270,76 @@
     write_rows(send_rows, ((white0,), (white3,)), *groups, sends)
 
 
-def rim_kernel(groups, first, earlier, last, offsets, before, main, rim, tail, taper, t_odd, t_even, send_rows, *rest):
+def swap_routes(n):
+    routes = []
+    for first in (0, 1):
+        partner = list(range(n))
+        for i in range(first, n - 1, 2):
+            partner[i], partner[i + 1] = i + 1, i
+        routes.append(list(enumerate(partner)))
+    return routes
+
+
+def pack_kernel(rows, offsets, main, *outs):
+    t = lax.axis_index("tm")
+    n = lax.axis_size("tm")
+    start = offsets[2] - 2 * STEP
+    high, low = start // 8, start % 8
+    lane = lax.broadcasted_iota(jnp.int32, (ROWS, HALF), 1)
+    for i, out in enumerate(outs):
+        chunk, swap = i // 2, i % 2
+        at = jnp.where(t % 2 == swap, 2 * HALF, 0)
+        lanes = pl.ds(pl.multiple_of(at, LANES), HALF)
+        alone = n % 2 != swap
+        keep = jnp.where(t == n - 1, 0.0, 1.0).astype(BF16) if alone else None
+        for r in range(0, rows, 64):
+            value = main[chunk * rows + r : chunk * rows + r + 64, lanes]
+            out[r : r + 64, :] = value if keep is None else value * keep
+        if chunk == 0:
+            out[rows:, :] = jnp.where(lane < NF, high, low).astype(F32).astype(BF16)
+
+
+def sent_start(ref, rows):
+    high = jnp.max(ref[rows:, 0:LANES].astype(F32))
+    low = jnp.max(ref[rows:, HALF - LANES :].astype(F32))
+    return (high * 8.0 + low).astype(jnp.int32)
+
+
+def rim_kernel(groups, first, earlier, last, offsets, main, *rest):
+    recv = rest[:2]
+    heads = rest[2:4] if earlier else recv
+    rest = rest[2 + 2 * earlier :]
+    taper, t_odd, t_even, send_rows = rest[:4]
+    rest = rest[4:]
     older = rest[: 2 * earlier]
-    white1, white2 = rest[2 * earlier : 2 * earlier + 2]
+    whites = rest[2 * earlier : 2 * earlier + 2]
     scratch = rest[-7:]
     sends = rest[2 * earlier + 2 : -7] + (scratch[6],)
-    count = rim.shape[0]
+    count = whites[0].shape[0]
     t = lax.axis_index("tm")
-    start1 = offsets[1]
-    start2 = jnp.where(t > 0, before[2] - 2 * STEP, 0)
-    live2 = jnp.where(t > 0, 1.0, 0.0).astype(F32)
-    get = shifted_rows(main, first)
-
-    def pick1(rows, c):
-        if c < HC:
-            return get(rows, 2 * HALF, c)
-        return jnp.where(slots(c) >= start1, get(rows, HALF, c - HC), part(rim, 0, rows, c - HC))
-
-    def pick2(rows, c):
-        if c >= HC:
-            return get(rows, 0, c - HC)
-        return jnp.where(slots(c) >= start2, part(tail, 0, rows, c), get(rows, HALF, c))
-
-    prepare(pick1, lax.rem(start1, WIN), count, 0, taper, scratch)
-    prepare(pick2, start2, count, count, taper, scratch)
+    lane = lax.broadcasted_iota(jnp.int32, (ROWS, LANES), 1)
+    for swap in range(2):
+        ahead = t % 2 == swap
+        start = jnp.where(ahead, offsets[1] - STEP, sent_start(heads[swap], count))
+        sign = jnp.where(ahead, 1, -1)
+        least = jnp.where(ahead, 0, 1)
+        whole = jnp.where(ahead, 2 * HALF, 0)
+        base = (lane - start) * sign
+
+        def pick(rows, c):
+            at = pl.ds(pl.multiple_of(rows.start + first, ROWS), ROWS)
+            if c >= HC:
+                return main[at, pl.ds(pl.multiple_of(whole + (c - HC) * LANES, LANES), LANES)].astype(F32)
+            own = part(main, HALF, at, c)
+            return jnp.where(base >= least - sign * (c * LANES), own, part(recv[swap], 0, rows, c))
+
+        prepare(pick, start, count, swap * count, taper, scratch)
     transform(t_odd, t_even, scratch)
-    whiten_rows(0, count, 1.0, white1, scratch)
-    whiten_rows(count, count, live2, white2, scratch)
+    live = jnp.where(t > 0, 1.0, 0.0).astype(F32)
+    whiten_rows(0, count, 1.0, whites[0], scratch)
+    whiten_rows(count, count, live, whites[1], scratch)
     if last:
-        write_rows(send_rows, (older[0::2] + (white1,), older[1::2] + (white2,)), *groups, sends)
+        write_rows(send_rows, (older[0::2] + whites[:1], older[1::2] + whites[1:]), *groups, sends)
 
 
 def add_pairs(groups, pieces, pair_first, pair_slot, spectra, incoming, cross):
@@ -382,14 +433,20 @@
 
     n_chunks = 2
     rows = stations // n_chunks
-    down = [(i + 1, i) for i in range(n_tm - 1)]
-    back = [(i, i + 1) for i in range(n_tm - 1)]
-    rims, tails = [], []
-    for i in range(n_chunks):
-        piece = traces[i * rows : (i + 1) * rows]
-        rims.append(lax.ppermute(piece[:, :HALF], "tm", down))
-        tails.append(lax.ppermute(piece[:, block_len - HALF :], "tm", back))
-    before = lax.ppermute(offsets, "tm", back)
+    main, = in_vmem(traces)
+    routes = swap_routes(n_tm)
+    packed = pl.pallas_call(
+        functools.partial(pack_kernel, rows),
+        out_shape=[
+            pltpu.VMEM((rows + (ROWS if i < 2 else 0), HALF), BF16) for i in range(2 * n_chunks)
+        ],
+        in_specs=[SMEM, VMEM],
+        out_specs=[VMEM] * (2 * n_chunks),
+        compiler_params=params(1),
+        cost_estimate=cost(0, 4 << 20),
+        name="pack_edges",
+    )(offsets, main)
+    edges = [lax.ppermute(x, "tm", routes[i % 2]) for i, x in enumerate(packed)]
 
     near = [0, 1, n_sta - 1] if n_sta > 2 else list(range(n_sta))
     far = [d for d in range(n_sta) if d not in near]
@@ -398,7 +455,6 @@
     first_row, slot_row = pair_first[None, :], pair_slot[None, :]
     cos_t, sin_t = (jnp.asarray(x) for x in small_tables())
     taper = jnp.asarray(taper_row())
-    main, = in_vmem(traces)
 
     buffers = [pltpu.VMEM((2 * (ROWS if d in far else cap), 2 * NF), BF16) for d in near + far]
     dft_flops = 2 * 2 * HALF * 2 * QB * 2
@@ -410,7 +466,7 @@
         in_specs=[SMEM] + [VMEM] * 5,
         out_specs=[VMEM] * (4 + len(buffers)),
         scratch_shapes=scratches(n_sta, cap),
-        compiler_params=params(14),
+        compiler_params=params(18),
         cost_estimate=cost(dft_flops * stations, 8 << 20),
         name="local_windows",
     )(offsets, main, cos_t, sin_t, taper, send_rows)
@@ -446,13 +502,20 @@
         result = pl.pallas_call(
             functools.partial(rim_kernel, groups, i * rows, i, last),
             out_shape=[chunk] * 2 + (buffers if last else []),
-            in_specs=[SMEM] * 2 + [VMEM] * (7 + 2 * i),
+            in_specs=[SMEM] + [VMEM] * (7 + 4 * i),
             out_specs=[VMEM] * (2 + (len(buffers) if last else 0)),
             scratch_shapes=scratches(n_sta, cap),
-            compiler_params=params(14),
+            compiler_params=params(18),
             cost_estimate=cost(dft_flops * rows, 4 << 20),
             name="rim_windows_%d" % i,
-        )(offsets, before, *in_vmem(main, rims[i], tails[i]), taper, *in_vmem(t_odd, t_even), send_rows, *in_vmem(*whites))
+        )(
+            offsets,
+            *in_vmem(main, *edges[2 * i : 2 * i + 2], *(edges[:2] * i)),
+            taper,
+            *in_vmem(t_odd, t_even),
+            send_rows,
+            *in_vmem(*whites),
+        )
         whites = whites + list(result[:2])
         late_out = result[2:]
     late_in = exchange(late_out)
@@ -470,7 +533,7 @@
             pltpu.VMEM((pairs, NF), BF16),
             pltpu.VMEM((pairs, NF), BF16),
         ],
-        compiler_params=params(14),
+        compiler_params=params(18),
         cost_estimate=cost(2 * 2 * pairs * (stations + width) * 2 * NF + 2 * NL * pairs * 2 * NF, 6 << 20),
         name="late_pairs",
     )(first_row, slot_row, *in_vmem(early, t_odd, t_even, *whites, *late_in))

time: 91.7 us -> 76.8 us (0.84)
  the two profiles are of different devices: /device:TPU:0 before, /device:TPU:9 now
where the time goes in v3:
time: 76.8 us; the launch traced here: 76.6 us
  Pallas kernels  29 us (38%)
  waiting for transfers between devices  25.3 us (33%)
  starting transfers between devices  15.5 us (20%)
  local copies, waits for them, and re-layouts  5.68 us (7%)
  other arithmetic  0.92 us (1%)
    ppermute x3, waiting for transfers between devices, on_device(): total = total + lax.ppermute(result[d], 'tm', route).astype(F32)  23.2 us
    pallas_call x2, Pallas kernels, on_device(): pl.pallas_call(functools.partial(rim_kernel, groups, i * rows, i, last),...  11.5 us
    pallas_call x1, Pallas kernels, on_device(): pl.pallas_call(functools.partial(local_kernel, groups), out_shape=[table]...  10.7 us
    ppermute x4, starting transfers between devices, on_device(): edges = [lax.ppermute(x, 'tm', routes[i % 2]) for i, x in enumerate(packed)]  6.54 us
    ppermute x6, starting transfers between devices, exchange(): got.append(lax.ppermute(piece, 'sta', route))  5.94 us
    unnamed x20, local copies, waits for them, and re-layouts  5.68 us
    pallas_call x1, Pallas kernels, on_device(): pl.pallas_call(functools.partial(late_kernel, groups, len(buffers), n_chu...  3.77 us
    ppermute x3, starting transfers between devices, on_device(): total = total + lax.ppermute(result[d], 'tm', route).astype(F32)  3.05 us
  transfers between devices with their start and end apart: 13, of which 5 were waited for; matrix products, arithmetic and copies ran while one was open for 0% of the time, Pallas kernels for 32%

profile of v3, /device:TPU:9, one launch (start us, length us, event | category | flops | bytes accessed | tf_op | source)
XLA Modules:
  0.0 76.6 jit_solution(13123978776065880983)
XLA Ops:
  0.0 1.9 %copy-done = bf16[512,3072]{1,0:T(8,128)(2,1)S(1)} copy-done((bf16[512,3072]{1,0:T(8,128)(2,1)S(1)}, bf16[512,3072]{1,0:T(8,128)(2,1)}, u32[]{:S(2)}) %copy-start) | copy-done | bytes 3145752
  1.9 0.7 copy-done.3
  2.6 0.7 pack_edges.1
  3.3 0.1 collective-permute-start.3
  3.3 4.5 %collective-permute-start.4 = (bf16[272,1024]{1,0:T(8,128)(2,1)S(1)}, bf16[272,1024]{1,0:T(8,128)(2,1)S(1)}, u32[]{:S(2)}, u32[]{:S(2)}) collective-permute-start(bf16[272,1024]{1,0:T(8,128)(2,1)S(1)} %get-tuple-element.38), channel_id=1, source_target_pairs={{0,0},{4,8},{8,4},{12,12},{1,1},{5,9},{9,5},{13,13},{2,2},{6,10},{... | collective-permute-start | bytes 1671176 | tf_op jit(solution)/shard_map/ppermute | solution.py:449
  7.8 0.1 collective-permute-start.5
  7.9 1.9 %collective-permute-start.6 = (bf16[256,1024]{1,0:T(8,128)(2,1)S(1)}, bf16[256,1024]{1,0:T(8,128)(2,1)S(1)}, u32[]{:S(2)}, u32[]{:S(2)}) collective-permute-start(bf16[256,1024]{1,0:T(8,128)(2,1)S(1)} %get-tuple-element.42), channel_id=1, source_target_pairs={{0,0},{4,8},{8,4},{12,12},{1,1},{5,9},{9,5},{13,13},{2,2},{6,10},{... | collective-permute-start | bytes 1572872 | tf_op jit(solution)/shard_map/ppermute | solution.py:449
  9.8 0.0 copy-start.4
  9.9 0.6 copy-done.4
  10.5 0.7 copy-done.5
  11.2 0.9 %copy-done.8 = f32[64,512]{1,0:T(8,128)S(1)} copy-done((f32[64,512]{1,0:T(8,128)S(1)}, f32[64,512]{1,0:T(8,128)}, u32[]{:S(2)}) %copy-start.8) | copy-done | bytes 131096
  12.1 0.9 %copy-done.9 = f32[64,512]{1,0:T(8,128)S(1)} copy-done((f32[64,512]{1,0:T(8,128)S(1)}, f32[64,512]{1,0:T(8,128)}, u32[]{:S(2)}) %copy-start.9) | copy-done | bytes 131096
  13.0 10.7 %local_windows.1 = (bf16[1024,512]{1,0:T(8,128)(2,1)S(1)}, bf16[1024,512]{1,0:T(8,128)(2,1)S(1)}, bf16[512,1024]{1,0:T(8,128)(2,1)S(1)}, bf16[512,1024]{1,0:T(8,...) custom-call(s32[3]{0:T(128)S(1)} %copy-done.4, ...), custom_call_target="tpu_custom_call" | custom-call | flops 2147483648 | bytes 8388608 | tf_op jit(solution)/shard_map/local_windows/pallas_call | solution.py:463
  23.7 1.3 %collective-permute-start.2 = (bf16[32,1024]{1,0:T(8,128)(2,1)S(1)}, bf16[32,1024]{1,0:T(8,128)(2,1)S(1)}, u32[]{:S(2)}, u32[]{:S(2)}) collective-permute-start(bf16[32,1024]{1,0:T(8,128)(2,1)S(1)} %get-tuple-element.34), channel_id=1, source_target_pairs={{0,2},{1,3},{2,0},{3,1},{4,6},{5,7},{6,4},{7,5},{8,10},{9,11},{10,... | collective-permute-start | bytes 196616 | tf_op jit(solution)/shard_map/ppermute | solution.py:482
  25.0 1.7 %collective-permute-start = (bf16[64,1024]{1,0:T(8,128)(2,1)S(1)}, bf16[64,1024]{1,0:T(8,128)(2,1)S(1)}, u32[]{:S(2)}, u32[]{:S(2)}) collective-permute-start(bf16[64,1024]{1,0:T(8,128)(2,1)S(1)} %get-tuple-element.32), channel_id=1, source_target_pairs={{0,1},{1,2},{2,3},{3,0},{4,5},{5,6},{6,7},{7,4},{8,9},{9,10},{10,1... | collective-permute-start | bytes 393224 | tf_op jit(solution)/shard_map/ppermute | solution.py:482
  26.6 5.5 %rim_windows_0.1 = (bf16[256,1024]{1,0:T(8,128)(2,1)S(1)}, bf16[256,1024]{1,0:T(8,128)(2,1)S(1)}) custom-call(s32[3]{0:T(128)S(1)} %copy-done.4, bf16[512,3072]{1,0:T(8,128)(2,1)S(1)} %copy-done.1, bf16[272,1024]{1,0:T(8,128)(2,1)S(1)} %collective-permute-done.3.rest_0_.rest_2_, bf16[272,1024]{1,0:T(8,128)(2,1)S(1)} %collective-permute-done.4.rest_1_.rest_3_, ...), custom_call_target="tpu_custom_call" | custom-call | flops 1073741824 | bytes 4194304 | tf_op jit(solution)/shard_map/rim_windows_0/pallas_call | solution.py:502
  32.1 0.0 copy-start.6
  32.1 6.0 %rim_windows_1.1 = (bf16[256,1024]{1,0:T(8,128)(2,1)S(1)}, bf16[256,1024]{1,0:T(8,128)(2,1)S(1)}, bf16[64,1024]{1,0:T(8,128)(2,1)S(1)}, bf16[64,1024]{1,0:T(8,12...) custom-call(s32[3]{0:T(128)S(1)} %copy-done.4, bf16[512,3072]{1,0:T(8,128)(2,1)S(1)} %copy-done.1, ...), custom_call_target="tpu_custom_call" | custom-call | flops 1073741824 | bytes 4194304 | tf_op jit(solution)/shard_map/rim_windows_1/pallas_call | solution.py:502
  38.1 1.8 %collective-permute-start.7 = (bf16[64,1024]{1,0:T(8,128)(2,1)S(1)}, bf16[64,1024]{1,0:T(8,128)(2,1)S(1)}, u32[]{:S(2)}, u32[]{:S(2)}) collective-permute-start(bf16[64,1024]{1,0:T(8,128)(2,1)S(1)} %get-tuple-element.46), channel_id=1, source_target_pairs={{0,1},{1,2},{2,3},{3,0},{4,5},{5,6},{6,7},{7,4},{8,9},{9,10},{10,1... | collective-permute-start | bytes 393224 | tf_op jit(solution)/shard_map/ppermute | solution.py:482
  39.9 0.1 collective-permute-start.8
  40.0 1.1 %collective-permute-start.9 = (bf16[32,1024]{1,0:T(8,128)(2,1)S(1)}, bf16[32,1024]{1,0:T(8,128)(2,1)S(1)}, u32[]{:S(2)}, u32[]{:S(2)}) collective-permute-start(bf16[32,1024]{1,0:T(8,128)(2,1)S(1)} %get-tuple-element.48), channel_id=1, source_target_pairs={{0,2},{1,3},{2,0},{3,1},{4,6},{5,7},{6,4},{7,5},{8,10},{9,11},{10,... | collective-permute-start | bytes 196616 | tf_op jit(solution)/shard_map/ppermute | solution.py:482
  41.2 2.4 %early_pairs.1.early = f32[512,1024]{1,0:T(8,128)S(1)} custom-call(s32[1,512]{1,0:T(1,128)S(1)} %bitcast.2, s32[1,512]{1,0:T(1,128)S(1)} %bitcast.4, bf16[512,1024]{1,0:T(8,128)(2,1)S(1)} %get-tuple-element.29.white0, bf16[512,1024]{1,0:T(8,128)(2,1)S(1)} %get-tuple-element.30.white3, bf16[64,1024]{1,0:T(8,128)(2,1)S(1)} %get-tuple-element.31.rest_0_, ...), custom_call_target="tpu_custom_call" | custom-call | flops 1342177280 | bytes 4194304 | tf_op jit(solution)/shard_map/early_pairs/pallas_call | solution.py:486
  43.5 1.9 %collective-permute-done.9.rest_7_ = bf16[32,1024]{1,0:T(8,128)(2,1)S(1)} collective-permute-done((bf16[32,1024]{1,0:T(8,128)(2,1)S(1)}, bf16[32,1024]{1,0:T(8,128)(2,1)S(1)}, u32[]{:S(2)}, u32[]{:S(2)}) %collective-permute-start.9) | collective-permute-done | bytes 65568 | tf_op jit(solution)/shard_map/ppermute | solution.py:482
  45.5 0.1 collective-permute-done.8.rest_6_
  45.6 3.8 %late_pairs.1 = (f32[256,512]{1,0:T(8,128)S(1)}, bf16[256,512]{1,0:T(8,128)(2,1)S(1)}, bf16[256,512]{1,0:T(8,128)(2,1)S(1)}, bf16[256,512]{1,0:T(8,128)(2,1)S(1)}) custom-call(s32[1,512]{1,0:T(1,128)S(1)} %bitcast.3, s32[1,512]{1,0:T(1,128)S(1)} %bitcast.5, f32[512,1024]{1,0:T(8,128)S(1)} %early_pairs.1.early, ...), custom_call_target="tpu_custom_call" | custom-call | flops 2415919104 | bytes 6291456 | tf_op jit(solution)/shard_map/late_pairs/pallas_call | solution.py:525
  49.4 1.8 %collective-permute-start.10 = (bf16[256,512]{1,0:T(8,128)(2,1)S(1)}, bf16[256,512]{1,0:T(8,128)(2,1)S(1)}, u32[]{:S(2)}, u32[]{:S(2)}) collective-permute-start(bf16[256,512]{1,0:T(8,128)(2,1)S(1)} %get-tuple-element.50), channel_id=1, source_target_pairs={{0,4},{4,8},{8,12},{12,0},{1,5},{5,9},{9,13},{13,1},{2,6},{6,10},{... | collective-permute-start | bytes 786440 | tf_op jit(solution)/shard_map/ppermute | solution.py:544
  51.2 0.8 %collective-permute-start.11 = (bf16[256,512]{1,0:T(8,128)(2,1)S(1)}, bf16[256,512]{1,0:T(8,128)(2,1)S(1)}, u32[]{:S(2)}, u32[]{:S(2)}) collective-permute-start(bf16[256,512]{1,0:T(8,128)(2,1)S(1)} %get-tuple-element.51), channel_id=1, source_target_pairs={{0,8},{4,12},{8,0},{12,4},{1,9},{5,13},{9,1},{13,5},{2,10},{6,14},... | collective-permute-start | bytes 786440 | tf_op jit(solution)/shard_map/ppermute | solution.py:544
  52.0 0.4 collective-permute-start.12
  52.4 3.5 %collective-permute-done.10 = bf16[256,512]{1,0:T(8,128)(2,1)S(1)} collective-permute-done((bf16[256,512]{1,0:T(8,128)(2,1)S(1)}, bf16[256,512]{1,0:T(8,128)(2,1)S(1)}, u32[]{:S(2)}, u32[]{:S(2)}) %collective-permute-start.10) | collective-permute-done | bytes 262176 | tf_op jit(solution)/shard_map/ppermute | solution.py:544
  55.9 16.4 %collective-permute-done.11 = bf16[256,512]{1,0:T(8,128)(2,1)S(1)} collective-permute-done((bf16[256,512]{1,0:T(8,128)(2,1)S(1)}, bf16[256,512]{1,0:T(8,128)(2,1)S(1)}, u32[]{:S(2)}, u32[]{:S(2)}) %collective-permute-start.11) | collective-permute-done | bytes 262176 | tf_op jit(solution)/shard_map/ppermute | solution.py:544
  72.3 3.4 %collective-permute-done.12 = bf16[256,512]{1,0:T(8,128)(2,1)S(1)} collective-permute-done((bf16[256,512]{1,0:T(8,128)(2,1)S(1)}, bf16[256,512]{1,0:T(8,128)(2,1)S(1)}, u32[]{:S(2)}, u32[]{:S(2)}) %collective-permute-start.12) | collective-permute-done | bytes 262176 | tf_op jit(solution)/shard_map/ppermute | solution.py:544
  75.7 0.9 %convert_add_fusion = f32[256,512]{1,0:T(8,128)} fusion(bf16[256,512]{1,0:T(8,128)(2,1)S(1)} %collective-permute-done.12, bf16[256,512]{1,0:T(8,128)(2,1)S(1)} %collective-permute-done.11, f32[256,512]{1,0:T(8,128)S(1)} %get-tuple-element.49, bf16[256,512]{1,0:T(8,128)(2,1)S(1)} %collective-permute-done.10), kind=kLoop, calls=%fused_computation | loop fusion | flops 786432 | bytes 1835008 | tf_op jit(solution)/shard_map/add | solution.py:544
  (21 shorter events, 0.0 us)
Async XLA Ops:
  0.0 1.9 %copy-start = (bf16[512,3072]{1,0:T(8,128)(2,1)S(1)}, bf16[512,3072]{1,0:T(8,128)(2,1)}, u32[]{:S(2)}) copy-start(bf16[512,3072]{1,0:T(8,128)(2,1)} %main.7) | copy-start | bytes 9437188
  1.9 0.7 copy-start.3
  2.5 7.3 %copy-start.1 = (bf16[512,3072]{1,0:T(8,128)(2,1)S(1)}, bf16[512,3072]{1,0:T(8,128)(2,1)}, u32[]{:S(2)}) copy-start(bf16[512,3072]{1,0:T(8,128)(2,1)} %main.7) | copy-start | bytes 9437188
  2.5 7.3 %copy-start.2 = (f32[1,2048]{1,0:T(1,128)S(1)}, f32[1,2048]{1,0:T(1,128)}, u32[]{:S(2)}) copy-start(f32[1,2048]{1,0:T(1,128)} %constant.8.clone.taper.rest_2_.rest_4_) | copy-start | bytes 24580
  3.3 21.7 %collective-permute-start.3 = (bf16[272,1024]{1,0:T(8,128)(2,1)S(1)}, bf16[272,1024]{1,0:T(8,128)(2,1)S(1)}, u32[]{:S(2)}, u32[]{:S(2)}) collective-permute-start(bf16[272,1024]{1,0:T(8,128)(2,1)S(1)} %get-tuple-element.37), channel_id=1, source_target_pairs={{0,4},{4,0},{8,12},{12,8},{1,5},{5,1},{9,13},{13,9},{2,6},{6,2},{1... | collective-permute-start | bytes 1671176 | tf_op jit(solution)/shard_map/ppermute | solution.py:449
  3.3 23.3 %collective-permute-start.4 = (bf16[272,1024]{1,0:T(8,128)(2,1)S(1)}, bf16[272,1024]{1,0:T(8,128)(2,1)S(1)}, u32[]{:S(2)}, u32[]{:S(2)}) collective-permute-start(bf16[272,1024]{1,0:T(8,128)(2,1)S(1)} %get-tuple-element.38), channel_id=1, source_target_pairs={{0,0},{4,8},{8,4},{12,12},{1,1},{5,9},{9,5},{13,13},{2,2},{6,10},{... | collective-permute-start | bytes 1671176 | tf_op jit(solution)/shard_map/ppermute | solution.py:449
  7.8 24.3 %collective-permute-start.5 = (bf16[256,1024]{1,0:T(8,128)(2,1)S(1)}, bf16[256,1024]{1,0:T(8,128)(2,1)S(1)}, u32[]{:S(2)}, u32[]{:S(2)}) collective-permute-start(bf16[256,1024]{1,0:T(8,128)(2,1)S(1)} %get-tuple-element.41), channel_id=1, source_target_pairs={{0,4},{4,0},{8,12},{12,8},{1,5},{5,1},{9,13},{13,9},{2,6},{6,2},{1... | collective-permute-start | bytes 1572872 | tf_op jit(solution)/shard_map/ppermute | solution.py:449
  7.9 24.2 %collective-permute-start.6 = (bf16[256,1024]{1,0:T(8,128)(2,1)S(1)}, bf16[256,1024]{1,0:T(8,128)(2,1)S(1)}, u32[]{:S(2)}, u32[]{:S(2)}) collective-permute-start(bf16[256,1024]{1,0:T(8,128)(2,1)S(1)} %get-tuple-element.42), channel_id=1, source_target_pairs={{0,0},{4,8},{8,4},{12,12},{1,1},{5,9},{9,5},{13,13},{2,2},{6,10},{... | collective-permute-start | bytes 1572872 | tf_op jit(solution)/shard_map/ppermute | solution.py:449
  9.8 0.7 copy-start.4
  10.5 0.7 copy-start.5
  11.2 0.9 %copy-start.8 = (f32[64,512]{1,0:T(8,128)S(1)}, f32[64,512]{1,0:T(8,128)}, u32[]{:S(2)}) copy-start(f32[64,512]{1,0:T(8,128)} %constant.7.clone.sin_t) | copy-start | bytes 393220
  12.1 0.9 %copy-start.9 = (f32[64,512]{1,0:T(8,128)S(1)}, f32[64,512]{1,0:T(8,128)}, u32[]{:S(2)}) copy-start(f32[64,512]{1,0:T(8,128)} %constant.6.clone.cos_t) | copy-start | bytes 393220
  23.7 16.4 %collective-permute-start.2 = (bf16[32,1024]{1,0:T(8,128)(2,1)S(1)}, bf16[32,1024]{1,0:T(8,128)(2,1)S(1)}, u32[]{:S(2)}, u32[]{:S(2)}) collective-permute-start(bf16[32,1024]{1,0:T(8,128)(2,1)S(1)} %get-tuple-element.34), channel_id=1, source_target_pairs={{0,2},{1,3},{2,0},{3,1},{4,6},{5,7},{6,4},{7,5},{8,10},{9,11},{10,... | collective-permute-start | bytes 196616 | tf_op jit(solution)/shard_map/ppermute | solution.py:482
  25.0 16.2 %collective-permute-start = (bf16[64,1024]{1,0:T(8,128)(2,1)S(1)}, bf16[64,1024]{1,0:T(8,128)(2,1)S(1)}, u32[]{:S(2)}, u32[]{:S(2)}) collective-permute-start(bf16[64,1024]{1,0:T(8,128)(2,1)S(1)} %get-tuple-element.32), channel_id=1, source_target_pairs={{0,1},{1,2},{2,3},{3,0},{4,5},{5,6},{6,7},{7,4},{8,9},{9,10},{10,1... | collective-permute-start | bytes 393224 | tf_op jit(solution)/shard_map/ppermute | solution.py:482
  26.6 14.5 %collective-permute-start.1 = (bf16[64,1024]{1,0:T(8,128)(2,1)S(1)}, bf16[64,1024]{1,0:T(8,128)(2,1)S(1)}, u32[]{:S(2)}, u32[]{:S(2)}) collective-permute-start(bf16[64,1024]{1,0:T(8,128)(2,1)S(1)} %get-tuple-element.33), channel_id=1, source_target_pairs={{0,3},{1,0},{2,1},{3,2},{4,7},{5,4},{6,5},{7,6},{8,11},{9,8},{10,9... | collective-permute-start | bytes 393224 | tf_op jit(solution)/shard_map/ppermute | solution.py:482
  32.1 9.0 %copy-start.6 = (s32[512]{0:T(512)S(1)}, s32[512]{0:T(512)}, u32[]{:S(2)}) copy-start(s32[512]{0:T(512)} %param.10) | copy-start | bytes 6148
  32.1 9.0 %copy-start.7 = (s32[512]{0:T(512)S(1)}, s32[512]{0:T(512)}, u32[]{:S(2)}) copy-start(s32[512]{0:T(512)} %param.11) | copy-start | bytes 6148
  38.1 7.3 %collective-permute-start.7 = (bf16[64,1024]{1,0:T(8,128)(2,1)S(1)}, bf16[64,1024]{1,0:T(8,128)(2,1)S(1)}, u32[]{:S(2)}, u32[]{:S(2)}) collective-permute-start(bf16[64,1024]{1,0:T(8,128)(2,1)S(1)} %get-tuple-element.46), channel_id=1, source_target_pairs={{0,1},{1,2},{2,3},{3,0},{4,5},{5,6},{6,7},{7,4},{8,9},{9,10},{10,1... | collective-permute-start | bytes 393224 | tf_op jit(solution)/shard_map/ppermute | solution.py:482
  39.9 5.7 %collective-permute-start.8 = (bf16[64,1024]{1,0:T(8,128)(2,1)S(1)}, bf16[64,1024]{1,0:T(8,128)(2,1)S(1)}, u32[]{:S(2)}, u32[]{:S(2)}) collective-permute-start(bf16[64,1024]{1,0:T(8,128)(2,1)S(1)} %get-tuple-element.47), channel_id=1, source_target_pairs={{0,3},{1,0},{2,1},{3,2},{4,7},{5,4},{6,5},{7,6},{8,11},{9,8},{10,9... | collective-permute-start | bytes 393224 | tf_op jit(solution)/shard_map/ppermute | solution.py:482
  40.0 5.4 %collective-permute-start.9 = (bf16[32,1024]{1,0:T(8,128)(2,1)S(1)}, bf16[32,1024]{1,0:T(8,128)(2,1)S(1)}, u32[]{:S(2)}, u32[]{:S(2)}) collective-permute-start(bf16[32,1024]{1,0:T(8,128)(2,1)S(1)} %get-tuple-element.48), channel_id=1, source_target_pairs={{0,2},{1,3},{2,0},{3,1},{4,6},{5,7},{6,4},{7,5},{8,10},{9,11},{10,... | collective-permute-start | bytes 196616 | tf_op jit(solution)/shard_map/ppermute | solution.py:482
  49.4 6.5 %collective-permute-start.10 = (bf16[256,512]{1,0:T(8,128)(2,1)S(1)}, bf16[256,512]{1,0:T(8,128)(2,1)S(1)}, u32[]{:S(2)}, u32[]{:S(2)}) collective-permute-start(bf16[256,512]{1,0:T(8,128)(2,1)S(1)} %get-tuple-element.50), channel_id=1, source_target_pairs={{0,4},{4,8},{8,12},{12,0},{1,5},{5,9},{9,13},{13,1},{2,6},{6,10},{... | collective-permute-start | bytes 786440 | tf_op jit(solution)/shard_map/ppermute | solution.py:544
  51.2 21.1 %collective-permute-start.11 = (bf16[256,512]{1,0:T(8,128)(2,1)S(1)}, bf16[256,512]{1,0:T(8,128)(2,1)S(1)}, u32[]{:S(2)}, u32[]{:S(2)}) collective-permute-start(bf16[256,512]{1,0:T(8,128)(2,1)S(1)} %get-tuple-element.51), channel_id=1, source_target_pairs={{0,8},{4,12},{8,0},{12,4},{1,9},{5,13},{9,1},{13,5},{2,10},{6,14},... | collective-permute-start | bytes 786440 | tf_op jit(solution)/shard_map/ppermute | solution.py:544
  52.0 23.7 %collective-permute-start.12 = (bf16[256,512]{1,0:T(8,128)(2,1)S(1)}, bf16[256,512]{1,0:T(8,128)(2,1)S(1)}, u32[]{:S(2)}, u32[]{:S(2)}) collective-permute-start(bf16[256,512]{1,0:T(8,128)(2,1)S(1)} %get-tuple-element.52), channel_id=1, source_target_pairs={{0,12},{4,0},{8,4},{12,8},{1,13},{5,1},{9,5},{13,9},{2,14},{6,2},{... | collective-permute-start | bytes 786440 | tf_op jit(solution)/shard_map/ppermute | solution.py:544

commit v4 on v3

--- a/solution.py
+++ b/solution.py
@@ -24,12 +24,14 @@
 F32 = jnp.float32
 BF16 = jnp.bfloat16
 ROWS = 16
+N_SMALL = 4
 UNIT = 512
 TURN_UNROLL = 4
 FOLD_UNROLL = 4
 WHITEN_UNROLL = 8
 VMEM = pl.BlockSpec(memory_space=pltpu.VMEM)
 SMEM = pl.BlockSpec(memory_space=pltpu.SMEM)
+ANY = pl.BlockSpec(memory_space=pltpu.HBM)
 
 
 def small_tables():
@@ -191,17 +193,6 @@
         pieces.append(jnp.where(lane.astype(F32) == col, 1.0, 0.0).astype(BF16))
     hot = pieces[0] if len(pieces) == 1 else jnp.concatenate(pieces, axis=1)
     return hot[:, :width]
-
-
-def lookup(col, spectra):
-    total = None
-    at = 0
-    for piece in spectra:
-        n = piece.shape[0]
-        term = jnp.dot(one_hot(col, n, at), piece[...], preferred_element_type=F32)
-        total = term if total is None else total + term
-        at += n
-    return total
 
 
 def write_rows(send_rows, spectra, near, far, n_sta, cap, refs):
@@ -223,7 +214,7 @@
         first = pl.multiple_of(lax.rem(g + d, n_sta) * cap, cap)
         for w in range(2):
             if d in far:
-                ref[w * ROWS : (w + 1) * ROWS, :] = rows[w, pl.ds(first, ROWS), :]
+                ref[w * CAP_FAR : (w + 1) * CAP_FAR, :] = rows[w, pl.ds(first, CAP_FAR), :]
             else:
                 ref[w * cap : (w + 1) * cap, :] = rows[w, pl.ds(first, cap), :]
 
@@ -280,23 +271,53 @@
     return routes
 
 
-def pack_kernel(rows, offsets, main, *outs):
+def pack_kernel(rows, n_out, offsets, main, *rest):
+    small = rest[: N_SMALL]
+    outs = rest[N_SMALL : N_SMALL + n_out]
+    offsets_out = rest[N_SMALL + n_out]
+    small_out = rest[N_SMALL + n_out + 1 : -1]
+    sems = rest[-1]
     t = lax.axis_index("tm")
     n = lax.axis_size("tm")
-    start = offsets[2] - 2 * STEP
-    high, low = start // 8, start % 8
-    lane = lax.broadcasted_iota(jnp.int32, (ROWS, HALF), 1)
-    for i, out in enumerate(outs):
+
+    def edge(i):
         chunk, swap = i // 2, i % 2
         at = jnp.where(t % 2 == swap, 2 * HALF, 0)
         lanes = pl.ds(pl.multiple_of(at, LANES), HALF)
-        alone = n % 2 != swap
-        keep = jnp.where(t == n - 1, 0.0, 1.0).astype(BF16) if alone else None
-        for r in range(0, rows, 64):
-            value = main[chunk * rows + r : chunk * rows + r + 64, lanes]
-            out[r : r + 64, :] = value if keep is None else value * keep
-        if chunk == 0:
-            out[rows:, :] = jnp.where(lane < NF, high, low).astype(F32).astype(BF16)
+        source = main.at[pl.ds(chunk * rows, rows), lanes]
+        return pltpu.make_async_copy(source, outs[i].at[pl.ds(0, rows)], sems.at[i])
+
+    first = pltpu.make_async_copy(offsets, offsets_out, sems.at[n_out])
+    first.start()
+    copies = []
+    for i in range(n_out):
+        if n % 2 == i % 2:
+            copies.append(edge(i))
+            copies[-1].start()
+        else:
+            @pl.when(t == n - 1)
+            def _():
+                outs[i][0:rows, :] = jnp.zeros((rows, HALF), BF16)
+
+            @pl.when(t < n - 1)
+            def _():
+                edge(i).start()
+    for k in range(N_SMALL):
+        copies.append(pltpu.make_async_copy(small[k], small_out[k], sems.at[n_out + 1 + k]))
+        copies[-1].start()
+    first.wait()
+    start = offsets_out[2] - 2 * STEP
+    high, low = start // 8, start % 8
+    lane = lax.broadcasted_iota(jnp.int32, (ROWS, HALF), 1)
+    for i in range(2):
+        outs[i][rows:, :] = jnp.where(lane < NF, high, low).astype(F32).astype(BF16)
+    for copy in copies:
+        copy.wait()
+    for i in range(n_out):
+        if n % 2 != i % 2:
+            @pl.when(t < n - 1)
+            def _():
+                edge(i).wait()
 
 
 def sent_start(ref, rows):
@@ -342,18 +363,8 @@
         write_rows(send_rows, (older[0::2] + whites[:1], older[1::2] + whites[1:]), *groups, sends)
 
 
-def add_pairs(groups, pieces, pair_first, pair_slot, spectra, incoming, cross):
+def slot_table(groups, pair_slot, width):
     near, far, n_sta, cap = groups
-    pairs = pair_first.shape[1]
-    width = incoming.shape[1]
-    for w in range(2):
-        at = 0
-        for i, d in enumerate(near + far):
-            n = ROWS if d in far else cap
-            incoming[w, at : at + n, :] = pieces[i][w * n : (w + 1) * n, :]
-            at += n
-        if at < width:
-            incoming[w, at:, :] = jnp.zeros((width - at, 2 * NF), BF16)
     g = lax.axis_index("sta")
     slot = pair_slot[...]
     distance = (g - slot // cap + n_sta) % n_sta
@@ -361,58 +372,136 @@
     at = 0
     for d in near + far:
         place = jnp.where(distance == d, at + slot % cap, place)
-        at += ROWS if d in far else cap
-    first_col = column(pair_first[...])
-    slot_col = column(place)
-    block = min(pairs, 256)
-    for p in range(0, pairs, block):
-        hot = one_hot(slot_col[p : p + block], width)
-        for w in range(2):
-            first = lookup(first_col[p : p + block], spectra[w])
-            second = jnp.dot(hot, incoming[w], preferred_element_type=F32)
-            a_i, b_i = first[:, :NF], first[:, NF:]
-            a_j, b_j = second[:, :NF], second[:, NF:]
-            cross[p : p + block, :NF] += a_i * a_j + b_i * b_j
-            cross[p : p + block, NF:] += b_i * a_j - a_i * b_j
-
-
-def early_kernel(groups, n_pieces, pair_first, pair_slot, white0, white3, *rest):
-    pieces = rest[:n_pieces]
-    cross, incoming = rest[n_pieces:]
-    cross[...] = jnp.zeros_like(cross)
-    add_pairs(groups, pieces, pair_first, pair_slot, ((white0,), (white3,)), incoming, cross)
-
-
-def late_kernel(groups, n_pieces, n_white, n_dest, scale, pair_first, pair_slot, early, t_odd, t_even, *rest):
-    whites = rest[: 2 * n_white]
-    pieces = rest[2 * n_white : 2 * n_white + n_pieces]
-    rest = rest[2 * n_white + n_pieces :]
-    own = rest[0]
-    outs = rest[1:n_dest]
-    incoming, cross, x_odd, x_even = rest[n_dest:]
-    cross[...] = early[...]
-    add_pairs(groups, pieces, pair_first, pair_slot, (whites[0::2], whites[1::2]), incoming, cross)
+        at += CAP_FAR if d in far else cap
+    return one_hot(column(place), width)
+
+
+def second_rows(groups, pieces, hot, incoming, out):
+    near, far, n_sta, cap = groups
+    width = incoming.shape[1]
+    for w in range(2):
+        at = 0
+        for i, d in enumerate(near + far):
+            n = CAP_FAR if d in far else cap
+            incoming[w, at : at + n, :] = pieces[i][w * n : (w + 1) * n, :]
+            at += n
+        if at < width:
+            incoming[w, at:, :] = jnp.zeros((width - at, 2 * NF), BF16)
+    for w in range(2):
+        for c in range(0, 2 * NF, NF):
+            out[w, :, c : c + NF] = jnp.dot(hot[...], incoming[w, :, c : c + NF], preferred_element_type=F32)
+
+
+def first_rows(hots, spectra, scale, out):
     lane = lax.broadcasted_iota(jnp.int32, (1, QB), 1)
     s = jnp.where(lane % 2 == 0, scale, -scale).astype(F32)
-    x_odd[:, :QB] = (cross[:, NF : NF + QB] * s).astype(BF16)
-    x_odd[:, QB:] = (cross[:, :QB] * -s).astype(BF16)
-    x_even[:, :QB] = (cross[:, QB:NF] * -s).astype(BF16)
-    x_even[:, QB:] = (cross[:, NF + QB :] * -s).astype(BF16)
+    for c in range(0, 2 * NF, QB):
+        total = None
+        for hot, piece in zip(hots, spectra):
+            term = jnp.dot(hot, piece[:, c : c + QB], preferred_element_type=F32)
+            total = term if total is None else total + term
+        out[:, c : c + QB] = total * (s if c % NF == 0 else -s)
+
+
+def station_tables(col, spectra):
+    hots, at = [], 0
+    for piece in spectra:
+        hots.append(one_hot(col, piece.shape[0], at))
+        at += piece.shape[0]
+    return hots
+
+
+def add_products(first, second, rows, c, start):
+    re_lanes = slice(c, c + LANES)
+    im_lanes = slice(NF + c, NF + c + LANES)
+    one, two = start
+    for w in range(2):
+        a_i, b_i = first[w, rows, re_lanes], first[w, rows, im_lanes]
+        a_j, b_j = second[w, rows, re_lanes], second[w, rows, im_lanes]
+        re = a_i * a_j + b_i * b_j
+        im = b_i * a_j - a_i * b_j
+        if c < QB:
+            one, two = one + im, two - re
+        else:
+            one, two = one + re, two + im
+    return one, two
+
+
+def early_kernel(groups, n_pieces, n_white, scale, pair_first, pair_slot, white0, white3, *rest):
+    whites = rest[: 2 * n_white]
+    rest = rest[2 * n_white :]
+    pieces = rest[:n_pieces]
+    cross, later, hot = rest[n_pieces : n_pieces + 3]
+    incoming, first, second = rest[n_pieces + 3 :]
+    pairs = pair_first.shape[1]
+    col = column(pair_first[...])
+    hots = station_tables(col, (white0,))
+    first_rows(hots, (white0,), scale, first.at[0])
+    first_rows(hots, (white3,), scale, first.at[1])
+    hot[...] = slot_table(groups, pair_slot, hot.shape[1])
+    second_rows(groups, pieces, hot, incoming, second)
+
+    def group(i, carry):
+        rows = pl.ds(pl.multiple_of(i * ROWS, ROWS), ROWS)
+        for c in range(0, NF, LANES):
+            one, two = add_products(first, second, rows, c, (0.0, 0.0))
+            cross[rows, c : c + LANES] = one
+            cross[rows, NF + c : NF + c + LANES] = two
+        return carry
+
+    lax.fori_loop(0, pairs // ROWS, group, 0, unroll=2)
+    hots = station_tables(col, whites[0::2])
+    first_rows(hots, whites[0::2], scale, later.at[0])
+    first_rows(hots, whites[1::2], scale, later.at[1])
+
+
+def late_kernel(groups, n_pieces, n_dest, early, first, hot, t_odd, t_even, *rest):
+    pieces = rest[:n_pieces]
+    own = rest[n_pieces]
+    outs = rest[n_pieces + 1 : n_pieces + n_dest]
+    incoming, second, x_odd, x_even = rest[n_pieces + n_dest :]
+    pairs = early.shape[0]
+    second_rows(groups, pieces, hot, incoming, second)
+
+    def group(i, carry):
+        rows = pl.ds(pl.multiple_of(i * ROWS, ROWS), ROWS)
+        for c in range(0, NF, LANES):
+            start = (early[rows, c : c + LANES], early[rows, NF + c : NF + c + LANES])
+            one, two = add_products(first, second, rows, c, start)
+            out = x_odd if c < QB else x_even
+            at = c % QB
+            out[rows, at : at + LANES] = one.astype(BF16)
+            out[rows, QB + at : QB + at + LANES] = two.astype(BF16)
+        return carry
+
+    lax.fori_loop(0, pairs // ROWS, group, 0, unroll=2)
     rows = own.shape[0]
     me = lax.axis_index("tm")
     dims = (((1,), (1,)), ((), ()))
-    for d in list(range(1, n_dest)) + [0]:
-        at = pl.ds(pl.multiple_of(lax.rem(me + d, n_dest) * rows, rows), rows)
-        value = lax.dot_general(t_odd[at, :], x_odd[...], dims, preferred_element_type=F32)
-        value = value + lax.dot_general(t_even[at, :], x_even[...], dims, preferred_element_type=F32)
+    order = list(range(n_dest))
+    spots = [pl.ds(pl.multiple_of(lax.rem(me + d, n_dest) * rows, rows), rows) for d in order]
+    odd = jnp.concatenate([t_odd[at, :] for at in spots], axis=0)
+    even = jnp.concatenate([t_even[at, :] for at in spots], axis=0)
+    value = lax.dot_general(odd, x_odd[...], dims, preferred_element_type=F32)
+    value = value + lax.dot_general(even, x_even[...], dims, preferred_element_type=F32)
+    for d in order:
+        piece = value[d * rows : (d + 1) * rows, :]
         if d == 0:
-            own[...] = value
+            own[...] = piece
         else:
-            outs[d - 1][...] = value.astype(BF16)
+            outs[d - 1][...] = piece.astype(BF16)
 
 
 def in_vmem(*arrays):
     return [pltpu.with_memory_space_constraint(a, pltpu.VMEM) for a in arrays]
+
+
+def in_smem(*arrays):
+    return [pltpu.with_memory_space_constraint(a, pltpu.SMEM) for a in arrays]
+
+
+def in_hbm(*arrays):
+    return [pltpu.with_memory_space_constraint(a, pltpu.HBM) for a in arrays]
 
 
 def params(mib):
@@ -435,28 +524,33 @@
     rows = stations // n_chunks
     main, = in_vmem(traces)
     routes = swap_routes(n_tm)
+    small = [jnp.asarray(x) for x in small_tables()] + [jnp.asarray(taper_row()), send_rows]
     packed = pl.pallas_call(
-        functools.partial(pack_kernel, rows),
+        functools.partial(pack_kernel, rows, 2 * n_chunks),
         out_shape=[
             pltpu.VMEM((rows + (ROWS if i < 2 else 0), HALF), BF16) for i in range(2 * n_chunks)
-        ],
-        in_specs=[SMEM, VMEM],
-        out_specs=[VMEM] * (2 * n_chunks),
+        ]
+        + [pltpu.SMEM(offsets.shape, jnp.int32)]
+        + [pltpu.VMEM(x.shape, x.dtype) for x in small],
+        in_specs=[ANY] * (2 + N_SMALL),
+        out_specs=[VMEM] * (2 * n_chunks) + [SMEM] + [VMEM] * N_SMALL,
+        scratch_shapes=[pltpu.SemaphoreType.DMA((2 * n_chunks + 1 + N_SMALL,))],
         compiler_params=params(1),
         cost_estimate=cost(0, 4 << 20),
         name="pack_edges",
-    )(offsets, main)
+    )(*in_hbm(offsets, traces, *small))
+    starts = packed[2 * n_chunks]
+    cos_t, sin_t, taper, send_rows = packed[2 * n_chunks + 1 :]
+    packed = packed[: 2 * n_chunks]
     edges = [lax.ppermute(x, "tm", routes[i % 2]) for i, x in enumerate(packed)]
 
     near = [0, 1, n_sta - 1] if n_sta > 2 else list(range(n_sta))
     far = [d for d in range(n_sta) if d not in near]
     groups = (near, far, n_sta, cap)
-    width = -(-(len(near) * cap + len(far) * ROWS) // LANES) * LANES
+    width = -(-(len(near) * cap + len(far) * CAP_FAR) // LANES) * LANES
     first_row, slot_row = pair_first[None, :], pair_slot[None, :]
-    cos_t, sin_t = (jnp.asarray(x) for x in small_tables())
-    taper = jnp.asarray(taper_row())
-
-    buffers = [pltpu.VMEM((2 * (ROWS if d in far else cap), 2 * NF), BF16) for d in near + far]
+
+    buffers = [pltpu.VMEM((2 * (CAP_FAR if d in far else cap), 2 * NF), BF16) for d in near + far]
     dft_flops = 2 * 2 * HALF * 2 * QB * 2
     spectrum = pltpu.VMEM((stations, 2 * NF), BF16)
     table = pltpu.VMEM((HALF, 2 * QB), BF16)
@@ -469,7 +563,7 @@
         compiler_params=params(18),
         cost_estimate=cost(dft_flops * stations, 8 << 20),
         name="local_windows",
-    )(offsets, main, cos_t, sin_t, taper, send_rows)
+    )(*in_smem(starts), *in_vmem(main, cos_t, sin_t, taper, send_rows))
     t_odd, t_even, white0, white3 = local[:4]
 
     def exchange(pieces):
@@ -483,17 +577,6 @@
         return got
 
     early_in = exchange(local[4:])
-    early = pl.pallas_call(
-        functools.partial(early_kernel, groups, len(buffers)),
-        out_shape=pltpu.VMEM((pairs, 2 * NF), F32),
-        in_specs=[VMEM] * (4 + len(buffers)),
-        out_specs=VMEM,
-        scratch_shapes=[pltpu.VMEM((2, width, 2 * NF), BF16)],
-        compiler_params=params(12),
-        cost_estimate=cost(2 * 2 * pairs * (stations + width) * 2 * NF, 4 << 20),
-        name="early_pairs",
-    )(first_row, slot_row, *in_vmem(white0, white3, *early_in))
-
     whites = []
     late_out = None
     for i in range(n_chunks):
@@ -509,34 +592,49 @@
             cost_estimate=cost(dft_flops * rows, 4 << 20),
             name="rim_windows_%d" % i,
         )(
-            offsets,
+            *in_smem(starts),
             *in_vmem(main, *edges[2 * i : 2 * i + 2], *(edges[:2] * i)),
-            taper,
-            *in_vmem(t_odd, t_even),
-            send_rows,
-            *in_vmem(*whites),
+            *in_vmem(taper, t_odd, t_even, send_rows, *whites),
         )
         whites = whites + list(result[:2])
         late_out = result[2:]
     late_in = exchange(late_out)
+    scale = 1.0 / math.sqrt(NF * windows * n_tm)
+    early, first, hot = pl.pallas_call(
+        functools.partial(early_kernel, groups, len(buffers), n_chunks, scale),
+        out_shape=[
+            pltpu.VMEM((pairs, 2 * NF), F32),
+            pltpu.VMEM((2, pairs, 2 * NF), F32),
+            pltpu.VMEM((pairs, width), BF16),
+        ],
+        in_specs=[VMEM] * (4 + 2 * n_chunks + len(buffers)),
+        out_specs=[VMEM] * 3,
+        scratch_shapes=[
+            pltpu.VMEM((2, width, 2 * NF), BF16),
+            pltpu.VMEM((2, pairs, 2 * NF), F32),
+            pltpu.VMEM((2, pairs, 2 * NF), F32),
+        ],
+        compiler_params=params(16),
+        cost_estimate=cost(2 * 2 * pairs * (2 * stations + width) * 2 * NF, 4 << 20),
+        name="early_pairs",
+    )(first_row, slot_row, *in_vmem(white0, white3, *whites, *early_in))
 
     lag_rows = NL // n_tm
-    scale = 1.0 / math.sqrt(NF * windows * n_tm)
     result = pl.pallas_call(
-        functools.partial(late_kernel, groups, len(buffers), n_chunks, n_tm, scale),
+        functools.partial(late_kernel, groups, len(buffers), n_tm),
         out_shape=[pltpu.VMEM((lag_rows, pairs), F32)] + [pltpu.VMEM((lag_rows, pairs), BF16)] * (n_tm - 1),
-        in_specs=[VMEM] * (5 + 2 * n_chunks + len(buffers)),
+        in_specs=[VMEM] * (5 + len(buffers)),
         out_specs=[VMEM] * n_tm,
         scratch_shapes=[
             pltpu.VMEM((2, width, 2 * NF), BF16),
-            pltpu.VMEM((pairs, 2 * NF), F32),
+            pltpu.VMEM((2, pairs, 2 * NF), F32),
             pltpu.VMEM((pairs, NF), BF16),
             pltpu.VMEM((pairs, NF), BF16),
         ],
         compiler_params=params(18),
-        cost_estimate=cost(2 * 2 * pairs * (stations + width) * 2 * NF + 2 * NL * pairs * 2 * NF, 6 << 20),
+        cost_estimate=cost(2 * 2 * pairs * width * 2 * NF + 2 * NL * pairs * 2 * NF, 6 << 20),
         name="late_pairs",
-    )(first_row, slot_row, *in_vmem(early, t_odd, t_even, *whites, *late_in))
+    )(*in_vmem(early, first, hot, t_odd, t_even, *late_in))
 
     total = result[0]
     for d in range(1, n_tm):

time: 76.8 us -> 72 us (0.938)
  the two profiles are of different devices: /device:TPU:9 before, /device:TPU:24 now
where the time goes in v4:
time: 72 us; the launch traced here: 71.8 us
  Pallas kernels  28.7 us (40%)
  waiting for transfers between devices  25.2 us (35%)
  starting transfers between devices  16.8 us (23%)
  other arithmetic  0.92 us (1%)
    ppermute x3, waiting for transfers between devices, on_device(): total = total + lax.ppermute(result[d], 'tm', route).astype(F32)  22.8 us
    pallas_call x2, Pallas kernels, on_device(): pl.pallas_call(functools.partial(rim_kernel, groups, i * rows, i, last),...  10.4 us
    pallas_call x1, Pallas kernels, on_device(): pl.pallas_call(functools.partial(local_kernel, groups), out_shape=[table]...  10.2 us
    ppermute x6, starting transfers between devices, exchange(): got.append(lax.ppermute(piece, 'sta', route))  6.6 us
    ppermute x3, starting transfers between devices, on_device(): total = total + lax.ppermute(result[d], 'tm', route).astype(F32)  5.44 us
    ppermute x4, starting transfers between devices, on_device(): edges = [lax.ppermute(x, 'tm', routes[i % 2]) for i, x in enumerate(packed)]  4.75 us
    pallas_call x1, Pallas kernels, on_device(): pl.pallas_call(functools.partial(early_kernel, groups, len(buffers), n_ch...  3.77 us
    pallas_call x1, Pallas kernels, on_device(): pl.pallas_call(functools.partial(late_kernel, groups, len(buffers), n_tm)...  2.88 us
  transfers between devices with their start and end apart: 13, of which 3 were waited for; matrix products, arithmetic and copies ran while one was open for 0% of the time, Pallas kernels for 34%

profile of v4, /device:TPU:24, one launch (start us, length us, event | category | flops | bytes accessed | tf_op | source)
XLA Modules:
  0.0 71.8 jit_solution(1591064069727793178)
XLA Ops:
  0.0 1.5 %pack_edges.1 = (bf16[272,1024]{1,0:T(8,128)(2,1)S(1)}, bf16[272,1024]{1,0:T(8,128)(2,1)S(1)}, bf16[256,1024]{1,0:T(8,128)(2,1)S(1)}, bf16[256,1024]{1,0:T(8,128...) custom-call(s32[3]{0:T(128)} %offsets.1, ...), custom_call_target="tpu_custom_call" | custom-call | bytes 4194304 | tf_op jit(solution)/shard_map/pack_edges/pallas_call | solution.py:528
  1.5 0.8 %collective-permute-start = (bf16[272,1024]{1,0:T(8,128)(2,1)S(1)}, bf16[272,1024]{1,0:T(8,128)(2,1)S(1)}, u32[]{:S(2)}, u32[]{:S(2)}) collective-permute-start(bf16[272,1024]{1,0:T(8,128)(2,1)S(1)} %get-tuple-element.44), channel_id=1, source_target_pairs={{0,4},{4,0},{8,12},{12,8},{1,5},{5,1},{9,13},{13,9},{2,6},{6,2},{1... | collective-permute-start | bytes 1671176 | tf_op jit(solution)/shard_map/ppermute | solution.py:545
  2.3 0.7 collective-permute-start.1
  3.0 2.5 %collective-permute-start.2 = (bf16[256,1024]{1,0:T(8,128)(2,1)S(1)}, bf16[256,1024]{1,0:T(8,128)(2,1)S(1)}, u32[]{:S(2)}, u32[]{:S(2)}) collective-permute-start(bf16[256,1024]{1,0:T(8,128)(2,1)S(1)} %get-tuple-element.50), channel_id=1, source_target_pairs={{0,4},{4,0},{8,12},{12,8},{1,5},{5,1},{9,13},{13,9},{2,6},{6,2},{1... | collective-permute-start | bytes 1572872 | tf_op jit(solution)/shard_map/ppermute | solution.py:545
  5.6 0.7 collective-permute-start.3
  6.3 10.2 %local_windows.1 = (bf16[1024,512]{1,0:T(8,128)(2,1)S(1)}, bf16[1024,512]{1,0:T(8,128)(2,1)S(1)}, bf16[512,1024]{1,0:T(8,128)(2,1)S(1)}, bf16[512,1024]{1,0:T(8,...) custom-call(s32[3]{0:T(128)S(4)} %get-tuple-element.37.offsets, ...), custom_call_target="tpu_custom_call" | custom-call | flops 2147483648 | bytes 8388608 | tf_op jit(solution)/shard_map/local_windows/pallas_call | solution.py:557
  16.5 1.6 %collective-permute-start.6 = (bf16[16,1024]{1,0:T(8,128)(2,1)S(1)}, bf16[16,1024]{1,0:T(8,128)(2,1)S(1)}, u32[]{:S(2)}, u32[]{:S(2)}) collective-permute-start(bf16[16,1024]{1,0:T(8,128)(2,1)S(1)} %get-tuple-element.57), channel_id=1, source_target_pairs={{0,2},{1,3},{2,0},{3,1},{4,6},{5,7},{6,4},{7,5},{8,10},{9,11},{10,... | collective-permute-start | bytes 98312 | tf_op jit(solution)/shard_map/ppermute | solution.py:576
  18.0 0.0 collective-permute-done.rest_0_.rest_2_
  18.0 0.0 collective-permute-start.4
  18.0 0.0 collective-permute-done.1.rest_1_.rest_3_
  18.1 1.7 %collective-permute-start.5 = (bf16[64,1024]{1,0:T(8,128)(2,1)S(1)}, bf16[64,1024]{1,0:T(8,128)(2,1)S(1)}, u32[]{:S(2)}, u32[]{:S(2)}) collective-permute-start(bf16[64,1024]{1,0:T(8,128)(2,1)S(1)} %get-tuple-element.56), channel_id=1, source_target_pairs={{0,3},{1,0},{2,1},{3,2},{4,7},{5,4},{6,5},{7,6},{8,11},{9,8},{10,9... | collective-permute-start | bytes 393224 | tf_op jit(solution)/shard_map/ppermute | solution.py:576
  19.8 4.9 %rim_windows_0.1 = (bf16[256,1024]{1,0:T(8,128)(2,1)S(1)}, bf16[256,1024]{1,0:T(8,128)(2,1)S(1)}) custom-call(s32[3]{0:T(128)S(4)} %get-tuple-element.37.offsets, bf16[512,3072]{1,0:T(8,128)(2,1)S(1)} %copy-done, bf16[272,1024]{1,0:T(8,128)(2,1)S(1)} %collective-permute-done.rest_0_.rest_2_, bf16[272,1024]{1,0:T(8,128)(2,1)S(1)} %collective-permute-done.1.rest_1_.rest_3_, ...), custom_call_target="tpu_custom_call" | custom-call | flops 1073741824 | bytes 4194304 | tf_op jit(solution)/shard_map/rim_windows_0/pallas_call | solution.py:585
  24.7 2.4 %collective-permute-done.2.rest_0_ = bf16[256,1024]{1,0:T(8,128)(2,1)S(1)} collective-permute-done((bf16[256,1024]{1,0:T(8,128)(2,1)S(1)}, bf16[256,1024]{1,0:T(8,128)(2,1)S(1)}, u32[]{:S(2)}, u32[]{:S(2)}) %collective-permute-start.2) | collective-permute-done | bytes 524320 | tf_op jit(solution)/shard_map/ppermute | solution.py:545
  27.2 0.0 collective-permute-done.3.rest_1_
  27.2 5.5 %rim_windows_1.1 = (bf16[256,1024]{1,0:T(8,128)(2,1)S(1)}, bf16[256,1024]{1,0:T(8,128)(2,1)S(1)}, bf16[64,1024]{1,0:T(8,128)(2,1)S(1)}, bf16[64,1024]{1,0:T(8,12...) custom-call(s32[3]{0:T(128)S(4)} %get-tuple-element.37.offsets, bf16[512,3072]{1,0:T(8,128)(2,1)S(1)} %copy-done, ...), custom_call_target="tpu_custom_call" | custom-call | flops 1073741824 | bytes 4194304 | tf_op jit(solution)/shard_map/rim_windows_1/pallas_call | solution.py:585
  32.7 1.6 %collective-permute-start.9 = (bf16[16,1024]{1,0:T(8,128)(2,1)S(1)}, bf16[16,1024]{1,0:T(8,128)(2,1)S(1)}, u32[]{:S(2)}, u32[]{:S(2)}) collective-permute-start(bf16[16,1024]{1,0:T(8,128)(2,1)S(1)} %get-tuple-element.64), channel_id=1, source_target_pairs={{0,2},{1,3},{2,0},{3,1},{4,6},{5,7},{6,4},{7,5},{8,10},{9,11},{10,... | collective-permute-start | bytes 98312 | tf_op jit(solution)/shard_map/ppermute | solution.py:576
  34.2 0.0 collective-permute-start.7
  34.2 0.0 collective-permute-done.6.rest_7_
  34.2 1.7 %collective-permute-start.8 = (bf16[64,1024]{1,0:T(8,128)(2,1)S(1)}, bf16[64,1024]{1,0:T(8,128)(2,1)S(1)}, u32[]{:S(2)}, u32[]{:S(2)}) collective-permute-start(bf16[64,1024]{1,0:T(8,128)(2,1)S(1)} %get-tuple-element.63), channel_id=1, source_target_pairs={{0,3},{1,0},{2,1},{3,2},{4,7},{5,4},{6,5},{7,6},{8,11},{9,8},{10,9... | collective-permute-start | bytes 393224 | tf_op jit(solution)/shard_map/ppermute | solution.py:576
  36.0 0.0 collective-permute-done.4.rest_5_
  36.0 0.0 collective-permute-done.5.rest_6_
  36.0 3.8 %early_pairs.1 = (f32[512,1024]{1,0:T(8,128)S(1)}, f32[2,512,1024]{2,1,0:T(8,128)S(1)}, bf16[512,128]{1,0:T(8,128)(2,1)S(1)}) custom-call(s32[1,512]{1,0:T(1,128)S(1)} %bitcast.2, s32[1,512]{1,0:T(1,128)S(1)} %bitcast.3, bf16[512,1024]{1,0:T(8,128)(2,1)S(1)} %get-tuple-element.42.white0, bf16[512,1024]{1,0:T(8,128)(2,1)S(1)} %get-tuple-element.43.white3, ...), custom_call_target="tpu_custom_call" | custom-call | flops 2415919104 | bytes 4194304 | tf_op jit(solution)/shard_map/early_pairs/pallas_call | solution.py:603
  39.8 0.0 collective-permute-done.7.rest_1_
  39.8 0.0 collective-permute-done.8.rest_2_
  39.8 2.9 %late_pairs.1 = (f32[256,512]{1,0:T(8,128)S(1)}, bf16[256,512]{1,0:T(8,128)(2,1)S(1)}, bf16[256,512]{1,0:T(8,128)(2,1)S(1)}, bf16[256,512]{1,0:T(8,128)(2,1)S(1)}) custom-call(f32[512,1024]{1,0:T(8,128)S(1)} %get-tuple-element.58.early, f32[2,512,1024]{2,1,0:T(8,128)S(1)} %get-tuple-element.59.first, bf16[512,128]{1,0:T(8,128)(2,1)S(1)} %get-tuple-element.60.hot, ...), custom_call_target="tpu_custom_call" | custom-call | flops 1342177280 | bytes 6291456 | tf_op jit(solution)/shard_map/late_pairs/pallas_call | solution.py:623
  42.7 0.6 collective-permute-start.10
  43.3 4.5 %collective-permute-start.11 = (bf16[256,512]{1,0:T(8,128)(2,1)S(1)}, bf16[256,512]{1,0:T(8,128)(2,1)S(1)}, u32[]{:S(2)}, u32[]{:S(2)}) collective-permute-start(bf16[256,512]{1,0:T(8,128)(2,1)S(1)} %get-tuple-element.67), channel_id=1, source_target_pairs={{0,8},{4,12},{8,0},{12,4},{1,9},{5,13},{9,1},{13,5},{2,10},{6,14},... | collective-permute-start | bytes 786440 | tf_op jit(solution)/shard_map/ppermute | solution.py:642
  47.8 0.3 collective-permute-start.12
  48.1 4.7 %collective-permute-done.10 = bf16[256,512]{1,0:T(8,128)(2,1)S(1)} collective-permute-done((bf16[256,512]{1,0:T(8,128)(2,1)S(1)}, bf16[256,512]{1,0:T(8,128)(2,1)S(1)}, u32[]{:S(2)}, u32[]{:S(2)}) %collective-permute-start.10) | collective-permute-done | bytes 262176 | tf_op jit(solution)/shard_map/ppermute | solution.py:642
  52.9 18.0 %collective-permute-done.11 = bf16[256,512]{1,0:T(8,128)(2,1)S(1)} collective-permute-done((bf16[256,512]{1,0:T(8,128)(2,1)S(1)}, bf16[256,512]{1,0:T(8,128)(2,1)S(1)}, u32[]{:S(2)}, u32[]{:S(2)}) %collective-permute-start.11) | collective-permute-done | bytes 262176 | tf_op jit(solution)/shard_map/ppermute | solution.py:642
  70.9 0.0 collective-permute-done.12
  70.9 0.9 %convert_add_fusion = f32[256,512]{1,0:T(8,128)} fusion(bf16[256,512]{1,0:T(8,128)(2,1)S(1)} %collective-permute-done.12, bf16[256,512]{1,0:T(8,128)(2,1)S(1)} %collective-permute-done.11, f32[256,512]{1,0:T(8,128)S(1)} %get-tuple-element.65, bf16[256,512]{1,0:T(8,128)(2,1)S(1)} %collective-permute-done.10), kind=kLoop, calls=%fused_computation | loop fusion | flops 786432 | bytes 1835008 | tf_op jit(solution)/shard_map/add | solution.py:642
  (7 shorter events, 0.0 us)
Async XLA Ops:
  0.0 6.3 %copy-start = (bf16[512,3072]{1,0:T(8,128)(2,1)S(1)}, bf16[512,3072]{1,0:T(8,128)(2,1)}, u32[]{:S(2)}) copy-start(bf16[512,3072]{1,0:T(8,128)(2,1)} %main.7) | copy-start | bytes 9437188
  1.5 16.5 %collective-permute-start = (bf16[272,1024]{1,0:T(8,128)(2,1)S(1)}, bf16[272,1024]{1,0:T(8,128)(2,1)S(1)}, u32[]{:S(2)}, u32[]{:S(2)}) collective-permute-start(bf16[272,1024]{1,0:T(8,128)(2,1)S(1)} %get-tuple-element.44), channel_id=1, source_target_pairs={{0,4},{4,0},{8,12},{12,8},{1,5},{5,1},{9,13},{13,9},{2,6},{6,2},{1... | collective-permute-start | bytes 1671176 | tf_op jit(solution)/shard_map/ppermute | solution.py:545
  2.3 15.7 %collective-permute-start.1 = (bf16[272,1024]{1,0:T(8,128)(2,1)S(1)}, bf16[272,1024]{1,0:T(8,128)(2,1)S(1)}, u32[]{:S(2)}, u32[]{:S(2)}) collective-permute-start(bf16[272,1024]{1,0:T(8,128)(2,1)S(1)} %get-tuple-element.45), channel_id=1, source_target_pairs={{0,0},{4,8},{8,4},{12,12},{1,1},{5,9},{9,5},{13,13},{2,2},{6,10},{... | collective-permute-start | bytes 1671176 | tf_op jit(solution)/shard_map/ppermute | solution.py:545
  3.0 24.1 %collective-permute-start.2 = (bf16[256,1024]{1,0:T(8,128)(2,1)S(1)}, bf16[256,1024]{1,0:T(8,128)(2,1)S(1)}, u32[]{:S(2)}, u32[]{:S(2)}) collective-permute-start(bf16[256,1024]{1,0:T(8,128)(2,1)S(1)} %get-tuple-element.50), channel_id=1, source_target_pairs={{0,4},{4,0},{8,12},{12,8},{1,5},{5,1},{9,13},{13,9},{2,6},{6,2},{1... | collective-permute-start | bytes 1572872 | tf_op jit(solution)/shard_map/ppermute | solution.py:545
  5.6 21.6 %collective-permute-start.3 = (bf16[256,1024]{1,0:T(8,128)(2,1)S(1)}, bf16[256,1024]{1,0:T(8,128)(2,1)S(1)}, u32[]{:S(2)}, u32[]{:S(2)}) collective-permute-start(bf16[256,1024]{1,0:T(8,128)(2,1)S(1)} %get-tuple-element.51), channel_id=1, source_target_pairs={{0,0},{4,8},{8,4},{12,12},{1,1},{5,9},{9,5},{13,13},{2,2},{6,10},{... | collective-permute-start | bytes 1572872 | tf_op jit(solution)/shard_map/ppermute | solution.py:545
  16.5 17.7 %collective-permute-start.6 = (bf16[16,1024]{1,0:T(8,128)(2,1)S(1)}, bf16[16,1024]{1,0:T(8,128)(2,1)S(1)}, u32[]{:S(2)}, u32[]{:S(2)}) collective-permute-start(bf16[16,1024]{1,0:T(8,128)(2,1)S(1)} %get-tuple-element.57), channel_id=1, source_target_pairs={{0,2},{1,3},{2,0},{3,1},{4,6},{5,7},{6,4},{7,5},{8,10},{9,11},{10,... | collective-permute-start | bytes 98312 | tf_op jit(solution)/shard_map/ppermute | solution.py:576
  18.0 17.9 %collective-permute-start.4 = (bf16[64,1024]{1,0:T(8,128)(2,1)S(1)}, bf16[64,1024]{1,0:T(8,128)(2,1)S(1)}, u32[]{:S(2)}, u32[]{:S(2)}) collective-permute-start(bf16[64,1024]{1,0:T(8,128)(2,1)S(1)} %get-tuple-element.55), channel_id=1, source_target_pairs={{0,1},{1,2},{2,3},{3,0},{4,5},{5,6},{6,7},{7,4},{8,9},{9,10},{10,1... | collective-permute-start | bytes 393224 | tf_op jit(solution)/shard_map/ppermute | solution.py:576
  18.1 17.9 %collective-permute-start.5 = (bf16[64,1024]{1,0:T(8,128)(2,1)S(1)}, bf16[64,1024]{1,0:T(8,128)(2,1)S(1)}, u32[]{:S(2)}, u32[]{:S(2)}) collective-permute-start(bf16[64,1024]{1,0:T(8,128)(2,1)S(1)} %get-tuple-element.56), channel_id=1, source_target_pairs={{0,3},{1,0},{2,1},{3,2},{4,7},{5,4},{6,5},{7,6},{8,11},{9,8},{10,9... | collective-permute-start | bytes 393224 | tf_op jit(solution)/shard_map/ppermute | solution.py:576
  27.2 8.8 %copy-start.1 = (s32[512]{0:T(512)S(1)}, s32[512]{0:T(512)}, u32[]{:S(2)}) copy-start(s32[512]{0:T(512)} %param.10) | copy-start | bytes 6148
  27.2 8.8 %copy-start.2 = (s32[512]{0:T(512)S(1)}, s32[512]{0:T(512)}, u32[]{:S(2)}) copy-start(s32[512]{0:T(512)} %param.11) | copy-start | bytes 6148
  32.7 7.1 %collective-permute-start.9 = (bf16[16,1024]{1,0:T(8,128)(2,1)S(1)}, bf16[16,1024]{1,0:T(8,128)(2,1)S(1)}, u32[]{:S(2)}, u32[]{:S(2)}) collective-permute-start(bf16[16,1024]{1,0:T(8,128)(2,1)S(1)} %get-tuple-element.64), channel_id=1, source_target_pairs={{0,2},{1,3},{2,0},{3,1},{4,6},{5,7},{6,4},{7,5},{8,10},{9,11},{10,... | collective-permute-start | bytes 98312 | tf_op jit(solution)/shard_map/ppermute | solution.py:576
  34.2 5.6 %collective-permute-start.7 = (bf16[64,1024]{1,0:T(8,128)(2,1)S(1)}, bf16[64,1024]{1,0:T(8,128)(2,1)S(1)}, u32[]{:S(2)}, u32[]{:S(2)}) collective-permute-start(bf16[64,1024]{1,0:T(8,128)(2,1)S(1)} %get-tuple-element.62), channel_id=1, source_target_pairs={{0,1},{1,2},{2,3},{3,0},{4,5},{5,6},{6,7},{7,4},{8,9},{9,10},{10,1... | collective-permute-start | bytes 393224 | tf_op jit(solution)/shard_map/ppermute | solution.py:576
  34.2 5.6 %collective-permute-start.8 = (bf16[64,1024]{1,0:T(8,128)(2,1)S(1)}, bf16[64,1024]{1,0:T(8,128)(2,1)S(1)}, u32[]{:S(2)}, u32[]{:S(2)}) collective-permute-start(bf16[64,1024]{1,0:T(8,128)(2,1)S(1)} %get-tuple-element.63), channel_id=1, source_target_pairs={{0,3},{1,0},{2,1},{3,2},{4,7},{5,4},{6,5},{7,6},{8,11},{9,8},{10,9... | collective-permute-start | bytes 393224 | tf_op jit(solution)/shard_map/ppermute | solution.py:576
  42.7 10.2 %collective-permute-start.10 = (bf16[256,512]{1,0:T(8,128)(2,1)S(1)}, bf16[256,512]{1,0:T(8,128)(2,1)S(1)}, u32[]{:S(2)}, u32[]{:S(2)}) collective-permute-start(bf16[256,512]{1,0:T(8,128)(2,1)S(1)} %get-tuple-element.66), channel_id=1, source_target_pairs={{0,4},{4,8},{8,12},{12,0},{1,5},{5,9},{9,13},{13,1},{2,6},{6,10},{... | collective-permute-start | bytes 786440 | tf_op jit(solution)/shard_map/ppermute | solution.py:642
  43.3 27.6 %collective-permute-start.11 = (bf16[256,512]{1,0:T(8,128)(2,1)S(1)}, bf16[256,512]{1,0:T(8,128)(2,1)S(1)}, u32[]{:S(2)}, u32[]{:S(2)}) collective-permute-start(bf16[256,512]{1,0:T(8,128)(2,1)S(1)} %get-tuple-element.67), channel_id=1, source_target_pairs={{0,8},{4,12},{8,0},{12,4},{1,9},{5,13},{9,1},{13,5},{2,10},{6,14},... | collective-permute-start | bytes 786440 | tf_op jit(solution)/shard_map/ppermute | solution.py:642
  47.8 23.1 %collective-permute-start.12 = (bf16[256,512]{1,0:T(8,128)(2,1)S(1)}, bf16[256,512]{1,0:T(8,128)(2,1)S(1)}, u32[]{:S(2)}, u32[]{:S(2)}) collective-permute-start(bf16[256,512]{1,0:T(8,128)(2,1)S(1)} %get-tuple-element.68), channel_id=1, source_target_pairs={{0,12},{4,0},{8,4},{12,8},{1,13},{5,1},{9,5},{13,9},{2,14},{6,2},{... | collective-permute-start | bytes 786440 | tf_op jit(solution)/shard_map/ppermute | solution.py:642

commit v5 on v4

--- a/solution.py
+++ b/solution.py
@@ -26,12 +26,15 @@
 ROWS = 16
 N_SMALL = 4
 UNIT = 512
-TURN_UNROLL = 4
-FOLD_UNROLL = 4
-WHITEN_UNROLL = 8
 VMEM = pl.BlockSpec(memory_space=pltpu.VMEM)
 SMEM = pl.BlockSpec(memory_space=pltpu.SMEM)
 ANY = pl.BlockSpec(memory_space=pltpu.HBM)
+
+
+def loop(count, most, body):
+    trips = count // ROWS
+    unroll = max(u for u in range(1, most + 1) if trips % u == 0)
+    lax.fori_loop(0, trips, body, 0, unroll=unroll)
 
 
 def small_tables():
@@ -92,15 +95,15 @@
         sums_ref[rows, :] = turned[0]
         return carry
 
-    lax.fori_loop(0, count // ROWS, turn, 0, unroll=TURN_UNROLL)
+    loop(count, 4, turn)
 
     def average(i, carry):
-        rows = pl.ds(pl.multiple_of(i * 8 * ROWS, ROWS), 8 * ROWS)
+        rows = pl.ds(pl.multiple_of(i * ROWS, ROWS), ROWS)
         mean = jnp.sum(sums_ref[rows, :], axis=1, keepdims=True) * (1.0 / WIN)
-        sums_ref[rows, :] = jnp.broadcast_to(mean, (8 * ROWS, LANES))
+        sums_ref[rows, :] = jnp.broadcast_to(mean, (ROWS, LANES))
         return carry
 
-    lax.fori_loop(0, count // (8 * ROWS), average, 0)
+    loop(count, 10, average)
 
     def fold(i, carry):
         rows = pl.ds(pl.multiple_of(i * ROWS, ROWS), ROWS)
@@ -116,15 +119,15 @@
             odd_ref[spots[c], put, :] = (low - high) * signs[c].astype(BF16)
         return carry
 
-    lax.fori_loop(0, count // ROWS, fold, 0, unroll=FOLD_UNROLL)
-
-
-def transform(t_odd, t_even, scratch):
+    loop(count, 4, fold)
+
+
+def transform(count, t_odd, t_even, scratch):
     even_ref, odd_ref, spec = scratch[3:6]
-    odd = jnp.concatenate([odd_ref[c] for c in range(HC)], axis=1)
-    spec[:, : 2 * QB] = jnp.dot(odd, t_odd[...], preferred_element_type=F32)
-    even = jnp.concatenate([even_ref[c] for c in range(HC)], axis=1)
-    spec[:, 2 * QB :] = jnp.dot(even, t_even[...], preferred_element_type=F32)
+    odd = jnp.concatenate([odd_ref[c, :count] for c in range(HC)], axis=1)
+    spec[:count, : 2 * QB] = jnp.dot(odd, t_odd[...], preferred_element_type=F32)
+    even = jnp.concatenate([even_ref[c, :count] for c in range(HC)], axis=1)
+    spec[:count, 2 * QB :] = jnp.dot(even, t_even[...], preferred_element_type=F32)
 
 
 def whiten_rows(first_row, count, live, out_ref, scratch):
@@ -162,7 +165,7 @@
         out_ref[to, 3 * QB :] = (e_im * inv_even).astype(BF16)
         return carry
 
-    lax.fori_loop(0, count // ROWS, group, 0, unroll=WHITEN_UNROLL)
+    loop(count, 8, group)
 
 
 def slots(c):
@@ -219,14 +222,14 @@
                 ref[w * cap : (w + 1) * cap, :] = rows[w, pl.ds(first, cap), :]
 
 
-def scratches(n_sta, cap):
+def scratches(n_sta, cap, rows):
     return [
         pltpu.VMEM((1, WIN), F32),
-        pltpu.VMEM((CHUNKS, UNIT, LANES), F32),
-        pltpu.VMEM((UNIT, LANES), F32),
-        pltpu.VMEM((HC, UNIT, LANES), BF16),
-        pltpu.VMEM((HC, UNIT, LANES), BF16),
-        pltpu.VMEM((UNIT, 2 * NF), F32),
+        pltpu.VMEM((CHUNKS, rows, LANES), F32),
+        pltpu.VMEM((rows, LANES), F32),
+        pltpu.VMEM((HC, rows, LANES), BF16),
+        pltpu.VMEM((HC, rows, LANES), BF16),
+        pltpu.VMEM((rows, 2 * NF), F32),
         pltpu.VMEM((2, n_sta * cap, 2 * NF), BF16),
     ]
 
@@ -256,7 +259,7 @@
 
         for pick, start, live, white in ((pick0, start0, 1.0, white0), (pick3, start3, live3, white3)):
             prepare(pick, start, count, 0, taper, scratch)
-            transform(t_odd, t_even, scratch)
+            transform(count, t_odd, t_even, scratch)
             whiten_rows(0, count, live, white.at[first : first + count], scratch)
     write_rows(send_rows, ((white0,), (white3,)), *groups, sends)
 
@@ -271,8 +274,9 @@
     return routes
 
 
-def pack_kernel(rows, n_out, offsets, main, *rest):
-    small = rest[: N_SMALL]
+def pack_kernel(sizes, offsets, main, *rest):
+    n_out = 2 * len(sizes)
+    small = rest[:N_SMALL]
     outs = rest[N_SMALL : N_SMALL + n_out]
     offsets_out = rest[N_SMALL + n_out]
     small_out = rest[N_SMALL + n_out + 1 : -1]
@@ -284,8 +288,8 @@
         chunk, swap = i // 2, i % 2
         at = jnp.where(t % 2 == swap, 2 * HALF, 0)
         lanes = pl.ds(pl.multiple_of(at, LANES), HALF)
-        source = main.at[pl.ds(chunk * rows, rows), lanes]
-        return pltpu.make_async_copy(source, outs[i].at[pl.ds(0, rows)], sems.at[i])
+        source = main.at[pl.ds(sum(sizes[:chunk]), sizes[chunk]), lanes]
+        return pltpu.make_async_copy(source, outs[i].at[pl.ds(0, sizes[chunk])], sems.at[i])
 
     first = pltpu.make_async_copy(offsets, offsets_out, sems.at[n_out])
     first.start()
@@ -297,7 +301,7 @@
         else:
             @pl.when(t == n - 1)
             def _():
-                outs[i][0:rows, :] = jnp.zeros((rows, HALF), BF16)
+                outs[i][0 : sizes[i // 2], :] = jnp.zeros((sizes[i // 2], HALF), BF16)
 
             @pl.when(t < n - 1)
             def _():
@@ -310,7 +314,7 @@
     high, low = start // 8, start % 8
     lane = lax.broadcasted_iota(jnp.int32, (ROWS, HALF), 1)
     for i in range(2):
-        outs[i][rows:, :] = jnp.where(lane < NF, high, low).astype(F32).astype(BF16)
+        outs[i][sizes[0] :, :] = jnp.where(lane < NF, high, low).astype(F32).astype(BF16)
     for copy in copies:
         copy.wait()
     for i in range(n_out):
@@ -320,7 +324,8 @@
                 edge(i).wait()
 
 
-def sent_start(ref, rows):
+def sent_start(ref):
+    rows = ref.shape[0] - ROWS
     high = jnp.max(ref[rows:, 0:LANES].astype(F32))
     low = jnp.max(ref[rows:, HALF - LANES :].astype(F32))
     return (high * 8.0 + low).astype(jnp.int32)
@@ -333,6 +338,7 @@
     taper, t_odd, t_even, send_rows = rest[:4]
     rest = rest[4:]
     older = rest[: 2 * earlier]
+    rest = rest[1:] if last else rest
     whites = rest[2 * earlier : 2 * earlier + 2]
     scratch = rest[-7:]
     sends = rest[2 * earlier + 2 : -7] + (scratch[6],)
@@ -341,7 +347,7 @@
     lane = lax.broadcasted_iota(jnp.int32, (ROWS, LANES), 1)
     for swap in range(2):
         ahead = t % 2 == swap
-        start = jnp.where(ahead, offsets[1] - STEP, sent_start(heads[swap], count))
+        start = jnp.where(ahead, offsets[1] - STEP, sent_start(heads[swap]))
         sign = jnp.where(ahead, 1, -1)
         least = jnp.where(ahead, 0, 1)
         whole = jnp.where(ahead, 2 * HALF, 0)
@@ -355,7 +361,7 @@
             return jnp.where(base >= least - sign * (c * LANES), own, part(recv[swap], 0, rows, c))
 
         prepare(pick, start, count, swap * count, taper, scratch)
-    transform(t_odd, t_even, scratch)
+    transform(2 * count, t_odd, t_even, scratch)
     live = jnp.where(t > 0, 1.0, 0.0).astype(F32)
     whiten_rows(0, count, 1.0, whites[0], scratch)
     whiten_rows(count, count, live, whites[1], scratch)
@@ -376,7 +382,7 @@
     return one_hot(column(place), width)
 
 
-def second_rows(groups, pieces, hot, incoming, out):
+def second_rows(groups, pieces, hot, first_pair, incoming, out):
     near, far, n_sta, cap = groups
     width = incoming.shape[1]
     for w in range(2):
@@ -389,7 +395,8 @@
             incoming[w, at:, :] = jnp.zeros((width - at, 2 * NF), BF16)
     for w in range(2):
         for c in range(0, 2 * NF, NF):
-            out[w, :, c : c + NF] = jnp.dot(hot[...], incoming[w, :, c : c + NF], preferred_element_type=F32)
+            rows = hot[first_pair : first_pair + out.shape[1], :]
+            out[w, :, c : c + NF] = jnp.dot(rows, incoming[w, :, c : c + NF], preferred_element_type=F32)
 
 
 def first_rows(hots, spectra, scale, out):
@@ -411,13 +418,13 @@
     return hots
 
 
-def add_products(first, second, rows, c, start):
+def add_products(first, second, first_at, second_at, c, start):
     re_lanes = slice(c, c + LANES)
     im_lanes = slice(NF + c, NF + c + LANES)
     one, two = start
     for w in range(2):
-        a_i, b_i = first[w, rows, re_lanes], first[w, rows, im_lanes]
-        a_j, b_j = second[w, rows, re_lanes], second[w, rows, im_lanes]
+        a_i, b_i = first[w, first_at, re_lanes], first[w, first_at, im_lanes]
+        a_j, b_j = second[w, second_at, re_lanes], second[w, second_at, im_lanes]
         re = a_i * a_j + b_i * b_j
         im = b_i * a_j - a_i * b_j
         if c < QB:
@@ -427,69 +434,85 @@
     return one, two
 
 
-def early_kernel(groups, n_pieces, n_white, scale, pair_first, pair_slot, white0, white3, *rest):
-    whites = rest[: 2 * n_white]
-    rest = rest[2 * n_white :]
+def early_kernel(groups, n_pieces, scale, pair_first, pair_slot, white0, white3, *rest):
     pieces = rest[:n_pieces]
-    cross, later, hot = rest[n_pieces : n_pieces + 3]
-    incoming, first, second = rest[n_pieces + 3 :]
+    cross, hot = rest[n_pieces : n_pieces + 2]
+    incoming, first, second = rest[n_pieces + 2 :]
     pairs = pair_first.shape[1]
-    col = column(pair_first[...])
-    hots = station_tables(col, (white0,))
+    hots = station_tables(column(pair_first[...]), (white0,))
     first_rows(hots, (white0,), scale, first.at[0])
     first_rows(hots, (white3,), scale, first.at[1])
     hot[...] = slot_table(groups, pair_slot, hot.shape[1])
-    second_rows(groups, pieces, hot, incoming, second)
+    second_rows(groups, pieces, hot, 0, incoming, second)
 
     def group(i, carry):
         rows = pl.ds(pl.multiple_of(i * ROWS, ROWS), ROWS)
         for c in range(0, NF, LANES):
-            one, two = add_products(first, second, rows, c, (0.0, 0.0))
+            one, two = add_products(first, second, rows, rows, c, (0.0, 0.0))
             cross[rows, c : c + LANES] = one
             cross[rows, NF + c : NF + c + LANES] = two
         return carry
 
-    lax.fori_loop(0, pairs // ROWS, group, 0, unroll=2)
-    hots = station_tables(col, whites[0::2])
-    first_rows(hots, whites[0::2], scale, later.at[0])
-    first_rows(hots, whites[1::2], scale, later.at[1])
-
-
-def late_kernel(groups, n_pieces, n_dest, early, first, hot, t_odd, t_even, *rest):
+    loop(pairs, 2, group)
+
+
+def first_kernel(scale, n_white, pair_first, *rest):
+    whites = rest[: 2 * n_white]
+    out = rest[2 * n_white]
+    hots = station_tables(column(pair_first[...]), whites[0::2])
+    first_rows(hots, whites[0::2], scale, out.at[0])
+    first_rows(hots, whites[1::2], scale, out.at[1])
+
+
+def late_kernel(groups, n_pieces, n_dest, first_pair, early, first, hot, t_odd, t_even, *rest):
     pieces = rest[:n_pieces]
-    own = rest[n_pieces]
-    outs = rest[n_pieces + 1 : n_pieces + n_dest]
-    incoming, second, x_odd, x_even = rest[n_pieces + n_dest :]
-    pairs = early.shape[0]
-    second_rows(groups, pieces, hot, incoming, second)
+    send, keep = rest[n_pieces : n_pieces + 2]
+    incoming, second, x_odd, x_even = rest[n_pieces + 2 :]
+    pairs = send.shape[1]
+    second_rows(groups, pieces, hot, first_pair, incoming, second)
 
     def group(i, carry):
         rows = pl.ds(pl.multiple_of(i * ROWS, ROWS), ROWS)
+        full = pl.ds(pl.multiple_of(first_pair + i * ROWS, ROWS), ROWS)
         for c in range(0, NF, LANES):
-            start = (early[rows, c : c + LANES], early[rows, NF + c : NF + c + LANES])
-            one, two = add_products(first, second, rows, c, start)
+            start = (early[full, c : c + LANES], early[full, NF + c : NF + c + LANES])
+            one, two = add_products(first, second, full, rows, c, start)
             out = x_odd if c < QB else x_even
             at = c % QB
             out[rows, at : at + LANES] = one.astype(BF16)
             out[rows, QB + at : QB + at + LANES] = two.astype(BF16)
         return carry
 
-    lax.fori_loop(0, pairs // ROWS, group, 0, unroll=2)
-    rows = own.shape[0]
+    loop(pairs, 2, group)
+    lag_rows = NL // n_dest
     me = lax.axis_index("tm")
     dims = (((1,), (1,)), ((), ()))
-    order = list(range(n_dest))
-    spots = [pl.ds(pl.multiple_of(lax.rem(me + d, n_dest) * rows, rows), rows) for d in order]
-    odd = jnp.concatenate([t_odd[at, :] for at in spots], axis=0)
-    even = jnp.concatenate([t_even[at, :] for at in spots], axis=0)
-    value = lax.dot_general(odd, x_odd[...], dims, preferred_element_type=F32)
-    value = value + lax.dot_general(even, x_even[...], dims, preferred_element_type=F32)
-    for d in order:
-        piece = value[d * rows : (d + 1) * rows, :]
-        if d == 0:
-            own[...] = piece
-        else:
-            outs[d - 1][...] = piece.astype(BF16)
+    for out, order in ((send, range(1, n_dest, 2)), (keep, range(0, n_dest, 2))):
+        spots = [
+            pl.ds(pl.multiple_of(jnp.bitwise_xor(me, r) * lag_rows, lag_rows), lag_rows) for r in order
+        ]
+        odd = jnp.concatenate([t_odd[at, :] for at in spots], axis=0)
+        even = jnp.concatenate([t_even[at, :] for at in spots], axis=0)
+        value = lax.dot_general(odd, x_odd[...], dims, preferred_element_type=F32)
+        value = value + lax.dot_general(even, x_even[...], dims, preferred_element_type=F32)
+        out[...] = value.astype(out.dtype)
+
+
+def merge_kernel(lag_rows, keep, received, send, kept):
+    for k in range(keep.shape[0] // lag_rows):
+        rows = slice(k * lag_rows, (k + 1) * lag_rows)
+        out, j = (send, k // 2) if k % 2 else (kept, k // 2)
+        value = keep[rows, :] + received[rows, :].astype(F32)
+        out[j * lag_rows : (j + 1) * lag_rows, :] = value.astype(out.dtype)
+
+
+def finish_kernel(*refs):
+    out = refs[-1]
+    at = 0
+    for keep, received in zip(refs[0:-1:2], refs[1:-1:2]):
+        width = keep.shape[1]
+        out[:, at : at + width] = keep[...] + received[...].astype(F32)
+        at += width
 
 
 def in_vmem(*arrays):
@@ -520,15 +543,16 @@
     pairs = pair_first.shape[0]
     cap = send_rows.shape[1] // n_sta
 
-    n_chunks = 2
-    rows = stations // n_chunks
+    sizes = (stations * 5 // 8, stations * 3 // 8)
+    n_chunks = len(sizes)
     main, = in_vmem(traces)
     routes = swap_routes(n_tm)
     small = [jnp.asarray(x) for x in small_tables()] + [jnp.asarray(taper_row()), send_rows]
     packed = pl.pallas_call(
-        functools.partial(pack_kernel, rows, 2 * n_chunks),
+        functools.partial(pack_kernel, sizes),
         out_shape=[
-            pltpu.VMEM((rows + (ROWS if i < 2 else 0), HALF), BF16) for i in range(2 * n_chunks)
+            pltpu.VMEM((sizes[i // 2] + (ROWS if i < 2 else 0), HALF), BF16)
+            for i in range(2 * n_chunks)
         ]
         + [pltpu.SMEM(offsets.shape, jnp.int32)]
         + [pltpu.VMEM(x.shape, x.dtype) for x in small],
@@ -559,7 +583,7 @@
         out_shape=[table] * 2 + [spectrum] * 2 + buffers,
         in_specs=[SMEM] + [VMEM] * 5,
         out_specs=[VMEM] * (4 + len(buffers)),
-        scratch_shapes=scratches(n_sta, cap),
+        scratch_shapes=scratches(n_sta, cap, UNIT),
         compiler_params=params(18),
         cost_estimate=cost(dft_flops * stations, 8 << 20),
         name="local_windows",
@@ -577,70 +601,112 @@
         return got
 
     early_in = exchange(local[4:])
+    scale = 1.0 / math.sqrt(NF * windows * n_tm)
+    pair_scratch = [
+        pltpu.VMEM((2, width, 2 * NF), BF16),
+        pltpu.VMEM((2, pairs, 2 * NF), F32),
+        pltpu.VMEM((2, pairs, 2 * NF), F32),
+    ]
+    early, hot = pl.pallas_call(
+        functools.partial(early_kernel, groups, len(buffers), scale),
+        out_shape=[pltpu.VMEM((pairs, 2 * NF), F32), pltpu.VMEM((pairs, width), BF16)],
+        in_specs=[VMEM] * (4 + len(buffers)),
+        out_specs=[VMEM] * 2,
+        scratch_shapes=pair_scratch,
+        compiler_params=params(16),
+        cost_estimate=cost(2 * 2 * pairs * (stations + width) * 2 * NF, 4 << 20),
+        name="early_pairs",
+    )(first_row, slot_row, *in_vmem(white0, white3, *early_in))
+
     whites = []
     late_out = None
     for i in range(n_chunks):
         last = i == n_chunks - 1
+        rows = sizes[i]
         chunk = pltpu.VMEM((rows, 2 * NF), BF16)
         result = pl.pallas_call(
-            functools.partial(rim_kernel, groups, i * rows, i, last),
+            functools.partial(rim_kernel, groups, sum(sizes[:i]), i, last),
             out_shape=[chunk] * 2 + (buffers if last else []),
-            in_specs=[SMEM] + [VMEM] * (7 + 4 * i),
+            in_specs=[SMEM] + [VMEM] * (7 + 4 * i + (1 if last else 0)),
             out_specs=[VMEM] * (2 + (len(buffers) if last else 0)),
-            scratch_shapes=scratches(n_sta, cap),
-            compiler_params=params(18),
+            scratch_shapes=scratches(n_sta, cap, 2 * rows),
+            compiler_params=params(22),
             cost_estimate=cost(dft_flops * rows, 4 << 20),
             name="rim_windows_%d" % i,
         )(
             *in_smem(starts),
             *in_vmem(main, *edges[2 * i : 2 * i + 2], *(edges[:2] * i)),
             *in_vmem(taper, t_odd, t_even, send_rows, *whites),
+            *in_vmem(*([hot] if last else [])),
         )
         whites = whites + list(result[:2])
         late_out = result[2:]
     late_in = exchange(late_out)
-    scale = 1.0 / math.sqrt(NF * windows * n_tm)
-    early, first, hot = pl.pallas_call(
-        functools.partial(early_kernel, groups, len(buffers), n_chunks, scale),
-        out_shape=[
-            pltpu.VMEM((pairs, 2 * NF), F32),
-            pltpu.VMEM((2, pairs, 2 * NF), F32),
-            pltpu.VMEM((pairs, width), BF16),
-        ],
-        in_specs=[VMEM] * (4 + 2 * n_chunks + len(buffers)),
-        out_specs=[VMEM] * 3,
-        scratch_shapes=[
-            pltpu.VMEM((2, width, 2 * NF), BF16),
-            pltpu.VMEM((2, pairs, 2 * NF), F32),
-            pltpu.VMEM((2, pairs, 2 * NF), F32),
-        ],
-        compiler_params=params(16),
-        cost_estimate=cost(2 * 2 * pairs * (2 * stations + width) * 2 * NF, 4 << 20),
-        name="early_pairs",
-    )(first_row, slot_row, *in_vmem(white0, white3, *whites, *early_in))
+    first = pl.pallas_call(
+        functools.partial(first_kernel, scale, n_chunks),
+        out_shape=pltpu.VMEM((2, pairs, 2 * NF), F32),
+        in_specs=[VMEM] * (1 + 2 * n_chunks),
+        out_specs=VMEM,
+        compiler_params=params(4),
+        cost_estimate=cost(2 * 2 * pairs * stations * 2 * NF, 4 << 20),
+        name="first_pairs",
+    )(first_row, *in_vmem(*whites))
 
     lag_rows = NL // n_tm
-    result = pl.pallas_call(
-        functools.partial(late_kernel, groups, len(buffers), n_tm),
-        out_shape=[pltpu.VMEM((lag_rows, pairs), F32)] + [pltpu.VMEM((lag_rows, pairs), BF16)] * (n_tm - 1),
-        in_specs=[VMEM] * (5 + len(buffers)),
-        out_specs=[VMEM] * n_tm,
-        scratch_shapes=[
-            pltpu.VMEM((2, width, 2 * NF), BF16),
-            pltpu.VMEM((2, pairs, 2 * NF), F32),
-            pltpu.VMEM((pairs, NF), BF16),
-            pltpu.VMEM((pairs, NF), BF16),
-        ],
-        compiler_params=params(18),
-        cost_estimate=cost(2 * 2 * pairs * width * 2 * NF + 2 * NL * pairs * 2 * NF, 6 << 20),
-        name="late_pairs",
-    )(*in_vmem(early, first, hot, t_odd, t_even, *late_in))
-
-    total = result[0]
-    for d in range(1, n_tm):
-        route = [(i, (i + d) % n_tm) for i in range(n_tm)]
-        total = total + lax.ppermute(result[d], "tm", route).astype(F32)
-    return total
+    n_half = 2
+    half = pairs // n_half
+    steps = [1 << k for k in range(n_tm.bit_length() - 1)]
+    done = []
+    parts = []
+    for h in range(n_half):
+        parts.append(
+            pl.pallas_call(
+                functools.partial(late_kernel, groups, len(buffers), n_tm, h * half),
+                out_shape=[pltpu.VMEM((NL // 2, half), BF16), pltpu.VMEM((NL // 2, half), F32)],
+                in_specs=[VMEM] * (5 + len(buffers)),
+                out_specs=[VMEM] * 2,
+                scratch_shapes=[
+                    pltpu.VMEM((2, width, 2 * NF), BF16),
+                    pltpu.VMEM((2, half, 2 * NF), F32),
+                    pltpu.VMEM((half, NF), BF16),
+                    pltpu.VMEM((half, NF), BF16),
+                ],
+                compiler_params=params(10),
+                cost_estimate=cost(2 * 2 * half * width * 2 * NF + 2 * NL * half * 2 * NF, 3 << 20),
+                name="late_pairs_%d" % h,
+            )(*in_vmem(early, first, hot, t_odd, t_even, *late_in))
+        )
+    for step in steps:
+        route = [(i, i ^ step) for i in range(n_tm)]
+        received = [lax.ppermute(send, "tm", route) for send, _ in parts]
+        if step == steps[-1]:
+            done = [x for (_, keep), got in zip(parts, received) for x in (keep, got)]
+            break
+        merged = []
+        for h in range(n_half):
+            keep = parts[h][1]
+            rows = keep.shape[0] // 2
+            merged.append(
+                pl.pallas_call(
+                    functools.partial(merge_kernel, lag_rows),
+                    out_shape=[pltpu.VMEM((rows, half), BF16), pltpu.VMEM((rows, half), F32)],
+                    in_specs=[VMEM] * 2,
+                    out_specs=[VMEM] * 2,
+                    compiler_params=params(1),
+                    cost_estimate=cost(rows * half, 1 << 20),
+                    name="merge_%d_%d" % (step, h),
+                )(*in_vmem(keep, received[h]))
+            )
+        parts = merged
+    return pl.pallas_call(
+        finish_kernel,
+        out_shape=jax.ShapeDtypeStruct((lag_rows, pairs), F32),
+        in_specs=[VMEM] * len(done),
+        out_specs=VMEM,
+        compiler_params=params(2),
+        cost_estimate=cost(lag_rows * pairs, 1 << 20),
+        name="finish",
+    )(*in_vmem(*done))
 
 
 def solution(mesh):

time: 72 us -> 76.2 us (1.058)
  the two profiles are of different devices: /device:TPU:24 before, /device:TPU:0 now
where the time goes in v5:
time: 76.2 us; the launch traced here: 76.1 us
  Pallas kernels  31.3 us (41%)
  starting transfers between devices  24.2 us (32%)
  waiting for transfers between devices  20.4 us (27%)
    ppermute x4, waiting for transfers between devices, on_device(): received = [lax.ppermute(send, 'tm', route) for send, _ in parts]  15.7 us
    pallas_call x2, Pallas kernels, on_device(): pl.pallas_call(functools.partial(rim_kernel, groups, sum(sizes[:i]), i, l...  11 us
    pallas_call x1, Pallas kernels, on_device(): pl.pallas_call(functools.partial(local_kernel, groups), out_shape=[table]...  10.2 us
    ppermute x4, starting transfers between devices, on_device(): received = [lax.ppermute(send, 'tm', route) for send, _ in parts]  9.88 us
    ppermute x4, starting transfers between devices, on_device(): edges = [lax.ppermute(x, 'tm', routes[i % 2]) for i, x in enumerate(packed)]  8.52 us
    ppermute x6, starting transfers between devices, exchange(): got.append(lax.ppermute(piece, 'sta', route))  5.77 us
    ppermute x6, waiting for transfers between devices, exchange(): got.append(lax.ppermute(piece, 'sta', route))  4.65 us
    pallas_call x2, Pallas kernels, on_device(): pl.pallas_call(functools.partial(late_kernel, groups, len(buffers), n_tm,...  3.09 us
  transfers between devices with their start and end apart: 14, of which 5 were waited for; matrix products, arithmetic and copies ran while one was open for 0% of the time, Pallas kernels for 29%

profile of v5, /device:TPU:0, one launch (start us, length us, event | category | flops | bytes accessed | tf_op | source)
XLA Modules:
  0.0 76.1 jit_solution(17198423387293452494)
XLA Ops:
  0.0 1.8 %pack_edges.1 = (bf16[336,1024]{1,0:T(8,128)(2,1)S(1)}, bf16[336,1024]{1,0:T(8,128)(2,1)S(1)}, bf16[192,1024]{1,0:T(8,128)(2,1)S(1)}, bf16[192,1024]{1,0:T(8,128...) custom-call(s32[3]{0:T(128)} %offsets.1, ...), custom_call_target="tpu_custom_call" | custom-call | bytes 4194304 | tf_op jit(solution)/shard_map/pack_edges/pallas_call | solution.py:551
  1.8 3.1 %collective-permute-start.3 = (bf16[336,1024]{1,0:T(8,128)(2,1)S(1)}, bf16[336,1024]{1,0:T(8,128)(2,1)S(1)}, u32[]{:S(2)}, u32[]{:S(2)}) collective-permute-start(bf16[336,1024]{1,0:T(8,128)(2,1)S(1)} %get-tuple-element.52), channel_id=1, source_target_pairs={{0,4},{4,0},{8,12},{12,8},{1,5},{5,1},{9,13},{13,9},{2,6},{6,2},{1... | collective-permute-start | bytes 2064392 | tf_op jit(solution)/shard_map/ppermute | solution.py:569
  4.9 0.7 collective-permute-start.4
  5.7 0.0 copy-start.1
  5.7 0.0 copy-start.2
  5.7 10.2 %local_windows.1 = (bf16[1024,512]{1,0:T(8,128)(2,1)S(1)}, bf16[1024,512]{1,0:T(8,128)(2,1)S(1)}, bf16[512,1024]{1,0:T(8,128)(2,1)S(1)}, bf16[512,1024]{1,0:T(8,...) custom-call(s32[3]{0:T(128)S(4)} %get-tuple-element.40.offsets, ...), custom_call_target="tpu_custom_call" | custom-call | flops 2147483648 | bytes 8388608 | tf_op jit(solution)/shard_map/local_windows/pallas_call | solution.py:581
  15.9 0.1 collective-permute-start
  16.0 1.6 %collective-permute-start.2 = (bf16[16,1024]{1,0:T(8,128)(2,1)S(1)}, bf16[16,1024]{1,0:T(8,128)(2,1)S(1)}, u32[]{:S(2)}, u32[]{:S(2)}) collective-permute-start(bf16[16,1024]{1,0:T(8,128)(2,1)S(1)} %get-tuple-element.50), channel_id=1, source_target_pairs={{0,2},{1,3},{2,0},{3,1},{4,6},{5,7},{6,4},{7,5},{8,10},{9,11},{10,... | collective-permute-start | bytes 98312 | tf_op jit(solution)/shard_map/ppermute | solution.py:600
  17.5 4.0 %collective-permute-start.5 = (bf16[192,1024]{1,0:T(8,128)(2,1)S(1)}, bf16[192,1024]{1,0:T(8,128)(2,1)S(1)}, u32[]{:S(2)}, u32[]{:S(2)}) collective-permute-start(bf16[192,1024]{1,0:T(8,128)(2,1)S(1)} %get-tuple-element.58), channel_id=1, source_target_pairs={{0,4},{4,0},{8,12},{12,8},{1,5},{5,1},{9,13},{13,9},{2,6},{6,2},{1... | collective-permute-start | bytes 1179656 | tf_op jit(solution)/shard_map/ppermute | solution.py:569
  21.6 0.7 collective-permute-start.6
  22.3 0.0 collective-permute-done.rest_1_
  22.3 1.2 %collective-permute-start.1 = (bf16[64,1024]{1,0:T(8,128)(2,1)S(1)}, bf16[64,1024]{1,0:T(8,128)(2,1)S(1)}, u32[]{:S(2)}, u32[]{:S(2)}) collective-permute-start(bf16[64,1024]{1,0:T(8,128)(2,1)S(1)} %get-tuple-element.49), channel_id=1, source_target_pairs={{0,3},{1,0},{2,1},{3,2},{4,7},{5,4},{6,5},{7,6},{8,11},{9,8},{10,9... | collective-permute-start | bytes 393224 | tf_op jit(solution)/shard_map/ppermute | solution.py:600
  23.4 2.5 %collective-permute-done.1.rest_2_ = bf16[64,1024]{1,0:T(8,128)(2,1)S(1)} collective-permute-done((bf16[64,1024]{1,0:T(8,128)(2,1)S(1)}, bf16[64,1024]{1,0:T(8,128)(2,1)S(1)}, u32[]{:S(2)}, u32[]{:S(2)}) %collective-permute-start.1) | collective-permute-done | bytes 131104 | tf_op jit(solution)/shard_map/ppermute | solution.py:600
  25.9 2.5 %early_pairs.1 = (f32[512,1024]{1,0:T(8,128)S(1)}, bf16[512,128]{1,0:T(8,128)(2,1)S(1)}) custom-call(s32[1,512]{1,0:T(1,128)S(1)} %bitcast.2, s32[1,512]{1,0:T(1,128)S(1)} %bitcast.4, bf16[512,1024]{1,0:T(8,128)(2,1)S(1)} %get-tuple-element.45.white0, bf16[512,1024]{1,0:T(8,128)(2,1)S(1)} %get-tuple-element.46.white3, ...), custom_call_target="tpu_custom_call" | custom-call | flops 1342177280 | bytes 4194304 | tf_op jit(solution)/shard_map/early_pairs/pallas_call | solution.py:610
  28.4 0.0 collective-permute-done.3.rest_0_.rest_2_
  28.4 6.2 %rim_windows_0.1 = (bf16[320,1024]{1,0:T(8,128)(2,1)S(1)}, bf16[320,1024]{1,0:T(8,128)(2,1)S(1)}) custom-call(s32[3]{0:T(128)S(4)} %get-tuple-element.40.offsets, bf16[512,3072]{1,0:T(8,128)(2,1)S(1)} %copy-done, bf16[336,1024]{1,0:T(8,128)(2,1)S(1)} %collective-permute-done.3.rest_0_.rest_2_, bf16[336,1024]{1,0:T(8,128)(2,1)S(1)} %collective-permute-done.4.rest_1_.rest_3_, ...), custom_call_target="tpu_custom_call" | custom-call | flops 1342177280 | bytes 4194304 | tf_op jit(solution)/shard_map/rim_windows_0/pallas_call | solution.py:627
  34.7 4.7 %rim_windows_1.1 = (bf16[192,1024]{1,0:T(8,128)(2,1)S(1)}, bf16[192,1024]{1,0:T(8,128)(2,1)S(1)}, bf16[64,1024]{1,0:T(8,128)(2,1)S(1)}, bf16[64,1024]{1,0:T(8,12...) custom-call(s32[3]{0:T(128)S(4)} %get-tuple-element.40.offsets, bf16[512,3072]{1,0:T(8,128)(2,1)S(1)} %copy-done, ...), custom_call_target="tpu_custom_call" | custom-call | flops 805306368 | bytes 4194304 | tf_op jit(solution)/shard_map/rim_windows_1/pallas_call | solution.py:627
  39.4 1.1 %collective-permute-start.7 = (bf16[64,1024]{1,0:T(8,128)(2,1)S(1)}, bf16[64,1024]{1,0:T(8,128)(2,1)S(1)}, u32[]{:S(2)}, u32[]{:S(2)}) collective-permute-start(bf16[64,1024]{1,0:T(8,128)(2,1)S(1)} %get-tuple-element.64), channel_id=1, source_target_pairs={{0,1},{1,2},{2,3},{3,0},{4,5},{5,6},{6,7},{7,4},{8,9},{9,10},{10,1... | collective-permute-start | bytes 393224 | tf_op jit(solution)/shard_map/ppermute | solution.py:600
  40.6 1.3 %collective-permute-start.8 = (bf16[64,1024]{1,0:T(8,128)(2,1)S(1)}, bf16[64,1024]{1,0:T(8,128)(2,1)S(1)}, u32[]{:S(2)}, u32[]{:S(2)}) collective-permute-start(bf16[64,1024]{1,0:T(8,128)(2,1)S(1)} %get-tuple-element.65), channel_id=1, source_target_pairs={{0,3},{1,0},{2,1},{3,2},{4,7},{5,4},{6,5},{7,6},{8,11},{9,8},{10,9... | collective-permute-start | bytes 393224 | tf_op jit(solution)/shard_map/ppermute | solution.py:600
  41.9 0.5 collective-permute-start.9
  42.4 1.9 %first_pairs.1.first = f32[2,512,1024]{2,1,0:T(8,128)S(1)} custom-call(s32[1,512]{1,0:T(1,128)S(1)} %bitcast.3, bf16[320,1024]{1,0:T(8,128)(2,1)S(1)} %get-tuple-element.56.rest_8_.rest_0_, bf16[320,1024]{1,0:T(8,128)(2,1)S(1)} %get-tuple-element.57.rest_9_.rest_1_, bf16[192,1024]{1,0:T(8,128)(2,1)S(1)} %get-tuple-element.61.rest_2_, ...), custom_call_target="tpu_custom_call" | custom-call | flops 1073741824 | bytes 4194304 | tf_op jit(solution)/shard_map/first_pairs/pallas_call | solution.py:645
  44.3 2.1 %collective-permute-done.9.rest_3_ = bf16[16,1024]{1,0:T(8,128)(2,1)S(1)} collective-permute-done((bf16[16,1024]{1,0:T(8,128)(2,1)S(1)}, bf16[16,1024]{1,0:T(8,128)(2,1)S(1)}, u32[]{:S(2)}, u32[]{:S(2)}) %collective-permute-start.9) | collective-permute-done | bytes 32800 | tf_op jit(solution)/shard_map/ppermute | solution.py:600
  46.4 1.5 %late_pairs_1.1 = (bf16[512,256]{1,0:T(8,128)(2,1)S(1)}, f32[512,256]{1,0:T(8,128)S(1)}) custom-call(f32[512,1024]{1,0:T(8,128)S(1)} %get-tuple-element.51.early, f32[2,512,1024]{2,1,0:T(8,128)S(1)} %first_pairs.1.first, bf16[512,128]{1,0:T(8,128)(2,1)S(1)} %get-tuple-element.60.rest_10_.hot, bf16[1024,512]{1,0:T(8,128)(2,1)S(1)} %get-tuple-element.54.rest_3_.rest_5_.t_odd, ...), custom_call_target="tpu_custom_call" | custom-call | flops 671088640 | bytes 3145728 | tf_op jit(solution)/shard_map/late_pairs_1/pallas_call | solution.py:663
  48.0 4.9 %collective-permute-start.12 = (bf16[512,256]{1,0:T(8,128)(2,1)S(1)}, bf16[512,256]{1,0:T(8,128)(2,1)S(1)}, u32[]{:S(2)}, u32[]{:S(2)}) collective-permute-start(bf16[512,256]{1,0:T(8,128)(2,1)S(1)} %get-tuple-element.72), channel_id=1, source_target_pairs={{0,4},{4,0},{8,12},{12,8},{1,5},{5,1},{9,13},{13,9},{2,6},{6,2},{1... | collective-permute-start | bytes 786440 | tf_op jit(solution)/shard_map/ppermute | solution.py:681
  52.9 1.5 %late_pairs_0.1 = (bf16[512,256]{1,0:T(8,128)(2,1)S(1)}, f32[512,256]{1,0:T(8,128)S(1)}) custom-call(f32[512,1024]{1,0:T(8,128)S(1)} %get-tuple-element.51.early, f32[2,512,1024]{2,1,0:T(8,128)S(1)} %first_pairs.1.first, bf16[512,128]{1,0:T(8,128)(2,1)S(1)} %get-tuple-element.60.rest_10_.hot, bf16[1024,512]{1,0:T(8,128)(2,1)S(1)} %get-tuple-element.54.rest_3_.rest_5_.t_odd, ...), custom_call_target="tpu_custom_call" | custom-call | flops 671088640 | bytes 3145728 | tf_op jit(solution)/shard_map/late_pairs_0/pallas_call | solution.py:663
  54.5 0.1 collective-permute-start.10
  54.5 5.5 %collective-permute-done.12.received = bf16[512,256]{1,0:T(8,128)(2,1)S(1)} collective-permute-done((bf16[512,256]{1,0:T(8,128)(2,1)S(1)}, bf16[512,256]{1,0:T(8,128)(2,1)S(1)}, u32[]{:S(2)}, u32[]{:S(2)}) %collective-permute-start.12) | collective-permute-done | bytes 262176 | tf_op jit(solution)/shard_map/ppermute | solution.py:681
  60.1 3.2 %collective-permute-start.13 = (bf16[256,256]{1,0:T(8,128)(2,1)S(1)}, bf16[256,256]{1,0:T(8,128)(2,1)S(1)}, u32[]{:S(2)}, u32[]{:S(2)}) collective-permute-start(bf16[256,256]{1,0:T(8,128)(2,1)S(1)} %get-tuple-element.74), channel_id=1, source_target_pairs={{0,8},{4,12},{8,0},{12,4},{1,9},{5,13},{9,1},{13,5},{2,10},{6,14},... | collective-permute-start | bytes 393224 | tf_op jit(solution)/shard_map/ppermute | solution.py:681
  63.4 3.8 %collective-permute-done.10.received = bf16[512,256]{1,0:T(8,128)(2,1)S(1)} collective-permute-done((bf16[512,256]{1,0:T(8,128)(2,1)S(1)}, bf16[512,256]{1,0:T(8,128)(2,1)S(1)}, u32[]{:S(2)}, u32[]{:S(2)}) %collective-permute-start.10) | collective-permute-done | bytes 262176 | tf_op jit(solution)/shard_map/ppermute | solution.py:681
  67.3 1.6 %collective-permute-start.11 = (bf16[256,256]{1,0:T(8,128)(2,1)S(1)}, bf16[256,256]{1,0:T(8,128)(2,1)S(1)}, u32[]{:S(2)}, u32[]{:S(2)}) collective-permute-start(bf16[256,256]{1,0:T(8,128)(2,1)S(1)} %get-tuple-element.70), channel_id=1, source_target_pairs={{0,8},{4,12},{8,0},{12,4},{1,9},{5,13},{9,1},{13,5},{2,10},{6,14},... | collective-permute-start | bytes 393224 | tf_op jit(solution)/shard_map/ppermute | solution.py:681
  68.9 6.3 %collective-permute-done.11.refs_1_ = bf16[256,256]{1,0:T(8,128)(2,1)S(1)} collective-permute-done((bf16[256,256]{1,0:T(8,128)(2,1)S(1)}, bf16[256,256]{1,0:T(8,128)(2,1)S(1)}, u32[]{:S(2)}, u32[]{:S(2)}) %collective-permute-start.11) | collective-permute-done | bytes 131104 | tf_op jit(solution)/shard_map/ppermute | solution.py:681
  75.2 0.8 %finish.1 = f32[256,512]{1,0:T(8,128)} custom-call(f32[256,256]{1,0:T(8,128)S(1)} %get-tuple-element.69.refs_0_, bf16[256,256]{1,0:T(8,128)(2,1)S(1)} %collective-permute-done.11.refs_1_, f32[256,256]{1,0:T(8,128)S(1)} %get-tuple-element.73.refs_2_, bf16[256,256]{1,0:T(8,128)(2,1)S(1)} %collective-permute-done.13.refs_3_), custom_call_target="tpu_custom_call" | custom-call | flops 131072 | bytes 1048576 | tf_op jit(solution)/shard_map/finish/pallas_call | solution.py:701
  (13 shorter events, 0.1 us)
Async XLA Ops:
  0.0 5.6 %copy-start = (bf16[512,3072]{1,0:T(8,128)(2,1)S(1)}, bf16[512,3072]{1,0:T(8,128)(2,1)}, u32[]{:S(2)}) copy-start(bf16[512,3072]{1,0:T(8,128)(2,1)} %main.7) | copy-start | bytes 9437188
  1.8 26.6 %collective-permute-start.3 = (bf16[336,1024]{1,0:T(8,128)(2,1)S(1)}, bf16[336,1024]{1,0:T(8,128)(2,1)S(1)}, u32[]{:S(2)}, u32[]{:S(2)}) collective-permute-start(bf16[336,1024]{1,0:T(8,128)(2,1)S(1)} %get-tuple-element.52), channel_id=1, source_target_pairs={{0,4},{4,0},{8,12},{12,8},{1,5},{5,1},{9,13},{13,9},{2,6},{6,2},{1... | collective-permute-start | bytes 2064392 | tf_op jit(solution)/shard_map/ppermute | solution.py:569
  4.9 23.5 %collective-permute-start.4 = (bf16[336,1024]{1,0:T(8,128)(2,1)S(1)}, bf16[336,1024]{1,0:T(8,128)(2,1)S(1)}, u32[]{:S(2)}, u32[]{:S(2)}) collective-permute-start(bf16[336,1024]{1,0:T(8,128)(2,1)S(1)} %get-tuple-element.53), channel_id=1, source_target_pairs={{0,0},{4,8},{8,4},{12,12},{1,1},{5,9},{9,5},{13,13},{2,2},{6,10},{... | collective-permute-start | bytes 2064392 | tf_op jit(solution)/shard_map/ppermute | solution.py:569
  5.7 20.3 %copy-start.1 = (s32[512]{0:T(512)S(1)}, s32[512]{0:T(512)}, u32[]{:S(2)}) copy-start(s32[512]{0:T(512)} %param.10) | copy-start | bytes 6148
  5.7 20.3 %copy-start.2 = (s32[512]{0:T(512)S(1)}, s32[512]{0:T(512)}, u32[]{:S(2)}) copy-start(s32[512]{0:T(512)} %param.11) | copy-start | bytes 6148
  15.9 6.3 %collective-permute-start = (bf16[64,1024]{1,0:T(8,128)(2,1)S(1)}, bf16[64,1024]{1,0:T(8,128)(2,1)S(1)}, u32[]{:S(2)}, u32[]{:S(2)}) collective-permute-start(bf16[64,1024]{1,0:T(8,128)(2,1)S(1)} %get-tuple-element.48), channel_id=1, source_target_pairs={{0,1},{1,2},{2,3},{3,0},{4,5},{5,6},{6,7},{7,4},{8,9},{9,10},{10,1... | collective-permute-start | bytes 393224 | tf_op jit(solution)/shard_map/ppermute | solution.py:600
  16.0 5.6 %collective-permute-start.2 = (bf16[16,1024]{1,0:T(8,128)(2,1)S(1)}, bf16[16,1024]{1,0:T(8,128)(2,1)S(1)}, u32[]{:S(2)}, u32[]{:S(2)}) collective-permute-start(bf16[16,1024]{1,0:T(8,128)(2,1)S(1)} %get-tuple-element.50), channel_id=1, source_target_pairs={{0,2},{1,3},{2,0},{3,1},{4,6},{5,7},{6,4},{7,5},{8,10},{9,11},{10,... | collective-permute-start | bytes 98312 | tf_op jit(solution)/shard_map/ppermute | solution.py:600
  17.5 17.1 %collective-permute-start.5 = (bf16[192,1024]{1,0:T(8,128)(2,1)S(1)}, bf16[192,1024]{1,0:T(8,128)(2,1)S(1)}, u32[]{:S(2)}, u32[]{:S(2)}) collective-permute-start(bf16[192,1024]{1,0:T(8,128)(2,1)S(1)} %get-tuple-element.58), channel_id=1, source_target_pairs={{0,4},{4,0},{8,12},{12,8},{1,5},{5,1},{9,13},{13,9},{2,6},{6,2},{1... | collective-permute-start | bytes 1179656 | tf_op jit(solution)/shard_map/ppermute | solution.py:569
  21.6 13.1 %collective-permute-start.6 = (bf16[192,1024]{1,0:T(8,128)(2,1)S(1)}, bf16[192,1024]{1,0:T(8,128)(2,1)S(1)}, u32[]{:S(2)}, u32[]{:S(2)}) collective-permute-start(bf16[192,1024]{1,0:T(8,128)(2,1)S(1)} %get-tuple-element.59), channel_id=1, source_target_pairs={{0,0},{4,8},{8,4},{12,12},{1,1},{5,9},{9,5},{13,13},{2,2},{6,10},{... | collective-permute-start | bytes 1179656 | tf_op jit(solution)/shard_map/ppermute | solution.py:569
  22.3 3.7 %collective-permute-start.1 = (bf16[64,1024]{1,0:T(8,128)(2,1)S(1)}, bf16[64,1024]{1,0:T(8,128)(2,1)S(1)}, u32[]{:S(2)}, u32[]{:S(2)}) collective-permute-start(bf16[64,1024]{1,0:T(8,128)(2,1)S(1)} %get-tuple-element.49), channel_id=1, source_target_pairs={{0,3},{1,0},{2,1},{3,2},{4,7},{5,4},{6,5},{7,6},{8,11},{9,8},{10,9... | collective-permute-start | bytes 393224 | tf_op jit(solution)/shard_map/ppermute | solution.py:600
  39.4 7.0 %collective-permute-start.7 = (bf16[64,1024]{1,0:T(8,128)(2,1)S(1)}, bf16[64,1024]{1,0:T(8,128)(2,1)S(1)}, u32[]{:S(2)}, u32[]{:S(2)}) collective-permute-start(bf16[64,1024]{1,0:T(8,128)(2,1)S(1)} %get-tuple-element.64), channel_id=1, source_target_pairs={{0,1},{1,2},{2,3},{3,0},{4,5},{5,6},{6,7},{7,4},{8,9},{9,10},{10,1... | collective-permute-start | bytes 393224 | tf_op jit(solution)/shard_map/ppermute | solution.py:600
  40.6 5.9 %collective-permute-start.8 = (bf16[64,1024]{1,0:T(8,128)(2,1)S(1)}, bf16[64,1024]{1,0:T(8,128)(2,1)S(1)}, u32[]{:S(2)}, u32[]{:S(2)}) collective-permute-start(bf16[64,1024]{1,0:T(8,128)(2,1)S(1)} %get-tuple-element.65), channel_id=1, source_target_pairs={{0,3},{1,0},{2,1},{3,2},{4,7},{5,4},{6,5},{7,6},{8,11},{9,8},{10,9... | collective-permute-start | bytes 393224 | tf_op jit(solution)/shard_map/ppermute | solution.py:600
  41.9 4.5 %collective-permute-start.9 = (bf16[16,1024]{1,0:T(8,128)(2,1)S(1)}, bf16[16,1024]{1,0:T(8,128)(2,1)S(1)}, u32[]{:S(2)}, u32[]{:S(2)}) collective-permute-start(bf16[16,1024]{1,0:T(8,128)(2,1)S(1)} %get-tuple-element.66), channel_id=1, source_target_pairs={{0,2},{1,3},{2,0},{3,1},{4,6},{5,7},{6,4},{7,5},{8,10},{9,11},{10,... | collective-permute-start | bytes 98312 | tf_op jit(solution)/shard_map/ppermute | solution.py:600
  48.0 12.1 %collective-permute-start.12 = (bf16[512,256]{1,0:T(8,128)(2,1)S(1)}, bf16[512,256]{1,0:T(8,128)(2,1)S(1)}, u32[]{:S(2)}, u32[]{:S(2)}) collective-permute-start(bf16[512,256]{1,0:T(8,128)(2,1)S(1)} %get-tuple-element.72), channel_id=1, source_target_pairs={{0,4},{4,0},{8,12},{12,8},{1,5},{5,1},{9,13},{13,9},{2,6},{6,2},{1... | collective-permute-start | bytes 786440 | tf_op jit(solution)/shard_map/ppermute | solution.py:681
  54.5 12.7 %collective-permute-start.10 = (bf16[512,256]{1,0:T(8,128)(2,1)S(1)}, bf16[512,256]{1,0:T(8,128)(2,1)S(1)}, u32[]{:S(2)}, u32[]{:S(2)}) collective-permute-start(bf16[512,256]{1,0:T(8,128)(2,1)S(1)} %get-tuple-element.68), channel_id=1, source_target_pairs={{0,4},{4,0},{8,12},{12,8},{1,5},{5,1},{9,13},{13,9},{2,6},{6,2},{1... | collective-permute-start | bytes 786440 | tf_op jit(solution)/shard_map/ppermute | solution.py:681
  60.1 8.8 %collective-permute-start.13 = (bf16[256,256]{1,0:T(8,128)(2,1)S(1)}, bf16[256,256]{1,0:T(8,128)(2,1)S(1)}, u32[]{:S(2)}, u32[]{:S(2)}) collective-permute-start(bf16[256,256]{1,0:T(8,128)(2,1)S(1)} %get-tuple-element.74), channel_id=1, source_target_pairs={{0,8},{4,12},{8,0},{12,4},{1,9},{5,13},{9,1},{13,5},{2,10},{6,14},... | collective-permute-start | bytes 393224 | tf_op jit(solution)/shard_map/ppermute | solution.py:681
  67.3 8.0 %collective-permute-start.11 = (bf16[256,256]{1,0:T(8,128)(2,1)S(1)}, bf16[256,256]{1,0:T(8,128)(2,1)S(1)}, u32[]{:S(2)}, u32[]{:S(2)}) collective-permute-start(bf16[256,256]{1,0:T(8,128)(2,1)S(1)} %get-tuple-element.70), channel_id=1, source_target_pairs={{0,8},{4,12},{8,0},{12,4},{1,9},{5,13},{9,1},{13,5},{2,10},{6,14},... | collective-permute-start | bytes 393224 | tf_op jit(solution)/shard_map/ppermute | solution.py:681

commit v6 on v5

--- a/solution.py
+++ b/solution.py
@@ -338,7 +338,6 @@
     taper, t_odd, t_even, send_rows = rest[:4]
     rest = rest[4:]
     older = rest[: 2 * earlier]
-    rest = rest[1:] if last else rest
     whites = rest[2 * earlier : 2 * earlier + 2]
     scratch = rest[-7:]
     sends = rest[2 * earlier + 2 : -7] + (scratch[6],)
@@ -434,12 +433,15 @@
     return one, two
 
 
-def early_kernel(groups, n_pieces, scale, pair_first, pair_slot, white0, white3, *rest):
+def early_kernel(groups, n_pieces, n_white, scale, pair_first, pair_slot, white0, white3, *rest):
+    whites = rest[: 2 * n_white]
+    rest = rest[2 * n_white :]
     pieces = rest[:n_pieces]
-    cross, hot = rest[n_pieces : n_pieces + 2]
-    incoming, first, second = rest[n_pieces + 2 :]
+    cross, later, hot = rest[n_pieces : n_pieces + 3]
+    incoming, first, second = rest[n_pieces + 3 :]
     pairs = pair_first.shape[1]
-    hots = station_tables(column(pair_first[...]), (white0,))
+    col = column(pair_first[...])
+    hots = station_tables(col, (white0,))
     first_rows(hots, (white0,), scale, first.at[0])
     first_rows(hots, (white3,), scale, first.at[1])
     hot[...] = slot_table(groups, pair_slot, hot.shape[1])
@@ -454,14 +456,9 @@
         return carry
 
     loop(pairs, 2, group)
-
-
-def first_kernel(scale, n_white, pair_first, *rest):
-    whites = rest[: 2 * n_white]
-    out = rest[2 * n_white]
-    hots = station_tables(column(pair_first[...]), whites[0::2])
-    first_rows(hots, whites[0::2], scale, out.at[0])
-    first_rows(hots, whites[1::2], scale, out.at[1])
+    hots = station_tables(col, whites[0::2])
+    first_rows(hots, whites[0::2], scale, later.at[0])
+    first_rows(hots, whites[1::2], scale, later.at[1])
 
 
 def late_kernel(groups, n_pieces, n_dest, first_pair, early, first, hot, t_odd, t_even, *rest):
@@ -543,7 +540,7 @@
     pairs = pair_first.shape[0]
     cap = send_rows.shape[1] // n_sta
 
-    sizes = (stations * 5 // 8, stations * 3 // 8)
+    sizes = (stations // 2, stations // 2)
     n_chunks = len(sizes)
     main, = in_vmem(traces)
     routes = swap_routes(n_tm)
@@ -607,17 +604,6 @@
         pltpu.VMEM((2, pairs, 2 * NF), F32),
         pltpu.VMEM((2, pairs, 2 * NF), F32),
     ]
-    early, hot = pl.pallas_call(
-        functools.partial(early_kernel, groups, len(buffers), scale),
-        out_shape=[pltpu.VMEM((pairs, 2 * NF), F32), pltpu.VMEM((pairs, width), BF16)],
-        in_specs=[VMEM] * (4 + len(buffers)),
-        out_specs=[VMEM] * 2,
-        scratch_shapes=pair_scratch,
-        compiler_params=params(16),
-        cost_estimate=cost(2 * 2 * pairs * (stations + width) * 2 * NF, 4 << 20),
-        name="early_pairs",
-    )(first_row, slot_row, *in_vmem(white0, white3, *early_in))
-
     whites = []
     late_out = None
     for i in range(n_chunks):
@@ -627,7 +613,7 @@
         result = pl.pallas_call(
             functools.partial(rim_kernel, groups, sum(sizes[:i]), i, last),
             out_shape=[chunk] * 2 + (buffers if last else []),
-            in_specs=[SMEM] + [VMEM] * (7 + 4 * i + (1 if last else 0)),
+            in_specs=[SMEM] + [VMEM] * (7 + 4 * i),
             out_specs=[VMEM] * (2 + (len(buffers) if last else 0)),
             scratch_shapes=scratches(n_sta, cap, 2 * rows),
             compiler_params=params(22),
@@ -637,20 +623,24 @@
             *in_smem(starts),
             *in_vmem(main, *edges[2 * i : 2 * i + 2], *(edges[:2] * i)),
             *in_vmem(taper, t_odd, t_even, send_rows, *whites),
-            *in_vmem(*([hot] if last else [])),
         )
         whites = whites + list(result[:2])
         late_out = result[2:]
     late_in = exchange(late_out)
-    first = pl.pallas_call(
-        functools.partial(first_kernel, scale, n_chunks),
-        out_shape=pltpu.VMEM((2, pairs, 2 * NF), F32),
-        in_specs=[VMEM] * (1 + 2 * n_chunks),
-        out_specs=VMEM,
-        compiler_params=params(4),
-        cost_estimate=cost(2 * 2 * pairs * stations * 2 * NF, 4 << 20),
-        name="first_pairs",
-    )(first_row, *in_vmem(*whites))
+    early, first, hot = pl.pallas_call(
+        functools.partial(early_kernel, groups, len(buffers), n_chunks, scale),
+        out_shape=[
+            pltpu.VMEM((pairs, 2 * NF), F32),
+            pltpu.VMEM((2, pairs, 2 * NF), F32),
+            pltpu.VMEM((pairs, width), BF16),
+        ],
+        in_specs=[VMEM] * (4 + 2 * n_chunks + len(buffers)),
+        out_specs=[VMEM] * 3,
+        scratch_shapes=pair_scratch,
+        compiler_params=params(16),
+        cost_estimate=cost(2 * 2 * pairs * (2 * stations + width) * 2 * NF, 4 << 20),
+        name="early_pairs",
+    )(first_row, slot_row, *in_vmem(white0, white3, *whites, *early_in))
 
     lag_rows = NL // n_tm
     n_half = 2

time: 76.2 us -> 72.1 us (0.946)
  waiting for transfers between devices: 20.4 us -> 17.5 us
  Pallas kernels: 31.3 us -> 30.3 us
    ppermute x6, waiting for transfers between devices: 4.65 us -> 0.02 us  [exchange(): got.append(lax.ppermute(piece, 'sta', route))]
    ppermute x4, waiting for transfers between devices: 15.7 us -> 17.5 us  [on_device(): received = [lax.ppermute(send, 'tm', route) for send, _ in parts]]
    ppermute x4, starting transfers between devices: 9.88 us -> 8.79 us  [on_device(): received = [lax.ppermute(send, 'tm', route) for send, _ in parts]]
    ppermute x6, starting transfers between devices: 5.77 us -> 6.6 us  [exchange(): got.append(lax.ppermute(piece, 'sta', route))]
    pallas_call x2 -> x1, Pallas kernels: 4.33 us -> 3.77 us  [on_device(): pl.pallas_call(functools.partial(early_kernel, groups, len(buffers), n_ch...]
  transfers between devices with their start and end apart: 14 -> 14, of which waited for: 5 -> 3; matrix products, arithmetic and copies ran while one was open for 0% -> 0% of each run, Pallas kernels for 29% -> 36%
where the time goes in v6:
time: 72.1 us; the launch traced here: 71.9 us
  Pallas kernels  30.3 us (42%)
  starting transfers between devices  24 us (33%)
  waiting for transfers between devices  17.5 us (24%)
    ppermute x4, waiting for transfers between devices, on_device(): received = [lax.ppermute(send, 'tm', route) for send, _ in parts]  17.5 us
    pallas_call x2, Pallas kernels, on_device(): pl.pallas_call(functools.partial(rim_kernel, groups, sum(sizes[:i]), i, l...  10.4 us
    pallas_call x1, Pallas kernels, on_device(): pl.pallas_call(functools.partial(local_kernel, groups), out_shape=[table]...  10.2 us
    ppermute x4, starting transfers between devices, on_device(): received = [lax.ppermute(send, 'tm', route) for send, _ in parts]  8.79 us
    ppermute x4, starting transfers between devices, on_device(): edges = [lax.ppermute(x, 'tm', routes[i % 2]) for i, x in enumerate(packed)]  8.6 us
    ppermute x6, starting transfers between devices, exchange(): got.append(lax.ppermute(piece, 'sta', route))  6.6 us
    pallas_call x1, Pallas kernels, on_device(): pl.pallas_call(functools.partial(early_kernel, groups, len(buffers), n_ch...  3.77 us
    pallas_call x2, Pallas kernels, on_device(): pl.pallas_call(functools.partial(late_kernel, groups, len(buffers), n_tm,...  3.13 us
  transfers between devices with their start and end apart: 14, of which 3 were waited for; matrix products, arithmetic and copies ran while one was open for 0% of the time, Pallas kernels for 36%

profile of v6, /device:TPU:0, one launch (start us, length us, event | category | flops | bytes accessed | tf_op | source)
XLA Modules:
  0.0 71.9 jit_solution(15388117602164035059)
XLA Ops:
  0.0 1.8 %pack_edges.1 = (bf16[272,1024]{1,0:T(8,128)(2,1)S(1)}, bf16[272,1024]{1,0:T(8,128)(2,1)S(1)}, bf16[256,1024]{1,0:T(8,128)(2,1)S(1)}, bf16[256,1024]{1,0:T(8,128...) custom-call(s32[3]{0:T(128)} %offsets.1, ...), custom_call_target="tpu_custom_call" | custom-call | bytes 4194304 | tf_op jit(solution)/shard_map/pack_edges/pallas_call | solution.py:548
  1.8 3.1 %collective-permute-start = (bf16[272,1024]{1,0:T(8,128)(2,1)S(1)}, bf16[272,1024]{1,0:T(8,128)(2,1)S(1)}, u32[]{:S(2)}, u32[]{:S(2)}) collective-permute-start(bf16[272,1024]{1,0:T(8,128)(2,1)S(1)} %get-tuple-element.48), channel_id=1, source_target_pairs={{0,4},{4,0},{8,12},{12,8},{1,5},{5,1},{9,13},{13,9},{2,6},{6,2},{1... | collective-permute-start | bytes 1671176 | tf_op jit(solution)/shard_map/ppermute | solution.py:566
  4.9 0.7 collective-permute-start.1
  5.6 4.1 %collective-permute-start.2 = (bf16[256,1024]{1,0:T(8,128)(2,1)S(1)}, bf16[256,1024]{1,0:T(8,128)(2,1)S(1)}, u32[]{:S(2)}, u32[]{:S(2)}) collective-permute-start(bf16[256,1024]{1,0:T(8,128)(2,1)S(1)} %get-tuple-element.54), channel_id=1, source_target_pairs={{0,4},{4,0},{8,12},{12,8},{1,5},{5,1},{9,13},{13,9},{2,6},{6,2},{1... | collective-permute-start | bytes 1572872 | tf_op jit(solution)/shard_map/ppermute | solution.py:566
  9.8 0.7 collective-permute-start.3
  10.5 10.2 %local_windows.1 = (bf16[1024,512]{1,0:T(8,128)(2,1)S(1)}, bf16[1024,512]{1,0:T(8,128)(2,1)S(1)}, bf16[512,1024]{1,0:T(8,128)(2,1)S(1)}, bf16[512,1024]{1,0:T(8,...) custom-call(s32[3]{0:T(128)S(4)} %get-tuple-element.41.offsets, ...), custom_call_target="tpu_custom_call" | custom-call | flops 2147483648 | bytes 8388608 | tf_op jit(solution)/shard_map/local_windows/pallas_call | solution.py:578
  20.7 1.6 %collective-permute-start.6 = (bf16[16,1024]{1,0:T(8,128)(2,1)S(1)}, bf16[16,1024]{1,0:T(8,128)(2,1)S(1)}, u32[]{:S(2)}, u32[]{:S(2)}) collective-permute-start(bf16[16,1024]{1,0:T(8,128)(2,1)S(1)} %get-tuple-element.61), channel_id=1, source_target_pairs={{0,2},{1,3},{2,0},{3,1},{4,6},{5,7},{6,4},{7,5},{8,10},{9,11},{10,... | collective-permute-start | bytes 98312 | tf_op jit(solution)/shard_map/ppermute | solution.py:597
  22.2 0.0 collective-permute-done.rest_0_.rest_2_
  22.2 0.0 collective-permute-start.4
  22.2 0.0 collective-permute-done.1.rest_1_.rest_3_
  22.2 1.7 %collective-permute-start.5 = (bf16[64,1024]{1,0:T(8,128)(2,1)S(1)}, bf16[64,1024]{1,0:T(8,128)(2,1)S(1)}, u32[]{:S(2)}, u32[]{:S(2)}) collective-permute-start(bf16[64,1024]{1,0:T(8,128)(2,1)S(1)} %get-tuple-element.60), channel_id=1, source_target_pairs={{0,3},{1,0},{2,1},{3,2},{4,7},{5,4},{6,5},{7,6},{8,11},{9,8},{10,9... | collective-permute-start | bytes 393224 | tf_op jit(solution)/shard_map/ppermute | solution.py:597
  24.0 5.0 %rim_windows_0.1 = (bf16[256,1024]{1,0:T(8,128)(2,1)S(1)}, bf16[256,1024]{1,0:T(8,128)(2,1)S(1)}) custom-call(s32[3]{0:T(128)S(4)} %get-tuple-element.41.offsets, bf16[512,3072]{1,0:T(8,128)(2,1)S(1)} %copy-done, bf16[272,1024]{1,0:T(8,128)(2,1)S(1)} %collective-permute-done.rest_0_.rest_2_, bf16[272,1024]{1,0:T(8,128)(2,1)S(1)} %collective-permute-done.1.rest_1_.rest_3_, ...), custom_call_target="tpu_custom_call" | custom-call | flops 1073741824 | bytes 4194304 | tf_op jit(solution)/shard_map/rim_windows_0/pallas_call | solution.py:613
  28.9 0.0 collective-permute-done.3.rest_1_
  29.0 0.0 copy-start.1
  29.0 0.0 copy-start.2
  29.0 5.5 %rim_windows_1.1 = (bf16[256,1024]{1,0:T(8,128)(2,1)S(1)}, bf16[256,1024]{1,0:T(8,128)(2,1)S(1)}, bf16[64,1024]{1,0:T(8,128)(2,1)S(1)}, bf16[64,1024]{1,0:T(8,12...) custom-call(s32[3]{0:T(128)S(4)} %get-tuple-element.41.offsets, bf16[512,3072]{1,0:T(8,128)(2,1)S(1)} %copy-done, ...), custom_call_target="tpu_custom_call" | custom-call | flops 1073741824 | bytes 4194304 | tf_op jit(solution)/shard_map/rim_windows_1/pallas_call | solution.py:613
  34.4 1.6 %collective-permute-start.9 = (bf16[16,1024]{1,0:T(8,128)(2,1)S(1)}, bf16[16,1024]{1,0:T(8,128)(2,1)S(1)}, u32[]{:S(2)}, u32[]{:S(2)}) collective-permute-start(bf16[16,1024]{1,0:T(8,128)(2,1)S(1)} %get-tuple-element.68), channel_id=1, source_target_pairs={{0,2},{1,3},{2,0},{3,1},{4,6},{5,7},{6,4},{7,5},{8,10},{9,11},{10,... | collective-permute-start | bytes 98312 | tf_op jit(solution)/shard_map/ppermute | solution.py:597
  36.0 0.0 collective-permute-done.6.rest_7_
  36.0 1.7 %collective-permute-start.8 = (bf16[64,1024]{1,0:T(8,128)(2,1)S(1)}, bf16[64,1024]{1,0:T(8,128)(2,1)S(1)}, u32[]{:S(2)}, u32[]{:S(2)}) collective-permute-start(bf16[64,1024]{1,0:T(8,128)(2,1)S(1)} %get-tuple-element.67), channel_id=1, source_target_pairs={{0,3},{1,0},{2,1},{3,2},{4,7},{5,4},{6,5},{7,6},{8,11},{9,8},{10,9... | collective-permute-start | bytes 393224 | tf_op jit(solution)/shard_map/ppermute | solution.py:597
  37.8 0.0 collective-permute-done.4.rest_5_
  37.8 0.0 collective-permute-done.5.rest_6_
  37.8 3.8 %early_pairs.1 = (f32[512,1024]{1,0:T(8,128)S(1)}, f32[2,512,1024]{2,1,0:T(8,128)S(1)}, bf16[512,128]{1,0:T(8,128)(2,1)S(1)}) custom-call(s32[1,512]{1,0:T(1,128)S(1)} %bitcast.2, s32[1,512]{1,0:T(1,128)S(1)} %bitcast.3, bf16[512,1024]{1,0:T(8,128)(2,1)S(1)} %get-tuple-element.46.white0, bf16[512,1024]{1,0:T(8,128)(2,1)S(1)} %get-tuple-element.47.white3, ...), custom_call_target="tpu_custom_call" | custom-call | flops 2415919104 | bytes 4194304 | tf_op jit(solution)/shard_map/early_pairs/pallas_call | solution.py:630
  41.6 1.6 %late_pairs_1.1 = (bf16[512,256]{1,0:T(8,128)(2,1)S(1)}, f32[512,256]{1,0:T(8,128)S(1)}) custom-call(f32[512,1024]{1,0:T(8,128)S(1)} %get-tuple-element.62.early, f32[2,512,1024]{2,1,0:T(8,128)S(1)} %get-tuple-element.63.first, bf16[512,128]{1,0:T(8,128)(2,1)S(1)} %get-tuple-element.64.hot, bf16[1024,512]{1,0:T(8,128)(2,1)S(1)} %get-tuple-element.50.rest_3_.rest_5_.t_odd, ...), custom_call_target="tpu_custom_call" | custom-call | flops 671088640 | bytes 3145728 | tf_op jit(solution)/shard_map/late_pairs_1/pallas_call | solution.py:653
  43.2 4.3 %collective-permute-start.12 = (bf16[512,256]{1,0:T(8,128)(2,1)S(1)}, bf16[512,256]{1,0:T(8,128)(2,1)S(1)}, u32[]{:S(2)}, u32[]{:S(2)}) collective-permute-start(bf16[512,256]{1,0:T(8,128)(2,1)S(1)} %get-tuple-element.74), channel_id=1, source_target_pairs={{0,4},{4,0},{8,12},{12,8},{1,5},{5,1},{9,13},{13,9},{2,6},{6,2},{1... | collective-permute-start | bytes 786440 | tf_op jit(solution)/shard_map/ppermute | solution.py:671
  47.5 1.6 %late_pairs_0.1 = (bf16[512,256]{1,0:T(8,128)(2,1)S(1)}, f32[512,256]{1,0:T(8,128)S(1)}) custom-call(f32[512,1024]{1,0:T(8,128)S(1)} %get-tuple-element.62.early, f32[2,512,1024]{2,1,0:T(8,128)S(1)} %get-tuple-element.63.first, bf16[512,128]{1,0:T(8,128)(2,1)S(1)} %get-tuple-element.64.hot, bf16[1024,512]{1,0:T(8,128)(2,1)S(1)} %get-tuple-element.50.rest_3_.rest_5_.t_odd, ...), custom_call_target="tpu_custom_call" | custom-call | flops 671088640 | bytes 3145728 | tf_op jit(solution)/shard_map/late_pairs_0/pallas_call | solution.py:653
  49.1 0.1 collective-permute-start.10
  49.2 5.5 %collective-permute-done.12.received = bf16[512,256]{1,0:T(8,128)(2,1)S(1)} collective-permute-done((bf16[512,256]{1,0:T(8,128)(2,1)S(1)}, bf16[512,256]{1,0:T(8,128)(2,1)S(1)}, u32[]{:S(2)}, u32[]{:S(2)}) %collective-permute-start.12) | collective-permute-done | bytes 262176 | tf_op jit(solution)/shard_map/ppermute | solution.py:671
  54.7 3.3 %collective-permute-start.13 = (bf16[256,256]{1,0:T(8,128)(2,1)S(1)}, bf16[256,256]{1,0:T(8,128)(2,1)S(1)}, u32[]{:S(2)}, u32[]{:S(2)}) collective-permute-start(bf16[256,256]{1,0:T(8,128)(2,1)S(1)} %get-tuple-element.76), channel_id=1, source_target_pairs={{0,8},{4,12},{8,0},{12,4},{1,9},{5,13},{9,1},{13,5},{2,10},{6,14},... | collective-permute-start | bytes 393224 | tf_op jit(solution)/shard_map/ppermute | solution.py:671
  58.0 4.5 %collective-permute-done.10.received = bf16[512,256]{1,0:T(8,128)(2,1)S(1)} collective-permute-done((bf16[512,256]{1,0:T(8,128)(2,1)S(1)}, bf16[512,256]{1,0:T(8,128)(2,1)S(1)}, u32[]{:S(2)}, u32[]{:S(2)}) %collective-permute-start.10) | collective-permute-done | bytes 262176 | tf_op jit(solution)/shard_map/ppermute | solution.py:671
  62.5 1.1 %collective-permute-start.11 = (bf16[256,256]{1,0:T(8,128)(2,1)S(1)}, bf16[256,256]{1,0:T(8,128)(2,1)S(1)}, u32[]{:S(2)}, u32[]{:S(2)}) collective-permute-start(bf16[256,256]{1,0:T(8,128)(2,1)S(1)} %get-tuple-element.72), channel_id=1, source_target_pairs={{0,8},{4,12},{8,0},{12,4},{1,9},{5,13},{9,1},{13,5},{2,10},{6,14},... | collective-permute-start | bytes 393224 | tf_op jit(solution)/shard_map/ppermute | solution.py:671
  63.6 7.5 %collective-permute-done.11.refs_1_ = bf16[256,256]{1,0:T(8,128)(2,1)S(1)} collective-permute-done((bf16[256,256]{1,0:T(8,128)(2,1)S(1)}, bf16[256,256]{1,0:T(8,128)(2,1)S(1)}, u32[]{:S(2)}, u32[]{:S(2)}) %collective-permute-start.11) | collective-permute-done | bytes 131104 | tf_op jit(solution)/shard_map/ppermute | solution.py:671
  71.1 0.8 %finish.1 = f32[256,512]{1,0:T(8,128)} custom-call(f32[256,256]{1,0:T(8,128)S(1)} %get-tuple-element.71.refs_0_, bf16[256,256]{1,0:T(8,128)(2,1)S(1)} %collective-permute-done.11.refs_1_, f32[256,256]{1,0:T(8,128)S(1)} %get-tuple-element.75.refs_2_, bf16[256,256]{1,0:T(8,128)(2,1)S(1)} %collective-permute-done.13.refs_3_), custom_call_target="tpu_custom_call" | custom-call | flops 131072 | bytes 1048576 | tf_op jit(solution)/shard_map/finish/pallas_call | solution.py:691
  (12 shorter events, 0.1 us)
Async XLA Ops:
  0.0 10.4 %copy-start = (bf16[512,3072]{1,0:T(8,128)(2,1)S(1)}, bf16[512,3072]{1,0:T(8,128)(2,1)}, u32[]{:S(2)}) copy-start(bf16[512,3072]{1,0:T(8,128)(2,1)} %main.7) | copy-start | bytes 9437188
  1.8 20.4 %collective-permute-start = (bf16[272,1024]{1,0:T(8,128)(2,1)S(1)}, bf16[272,1024]{1,0:T(8,128)(2,1)S(1)}, u32[]{:S(2)}, u32[]{:S(2)}) collective-permute-start(bf16[272,1024]{1,0:T(8,128)(2,1)S(1)} %get-tuple-element.48), channel_id=1, source_target_pairs={{0,4},{4,0},{8,12},{12,8},{1,5},{5,1},{9,13},{13,9},{2,6},{6,2},{1... | collective-permute-start | bytes 1671176 | tf_op jit(solution)/shard_map/ppermute | solution.py:566
  4.9 17.3 %collective-permute-start.1 = (bf16[272,1024]{1,0:T(8,128)(2,1)S(1)}, bf16[272,1024]{1,0:T(8,128)(2,1)S(1)}, u32[]{:S(2)}, u32[]{:S(2)}) collective-permute-start(bf16[272,1024]{1,0:T(8,128)(2,1)S(1)} %get-tuple-element.49), channel_id=1, source_target_pairs={{0,0},{4,8},{8,4},{12,12},{1,1},{5,9},{9,5},{13,13},{2,2},{6,10},{... | collective-permute-start | bytes 1671176 | tf_op jit(solution)/shard_map/ppermute | solution.py:566
  5.6 23.3 %collective-permute-start.2 = (bf16[256,1024]{1,0:T(8,128)(2,1)S(1)}, bf16[256,1024]{1,0:T(8,128)(2,1)S(1)}, u32[]{:S(2)}, u32[]{:S(2)}) collective-permute-start(bf16[256,1024]{1,0:T(8,128)(2,1)S(1)} %get-tuple-element.54), channel_id=1, source_target_pairs={{0,4},{4,0},{8,12},{12,8},{1,5},{5,1},{9,13},{13,9},{2,6},{6,2},{1... | collective-permute-start | bytes 1572872 | tf_op jit(solution)/shard_map/ppermute | solution.py:566
  9.8 19.2 %collective-permute-start.3 = (bf16[256,1024]{1,0:T(8,128)(2,1)S(1)}, bf16[256,1024]{1,0:T(8,128)(2,1)S(1)}, u32[]{:S(2)}, u32[]{:S(2)}) collective-permute-start(bf16[256,1024]{1,0:T(8,128)(2,1)S(1)} %get-tuple-element.55), channel_id=1, source_target_pairs={{0,0},{4,8},{8,4},{12,12},{1,1},{5,9},{9,5},{13,13},{2,2},{6,10},{... | collective-permute-start | bytes 1572872 | tf_op jit(solution)/shard_map/ppermute | solution.py:566
  20.7 15.4 %collective-permute-start.6 = (bf16[16,1024]{1,0:T(8,128)(2,1)S(1)}, bf16[16,1024]{1,0:T(8,128)(2,1)S(1)}, u32[]{:S(2)}, u32[]{:S(2)}) collective-permute-start(bf16[16,1024]{1,0:T(8,128)(2,1)S(1)} %get-tuple-element.61), channel_id=1, source_target_pairs={{0,2},{1,3},{2,0},{3,1},{4,6},{5,7},{6,4},{7,5},{8,10},{9,11},{10,... | collective-permute-start | bytes 98312 | tf_op jit(solution)/shard_map/ppermute | solution.py:597
  22.2 15.5 %collective-permute-start.4 = (bf16[64,1024]{1,0:T(8,128)(2,1)S(1)}, bf16[64,1024]{1,0:T(8,128)(2,1)S(1)}, u32[]{:S(2)}, u32[]{:S(2)}) collective-permute-start(bf16[64,1024]{1,0:T(8,128)(2,1)S(1)} %get-tuple-element.59), channel_id=1, source_target_pairs={{0,1},{1,2},{2,3},{3,0},{4,5},{5,6},{6,7},{7,4},{8,9},{9,10},{10,1... | collective-permute-start | bytes 393224 | tf_op jit(solution)/shard_map/ppermute | solution.py:597
  22.2 15.5 %collective-permute-start.5 = (bf16[64,1024]{1,0:T(8,128)(2,1)S(1)}, bf16[64,1024]{1,0:T(8,128)(2,1)S(1)}, u32[]{:S(2)}, u32[]{:S(2)}) collective-permute-start(bf16[64,1024]{1,0:T(8,128)(2,1)S(1)} %get-tuple-element.60), channel_id=1, source_target_pairs={{0,3},{1,0},{2,1},{3,2},{4,7},{5,4},{6,5},{7,6},{8,11},{9,8},{10,9... | collective-permute-start | bytes 393224 | tf_op jit(solution)/shard_map/ppermute | solution.py:597
  29.0 8.8 %copy-start.1 = (s32[512]{0:T(512)S(1)}, s32[512]{0:T(512)}, u32[]{:S(2)}) copy-start(s32[512]{0:T(512)} %param.10) | copy-start | bytes 6148
  29.0 8.8 %copy-start.2 = (s32[512]{0:T(512)S(1)}, s32[512]{0:T(512)}, u32[]{:S(2)}) copy-start(s32[512]{0:T(512)} %param.11) | copy-start | bytes 6148
  34.4 7.1 %collective-permute-start.9 = (bf16[16,1024]{1,0:T(8,128)(2,1)S(1)}, bf16[16,1024]{1,0:T(8,128)(2,1)S(1)}, u32[]{:S(2)}, u32[]{:S(2)}) collective-permute-start(bf16[16,1024]{1,0:T(8,128)(2,1)S(1)} %get-tuple-element.68), channel_id=1, source_target_pairs={{0,2},{1,3},{2,0},{3,1},{4,6},{5,7},{6,4},{7,5},{8,10},{9,11},{10,... | collective-permute-start | bytes 98312 | tf_op jit(solution)/shard_map/ppermute | solution.py:597
  36.0 5.6 %collective-permute-start.7 = (bf16[64,1024]{1,0:T(8,128)(2,1)S(1)}, bf16[64,1024]{1,0:T(8,128)(2,1)S(1)}, u32[]{:S(2)}, u32[]{:S(2)}) collective-permute-start(bf16[64,1024]{1,0:T(8,128)(2,1)S(1)} %get-tuple-element.66), channel_id=1, source_target_pairs={{0,1},{1,2},{2,3},{3,0},{4,5},{5,6},{6,7},{7,4},{8,9},{9,10},{10,1... | collective-permute-start | bytes 393224 | tf_op jit(solution)/shard_map/ppermute | solution.py:597
  36.0 5.6 %collective-permute-start.8 = (bf16[64,1024]{1,0:T(8,128)(2,1)S(1)}, bf16[64,1024]{1,0:T(8,128)(2,1)S(1)}, u32[]{:S(2)}, u32[]{:S(2)}) collective-permute-start(bf16[64,1024]{1,0:T(8,128)(2,1)S(1)} %get-tuple-element.67), channel_id=1, source_target_pairs={{0,3},{1,0},{2,1},{3,2},{4,7},{5,4},{6,5},{7,6},{8,11},{9,8},{10,9... | collective-permute-start | bytes 393224 | tf_op jit(solution)/shard_map/ppermute | solution.py:597
  43.2 11.5 %collective-permute-start.12 = (bf16[512,256]{1,0:T(8,128)(2,1)S(1)}, bf16[512,256]{1,0:T(8,128)(2,1)S(1)}, u32[]{:S(2)}, u32[]{:S(2)}) collective-permute-start(bf16[512,256]{1,0:T(8,128)(2,1)S(1)} %get-tuple-element.74), channel_id=1, source_target_pairs={{0,4},{4,0},{8,12},{12,8},{1,5},{5,1},{9,13},{13,9},{2,6},{6,2},{1... | collective-permute-start | bytes 786440 | tf_op jit(solution)/shard_map/ppermute | solution.py:671
  49.1 13.4 %collective-permute-start.10 = (bf16[512,256]{1,0:T(8,128)(2,1)S(1)}, bf16[512,256]{1,0:T(8,128)(2,1)S(1)}, u32[]{:S(2)}, u32[]{:S(2)}) collective-permute-start(bf16[512,256]{1,0:T(8,128)(2,1)S(1)} %get-tuple-element.70), channel_id=1, source_target_pairs={{0,4},{4,0},{8,12},{12,8},{1,5},{5,1},{9,13},{13,9},{2,6},{6,2},{1... | collective-permute-start | bytes 786440 | tf_op jit(solution)/shard_map/ppermute | solution.py:671
  54.7 8.9 %collective-permute-start.13 = (bf16[256,256]{1,0:T(8,128)(2,1)S(1)}, bf16[256,256]{1,0:T(8,128)(2,1)S(1)}, u32[]{:S(2)}, u32[]{:S(2)}) collective-permute-start(bf16[256,256]{1,0:T(8,128)(2,1)S(1)} %get-tuple-element.76), channel_id=1, source_target_pairs={{0,8},{4,12},{8,0},{12,4},{1,9},{5,13},{9,1},{13,5},{2,10},{6,14},... | collective-permute-start | bytes 393224 | tf_op jit(solution)/shard_map/ppermute | solution.py:671
  62.5 8.6 %collective-permute-start.11 = (bf16[256,256]{1,0:T(8,128)(2,1)S(1)}, bf16[256,256]{1,0:T(8,128)(2,1)S(1)}, u32[]{:S(2)}, u32[]{:S(2)}) collective-permute-start(bf16[256,256]{1,0:T(8,128)(2,1)S(1)} %get-tuple-element.72), channel_id=1, source_target_pairs={{0,8},{4,12},{8,0},{12,4},{1,9},{5,13},{9,1},{13,5},{2,10},{6,14},... | collective-permute-start | bytes 393224 | tf_op jit(solution)/shard_map/ppermute | solution.py:671

commit v7 on v6

--- a/solution.py
+++ b/solution.py
@@ -8,6 +8,7 @@
 from jax.experimental import pallas as pl
 from jax.experimental.pallas import tpu as pltpu
 from jax.sharding import PartitionSpec as P
+
 
 WIN = 2048
 NF = 512
@@ -24,7 +25,6 @@
 F32 = jnp.float32
 BF16 = jnp.bfloat16
 ROWS = 16
-N_SMALL = 4
 UNIT = 512
 VMEM = pl.BlockSpec(memory_space=pltpu.VMEM)
 SMEM = pl.BlockSpec(memory_space=pltpu.SMEM)
@@ -198,28 +198,22 @@
     return hot[:, :width]
 
 
-def write_rows(send_rows, spectra, near, far, n_sta, cap, refs):
+def outgoing(send_rows, first, spectra, before, out):
+    col = column(send_rows[...])
+    hot = one_hot(col, spectra[0].shape[0], first)
+    for w in range(2):
+        value = jnp.dot(hot, spectra[w][...], preferred_element_type=F32)
+        out[w] = value if before is None else before[w] + value
+
+
+def write_rows(groups, rows, refs):
+    near, far, n_sta, cap = groups
     g = lax.axis_index("sta")
-    lane = lax.broadcasted_iota(jnp.int32, (1, n_sta * cap), 1)
-    col = column(send_rows[...])
-    hots = one_hot(col, sum(p.shape[0] for p in spectra[0]))
-    for w in range(2):
-        result = None
-        at = 0
-        for piece in spectra[w]:
-            n = piece.shape[0]
-            term = jnp.dot(hots[:, at : at + n], piece[...], preferred_element_type=F32)
-            result = term if result is None else result + term
-            at += n
-        refs[-1][w] = result.astype(BF16)
-    rows = refs[-1]
     for ref, d in zip(refs, near + far):
-        first = pl.multiple_of(lax.rem(g + d, n_sta) * cap, cap)
+        first = pl.multiple_of(peer(d, g, n_sta) * cap, cap)
+        n = CAP_FAR if d in far else cap
         for w in range(2):
-            if d in far:
-                ref[w * CAP_FAR : (w + 1) * CAP_FAR, :] = rows[w, pl.ds(first, CAP_FAR), :]
-            else:
-                ref[w * cap : (w + 1) * cap, :] = rows[w, pl.ds(first, cap), :]
+            ref[w * n : (w + 1) * n, :] = rows[w, pl.ds(first, n), :].astype(BF16)
 
 
 def scratches(n_sta, cap, rows):
@@ -230,14 +224,14 @@
         pltpu.VMEM((HC, rows, LANES), BF16),
         pltpu.VMEM((HC, rows, LANES), BF16),
         pltpu.VMEM((rows, 2 * NF), F32),
-        pltpu.VMEM((2, n_sta * cap, 2 * NF), BF16),
+        pltpu.VMEM((2, n_sta * cap, 2 * NF), F32),
     ]
 
 
 def local_kernel(groups, offsets, main, cos_t, sin_t, taper, send_rows, *rest):
     t_odd, t_even, white0, white3 = rest[:4]
     scratch = rest[-7:]
-    sends = rest[4:-7] + (scratch[6],)
+    sends = rest[4:-7]
     fill_tables(cos_t, sin_t, t_odd, t_even)
     start0 = offsets[0]
     start3 = offsets[2] - 2 * STEP
@@ -261,7 +255,18 @@
             prepare(pick, start, count, 0, taper, scratch)
             transform(count, t_odd, t_even, scratch)
             whiten_rows(0, count, live, white.at[first : first + count], scratch)
-    write_rows(send_rows, ((white0,), (white3,)), *groups, sends)
+    outgoing(send_rows, 0, (white0, white3), None, scratch[6])
+    write_rows(groups, scratch[6], sends)
+
+
+def peer(d, g, n):
+    if d == "own":
+        return g
+    if d == "even":
+        return g + 1 - 2 * (g % 2)
+    if d == "odd":
+        return (g - 1 + 2 * (g % 2) + n) % n
+    return (g + d) % n
 
 
 def swap_routes(n):
@@ -274,54 +279,53 @@
     return routes
 
 
-def pack_kernel(sizes, offsets, main, *rest):
-    n_out = 2 * len(sizes)
-    small = rest[:N_SMALL]
-    outs = rest[N_SMALL : N_SMALL + n_out]
-    offsets_out = rest[N_SMALL + n_out]
-    small_out = rest[N_SMALL + n_out + 1 : -1]
+def pack_kernel(first, count, n_small, head, offsets, main, *rest):
+    small = rest[:n_small]
+    outs = rest[n_small : n_small + 2]
+    small_out = rest[n_small + 2 : 2 * n_small + 2]
+    offsets_out = rest[2 * n_small + 2]
     sems = rest[-1]
     t = lax.axis_index("tm")
     n = lax.axis_size("tm")
 
-    def edge(i):
-        chunk, swap = i // 2, i % 2
+    def edge(swap):
         at = jnp.where(t % 2 == swap, 2 * HALF, 0)
         lanes = pl.ds(pl.multiple_of(at, LANES), HALF)
-        source = main.at[pl.ds(sum(sizes[:chunk]), sizes[chunk]), lanes]
-        return pltpu.make_async_copy(source, outs[i].at[pl.ds(0, sizes[chunk])], sems.at[i])
-
-    first = pltpu.make_async_copy(offsets, offsets_out, sems.at[n_out])
-    first.start()
+        source = main.at[pl.ds(first, count), lanes]
+        return pltpu.make_async_copy(source, outs[swap].at[pl.ds(0, count)], sems.at[swap])
+
     copies = []
-    for i in range(n_out):
-        if n % 2 == i % 2:
-            copies.append(edge(i))
+    for swap in range(2):
+        if n % 2 == swap:
+            copies.append(edge(swap))
             copies[-1].start()
         else:
             @pl.when(t == n - 1)
             def _():
-                outs[i][0 : sizes[i // 2], :] = jnp.zeros((sizes[i // 2], HALF), BF16)
+                outs[swap][0:count, :] = jnp.zeros((count, HALF), BF16)
 
             @pl.when(t < n - 1)
             def _():
-                edge(i).start()
-    for k in range(N_SMALL):
-        copies.append(pltpu.make_async_copy(small[k], small_out[k], sems.at[n_out + 1 + k]))
+                edge(swap).start()
+    for k in range(n_small):
+        copies.append(pltpu.make_async_copy(small[k], small_out[k], sems.at[3 + k]))
         copies[-1].start()
-    first.wait()
-    start = offsets_out[2] - 2 * STEP
-    high, low = start // 8, start % 8
-    lane = lax.broadcasted_iota(jnp.int32, (ROWS, HALF), 1)
-    for i in range(2):
-        outs[i][sizes[0] :, :] = jnp.where(lane < NF, high, low).astype(F32).astype(BF16)
+    if head:
+        numbers = pltpu.make_async_copy(offsets, offsets_out, sems.at[2])
+        numbers.start()
+        numbers.wait()
+        start = offsets_out[2] - 2 * STEP
+        high, low = start // 8, start % 8
+        lane = lax.broadcasted_iota(jnp.int32, (ROWS, HALF), 1)
+        for out in outs:
+            out[count:, :] = jnp.where(lane < NF, high, low).astype(F32).astype(BF16)
     for copy in copies:
         copy.wait()
-    for i in range(n_out):
-        if n % 2 != i % 2:
+    for swap in range(2):
+        if n % 2 != swap:
             @pl.when(t < n - 1)
             def _():
-                edge(i).wait()
+                edge(swap).wait()
 
 
 def sent_start(ref):
@@ -334,13 +338,14 @@
 def rim_kernel(groups, first, earlier, last, offsets, main, *rest):
     recv = rest[:2]
     heads = rest[2:4] if earlier else recv
-    rest = rest[2 + 2 * earlier :]
+    rest = rest[4 if earlier else 2 :]
     taper, t_odd, t_even, send_rows = rest[:4]
     rest = rest[4:]
-    older = rest[: 2 * earlier]
-    whites = rest[2 * earlier : 2 * earlier + 2]
+    before = rest[0] if earlier else None
+    rest = rest[1:] if earlier else rest
+    whites = rest[:2]
     scratch = rest[-7:]
-    sends = rest[2 * earlier + 2 : -7] + (scratch[6],)
+    sends = rest[2:-7]
     count = whites[0].shape[0]
     t = lax.axis_index("tm")
     lane = lax.broadcasted_iota(jnp.int32, (ROWS, LANES), 1)
@@ -365,24 +370,27 @@
     whiten_rows(0, count, 1.0, whites[0], scratch)
     whiten_rows(count, count, live, whites[1], scratch)
     if last:
-        write_rows(send_rows, (older[0::2] + whites[:1], older[1::2] + whites[1:]), *groups, sends)
+        outgoing(send_rows, first, whites, before, scratch[6])
+        write_rows(groups, scratch[6], sends)
+    else:
+        outgoing(send_rows, first, whites, before, sends[0])
 
 
 def slot_table(groups, pair_slot, width):
     near, far, n_sta, cap = groups
     g = lax.axis_index("sta")
     slot = pair_slot[...]
-    distance = (g - slot // cap + n_sta) % n_sta
     place = jnp.zeros_like(slot)
     at = 0
     for d in near + far:
-        place = jnp.where(distance == d, at + slot % cap, place)
+        source = (g - d + n_sta) % n_sta if d in far else peer(d, g, n_sta)
+        place = jnp.where(slot // cap == source, at + slot % cap, place)
         at += CAP_FAR if d in far else cap
     return one_hot(column(place), width)
 
 
 def second_rows(groups, pieces, hot, first_pair, incoming, out):
-    near, far, n_sta, cap = groups
+    near, far, _, cap = groups
     width = incoming.shape[1]
     for w in range(2):
         at = 0
@@ -533,40 +541,44 @@
 
 
 def on_device(traces, offsets, pair_first, pair_slot, send_rows):
-    stations, block_len = traces.shape
+    stations, _ = traces.shape
     n_tm = lax.axis_size("tm")
     n_sta = lax.axis_size("sta")
     windows = offsets.shape[0]
     pairs = pair_first.shape[0]
     cap = send_rows.shape[1] // n_sta
 
-    sizes = (stations // 2, stations // 2)
+    sizes = (stations * 5 // 8, stations * 3 // 8)
     n_chunks = len(sizes)
     main, = in_vmem(traces)
     routes = swap_routes(n_tm)
     small = [jnp.asarray(x) for x in small_tables()] + [jnp.asarray(taper_row()), send_rows]
-    packed = pl.pallas_call(
-        functools.partial(pack_kernel, sizes),
-        out_shape=[
-            pltpu.VMEM((sizes[i // 2] + (ROWS if i < 2 else 0), HALF), BF16)
-            for i in range(2 * n_chunks)
-        ]
-        + [pltpu.SMEM(offsets.shape, jnp.int32)]
-        + [pltpu.VMEM(x.shape, x.dtype) for x in small],
-        in_specs=[ANY] * (2 + N_SMALL),
-        out_specs=[VMEM] * (2 * n_chunks) + [SMEM] + [VMEM] * N_SMALL,
-        scratch_shapes=[pltpu.SemaphoreType.DMA((2 * n_chunks + 1 + N_SMALL,))],
-        compiler_params=params(1),
-        cost_estimate=cost(0, 4 << 20),
-        name="pack_edges",
-    )(*in_hbm(offsets, traces, *small))
-    starts = packed[2 * n_chunks]
-    cos_t, sin_t, taper, send_rows = packed[2 * n_chunks + 1 :]
-    packed = packed[: 2 * n_chunks]
-    edges = [lax.ppermute(x, "tm", routes[i % 2]) for i, x in enumerate(packed)]
-
-    near = [0, 1, n_sta - 1] if n_sta > 2 else list(range(n_sta))
-    far = [d for d in range(n_sta) if d not in near]
+    edges = []
+    for i, rows in enumerate(sizes):
+        head = i == 0
+        extra = [] if head else small
+        packed = pl.pallas_call(
+            functools.partial(pack_kernel, sum(sizes[:i]), rows, len(extra), head),
+            out_shape=[pltpu.VMEM((rows + (ROWS if head else 0), HALF), BF16)] * 2
+            + [pltpu.VMEM(x.shape, x.dtype) for x in extra]
+            + [pltpu.SMEM(offsets.shape, jnp.int32)],
+            in_specs=[ANY] * (2 + len(extra)),
+            out_specs=[VMEM] * (2 + len(extra)) + [SMEM],
+            scratch_shapes=[pltpu.SemaphoreType.DMA((3 + len(extra),))],
+            compiler_params=params(1),
+            cost_estimate=cost(0, 2 << 20),
+        )(*in_hbm(offsets, traces, *extra))
+        if head:
+            starts = packed[-1]
+        else:
+            cos_t, sin_t, taper, send_rows = packed[2:-1]
+        got = [None, None]
+        for swap in (1, 0):
+            got[swap] = lax.ppermute(packed[swap], "tm", routes[swap])
+        edges += got
+
+    near = ["own", "even", "odd"]
+    far = list(range(2, n_sta - 1))
     groups = (near, far, n_sta, cap)
     width = -(-(len(near) * cap + len(far) * CAP_FAR) // LANES) * LANES
     first_row, slot_row = pair_first[None, :], pair_slot[None, :]
@@ -588,13 +600,11 @@
     t_odd, t_even, white0, white3 = local[:4]
 
     def exchange(pieces):
-        got = []
-        for d, piece in zip(near + far, pieces):
-            if d == 0:
-                got.append(piece)
-            else:
-                route = [(i, (i + d) % n_sta) for i in range(n_sta)]
-                got.append(lax.ppermute(piece, "sta", route))
+        got = list(pieces)
+        for i, d in sorted(enumerate(near + far), key=lambda x: (2, 1, 0)[near.index(x[1])] if x[1] in near else 3):
+            if d != "own":
+                route = [(k, peer(d, k, n_sta)) for k in range(n_sta)]
+                got[i] = lax.ppermute(pieces[i], "sta", route)
         return got
 
     early_in = exchange(local[4:])
@@ -605,24 +615,24 @@
         pltpu.VMEM((2, pairs, 2 * NF), F32),
     ]
     whites = []
-    late_out = None
+    late_out = []
+    outgoing_rows = pltpu.VMEM((2, n_sta * cap, 2 * NF), F32)
     for i in range(n_chunks):
         last = i == n_chunks - 1
         rows = sizes[i]
         chunk = pltpu.VMEM((rows, 2 * NF), BF16)
         result = pl.pallas_call(
             functools.partial(rim_kernel, groups, sum(sizes[:i]), i, last),
-            out_shape=[chunk] * 2 + (buffers if last else []),
-            in_specs=[SMEM] + [VMEM] * (7 + 4 * i),
-            out_specs=[VMEM] * (2 + (len(buffers) if last else 0)),
+            out_shape=[chunk] * 2 + (buffers if last else [outgoing_rows]),
+            in_specs=[SMEM] + [VMEM] * (7 + 3 * min(i, 1)),
+            out_specs=[VMEM] * (2 + (len(buffers) if last else 1)),
             scratch_shapes=scratches(n_sta, cap, 2 * rows),
             compiler_params=params(22),
             cost_estimate=cost(dft_flops * rows, 4 << 20),
-            name="rim_windows_%d" % i,
         )(
             *in_smem(starts),
-            *in_vmem(main, *edges[2 * i : 2 * i + 2], *(edges[:2] * i)),
-            *in_vmem(taper, t_odd, t_even, send_rows, *whites),
+            *in_vmem(main, *edges[2 * i : 2 * i + 2], *(edges[:2] if i else [])),
+            *in_vmem(taper, t_odd, t_even, send_rows, *late_out),
         )
         whites = whites + list(result[:2])
         late_out = result[2:]
@@ -663,7 +673,6 @@
                 ],
                 compiler_params=params(10),
                 cost_estimate=cost(2 * 2 * half * width * 2 * NF + 2 * NL * half * 2 * NF, 3 << 20),
-                name="late_pairs_%d" % h,
             )(*in_vmem(early, first, hot, t_odd, t_even, *late_in))
         )
     for step in steps:
@@ -684,7 +693,6 @@
                     out_specs=[VMEM] * 2,
                     compiler_params=params(1),
                     cost_estimate=cost(rows * half, 1 << 20),
-                    name="merge_%d_%d" % (step, h),
                 )(*in_vmem(keep, received[h]))
             )
         parts = merged

time: 72.1 us -> 71.5 us (level)
  starting transfers between devices: 24 us -> 20.4 us
  Pallas kernels: 30.3 us -> 32.4 us
  waiting for transfers between devices: 17.5 us -> 18.4 us
    ppermute x10, starting transfers between devices: 15.2 us -> 13.1 us  [the longest x4 8.71 us: on_device(): got[swap] = lax.ppermute(packed[swap], 'tm', routes[swap])]
    ppermute x4, starting transfers between devices: 8.79 us -> 7.24 us  [on_device(): received = [lax.ppermute(send, 'tm', route) for send, _ in parts]]
    pallas_call x1 -> x2, Pallas kernels: 1.82 us -> 2.73 us  [on_device(): pl.pallas_call(functools.partial(pack_kernel, sum(sizes[:i]), rows, len(e...]
    ppermute x4, waiting for transfers between devices: 17.5 us -> 18.3 us  [on_device(): received = [lax.ppermute(send, 'tm', route) for send, _ in parts]]
  transfers between devices with their start and end apart: 14 -> 14, of which waited for: 3 -> 4; matrix products, arithmetic and copies ran while one was open for 0% -> 0% of each run, Pallas kernels for 36% -> 40%
where the time goes in v7:
time: 71.5 us; the launch traced here: 71.3 us
  Pallas kernels  32.4 us (45%)
  starting transfers between devices  20.4 us (29%)
  waiting for transfers between devices  18.4 us (26%)
    ppermute x4, waiting for transfers between devices, on_device(): received = [lax.ppermute(send, 'tm', route) for send, _ in parts]  18.3 us
    pallas_call x2, Pallas kernels, on_device(): pl.pallas_call(functools.partial(rim_kernel, groups, sum(sizes[:i]), i, l...  11.1 us
    pallas_call x1, Pallas kernels, on_device(): pl.pallas_call(functools.partial(local_kernel, groups), out_shape=[table]...  10.2 us
    ppermute x4, starting transfers between devices, on_device(): got[swap] = lax.ppermute(packed[swap], 'tm', routes[swap])  8.71 us
    ppermute x4, starting transfers between devices, on_device(): received = [lax.ppermute(send, 'tm', route) for send, _ in parts]  7.24 us
    ppermute x6, starting transfers between devices, exchange(): got[i] = lax.ppermute(pieces[i], 'sta', route)  4.41 us
    pallas_call x1, Pallas kernels, on_device(): pl.pallas_call(functools.partial(early_kernel, groups, len(buffers), n_ch...  4.33 us
    pallas_call x2, Pallas kernels, on_device(): pl.pallas_call(functools.partial(late_kernel, groups, len(buffers), n_tm,...  3.12 us
  transfers between devices with their start and end apart: 14, of which 4 were waited for; matrix products, arithmetic and copies ran while one was open for 0% of the time, Pallas kernels for 40%

profile of v7, /device:TPU:0, one launch (start us, length us, event | category | flops | bytes accessed | tf_op | source)
XLA Modules:
  0.0 71.3 jit_solution(3864315191407499606)
XLA Ops:
  0.0 1.5 %shard_map.82 = (bf16[336,1024]{1,0:T(8,128)(2,1)S(1)}, bf16[336,1024]{1,0:T(8,128)(2,1)S(1)}, s32[3]{0:T(128)S(4)}) custom-call(s32[3]{0:T(128)} %offsets.3, bf16[512,3072]{1,0:T(8,128)(2,1)} %main.9), custom_call_target="tpu_custom_call" | custom-call | bytes 2097152 | tf_op jit(solution)/shard_map/pallas_call | solution.py:560
  1.5 3.1 %collective-permute-start = (bf16[336,1024]{1,0:T(8,128)(2,1)S(1)}, bf16[336,1024]{1,0:T(8,128)(2,1)S(1)}, u32[]{:S(2)}, u32[]{:S(2)}) collective-permute-start(bf16[336,1024]{1,0:T(8,128)(2,1)S(1)} %get-tuple-element.49), channel_id=1, source_target_pairs={{0,4},{4,0},{8,12},{12,8},{1,5},{5,1},{9,13},{13,9},{2,6},{6,2},{1... | collective-permute-start | bytes 2064392 | tf_op jit(solution)/shard_map/ppermute | solution.py:577
  4.6 0.7 collective-permute-start.1
  5.3 1.3 %shard_map.83 = (bf16[192,1024]{1,0:T(8,128)(2,1)S(1)}, bf16[192,1024]{1,0:T(8,128)(2,1)S(1)}, f32[64,512]{1,0:T(8,128)S(1)}, f32[64,512]{1,0:T(8,128)S(1)}, f32...) custom-call(s32[3]{0:T(128)} %offsets.3, bf16[512,3072]{1,0:T(8,128)(2,1)} %main.9, ...), custom_call_target="tpu_custom_call" | custom-call | bytes 2097152 | tf_op jit(solution)/shard_map/pallas_call | solution.py:560
  6.6 4.2 %collective-permute-start.2 = (bf16[192,1024]{1,0:T(8,128)(2,1)S(1)}, bf16[192,1024]{1,0:T(8,128)(2,1)S(1)}, u32[]{:S(2)}, u32[]{:S(2)}) collective-permute-start(bf16[192,1024]{1,0:T(8,128)(2,1)S(1)} %get-tuple-element.55), channel_id=1, source_target_pairs={{0,4},{4,0},{8,12},{12,8},{1,5},{5,1},{9,13},{13,9},{2,6},{6,2},{1... | collective-permute-start | bytes 1179656 | tf_op jit(solution)/shard_map/ppermute | solution.py:577
  10.8 0.7 collective-permute-start.3
  11.5 10.2 %local_windows.1 = (bf16[1024,512]{1,0:T(8,128)(2,1)S(1)}, bf16[1024,512]{1,0:T(8,128)(2,1)S(1)}, bf16[512,1024]{1,0:T(8,128)(2,1)S(1)}, bf16[512,1024]{1,0:T(8,...) custom-call(s32[3]{0:T(128)S(4)} %get-tuple-element.42.offsets, ...), custom_call_target="tpu_custom_call" | custom-call | flops 2147483648 | bytes 8388608 | tf_op jit(solution)/shard_map/local_windows/pallas_call | solution.py:590
  21.7 1.6 %collective-permute-start.6 = (bf16[16,1024]{1,0:T(8,128)(2,1)S(1)}, bf16[16,1024]{1,0:T(8,128)(2,1)S(1)}, u32[]{:S(2)}, u32[]{:S(2)}) collective-permute-start(bf16[16,1024]{1,0:T(8,128)(2,1)S(1)} %get-tuple-element.63), channel_id=1, source_target_pairs={{0,2},{1,3},{2,0},{3,1},{4,6},{5,7},{6,4},{7,5},{8,10},{9,11},{10,... | collective-permute-start | bytes 98312 | tf_op jit(solution)/shard_map/ppermute | solution.py:607
  23.3 0.0 collective-permute-start.4
  23.3 0.0 collective-permute-done.1.rest_1_.rest_3_
  23.3 0.6 collective-permute-start.5
  23.9 6.7 %shard_map.84 = (bf16[320,1024]{1,0:T(8,128)(2,1)S(1)}, bf16[320,1024]{1,0:T(8,128)(2,1)S(1)}, f32[2,128,1024]{2,1,0:T(8,128)S(1)}) custom-call(s32[3]{0:T(128)S(4)} %get-tuple-element.42.offsets, bf16[512,3072]{1,0:T(8,128)(2,1)S(1)} %copy-done, bf16[336,1024]{1,0:T(8,128)(2,1)S(1)} %collective-permute-done.rest_0_.rest_2_, ...), custom_call_target="tpu_custom_call" | custom-call | flops 1342177280 | bytes 4194304 | tf_op jit(solution)/shard_map/pallas_call | solution.py:624
  30.6 0.0 collective-permute-done.2.rest_0_
  30.6 0.0 collective-permute-done.3.rest_1_
  30.6 0.0 copy-start.1
  30.7 0.0 copy-start.2
  30.7 4.4 %shard_map.85 = (bf16[192,1024]{1,0:T(8,128)(2,1)S(1)}, bf16[192,1024]{1,0:T(8,128)(2,1)S(1)}, bf16[64,1024]{1,0:T(8,128)(2,1)S(1)}, bf16[64,1024]{1,0:T(8,128)(...) custom-call(s32[3]{0:T(128)S(4)} %get-tuple-element.42.offsets, bf16[512,3072]{1,0:T(8,128)(2,1)S(1)} %copy-done, ...), custom_call_target="tpu_custom_call" | custom-call | flops 805306368 | bytes 4194304 | tf_op jit(solution)/shard_map/pallas_call | solution.py:624
  35.1 1.6 %collective-permute-start.9 = (bf16[16,1024]{1,0:T(8,128)(2,1)S(1)}, bf16[16,1024]{1,0:T(8,128)(2,1)S(1)}, u32[]{:S(2)}, u32[]{:S(2)}) collective-permute-start(bf16[16,1024]{1,0:T(8,128)(2,1)S(1)} %get-tuple-element.70), channel_id=1, source_target_pairs={{0,2},{1,3},{2,0},{3,1},{4,6},{5,7},{6,4},{7,5},{8,10},{9,11},{10,... | collective-permute-start | bytes 98312 | tf_op jit(solution)/shard_map/ppermute | solution.py:607
  36.6 0.0 collective-permute-start.7
  36.6 0.6 collective-permute-start.8
  37.3 4.3 %early_pairs.1 = (f32[512,1024]{1,0:T(8,128)S(1)}, f32[2,512,1024]{2,1,0:T(8,128)S(1)}, bf16[512,128]{1,0:T(8,128)(2,1)S(1)}) custom-call(s32[1,512]{1,0:T(1,128)S(1)} %bitcast.2, s32[1,512]{1,0:T(1,128)S(1)} %bitcast.3, bf16[512,1024]{1,0:T(8,128)(2,1)S(1)} %get-tuple-element.47.white0, bf16[512,1024]{1,0:T(8,128)(2,1)S(1)} %get-tuple-element.48.white3, ...), custom_call_target="tpu_custom_call" | custom-call | flops 2415919104 | bytes 4194304 | tf_op jit(solution)/shard_map/early_pairs/pallas_call | solution.py:640
  41.7 0.1 collective-permute-done.8.rest_2_
  41.7 1.6 %shard_map.88 = (bf16[512,256]{1,0:T(8,128)(2,1)S(1)}, f32[512,256]{1,0:T(8,128)S(1)}) custom-call(f32[512,1024]{1,0:T(8,128)S(1)} %get-tuple-element.64.early, f32[2,512,1024]{2,1,0:T(8,128)S(1)} %get-tuple-element.65.first, bf16[512,128]{1,0:T(8,128)(2,1)S(1)} %get-tuple-element.66.hot, bf16[1024,512]{1,0:T(8,128)(2,1)S(1)} %get-tuple-element.51.rest_3_.rest_5_.t_odd, ...), custom_call_target="tpu_custom_call" | custom-call | flops 671088640 | bytes 3145728 | tf_op jit(solution)/shard_map/pallas_call | solution.py:663
  43.3 2.6 %collective-permute-start.12 = (bf16[512,256]{1,0:T(8,128)(2,1)S(1)}, bf16[512,256]{1,0:T(8,128)(2,1)S(1)}, u32[]{:S(2)}, u32[]{:S(2)}) collective-permute-start(bf16[512,256]{1,0:T(8,128)(2,1)S(1)} %get-tuple-element.76), channel_id=1, source_target_pairs={{0,4},{4,0},{8,12},{12,8},{1,5},{5,1},{9,13},{13,9},{2,6},{6,2},{1... | collective-permute-start | bytes 786440 | tf_op jit(solution)/shard_map/ppermute | solution.py:680
  45.9 1.6 %shard_map.86 = (bf16[512,256]{1,0:T(8,128)(2,1)S(1)}, f32[512,256]{1,0:T(8,128)S(1)}) custom-call(f32[512,1024]{1,0:T(8,128)S(1)} %get-tuple-element.64.early, f32[2,512,1024]{2,1,0:T(8,128)S(1)} %get-tuple-element.65.first, bf16[512,128]{1,0:T(8,128)(2,1)S(1)} %get-tuple-element.66.hot, bf16[1024,512]{1,0:T(8,128)(2,1)S(1)} %get-tuple-element.51.rest_3_.rest_5_.t_odd, ...), custom_call_target="tpu_custom_call" | custom-call | flops 671088640 | bytes 3145728 | tf_op jit(solution)/shard_map/pallas_call | solution.py:663
  47.5 0.1 collective-permute-start.10
  47.6 5.5 %collective-permute-done.12.received = bf16[512,256]{1,0:T(8,128)(2,1)S(1)} collective-permute-done((bf16[512,256]{1,0:T(8,128)(2,1)S(1)}, bf16[512,256]{1,0:T(8,128)(2,1)S(1)}, u32[]{:S(2)}, u32[]{:S(2)}) %collective-permute-start.12) | collective-permute-done | bytes 262176 | tf_op jit(solution)/shard_map/ppermute | solution.py:680
  53.1 3.5 %collective-permute-start.13 = (bf16[256,256]{1,0:T(8,128)(2,1)S(1)}, bf16[256,256]{1,0:T(8,128)(2,1)S(1)}, u32[]{:S(2)}, u32[]{:S(2)}) collective-permute-start(bf16[256,256]{1,0:T(8,128)(2,1)S(1)} %get-tuple-element.78), channel_id=1, source_target_pairs={{0,8},{4,12},{8,0},{12,4},{1,9},{5,13},{9,1},{13,5},{2,10},{6,14},... | collective-permute-start | bytes 393224 | tf_op jit(solution)/shard_map/ppermute | solution.py:680
  56.7 4.7 %collective-permute-done.10.received = bf16[512,256]{1,0:T(8,128)(2,1)S(1)} collective-permute-done((bf16[512,256]{1,0:T(8,128)(2,1)S(1)}, bf16[512,256]{1,0:T(8,128)(2,1)S(1)}, u32[]{:S(2)}, u32[]{:S(2)}) %collective-permute-start.10) | collective-permute-done | bytes 262176 | tf_op jit(solution)/shard_map/ppermute | solution.py:680
  61.4 1.0 %collective-permute-start.11 = (bf16[256,256]{1,0:T(8,128)(2,1)S(1)}, bf16[256,256]{1,0:T(8,128)(2,1)S(1)}, u32[]{:S(2)}, u32[]{:S(2)}) collective-permute-start(bf16[256,256]{1,0:T(8,128)(2,1)S(1)} %get-tuple-element.74), channel_id=1, source_target_pairs={{0,8},{4,12},{8,0},{12,4},{1,9},{5,13},{9,1},{13,5},{2,10},{6,14},... | collective-permute-start | bytes 393224 | tf_op jit(solution)/shard_map/ppermute | solution.py:680
  62.4 8.1 %collective-permute-done.11.refs_1_ = bf16[256,256]{1,0:T(8,128)(2,1)S(1)} collective-permute-done((bf16[256,256]{1,0:T(8,128)(2,1)S(1)}, bf16[256,256]{1,0:T(8,128)(2,1)S(1)}, u32[]{:S(2)}, u32[]{:S(2)}) %collective-permute-start.11) | collective-permute-done | bytes 131104 | tf_op jit(solution)/shard_map/ppermute | solution.py:680
  70.5 0.8 %finish.1 = f32[256,512]{1,0:T(8,128)} custom-call(f32[256,256]{1,0:T(8,128)S(1)} %get-tuple-element.73.refs_0_, bf16[256,256]{1,0:T(8,128)(2,1)S(1)} %collective-permute-done.11.refs_1_, f32[256,256]{1,0:T(8,128)S(1)} %get-tuple-element.77.refs_2_, bf16[256,256]{1,0:T(8,128)(2,1)S(1)} %collective-permute-done.13.refs_3_), custom_call_target="tpu_custom_call" | custom-call | flops 131072 | bytes 1048576 | tf_op jit(solution)/shard_map/finish/pallas_call | solution.py:699
  (13 shorter events, 0.1 us)
Async XLA Ops:
  0.0 11.5 %copy-start = (bf16[512,3072]{1,0:T(8,128)(2,1)S(1)}, bf16[512,3072]{1,0:T(8,128)(2,1)}, u32[]{:S(2)}) copy-start(bf16[512,3072]{1,0:T(8,128)(2,1)} %main.9) | copy-start | bytes 9437188
  1.5 21.8 %collective-permute-start = (bf16[336,1024]{1,0:T(8,128)(2,1)S(1)}, bf16[336,1024]{1,0:T(8,128)(2,1)S(1)}, u32[]{:S(2)}, u32[]{:S(2)}) collective-permute-start(bf16[336,1024]{1,0:T(8,128)(2,1)S(1)} %get-tuple-element.49), channel_id=1, source_target_pairs={{0,4},{4,0},{8,12},{12,8},{1,5},{5,1},{9,13},{13,9},{2,6},{6,2},{1... | collective-permute-start | bytes 2064392 | tf_op jit(solution)/shard_map/ppermute | solution.py:577
  4.6 18.7 %collective-permute-start.1 = (bf16[336,1024]{1,0:T(8,128)(2,1)S(1)}, bf16[336,1024]{1,0:T(8,128)(2,1)S(1)}, u32[]{:S(2)}, u32[]{:S(2)}) collective-permute-start(bf16[336,1024]{1,0:T(8,128)(2,1)S(1)} %get-tuple-element.50), channel_id=1, source_target_pairs={{0,0},{4,8},{8,4},{12,12},{1,1},{5,9},{9,5},{13,13},{2,2},{6,10},{... | collective-permute-start | bytes 2064392 | tf_op jit(solution)/shard_map/ppermute | solution.py:577
  6.6 24.1 %collective-permute-start.2 = (bf16[192,1024]{1,0:T(8,128)(2,1)S(1)}, bf16[192,1024]{1,0:T(8,128)(2,1)S(1)}, u32[]{:S(2)}, u32[]{:S(2)}) collective-permute-start(bf16[192,1024]{1,0:T(8,128)(2,1)S(1)} %get-tuple-element.55), channel_id=1, source_target_pairs={{0,4},{4,0},{8,12},{12,8},{1,5},{5,1},{9,13},{13,9},{2,6},{6,2},{1... | collective-permute-start | bytes 1179656 | tf_op jit(solution)/shard_map/ppermute | solution.py:577
  10.8 19.8 %collective-permute-start.3 = (bf16[192,1024]{1,0:T(8,128)(2,1)S(1)}, bf16[192,1024]{1,0:T(8,128)(2,1)S(1)}, u32[]{:S(2)}, u32[]{:S(2)}) collective-permute-start(bf16[192,1024]{1,0:T(8,128)(2,1)S(1)} %get-tuple-element.56), channel_id=1, source_target_pairs={{0,0},{4,8},{8,4},{12,12},{1,1},{5,9},{9,5},{13,13},{2,2},{6,10},{... | collective-permute-start | bytes 1179656 | tf_op jit(solution)/shard_map/ppermute | solution.py:577
  21.7 14.9 %collective-permute-start.6 = (bf16[16,1024]{1,0:T(8,128)(2,1)S(1)}, bf16[16,1024]{1,0:T(8,128)(2,1)S(1)}, u32[]{:S(2)}, u32[]{:S(2)}) collective-permute-start(bf16[16,1024]{1,0:T(8,128)(2,1)S(1)} %get-tuple-element.63), channel_id=1, source_target_pairs={{0,2},{1,3},{2,0},{3,1},{4,6},{5,7},{6,4},{7,5},{8,10},{9,11},{10,... | collective-permute-start | bytes 98312 | tf_op jit(solution)/shard_map/ppermute | solution.py:607
  23.3 14.0 %collective-permute-start.4 = (bf16[64,1024]{1,0:T(8,128)(2,1)S(1)}, bf16[64,1024]{1,0:T(8,128)(2,1)S(1)}, u32[]{:S(2)}, u32[]{:S(2)}) collective-permute-start(bf16[64,1024]{1,0:T(8,128)(2,1)S(1)} %get-tuple-element.61), channel_id=1, source_target_pairs={{0,1},{1,0},{2,3},{3,2},{4,5},{5,4},{6,7},{7,6},{8,9},{9,8},{10,11... | collective-permute-start | bytes 393224 | tf_op jit(solution)/shard_map/ppermute | solution.py:607
  23.3 14.0 %collective-permute-start.5 = (bf16[64,1024]{1,0:T(8,128)(2,1)S(1)}, bf16[64,1024]{1,0:T(8,128)(2,1)S(1)}, u32[]{:S(2)}, u32[]{:S(2)}) collective-permute-start(bf16[64,1024]{1,0:T(8,128)(2,1)S(1)} %get-tuple-element.62), channel_id=1, source_target_pairs={{0,3},{1,2},{2,1},{3,0},{4,7},{5,6},{6,5},{7,4},{8,11},{9,10},{10,... | collective-permute-start | bytes 393224 | tf_op jit(solution)/shard_map/ppermute | solution.py:607
  30.6 6.7 %copy-start.1 = (s32[512]{0:T(512)S(1)}, s32[512]{0:T(512)}, u32[]{:S(2)}) copy-start(s32[512]{0:T(512)} %param.10) | copy-start | bytes 6148
  30.7 6.7 %copy-start.2 = (s32[512]{0:T(512)S(1)}, s32[512]{0:T(512)}, u32[]{:S(2)}) copy-start(s32[512]{0:T(512)} %param.11) | copy-start | bytes 6148
  35.1 6.6 %collective-permute-start.9 = (bf16[16,1024]{1,0:T(8,128)(2,1)S(1)}, bf16[16,1024]{1,0:T(8,128)(2,1)S(1)}, u32[]{:S(2)}, u32[]{:S(2)}) collective-permute-start(bf16[16,1024]{1,0:T(8,128)(2,1)S(1)} %get-tuple-element.70), channel_id=1, source_target_pairs={{0,2},{1,3},{2,0},{3,1},{4,6},{5,7},{6,4},{7,5},{8,10},{9,11},{10,... | collective-permute-start | bytes 98312 | tf_op jit(solution)/shard_map/ppermute | solution.py:607
  36.6 5.0 %collective-permute-start.7 = (bf16[64,1024]{1,0:T(8,128)(2,1)S(1)}, bf16[64,1024]{1,0:T(8,128)(2,1)S(1)}, u32[]{:S(2)}, u32[]{:S(2)}) collective-permute-start(bf16[64,1024]{1,0:T(8,128)(2,1)S(1)} %get-tuple-element.68), channel_id=1, source_target_pairs={{0,1},{1,0},{2,3},{3,2},{4,5},{5,4},{6,7},{7,6},{8,9},{9,8},{10,11... | collective-permute-start | bytes 393224 | tf_op jit(solution)/shard_map/ppermute | solution.py:607
  36.6 5.1 %collective-permute-start.8 = (bf16[64,1024]{1,0:T(8,128)(2,1)S(1)}, bf16[64,1024]{1,0:T(8,128)(2,1)S(1)}, u32[]{:S(2)}, u32[]{:S(2)}) collective-permute-start(bf16[64,1024]{1,0:T(8,128)(2,1)S(1)} %get-tuple-element.69), channel_id=1, source_target_pairs={{0,3},{1,2},{2,1},{3,0},{4,7},{5,6},{6,5},{7,4},{8,11},{9,10},{10,... | collective-permute-start | bytes 393224 | tf_op jit(solution)/shard_map/ppermute | solution.py:607
  43.3 9.8 %collective-permute-start.12 = (bf16[512,256]{1,0:T(8,128)(2,1)S(1)}, bf16[512,256]{1,0:T(8,128)(2,1)S(1)}, u32[]{:S(2)}, u32[]{:S(2)}) collective-permute-start(bf16[512,256]{1,0:T(8,128)(2,1)S(1)} %get-tuple-element.76), channel_id=1, source_target_pairs={{0,4},{4,0},{8,12},{12,8},{1,5},{5,1},{9,13},{13,9},{2,6},{6,2},{1... | collective-permute-start | bytes 786440 | tf_op jit(solution)/shard_map/ppermute | solution.py:680
  47.5 13.8 %collective-permute-start.10 = (bf16[512,256]{1,0:T(8,128)(2,1)S(1)}, bf16[512,256]{1,0:T(8,128)(2,1)S(1)}, u32[]{:S(2)}, u32[]{:S(2)}) collective-permute-start(bf16[512,256]{1,0:T(8,128)(2,1)S(1)} %get-tuple-element.72), channel_id=1, source_target_pairs={{0,4},{4,0},{8,12},{12,8},{1,5},{5,1},{9,13},{13,9},{2,6},{6,2},{1... | collective-permute-start | bytes 786440 | tf_op jit(solution)/shard_map/ppermute | solution.py:680
  53.1 9.3 %collective-permute-start.13 = (bf16[256,256]{1,0:T(8,128)(2,1)S(1)}, bf16[256,256]{1,0:T(8,128)(2,1)S(1)}, u32[]{:S(2)}, u32[]{:S(2)}) collective-permute-start(bf16[256,256]{1,0:T(8,128)(2,1)S(1)} %get-tuple-element.78), channel_id=1, source_target_pairs={{0,8},{4,12},{8,0},{12,4},{1,9},{5,13},{9,1},{13,5},{2,10},{6,14},... | collective-permute-start | bytes 393224 | tf_op jit(solution)/shard_map/ppermute | solution.py:680
  61.4 9.1 %collective-permute-start.11 = (bf16[256,256]{1,0:T(8,128)(2,1)S(1)}, bf16[256,256]{1,0:T(8,128)(2,1)S(1)}, u32[]{:S(2)}, u32[]{:S(2)}) collective-permute-start(bf16[256,256]{1,0:T(8,128)(2,1)S(1)} %get-tuple-element.74), channel_id=1, source_target_pairs={{0,8},{4,12},{8,0},{12,4},{1,9},{5,13},{9,1},{13,5},{2,10},{6,14},... | collective-permute-start | bytes 393224 | tf_op jit(solution)/shard_map/ppermute | solution.py:680

commit v8 on v7

--- a/solution.py
+++ b/solution.py
@@ -69,19 +69,11 @@
 
 
 def prepare(pick, start, count, to, taper_ref, scratch):
-    turned_ref, rolled_ref, sums_ref, even_ref, odd_ref = scratch[:5]
+    rolled_ref, sums_ref, even_ref, odd_ref = scratch[:4]
     q = start // LANES
     s = start % LANES
     shift = (LANES - s) % LANES
-    spots, signs = [], []
-    for c in range(CHUNKS):
-        j = (c - q + CHUNKS) % CHUNKS
-        turned_ref[:, c * LANES : (c + 1) * LANES] = taper_ref[
-            :, pl.ds(pl.multiple_of(j * LANES, LANES), LANES)
-        ]
-        if c < HC:
-            spots.append(j % HC)
-            signs.append(jnp.where(j < HC, 1.0, -1.0).astype(F32))
+    places = [(c + q) % CHUNKS for c in range(CHUNKS)]
     keep = lax.broadcasted_iota(jnp.int32, (ROWS, LANES), 1) < LANES - s
 
     def turn(i, carry):
@@ -103,27 +95,27 @@
         sums_ref[rows, :] = jnp.broadcast_to(mean, (ROWS, LANES))
         return carry
 
-    loop(count, 10, average)
+    loop(count, 16, average)
 
     def fold(i, carry):
         rows = pl.ds(pl.multiple_of(i * ROWS, ROWS), ROWS)
         put = pl.ds(pl.multiple_of(to + i * ROWS, ROWS), ROWS)
         mean = sums_ref[rows, :]
         for c in range(HC):
-            low = rolled_ref[c, rows, :]
-            high = rolled_ref[c + HC, rows, :]
-            low = ((low - mean) * turned_ref[:, c * LANES : (c + 1) * LANES]).astype(BF16)
-            high = (high - mean) * turned_ref[:, (c + HC) * LANES : (c + HC + 1) * LANES]
+            low = rolled_ref[places[c], rows, :]
+            high = rolled_ref[places[c + HC], rows, :]
+            low = ((low - mean) * taper_ref[:, c * LANES : (c + 1) * LANES]).astype(BF16)
+            high = (high - mean) * taper_ref[:, (c + HC) * LANES : (c + HC + 1) * LANES]
             high = high.astype(BF16)
-            even_ref[spots[c], put, :] = low + high
-            odd_ref[spots[c], put, :] = (low - high) * signs[c].astype(BF16)
+            even_ref[c, put, :] = low + high
+            odd_ref[c, put, :] = low - high
         return carry
 
     loop(count, 4, fold)
 
 
 def transform(count, t_odd, t_even, scratch):
-    even_ref, odd_ref, spec = scratch[3:6]
+    even_ref, odd_ref, spec = scratch[2:5]
     odd = jnp.concatenate([odd_ref[c, :count] for c in range(HC)], axis=1)
     spec[:count, : 2 * QB] = jnp.dot(odd, t_odd[...], preferred_element_type=F32)
     even = jnp.concatenate([even_ref[c, :count] for c in range(HC)], axis=1)
@@ -131,41 +123,48 @@
 
 
 def whiten_rows(first_row, count, live, out_ref, scratch):
-    spec_ref = scratch[5]
-    lane = lax.broadcasted_iota(jnp.int32, (ROWS, QB), 1)
+    spec_ref = scratch[4]
+    lane = lax.broadcasted_iota(jnp.int32, (ROWS, LANES), 1)
     not_first = lane > 0
-    not_last = lane < QB - 1
+    not_last = lane < LANES - 1
     numerator = live * (5.0 * ROOT)
 
     def up(x):
-        return jnp.where(not_first, pltpu.roll(x, 1, 1), 0.0)
+        a, b = (pltpu.roll(h, 1, 1) for h in x)
+        return jnp.where(not_first, a, 0.0), jnp.where(not_first, b, a)
 
     def down(x):
-        return jnp.where(not_last, pltpu.roll(x, QB - 1, 1), 0.0)
+        a, b = (pltpu.roll(h, LANES - 1, 1) for h in x)
+        return jnp.where(not_last, a, b), jnp.where(not_last, b, 0.0)
 
     def amplitude(re, im):
         power = (re * re + im * im) * (1.0 / WIN) + 1e-06
         return power * lax.rsqrt(power)
 
+    def inverse(*terms):
+        return [
+            numerator / jnp.maximum(a + b + c, 5.0 * FLOOR) for a, b, c in zip(*terms)
+        ]
+
     def group(i, carry):
         rows = pl.ds(pl.multiple_of(first_row + i * ROWS, ROWS), ROWS)
-        o_re = spec_ref[rows, 0:QB]
-        o_im = spec_ref[rows, QB : 2 * QB]
-        e_re = spec_ref[rows, 2 * QB : 3 * QB]
-        e_im = spec_ref[rows, 3 * QB :]
-        odd = amplitude(o_re, o_im)
-        even = amplitude(e_re, e_im)
-        both = odd + even
-        inv_odd = numerator / jnp.maximum(up(both) + both + down(odd), 5.0 * FLOOR)
-        inv_even = numerator / jnp.maximum(up(even) + both + down(both), 5.0 * FLOOR)
         to = pl.ds(pl.multiple_of(i * ROWS, ROWS), ROWS)
-        out_ref[to, 0:QB] = (o_re * inv_odd).astype(BF16)
-        out_ref[to, QB : 2 * QB] = (e_re * inv_even).astype(BF16)
-        out_ref[to, 2 * QB : 3 * QB] = (o_im * inv_odd).astype(BF16)
-        out_ref[to, 3 * QB :] = (e_im * inv_even).astype(BF16)
+        parts = [
+            [spec_ref[rows, k * QB + h * LANES : k * QB + (h + 1) * LANES] for h in range(2)]
+            for k in range(4)
+        ]
+        odd = [amplitude(parts[0][h], parts[1][h]) for h in range(2)]
+        even = [amplitude(parts[2][h], parts[3][h]) for h in range(2)]
+        both = [odd[h] + even[h] for h in range(2)]
+        inv_odd = inverse(up(both), both, down(odd))
+        inv_even = inverse(up(even), both, down(both))
+        for h in range(2):
+            at = h * LANES
+            for k, j, inv in ((0, 0, inv_odd), (1, 2, inv_odd), (2, 1, inv_even), (3, 3, inv_even)):
+                out_ref[to, j * QB + at : j * QB + at + LANES] = (parts[k][h] * inv[h]).astype(BF16)
         return carry
 
-    loop(count, 8, group)
+    loop(count, 12, group)
 
 
 def slots(c):
@@ -218,7 +217,6 @@
 
 def scratches(n_sta, cap, rows):
     return [
-        pltpu.VMEM((1, WIN), F32),
         pltpu.VMEM((CHUNKS, rows, LANES), F32),
         pltpu.VMEM((rows, LANES), F32),
         pltpu.VMEM((HC, rows, LANES), BF16),
@@ -230,8 +228,8 @@
 
 def local_kernel(groups, offsets, main, cos_t, sin_t, taper, send_rows, *rest):
     t_odd, t_even, white0, white3 = rest[:4]
-    scratch = rest[-7:]
-    sends = rest[4:-7]
+    scratch = rest[-6:]
+    sends = rest[4:-6]
     fill_tables(cos_t, sin_t, t_odd, t_even)
     start0 = offsets[0]
     start3 = offsets[2] - 2 * STEP
@@ -255,8 +253,8 @@
             prepare(pick, start, count, 0, taper, scratch)
             transform(count, t_odd, t_even, scratch)
             whiten_rows(0, count, live, white.at[first : first + count], scratch)
-    outgoing(send_rows, 0, (white0, white3), None, scratch[6])
-    write_rows(groups, scratch[6], sends)
+    outgoing(send_rows, 0, (white0, white3), None, scratch[5])
+    write_rows(groups, scratch[5], sends)
 
 
 def peer(d, g, n):
@@ -342,10 +340,10 @@
     taper, t_odd, t_even, send_rows = rest[:4]
     rest = rest[4:]
     before = rest[0] if earlier else None
-    rest = rest[1:] if earlier else rest
+    rest = rest[2:] if earlier else rest
     whites = rest[:2]
-    scratch = rest[-7:]
-    sends = rest[2:-7]
+    scratch = rest[-6:]
+    sends = rest[2:-6]
     count = whites[0].shape[0]
     t = lax.axis_index("tm")
     lane = lax.broadcasted_iota(jnp.int32, (ROWS, LANES), 1)
@@ -370,8 +368,8 @@
     whiten_rows(0, count, 1.0, whites[0], scratch)
     whiten_rows(count, count, live, whites[1], scratch)
     if last:
-        outgoing(send_rows, first, whites, before, scratch[6])
-        write_rows(groups, scratch[6], sends)
+        outgoing(send_rows, first, whites, before, scratch[5])
+        write_rows(groups, scratch[5], sends)
     else:
         outgoing(send_rows, first, whites, before, sends[0])
 
@@ -441,15 +439,12 @@
     return one, two
 
 
-def early_kernel(groups, n_pieces, n_white, scale, pair_first, pair_slot, white0, white3, *rest):
-    whites = rest[: 2 * n_white]
-    rest = rest[2 * n_white :]
+def early_kernel(groups, n_pieces, scale, pair_first, pair_slot, white0, white3, *rest):
     pieces = rest[:n_pieces]
-    cross, later, hot = rest[n_pieces : n_pieces + 3]
+    cross, hot = rest[n_pieces + 1 : n_pieces + 3]
     incoming, first, second = rest[n_pieces + 3 :]
     pairs = pair_first.shape[1]
-    col = column(pair_first[...])
-    hots = station_tables(col, (white0,))
+    hots = station_tables(column(pair_first[...]), (white0,))
     first_rows(hots, (white0,), scale, first.at[0])
     first_rows(hots, (white3,), scale, first.at[1])
     hot[...] = slot_table(groups, pair_slot, hot.shape[1])
@@ -464,9 +459,14 @@
         return carry
 
     loop(pairs, 2, group)
-    hots = station_tables(col, whites[0::2])
-    first_rows(hots, whites[0::2], scale, later.at[0])
-    first_rows(hots, whites[1::2], scale, later.at[1])
+
+
+def first_kernel(scale, n_white, pair_first, *rest):
+    whites = rest[: 2 * n_white]
+    out = rest[2 * n_white]
+    hots = station_tables(column(pair_first[...]), whites[0::2])
+    first_rows(hots, whites[0::2], scale, out.at[0])
+    first_rows(hots, whites[1::2], scale, out.at[1])
 
 
 def late_kernel(groups, n_pieces, n_dest, first_pair, early, first, hot, t_odd, t_even, *rest):
@@ -624,7 +624,7 @@
         result = pl.pallas_call(
             functools.partial(rim_kernel, groups, sum(sizes[:i]), i, last),
             out_shape=[chunk] * 2 + (buffers if last else [outgoing_rows]),
-            in_specs=[SMEM] + [VMEM] * (7 + 3 * min(i, 1)),
+            in_specs=[SMEM] + [VMEM] * (7 + 4 * min(i, 1)),
             out_specs=[VMEM] * (2 + (len(buffers) if last else 1)),
             scratch_shapes=scratches(n_sta, cap, 2 * rows),
             compiler_params=params(22),
@@ -632,25 +632,31 @@
         )(
             *in_smem(starts),
             *in_vmem(main, *edges[2 * i : 2 * i + 2], *(edges[:2] if i else [])),
-            *in_vmem(taper, t_odd, t_even, send_rows, *late_out),
+            *in_vmem(taper, t_odd, t_even, send_rows, *late_out, *([hot] if i else [])),
         )
         whites = whites + list(result[:2])
         late_out = result[2:]
+        if i == 0:
+            early, hot = pl.pallas_call(
+                functools.partial(early_kernel, groups, len(buffers), scale),
+                out_shape=[pltpu.VMEM((pairs, 2 * NF), F32), pltpu.VMEM((pairs, width), BF16)],
+                in_specs=[VMEM] * (5 + len(buffers)),
+                out_specs=[VMEM] * 2,
+                scratch_shapes=pair_scratch,
+                compiler_params=params(16),
+                cost_estimate=cost(2 * 2 * pairs * (stations + width) * 2 * NF, 4 << 20),
+                name="early_pairs",
+            )(first_row, slot_row, *in_vmem(white0, white3, *early_in, *late_out))
     late_in = exchange(late_out)
-    early, first, hot = pl.pallas_call(
-        functools.partial(early_kernel, groups, len(buffers), n_chunks, scale),
-        out_shape=[
-            pltpu.VMEM((pairs, 2 * NF), F32),
-            pltpu.VMEM((2, pairs, 2 * NF), F32),
-            pltpu.VMEM((pairs, width), BF16),
-        ],
-        in_specs=[VMEM] * (4 + 2 * n_chunks + len(buffers)),
-        out_specs=[VMEM] * 3,
-        scratch_shapes=pair_scratch,
-        compiler_params=params(16),
-        cost_estimate=cost(2 * 2 * pairs * (2 * stations + width) * 2 * NF, 4 << 20),
-        name="early_pairs",
-    )(first_row, slot_row, *in_vmem(white0, white3, *whites, *early_in))
+    first = pl.pallas_call(
+        functools.partial(first_kernel, scale, n_chunks),
+        out_shape=pltpu.VMEM((2, pairs, 2 * NF), F32),
+        in_specs=[VMEM] * (1 + 2 * n_chunks),
+        out_specs=VMEM,
+        compiler_params=params(4),
+        cost_estimate=cost(2 * 2 * pairs * stations * 2 * NF, 4 << 20),
+        name="first_pairs",
+    )(first_row, *in_vmem(*whites))
 
     lag_rows = NL // n_tm
     n_half = 2

time: 71.5 us -> 71.4 us (level)
  starting transfers between devices: 20.4 us -> 22.8 us
  Pallas kernels: 32.4 us -> 30.6 us
  waiting for transfers between devices: 18.4 us -> 17.6 us
    ppermute x4, waiting for transfers between devices: 18.3 us -> 15 us  [on_device(): received = [lax.ppermute(send, 'tm', route) for send, _ in parts]]
    ppermute x4, starting transfers between devices: 7.24 us -> 9.74 us  [on_device(): received = [lax.ppermute(send, 'tm', route) for send, _ in parts]]
    ppermute x6, waiting for transfers between devices: 0.09 us -> 2.58 us  [exchange(): got[i] = lax.ppermute(pieces[i], 'sta', route)]
    pallas_call x2, Pallas kernels: 11.1 us -> 9.83 us  [on_device(): pl.pallas_call(functools.partial(rim_kernel, groups, sum(sizes[:i]), i, l...]
    pallas_call x1 -> x2, Pallas kernels: 4.33 us -> 4.33 us  [the longest x1 2.47 us: on_device(): pl.pallas_call(functools.partial(early_kernel, groups, len(buffers), scal...]
  transfers between devices with their start and end apart: 14 -> 14, of which waited for: 4 -> 4; matrix products, arithmetic and copies ran while one was open for 0% -> 0% of each run, Pallas kernels for 40% -> 32%
where the time goes in v8:
time: 71.4 us; the launch traced here: 71.2 us
  Pallas kernels  30.6 us (43%)
  starting transfers between devices  22.8 us (32%)
  waiting for transfers between devices  17.6 us (25%)
    ppermute x4, waiting for transfers between devices, on_device(): received = [lax.ppermute(send, 'tm', route) for send, _ in parts]  15 us
    pallas_call x2, Pallas kernels, on_device(): pl.pallas_call(functools.partial(rim_kernel, groups, sum(sizes[:i]), i, l...  9.83 us
    ppermute x4, starting transfers between devices, on_device(): received = [lax.ppermute(send, 'tm', route) for send, _ in parts]  9.74 us
    pallas_call x1, Pallas kernels, on_device(): pl.pallas_call(functools.partial(local_kernel, groups), out_shape=[table]...  9.67 us
    ppermute x4, starting transfers between devices, on_device(): got[swap] = lax.ppermute(packed[swap], 'tm', routes[swap])  8.71 us
    ppermute x6, starting transfers between devices, exchange(): got[i] = lax.ppermute(pieces[i], 'sta', route)  4.39 us
    pallas_call x2, Pallas kernels, on_device(): pl.pallas_call(functools.partial(late_kernel, groups, len(buffers), n_tm,...  3.08 us
    pallas_call x2, Pallas kernels, on_device(): pl.pallas_call(functools.partial(pack_kernel, sum(sizes[:i]), rows, len(e...  2.73 us
  transfers between devices with their start and end apart: 14, of which 4 were waited for; matrix products, arithmetic and copies ran while one was open for 0% of the time, Pallas kernels for 32%

profile of v8, /device:TPU:0, one launch (start us, length us, event | category | flops | bytes accessed | tf_op | source)
XLA Modules:
  0.0 71.2 jit_solution(1102084607042092699)
XLA Ops:
  0.0 1.5 %shard_map.82 = (bf16[336,1024]{1,0:T(8,128)(2,1)S(1)}, bf16[336,1024]{1,0:T(8,128)(2,1)S(1)}, s32[3]{0:T(128)S(4)}) custom-call(s32[3]{0:T(128)} %offsets.3, bf16[512,3072]{1,0:T(8,128)(2,1)} %main.9), custom_call_target="tpu_custom_call" | custom-call | bytes 2097152 | tf_op jit(solution)/shard_map/pallas_call | solution.py:560
  1.5 3.1 %collective-permute-start.3 = (bf16[336,1024]{1,0:T(8,128)(2,1)S(1)}, bf16[336,1024]{1,0:T(8,128)(2,1)S(1)}, u32[]{:S(2)}, u32[]{:S(2)}) collective-permute-start(bf16[336,1024]{1,0:T(8,128)(2,1)S(1)} %get-tuple-element.52), channel_id=1, source_target_pairs={{0,4},{4,0},{8,12},{12,8},{1,5},{5,1},{9,13},{13,9},{2,6},{6,2},{1... | collective-permute-start | bytes 2064392 | tf_op jit(solution)/shard_map/ppermute | solution.py:577
  4.6 0.7 collective-permute-start.4
  5.3 1.3 %shard_map.83 = (bf16[192,1024]{1,0:T(8,128)(2,1)S(1)}, bf16[192,1024]{1,0:T(8,128)(2,1)S(1)}, f32[64,512]{1,0:T(8,128)S(1)}, f32[64,512]{1,0:T(8,128)S(1)}, f32...) custom-call(s32[3]{0:T(128)} %offsets.3, bf16[512,3072]{1,0:T(8,128)(2,1)} %main.9, ...), custom_call_target="tpu_custom_call" | custom-call | bytes 2097152 | tf_op jit(solution)/shard_map/pallas_call | solution.py:560
  6.6 4.2 %collective-permute-start.5 = (bf16[192,1024]{1,0:T(8,128)(2,1)S(1)}, bf16[192,1024]{1,0:T(8,128)(2,1)S(1)}, u32[]{:S(2)}, u32[]{:S(2)}) collective-permute-start(bf16[192,1024]{1,0:T(8,128)(2,1)S(1)} %get-tuple-element.60), channel_id=1, source_target_pairs={{0,4},{4,0},{8,12},{12,8},{1,5},{5,1},{9,13},{13,9},{2,6},{6,2},{1... | collective-permute-start | bytes 1179656 | tf_op jit(solution)/shard_map/ppermute | solution.py:577
  10.8 0.7 collective-permute-start.6
  11.5 9.7 %local_windows.1 = (bf16[1024,512]{1,0:T(8,128)(2,1)S(1)}, bf16[1024,512]{1,0:T(8,128)(2,1)S(1)}, bf16[512,1024]{1,0:T(8,128)(2,1)S(1)}, bf16[512,1024]{1,0:T(8,...) custom-call(s32[3]{0:T(128)S(4)} %get-tuple-element.41.offsets, ...), custom_call_target="tpu_custom_call" | custom-call | flops 2147483648 | bytes 8388608 | tf_op jit(solution)/shard_map/local_windows/pallas_call | solution.py:590
  21.2 0.1 collective-permute-start
  21.2 0.0 collective-permute-done.3.rest_0_.rest_2_
  21.3 1.6 %collective-permute-start.1 = (bf16[64,1024]{1,0:T(8,128)(2,1)S(1)}, bf16[64,1024]{1,0:T(8,128)(2,1)S(1)}, u32[]{:S(2)}, u32[]{:S(2)}) collective-permute-start(bf16[64,1024]{1,0:T(8,128)(2,1)S(1)} %get-tuple-element.50), channel_id=1, source_target_pairs={{0,3},{1,2},{2,1},{3,0},{4,7},{5,6},{6,5},{7,4},{8,11},{9,10},{10,... | collective-permute-start | bytes 393224 | tf_op jit(solution)/shard_map/ppermute | solution.py:607
  22.8 0.5 collective-permute-start.2
  23.4 6.2 %shard_map.84 = (bf16[320,1024]{1,0:T(8,128)(2,1)S(1)}, bf16[320,1024]{1,0:T(8,128)(2,1)S(1)}, f32[2,128,1024]{2,1,0:T(8,128)S(1)}) custom-call(s32[3]{0:T(128)S(4)} %get-tuple-element.41.offsets, bf16[512,3072]{1,0:T(8,128)(2,1)S(1)} %copy-done, bf16[336,1024]{1,0:T(8,128)(2,1)S(1)} %collective-permute-done.3.rest_0_.rest_2_, ...), custom_call_target="tpu_custom_call" | custom-call | flops 1342177280 | bytes 4194304 | tf_op jit(solution)/shard_map/pallas_call | solution.py:624
  29.6 0.0 collective-permute-done.2.rest_3_
  29.6 0.0 collective-permute-done.rest_1_
  29.6 2.5 %early_pairs.1 = (f32[512,1024]{1,0:T(8,128)S(1)}, bf16[512,128]{1,0:T(8,128)(2,1)S(1)}) custom-call(s32[1,512]{1,0:T(1,128)S(1)} %bitcast.2, s32[1,512]{1,0:T(1,128)S(1)} %bitcast.4, bf16[512,1024]{1,0:T(8,128)(2,1)S(1)} %get-tuple-element.46.white0, bf16[512,1024]{1,0:T(8,128)(2,1)S(1)} %get-tuple-element.47.white3, ...), custom_call_target="tpu_custom_call" | custom-call | flops 1342177280 | bytes 4194304 | tf_op jit(solution)/shard_map/early_pairs/pallas_call | solution.py:640
  32.1 3.7 %shard_map.85 = (bf16[192,1024]{1,0:T(8,128)(2,1)S(1)}, bf16[192,1024]{1,0:T(8,128)(2,1)S(1)}, bf16[64,1024]{1,0:T(8,128)(2,1)S(1)}, bf16[64,1024]{1,0:T(8,128)(...) custom-call(s32[3]{0:T(128)S(4)} %get-tuple-element.41.offsets, bf16[512,3072]{1,0:T(8,128)(2,1)S(1)} %copy-done, ...), custom_call_target="tpu_custom_call" | custom-call | flops 805306368 | bytes 4194304 | tf_op jit(solution)/shard_map/pallas_call | solution.py:624
  35.8 0.1 collective-permute-start.7
  35.9 1.6 %collective-permute-start.8 = (bf16[64,1024]{1,0:T(8,128)(2,1)S(1)}, bf16[64,1024]{1,0:T(8,128)(2,1)S(1)}, u32[]{:S(2)}, u32[]{:S(2)}) collective-permute-start(bf16[64,1024]{1,0:T(8,128)(2,1)S(1)} %get-tuple-element.67), channel_id=1, source_target_pairs={{0,3},{1,2},{2,1},{3,0},{4,7},{5,6},{6,5},{7,4},{8,11},{9,10},{10,... | collective-permute-start | bytes 393224 | tf_op jit(solution)/shard_map/ppermute | solution.py:607
  37.5 0.5 collective-permute-start.9
  38.0 1.9 %first_pairs.1.first = f32[2,512,1024]{2,1,0:T(8,128)S(1)} custom-call(s32[1,512]{1,0:T(1,128)S(1)} %bitcast.3, bf16[320,1024]{1,0:T(8,128)(2,1)S(1)} %get-tuple-element.58.rest_0_, bf16[320,1024]{1,0:T(8,128)(2,1)S(1)} %get-tuple-element.59.rest_1_, bf16[192,1024]{1,0:T(8,128)(2,1)S(1)} %get-tuple-element.63.rest_2_, ...), custom_call_target="tpu_custom_call" | custom-call | flops 1073741824 | bytes 4194304 | tf_op jit(solution)/shard_map/first_pairs/pallas_call | solution.py:651
  39.9 2.6 %collective-permute-done.9.rest_3_ = bf16[16,1024]{1,0:T(8,128)(2,1)S(1)} collective-permute-done((bf16[16,1024]{1,0:T(8,128)(2,1)S(1)}, bf16[16,1024]{1,0:T(8,128)(2,1)S(1)}, u32[]{:S(2)}, u32[]{:S(2)}) %collective-permute-start.9) | collective-permute-done | bytes 32800 | tf_op jit(solution)/shard_map/ppermute | solution.py:607
  42.4 0.0 collective-permute-done.7.rest_1_
  42.4 1.5 %shard_map.88 = (bf16[512,256]{1,0:T(8,128)(2,1)S(1)}, f32[512,256]{1,0:T(8,128)S(1)}) custom-call(f32[512,1024]{1,0:T(8,128)S(1)} %get-tuple-element.57.early, f32[2,512,1024]{2,1,0:T(8,128)S(1)} %first_pairs.1.first, bf16[512,128]{1,0:T(8,128)(2,1)S(1)} %get-tuple-element.62.rest_9_.hot, bf16[1024,512]{1,0:T(8,128)(2,1)S(1)} %get-tuple-element.54.rest_3_.rest_5_.t_odd, ...), custom_call_target="tpu_custom_call" | custom-call | flops 671088640 | bytes 3145728 | tf_op jit(solution)/shard_map/pallas_call | solution.py:669
  44.0 3.9 %collective-permute-start.12 = (bf16[512,256]{1,0:T(8,128)(2,1)S(1)}, bf16[512,256]{1,0:T(8,128)(2,1)S(1)}, u32[]{:S(2)}, u32[]{:S(2)}) collective-permute-start(bf16[512,256]{1,0:T(8,128)(2,1)S(1)} %get-tuple-element.74), channel_id=1, source_target_pairs={{0,4},{4,0},{8,12},{12,8},{1,5},{5,1},{9,13},{13,9},{2,6},{6,2},{1... | collective-permute-start | bytes 786440 | tf_op jit(solution)/shard_map/ppermute | solution.py:686
  47.9 1.5 %shard_map.86 = (bf16[512,256]{1,0:T(8,128)(2,1)S(1)}, f32[512,256]{1,0:T(8,128)S(1)}) custom-call(f32[512,1024]{1,0:T(8,128)S(1)} %get-tuple-element.57.early, f32[2,512,1024]{2,1,0:T(8,128)S(1)} %first_pairs.1.first, bf16[512,128]{1,0:T(8,128)(2,1)S(1)} %get-tuple-element.62.rest_9_.hot, bf16[1024,512]{1,0:T(8,128)(2,1)S(1)} %get-tuple-element.54.rest_3_.rest_5_.t_odd, ...), custom_call_target="tpu_custom_call" | custom-call | flops 671088640 | bytes 3145728 | tf_op jit(solution)/shard_map/pallas_call | solution.py:669
  49.4 0.1 collective-permute-start.10
  49.5 5.5 %collective-permute-done.12.received = bf16[512,256]{1,0:T(8,128)(2,1)S(1)} collective-permute-done((bf16[512,256]{1,0:T(8,128)(2,1)S(1)}, bf16[512,256]{1,0:T(8,128)(2,1)S(1)}, u32[]{:S(2)}, u32[]{:S(2)}) %collective-permute-start.12) | collective-permute-done | bytes 262176 | tf_op jit(solution)/shard_map/ppermute | solution.py:686
  55.1 3.5 %collective-permute-start.13 = (bf16[256,256]{1,0:T(8,128)(2,1)S(1)}, bf16[256,256]{1,0:T(8,128)(2,1)S(1)}, u32[]{:S(2)}, u32[]{:S(2)}) collective-permute-start(bf16[256,256]{1,0:T(8,128)(2,1)S(1)} %get-tuple-element.76), channel_id=1, source_target_pairs={{0,8},{4,12},{8,0},{12,4},{1,9},{5,13},{9,1},{13,5},{2,10},{6,14},... | collective-permute-start | bytes 393224 | tf_op jit(solution)/shard_map/ppermute | solution.py:686
  58.6 3.2 %collective-permute-done.10.received = bf16[512,256]{1,0:T(8,128)(2,1)S(1)} collective-permute-done((bf16[512,256]{1,0:T(8,128)(2,1)S(1)}, bf16[512,256]{1,0:T(8,128)(2,1)S(1)}, u32[]{:S(2)}, u32[]{:S(2)}) %collective-permute-start.10) | collective-permute-done | bytes 262176 | tf_op jit(solution)/shard_map/ppermute | solution.py:686
  61.9 2.2 %collective-permute-start.11 = (bf16[256,256]{1,0:T(8,128)(2,1)S(1)}, bf16[256,256]{1,0:T(8,128)(2,1)S(1)}, u32[]{:S(2)}, u32[]{:S(2)}) collective-permute-start(bf16[256,256]{1,0:T(8,128)(2,1)S(1)} %get-tuple-element.72), channel_id=1, source_target_pairs={{0,8},{4,12},{8,0},{12,4},{1,9},{5,13},{9,1},{13,5},{2,10},{6,14},... | collective-permute-start | bytes 393224 | tf_op jit(solution)/shard_map/ppermute | solution.py:686
  64.1 6.2 %collective-permute-done.11.refs_1_ = bf16[256,256]{1,0:T(8,128)(2,1)S(1)} collective-permute-done((bf16[256,256]{1,0:T(8,128)(2,1)S(1)}, bf16[256,256]{1,0:T(8,128)(2,1)S(1)}, u32[]{:S(2)}, u32[]{:S(2)}) %collective-permute-start.11) | collective-permute-done | bytes 131104 | tf_op jit(solution)/shard_map/ppermute | solution.py:686
  70.4 0.8 %finish.1 = f32[256,512]{1,0:T(8,128)} custom-call(f32[256,256]{1,0:T(8,128)S(1)} %get-tuple-element.71.refs_0_, bf16[256,256]{1,0:T(8,128)(2,1)S(1)} %collective-permute-done.11.refs_1_, f32[256,256]{1,0:T(8,128)S(1)} %get-tuple-element.75.refs_2_, bf16[256,256]{1,0:T(8,128)(2,1)S(1)} %collective-permute-done.13.refs_3_), custom_call_target="tpu_custom_call" | custom-call | flops 131072 | bytes 1048576 | tf_op jit(solution)/shard_map/finish/pallas_call | solution.py:705
  (14 shorter events, 0.1 us)
Async XLA Ops:
  0.0 11.5 %copy-start = (bf16[512,3072]{1,0:T(8,128)(2,1)S(1)}, bf16[512,3072]{1,0:T(8,128)(2,1)}, u32[]{:S(2)}) copy-start(bf16[512,3072]{1,0:T(8,128)(2,1)} %main.9) | copy-start | bytes 9437188
  1.5 19.8 %collective-permute-start.3 = (bf16[336,1024]{1,0:T(8,128)(2,1)S(1)}, bf16[336,1024]{1,0:T(8,128)(2,1)S(1)}, u32[]{:S(2)}, u32[]{:S(2)}) collective-permute-start(bf16[336,1024]{1,0:T(8,128)(2,1)S(1)} %get-tuple-element.52), channel_id=1, source_target_pairs={{0,4},{4,0},{8,12},{12,8},{1,5},{5,1},{9,13},{13,9},{2,6},{6,2},{1... | collective-permute-start | bytes 2064392 | tf_op jit(solution)/shard_map/ppermute | solution.py:577
  4.6 18.3 %collective-permute-start.4 = (bf16[336,1024]{1,0:T(8,128)(2,1)S(1)}, bf16[336,1024]{1,0:T(8,128)(2,1)S(1)}, u32[]{:S(2)}, u32[]{:S(2)}) collective-permute-start(bf16[336,1024]{1,0:T(8,128)(2,1)S(1)} %get-tuple-element.53), channel_id=1, source_target_pairs={{0,0},{4,8},{8,4},{12,12},{1,1},{5,9},{9,5},{13,13},{2,2},{6,10},{... | collective-permute-start | bytes 2064392 | tf_op jit(solution)/shard_map/ppermute | solution.py:577
  6.6 25.5 %collective-permute-start.5 = (bf16[192,1024]{1,0:T(8,128)(2,1)S(1)}, bf16[192,1024]{1,0:T(8,128)(2,1)S(1)}, u32[]{:S(2)}, u32[]{:S(2)}) collective-permute-start(bf16[192,1024]{1,0:T(8,128)(2,1)S(1)} %get-tuple-element.60), channel_id=1, source_target_pairs={{0,4},{4,0},{8,12},{12,8},{1,5},{5,1},{9,13},{13,9},{2,6},{6,2},{1... | collective-permute-start | bytes 1179656 | tf_op jit(solution)/shard_map/ppermute | solution.py:577
  10.8 21.3 %collective-permute-start.6 = (bf16[192,1024]{1,0:T(8,128)(2,1)S(1)}, bf16[192,1024]{1,0:T(8,128)(2,1)S(1)}, u32[]{:S(2)}, u32[]{:S(2)}) collective-permute-start(bf16[192,1024]{1,0:T(8,128)(2,1)S(1)} %get-tuple-element.61), channel_id=1, source_target_pairs={{0,0},{4,8},{8,4},{12,12},{1,1},{5,9},{9,5},{13,13},{2,2},{6,10},{... | collective-permute-start | bytes 1179656 | tf_op jit(solution)/shard_map/ppermute | solution.py:577
  21.2 8.4 %collective-permute-start = (bf16[64,1024]{1,0:T(8,128)(2,1)S(1)}, bf16[64,1024]{1,0:T(8,128)(2,1)S(1)}, u32[]{:S(2)}, u32[]{:S(2)}) collective-permute-start(bf16[64,1024]{1,0:T(8,128)(2,1)S(1)} %get-tuple-element.49), channel_id=1, source_target_pairs={{0,1},{1,0},{2,3},{3,2},{4,5},{5,4},{6,7},{7,6},{8,9},{9,8},{10,11... | collective-permute-start | bytes 393224 | tf_op jit(solution)/shard_map/ppermute | solution.py:607
  21.3 8.3 %collective-permute-start.1 = (bf16[64,1024]{1,0:T(8,128)(2,1)S(1)}, bf16[64,1024]{1,0:T(8,128)(2,1)S(1)}, u32[]{:S(2)}, u32[]{:S(2)}) collective-permute-start(bf16[64,1024]{1,0:T(8,128)(2,1)S(1)} %get-tuple-element.50), channel_id=1, source_target_pairs={{0,3},{1,2},{2,1},{3,0},{4,7},{5,6},{6,5},{7,4},{8,11},{9,10},{10,... | collective-permute-start | bytes 393224 | tf_op jit(solution)/shard_map/ppermute | solution.py:607
  22.8 6.7 %collective-permute-start.2 = (bf16[16,1024]{1,0:T(8,128)(2,1)S(1)}, bf16[16,1024]{1,0:T(8,128)(2,1)S(1)}, u32[]{:S(2)}, u32[]{:S(2)}) collective-permute-start(bf16[16,1024]{1,0:T(8,128)(2,1)S(1)} %get-tuple-element.51), channel_id=1, source_target_pairs={{0,2},{1,3},{2,0},{3,1},{4,6},{5,7},{6,4},{7,5},{8,10},{9,11},{10,... | collective-permute-start | bytes 98312 | tf_op jit(solution)/shard_map/ppermute | solution.py:607
  23.4 6.2 %copy-start.1 = (s32[512]{0:T(512)S(1)}, s32[512]{0:T(512)}, u32[]{:S(2)}) copy-start(s32[512]{0:T(512)} %param.10) | copy-start | bytes 6148
  23.4 6.2 %copy-start.2 = (s32[512]{0:T(512)S(1)}, s32[512]{0:T(512)}, u32[]{:S(2)}) copy-start(s32[512]{0:T(512)} %param.11) | copy-start | bytes 6148
  35.8 6.6 %collective-permute-start.7 = (bf16[64,1024]{1,0:T(8,128)(2,1)S(1)}, bf16[64,1024]{1,0:T(8,128)(2,1)S(1)}, u32[]{:S(2)}, u32[]{:S(2)}) collective-permute-start(bf16[64,1024]{1,0:T(8,128)(2,1)S(1)} %get-tuple-element.66), channel_id=1, source_target_pairs={{0,1},{1,0},{2,3},{3,2},{4,5},{5,4},{6,7},{7,6},{8,9},{9,8},{10,11... | collective-permute-start | bytes 393224 | tf_op jit(solution)/shard_map/ppermute | solution.py:607
  35.9 6.6 %collective-permute-start.8 = (bf16[64,1024]{1,0:T(8,128)(2,1)S(1)}, bf16[64,1024]{1,0:T(8,128)(2,1)S(1)}, u32[]{:S(2)}, u32[]{:S(2)}) collective-permute-start(bf16[64,1024]{1,0:T(8,128)(2,1)S(1)} %get-tuple-element.67), channel_id=1, source_target_pairs={{0,3},{1,2},{2,1},{3,0},{4,7},{5,6},{6,5},{7,4},{8,11},{9,10},{10,... | collective-permute-start | bytes 393224 | tf_op jit(solution)/shard_map/ppermute | solution.py:607
  37.5 5.0 %collective-permute-start.9 = (bf16[16,1024]{1,0:T(8,128)(2,1)S(1)}, bf16[16,1024]{1,0:T(8,128)(2,1)S(1)}, u32[]{:S(2)}, u32[]{:S(2)}) collective-permute-start(bf16[16,1024]{1,0:T(8,128)(2,1)S(1)} %get-tuple-element.68), channel_id=1, source_target_pairs={{0,2},{1,3},{2,0},{3,1},{4,6},{5,7},{6,4},{7,5},{8,10},{9,11},{10,... | collective-permute-start | bytes 98312 | tf_op jit(solution)/shard_map/ppermute | solution.py:607
  44.0 11.0 %collective-permute-start.12 = (bf16[512,256]{1,0:T(8,128)(2,1)S(1)}, bf16[512,256]{1,0:T(8,128)(2,1)S(1)}, u32[]{:S(2)}, u32[]{:S(2)}) collective-permute-start(bf16[512,256]{1,0:T(8,128)(2,1)S(1)} %get-tuple-element.74), channel_id=1, source_target_pairs={{0,4},{4,0},{8,12},{12,8},{1,5},{5,1},{9,13},{13,9},{2,6},{6,2},{1... | collective-permute-start | bytes 786440 | tf_op jit(solution)/shard_map/ppermute | solution.py:686
  49.4 12.4 %collective-permute-start.10 = (bf16[512,256]{1,0:T(8,128)(2,1)S(1)}, bf16[512,256]{1,0:T(8,128)(2,1)S(1)}, u32[]{:S(2)}, u32[]{:S(2)}) collective-permute-start(bf16[512,256]{1,0:T(8,128)(2,1)S(1)} %get-tuple-element.70), channel_id=1, source_target_pairs={{0,4},{4,0},{8,12},{12,8},{1,5},{5,1},{9,13},{13,9},{2,6},{6,2},{1... | collective-permute-start | bytes 786440 | tf_op jit(solution)/shard_map/ppermute | solution.py:686
  55.1 9.1 %collective-permute-start.13 = (bf16[256,256]{1,0:T(8,128)(2,1)S(1)}, bf16[256,256]{1,0:T(8,128)(2,1)S(1)}, u32[]{:S(2)}, u32[]{:S(2)}) collective-permute-start(bf16[256,256]{1,0:T(8,128)(2,1)S(1)} %get-tuple-element.76), channel_id=1, source_target_pairs={{0,8},{4,12},{8,0},{12,4},{1,9},{5,13},{9,1},{13,5},{2,10},{6,14},... | collective-permute-start | bytes 393224 | tf_op jit(solution)/shard_map/ppermute | solution.py:686
  61.9 8.4 %collective-permute-start.11 = (bf16[256,256]{1,0:T(8,128)(2,1)S(1)}, bf16[256,256]{1,0:T(8,128)(2,1)S(1)}, u32[]{:S(2)}, u32[]{:S(2)}) collective-permute-start(bf16[256,256]{1,0:T(8,128)(2,1)S(1)} %get-tuple-element.72), channel_id=1, source_target_pairs={{0,8},{4,12},{8,0},{12,4},{1,9},{5,13},{9,1},{13,5},{2,10},{6,14},... | collective-permute-start | bytes 393224 | tf_op jit(solution)/shard_map/ppermute | solution.py:686

commit v9 on v8

--- a/solution.py
+++ b/solution.py
@@ -340,7 +340,7 @@
     taper, t_odd, t_even, send_rows = rest[:4]
     rest = rest[4:]
     before = rest[0] if earlier else None
-    rest = rest[2:] if earlier else rest
+    rest = rest[1:] if earlier else rest
     whites = rest[:2]
     scratch = rest[-6:]
     sends = rest[2:-6]
@@ -439,12 +439,15 @@
     return one, two
 
 
-def early_kernel(groups, n_pieces, scale, pair_first, pair_slot, white0, white3, *rest):
+def early_kernel(groups, n_pieces, n_white, scale, pair_first, pair_slot, white0, white3, *rest):
+    whites = rest[: 2 * n_white]
+    rest = rest[2 * n_white :]
     pieces = rest[:n_pieces]
-    cross, hot = rest[n_pieces + 1 : n_pieces + 3]
+    cross, later, hot = rest[n_pieces : n_pieces + 3]
     incoming, first, second = rest[n_pieces + 3 :]
     pairs = pair_first.shape[1]
-    hots = station_tables(column(pair_first[...]), (white0,))
+    col = column(pair_first[...])
+    hots = station_tables(col, (white0,))
     first_rows(hots, (white0,), scale, first.at[0])
     first_rows(hots, (white3,), scale, first.at[1])
     hot[...] = slot_table(groups, pair_slot, hot.shape[1])
@@ -459,14 +462,9 @@
         return carry
 
     loop(pairs, 2, group)
-
-
-def first_kernel(scale, n_white, pair_first, *rest):
-    whites = rest[: 2 * n_white]
-    out = rest[2 * n_white]
-    hots = station_tables(column(pair_first[...]), whites[0::2])
-    first_rows(hots, whites[0::2], scale, out.at[0])
-    first_rows(hots, whites[1::2], scale, out.at[1])
+    hots = station_tables(col, whites[0::2])
+    first_rows(hots, whites[0::2], scale, later.at[0])
+    first_rows(hots, whites[1::2], scale, later.at[1])
 
 
 def late_kernel(groups, n_pieces, n_dest, first_pair, early, first, hot, t_odd, t_even, *rest):
@@ -573,7 +571,7 @@
         else:
             cos_t, sin_t, taper, send_rows = packed[2:-1]
         got = [None, None]
-        for swap in (1, 0):
+        for swap in (0, 1):
             got[swap] = lax.ppermute(packed[swap], "tm", routes[swap])
         edges += got
 
@@ -601,7 +599,7 @@
 
     def exchange(pieces):
         got = list(pieces)
-        for i, d in sorted(enumerate(near + far), key=lambda x: (2, 1, 0)[near.index(x[1])] if x[1] in near else 3):
+        for i, d in enumerate(near + far):
             if d != "own":
                 route = [(k, peer(d, k, n_sta)) for k in range(n_sta)]
                 got[i] = lax.ppermute(pieces[i], "sta", route)
@@ -624,7 +622,7 @@
         result = pl.pallas_call(
             functools.partial(rim_kernel, groups, sum(sizes[:i]), i, last),
             out_shape=[chunk] * 2 + (buffers if last else [outgoing_rows]),
-            in_specs=[SMEM] + [VMEM] * (7 + 4 * min(i, 1)),
+            in_specs=[SMEM] + [VMEM] * (7 + 3 * min(i, 1)),
             out_specs=[VMEM] * (2 + (len(buffers) if last else 1)),
             scratch_shapes=scratches(n_sta, cap, 2 * rows),
             compiler_params=params(22),
@@ -632,31 +630,25 @@
         )(
             *in_smem(starts),
             *in_vmem(main, *edges[2 * i : 2 * i + 2], *(edges[:2] if i else [])),
-            *in_vmem(taper, t_odd, t_even, send_rows, *late_out, *([hot] if i else [])),
+            *in_vmem(taper, t_odd, t_even, send_rows, *late_out),
         )
         whites = whites + list(result[:2])
         late_out = result[2:]
-        if i == 0:
-            early, hot = pl.pallas_call(
-                functools.partial(early_kernel, groups, len(buffers), scale),
-                out_shape=[pltpu.VMEM((pairs, 2 * NF), F32), pltpu.VMEM((pairs, width), BF16)],
-                in_specs=[VMEM] * (5 + len(buffers)),
-                out_specs=[VMEM] * 2,
-                scratch_shapes=pair_scratch,
-                compiler_params=params(16),
-                cost_estimate=cost(2 * 2 * pairs * (stations + width) * 2 * NF, 4 << 20),
-                name="early_pairs",
-            )(first_row, slot_row, *in_vmem(white0, white3, *early_in, *late_out))
     late_in = exchange(late_out)
-    first = pl.pallas_call(
-        functools.partial(first_kernel, scale, n_chunks),
-        out_shape=pltpu.VMEM((2, pairs, 2 * NF), F32),
-        in_specs=[VMEM] * (1 + 2 * n_chunks),
-        out_specs=VMEM,
-        compiler_params=params(4),
-        cost_estimate=cost(2 * 2 * pairs * stations * 2 * NF, 4 << 20),
-        name="first_pairs",
-    )(first_row, *in_vmem(*whites))
+    early, first, hot = pl.pallas_call(
+        functools.partial(early_kernel, groups, len(buffers), n_chunks, scale),
+        out_shape=[
+            pltpu.VMEM((pairs, 2 * NF), F32),
+            pltpu.VMEM((2, pairs, 2 * NF), F32),
+            pltpu.VMEM((pairs, width), BF16),
+        ],
+        in_specs=[VMEM] * (4 + 2 * n_chunks + len(buffers)),
+        out_specs=[VMEM] * 3,
+        scratch_shapes=pair_scratch,
+        compiler_params=params(16),
+        cost_estimate=cost(2 * 2 * pairs * (2 * stations + width) * 2 * NF, 4 << 20),
+        name="early_pairs",
+    )(first_row, slot_row, *in_vmem(white0, white3, *whites, *early_in))
 
     lag_rows = NL // n_tm
     n_half = 2

time: 71.4 us -> 70.5 us (0.987)
  starting transfers between devices: 22.8 us -> 20.8 us
  waiting for transfers between devices: 17.6 us -> 18.9 us
    ppermute x4, waiting for transfers between devices: 15 us -> 18.8 us  [on_device(): received = [lax.ppermute(send, 'tm', route) for send, _ in parts]]
    ppermute x6, waiting for transfers between devices: 2.58 us -> 0.09 us  [exchange(): got[i] = lax.ppermute(pieces[i], 'sta', route)]
    ppermute x4, starting transfers between devices: 9.74 us -> 7.63 us  [on_device(): received = [lax.ppermute(send, 'tm', route) for send, _ in parts]]
    pallas_call x2 -> x1, Pallas kernels: 4.33 us -> 4.33 us  [on_device(): pl.pallas_call(functools.partial(early_kernel, groups, len(buffers), n_ch...]
  transfers between devices with their start and end apart: 14 -> 14, of which waited for: 4 -> 4; matrix products, arithmetic and copies ran while one was open for 0% -> 0% of each run, Pallas kernels for 32% -> 38%
where the time goes in v9:
time: 70.5 us; the launch traced here: 70.4 us
  Pallas kernels  30.6 us (43%)
  starting transfers between devices  20.8 us (30%)
  waiting for transfers between devices  18.9 us (27%)
    ppermute x4, waiting for transfers between devices, on_device(): received = [lax.ppermute(send, 'tm', route) for send, _ in parts]  18.8 us
    pallas_call x2, Pallas kernels, on_device(): pl.pallas_call(functools.partial(rim_kernel, groups, sum(sizes[:i]), i, l...  9.81 us
    pallas_call x1, Pallas kernels, on_device(): pl.pallas_call(functools.partial(local_kernel, groups), out_shape=[table]...  9.66 us
    ppermute x4, starting transfers between devices, on_device(): got[swap] = lax.ppermute(packed[swap], 'tm', routes[swap])  8.71 us
    ppermute x4, starting transfers between devices, on_device(): received = [lax.ppermute(send, 'tm', route) for send, _ in parts]  7.63 us
    ppermute x6, starting transfers between devices, exchange(): got[i] = lax.ppermute(pieces[i], 'sta', route)  4.41 us
    pallas_call x1, Pallas kernels, on_device(): pl.pallas_call(functools.partial(early_kernel, groups, len(buffers), n_ch...  4.33 us
    pallas_call x2, Pallas kernels, on_device(): pl.pallas_call(functools.partial(late_kernel, groups, len(buffers), n_tm,...  3.13 us
  transfers between devices with their start and end apart: 14, of which 4 were waited for; matrix products, arithmetic and copies ran while one was open for 0% of the time, Pallas kernels for 38%

profile of v9, /device:TPU:0, one launch (start us, length us, event | category | flops | bytes accessed | tf_op | source)
XLA Modules:
  0.0 70.4 jit_solution(17844666876067813333)
XLA Ops:
  0.0 1.5 %shard_map.82 = (bf16[336,1024]{1,0:T(8,128)(2,1)S(1)}, bf16[336,1024]{1,0:T(8,128)(2,1)S(1)}, s32[3]{0:T(128)S(4)}) custom-call(s32[3]{0:T(128)} %offsets.3, bf16[512,3072]{1,0:T(8,128)(2,1)} %main.9), custom_call_target="tpu_custom_call" | custom-call | bytes 2097152 | tf_op jit(solution)/shard_map/pallas_call | solution.py:558
  1.5 3.1 %collective-permute-start = (bf16[336,1024]{1,0:T(8,128)(2,1)S(1)}, bf16[336,1024]{1,0:T(8,128)(2,1)S(1)}, u32[]{:S(2)}, u32[]{:S(2)}) collective-permute-start(bf16[336,1024]{1,0:T(8,128)(2,1)S(1)} %get-tuple-element.49), channel_id=1, source_target_pairs={{0,4},{4,0},{8,12},{12,8},{1,5},{5,1},{9,13},{13,9},{2,6},{6,2},{1... | collective-permute-start | bytes 2064392 | tf_op jit(solution)/shard_map/ppermute | solution.py:575
  4.6 0.7 collective-permute-start.1
  5.3 1.3 %shard_map.83 = (bf16[192,1024]{1,0:T(8,128)(2,1)S(1)}, bf16[192,1024]{1,0:T(8,128)(2,1)S(1)}, f32[64,512]{1,0:T(8,128)S(1)}, f32[64,512]{1,0:T(8,128)S(1)}, f32...) custom-call(s32[3]{0:T(128)} %offsets.3, bf16[512,3072]{1,0:T(8,128)(2,1)} %main.9, ...), custom_call_target="tpu_custom_call" | custom-call | bytes 2097152 | tf_op jit(solution)/shard_map/pallas_call | solution.py:558
  6.6 4.2 %collective-permute-start.2 = (bf16[192,1024]{1,0:T(8,128)(2,1)S(1)}, bf16[192,1024]{1,0:T(8,128)(2,1)S(1)}, u32[]{:S(2)}, u32[]{:S(2)}) collective-permute-start(bf16[192,1024]{1,0:T(8,128)(2,1)S(1)} %get-tuple-element.55), channel_id=1, source_target_pairs={{0,4},{4,0},{8,12},{12,8},{1,5},{5,1},{9,13},{13,9},{2,6},{6,2},{1... | collective-permute-start | bytes 1179656 | tf_op jit(solution)/shard_map/ppermute | solution.py:575
  10.8 0.7 collective-permute-start.3
  11.5 9.7 %local_windows.1 = (bf16[1024,512]{1,0:T(8,128)(2,1)S(1)}, bf16[1024,512]{1,0:T(8,128)(2,1)S(1)}, bf16[512,1024]{1,0:T(8,128)(2,1)S(1)}, bf16[512,1024]{1,0:T(8,...) custom-call(s32[3]{0:T(128)S(4)} %get-tuple-element.42.offsets, ...), custom_call_target="tpu_custom_call" | custom-call | flops 2147483648 | bytes 8388608 | tf_op jit(solution)/shard_map/local_windows/pallas_call | solution.py:588
  21.2 1.6 %collective-permute-start.6 = (bf16[16,1024]{1,0:T(8,128)(2,1)S(1)}, bf16[16,1024]{1,0:T(8,128)(2,1)S(1)}, u32[]{:S(2)}, u32[]{:S(2)}) collective-permute-start(bf16[16,1024]{1,0:T(8,128)(2,1)S(1)} %get-tuple-element.63), channel_id=1, source_target_pairs={{0,2},{1,3},{2,0},{3,1},{4,6},{5,7},{6,4},{7,5},{8,10},{9,11},{10,... | collective-permute-start | bytes 98312 | tf_op jit(solution)/shard_map/ppermute | solution.py:605
  22.7 0.0 collective-permute-done.rest_0_.rest_2_
  22.7 0.0 collective-permute-start.4
  22.7 0.0 collective-permute-done.1.rest_1_.rest_3_
  22.7 0.6 collective-permute-start.5
  23.4 6.2 %shard_map.84 = (bf16[320,1024]{1,0:T(8,128)(2,1)S(1)}, bf16[320,1024]{1,0:T(8,128)(2,1)S(1)}, f32[2,128,1024]{2,1,0:T(8,128)S(1)}) custom-call(s32[3]{0:T(128)S(4)} %get-tuple-element.42.offsets, bf16[512,3072]{1,0:T(8,128)(2,1)S(1)} %copy-done, bf16[336,1024]{1,0:T(8,128)(2,1)S(1)} %collective-permute-done.rest_0_.rest_2_, ...), custom_call_target="tpu_custom_call" | custom-call | flops 1342177280 | bytes 4194304 | tf_op jit(solution)/shard_map/pallas_call | solution.py:622
  29.5 0.0 collective-permute-done.3.rest_1_
  29.6 0.0 copy-start.1
  29.6 0.0 copy-start.2
  29.6 3.7 %shard_map.85 = (bf16[192,1024]{1,0:T(8,128)(2,1)S(1)}, bf16[192,1024]{1,0:T(8,128)(2,1)S(1)}, bf16[64,1024]{1,0:T(8,128)(2,1)S(1)}, bf16[64,1024]{1,0:T(8,128)(...) custom-call(s32[3]{0:T(128)S(4)} %get-tuple-element.42.offsets, bf16[512,3072]{1,0:T(8,128)(2,1)S(1)} %copy-done, ...), custom_call_target="tpu_custom_call" | custom-call | flops 805306368 | bytes 4194304 | tf_op jit(solution)/shard_map/pallas_call | solution.py:622
  33.2 1.5 %collective-permute-start.9 = (bf16[16,1024]{1,0:T(8,128)(2,1)S(1)}, bf16[16,1024]{1,0:T(8,128)(2,1)S(1)}, u32[]{:S(2)}, u32[]{:S(2)}) collective-permute-start(bf16[16,1024]{1,0:T(8,128)(2,1)S(1)} %get-tuple-element.70), channel_id=1, source_target_pairs={{0,2},{1,3},{2,0},{3,1},{4,6},{5,7},{6,4},{7,5},{8,10},{9,11},{10,... | collective-permute-start | bytes 98312 | tf_op jit(solution)/shard_map/ppermute | solution.py:605
  34.8 0.0 collective-permute-start.7
  34.8 0.7 collective-permute-start.8
  35.5 4.3 %early_pairs.1 = (f32[512,1024]{1,0:T(8,128)S(1)}, f32[2,512,1024]{2,1,0:T(8,128)S(1)}, bf16[512,128]{1,0:T(8,128)(2,1)S(1)}) custom-call(s32[1,512]{1,0:T(1,128)S(1)} %bitcast.2, s32[1,512]{1,0:T(1,128)S(1)} %bitcast.3, bf16[512,1024]{1,0:T(8,128)(2,1)S(1)} %get-tuple-element.47.white0, bf16[512,1024]{1,0:T(8,128)(2,1)S(1)} %get-tuple-element.48.white3, ...), custom_call_target="tpu_custom_call" | custom-call | flops 2415919104 | bytes 4194304 | tf_op jit(solution)/shard_map/early_pairs/pallas_call | solution.py:638
  39.8 0.1 collective-permute-done.8.rest_2_
  39.9 1.6 %shard_map.88 = (bf16[512,256]{1,0:T(8,128)(2,1)S(1)}, f32[512,256]{1,0:T(8,128)S(1)}) custom-call(f32[512,1024]{1,0:T(8,128)S(1)} %get-tuple-element.64.early, f32[2,512,1024]{2,1,0:T(8,128)S(1)} %get-tuple-element.65.first, bf16[512,128]{1,0:T(8,128)(2,1)S(1)} %get-tuple-element.66.hot, bf16[1024,512]{1,0:T(8,128)(2,1)S(1)} %get-tuple-element.51.rest_3_.rest_5_.t_odd, ...), custom_call_target="tpu_custom_call" | custom-call | flops 671088640 | bytes 3145728 | tf_op jit(solution)/shard_map/pallas_call | solution.py:661
  41.5 3.5 %collective-permute-start.12 = (bf16[512,256]{1,0:T(8,128)(2,1)S(1)}, bf16[512,256]{1,0:T(8,128)(2,1)S(1)}, u32[]{:S(2)}, u32[]{:S(2)}) collective-permute-start(bf16[512,256]{1,0:T(8,128)(2,1)S(1)} %get-tuple-element.76), channel_id=1, source_target_pairs={{0,4},{4,0},{8,12},{12,8},{1,5},{5,1},{9,13},{13,9},{2,6},{6,2},{1... | collective-permute-start | bytes 786440 | tf_op jit(solution)/shard_map/ppermute | solution.py:678
  45.0 1.6 %shard_map.86 = (bf16[512,256]{1,0:T(8,128)(2,1)S(1)}, f32[512,256]{1,0:T(8,128)S(1)}) custom-call(f32[512,1024]{1,0:T(8,128)S(1)} %get-tuple-element.64.early, f32[2,512,1024]{2,1,0:T(8,128)S(1)} %get-tuple-element.65.first, bf16[512,128]{1,0:T(8,128)(2,1)S(1)} %get-tuple-element.66.hot, bf16[1024,512]{1,0:T(8,128)(2,1)S(1)} %get-tuple-element.51.rest_3_.rest_5_.t_odd, ...), custom_call_target="tpu_custom_call" | custom-call | flops 671088640 | bytes 3145728 | tf_op jit(solution)/shard_map/pallas_call | solution.py:661
  46.5 0.1 collective-permute-start.10
  46.6 5.5 %collective-permute-done.12.received = bf16[512,256]{1,0:T(8,128)(2,1)S(1)} collective-permute-done((bf16[512,256]{1,0:T(8,128)(2,1)S(1)}, bf16[512,256]{1,0:T(8,128)(2,1)S(1)}, u32[]{:S(2)}, u32[]{:S(2)}) %collective-permute-start.12) | collective-permute-done | bytes 262176 | tf_op jit(solution)/shard_map/ppermute | solution.py:678
  52.2 3.3 %collective-permute-start.13 = (bf16[256,256]{1,0:T(8,128)(2,1)S(1)}, bf16[256,256]{1,0:T(8,128)(2,1)S(1)}, u32[]{:S(2)}, u32[]{:S(2)}) collective-permute-start(bf16[256,256]{1,0:T(8,128)(2,1)S(1)} %get-tuple-element.78), channel_id=1, source_target_pairs={{0,8},{4,12},{8,0},{12,4},{1,9},{5,13},{9,1},{13,5},{2,10},{6,14},... | collective-permute-start | bytes 393224 | tf_op jit(solution)/shard_map/ppermute | solution.py:678
  55.5 4.9 %collective-permute-done.10.received = bf16[512,256]{1,0:T(8,128)(2,1)S(1)} collective-permute-done((bf16[512,256]{1,0:T(8,128)(2,1)S(1)}, bf16[512,256]{1,0:T(8,128)(2,1)S(1)}, u32[]{:S(2)}, u32[]{:S(2)}) %collective-permute-start.10) | collective-permute-done | bytes 262176 | tf_op jit(solution)/shard_map/ppermute | solution.py:678
  60.4 0.8 %collective-permute-start.11 = (bf16[256,256]{1,0:T(8,128)(2,1)S(1)}, bf16[256,256]{1,0:T(8,128)(2,1)S(1)}, u32[]{:S(2)}, u32[]{:S(2)}) collective-permute-start(bf16[256,256]{1,0:T(8,128)(2,1)S(1)} %get-tuple-element.74), channel_id=1, source_target_pairs={{0,8},{4,12},{8,0},{12,4},{1,9},{5,13},{9,1},{13,5},{2,10},{6,14},... | collective-permute-start | bytes 393224 | tf_op jit(solution)/shard_map/ppermute | solution.py:678
  61.2 8.3 %collective-permute-done.11.refs_1_ = bf16[256,256]{1,0:T(8,128)(2,1)S(1)} collective-permute-done((bf16[256,256]{1,0:T(8,128)(2,1)S(1)}, bf16[256,256]{1,0:T(8,128)(2,1)S(1)}, u32[]{:S(2)}, u32[]{:S(2)}) %collective-permute-start.11) | collective-permute-done | bytes 131104 | tf_op jit(solution)/shard_map/ppermute | solution.py:678
  69.5 0.8 %finish.1 = f32[256,512]{1,0:T(8,128)} custom-call(f32[256,256]{1,0:T(8,128)S(1)} %get-tuple-element.73.refs_0_, bf16[256,256]{1,0:T(8,128)(2,1)S(1)} %collective-permute-done.11.refs_1_, f32[256,256]{1,0:T(8,128)S(1)} %get-tuple-element.77.refs_2_, bf16[256,256]{1,0:T(8,128)(2,1)S(1)} %collective-permute-done.13.refs_3_), custom_call_target="tpu_custom_call" | custom-call | flops 131072 | bytes 1048576 | tf_op jit(solution)/shard_map/finish/pallas_call | solution.py:697
  (13 shorter events, 0.1 us)
Async XLA Ops:
  0.0 11.5 %copy-start = (bf16[512,3072]{1,0:T(8,128)(2,1)S(1)}, bf16[512,3072]{1,0:T(8,128)(2,1)}, u32[]{:S(2)}) copy-start(bf16[512,3072]{1,0:T(8,128)(2,1)} %main.9) | copy-start | bytes 9437188
  1.5 21.2 %collective-permute-start = (bf16[336,1024]{1,0:T(8,128)(2,1)S(1)}, bf16[336,1024]{1,0:T(8,128)(2,1)S(1)}, u32[]{:S(2)}, u32[]{:S(2)}) collective-permute-start(bf16[336,1024]{1,0:T(8,128)(2,1)S(1)} %get-tuple-element.49), channel_id=1, source_target_pairs={{0,4},{4,0},{8,12},{12,8},{1,5},{5,1},{9,13},{13,9},{2,6},{6,2},{1... | collective-permute-start | bytes 2064392 | tf_op jit(solution)/shard_map/ppermute | solution.py:575
  4.6 18.1 %collective-permute-start.1 = (bf16[336,1024]{1,0:T(8,128)(2,1)S(1)}, bf16[336,1024]{1,0:T(8,128)(2,1)S(1)}, u32[]{:S(2)}, u32[]{:S(2)}) collective-permute-start(bf16[336,1024]{1,0:T(8,128)(2,1)S(1)} %get-tuple-element.50), channel_id=1, source_target_pairs={{0,0},{4,8},{8,4},{12,12},{1,1},{5,9},{9,5},{13,13},{2,2},{6,10},{... | collective-permute-start | bytes 2064392 | tf_op jit(solution)/shard_map/ppermute | solution.py:575
  6.6 23.0 %collective-permute-start.2 = (bf16[192,1024]{1,0:T(8,128)(2,1)S(1)}, bf16[192,1024]{1,0:T(8,128)(2,1)S(1)}, u32[]{:S(2)}, u32[]{:S(2)}) collective-permute-start(bf16[192,1024]{1,0:T(8,128)(2,1)S(1)} %get-tuple-element.55), channel_id=1, source_target_pairs={{0,4},{4,0},{8,12},{12,8},{1,5},{5,1},{9,13},{13,9},{2,6},{6,2},{1... | collective-permute-start | bytes 1179656 | tf_op jit(solution)/shard_map/ppermute | solution.py:575
  10.8 18.7 %collective-permute-start.3 = (bf16[192,1024]{1,0:T(8,128)(2,1)S(1)}, bf16[192,1024]{1,0:T(8,128)(2,1)S(1)}, u32[]{:S(2)}, u32[]{:S(2)}) collective-permute-start(bf16[192,1024]{1,0:T(8,128)(2,1)S(1)} %get-tuple-element.56), channel_id=1, source_target_pairs={{0,0},{4,8},{8,4},{12,12},{1,1},{5,9},{9,5},{13,13},{2,2},{6,10},{... | collective-permute-start | bytes 1179656 | tf_op jit(solution)/shard_map/ppermute | solution.py:575
  21.2 13.6 %collective-permute-start.6 = (bf16[16,1024]{1,0:T(8,128)(2,1)S(1)}, bf16[16,1024]{1,0:T(8,128)(2,1)S(1)}, u32[]{:S(2)}, u32[]{:S(2)}) collective-permute-start(bf16[16,1024]{1,0:T(8,128)(2,1)S(1)} %get-tuple-element.63), channel_id=1, source_target_pairs={{0,2},{1,3},{2,0},{3,1},{4,6},{5,7},{6,4},{7,5},{8,10},{9,11},{10,... | collective-permute-start | bytes 98312 | tf_op jit(solution)/shard_map/ppermute | solution.py:605
  22.7 12.7 %collective-permute-start.4 = (bf16[64,1024]{1,0:T(8,128)(2,1)S(1)}, bf16[64,1024]{1,0:T(8,128)(2,1)S(1)}, u32[]{:S(2)}, u32[]{:S(2)}) collective-permute-start(bf16[64,1024]{1,0:T(8,128)(2,1)S(1)} %get-tuple-element.61), channel_id=1, source_target_pairs={{0,1},{1,0},{2,3},{3,2},{4,5},{5,4},{6,7},{7,6},{8,9},{9,8},{10,11... | collective-permute-start | bytes 393224 | tf_op jit(solution)/shard_map/ppermute | solution.py:605
  22.7 12.7 %collective-permute-start.5 = (bf16[64,1024]{1,0:T(8,128)(2,1)S(1)}, bf16[64,1024]{1,0:T(8,128)(2,1)S(1)}, u32[]{:S(2)}, u32[]{:S(2)}) collective-permute-start(bf16[64,1024]{1,0:T(8,128)(2,1)S(1)} %get-tuple-element.62), channel_id=1, source_target_pairs={{0,3},{1,2},{2,1},{3,0},{4,7},{5,6},{6,5},{7,4},{8,11},{9,10},{10,... | collective-permute-start | bytes 393224 | tf_op jit(solution)/shard_map/ppermute | solution.py:605
  29.6 5.9 %copy-start.1 = (s32[512]{0:T(512)S(1)}, s32[512]{0:T(512)}, u32[]{:S(2)}) copy-start(s32[512]{0:T(512)} %param.10) | copy-start | bytes 6148
  29.6 5.9 %copy-start.2 = (s32[512]{0:T(512)S(1)}, s32[512]{0:T(512)}, u32[]{:S(2)}) copy-start(s32[512]{0:T(512)} %param.11) | copy-start | bytes 6148
  33.2 6.6 %collective-permute-start.9 = (bf16[16,1024]{1,0:T(8,128)(2,1)S(1)}, bf16[16,1024]{1,0:T(8,128)(2,1)S(1)}, u32[]{:S(2)}, u32[]{:S(2)}) collective-permute-start(bf16[16,1024]{1,0:T(8,128)(2,1)S(1)} %get-tuple-element.70), channel_id=1, source_target_pairs={{0,2},{1,3},{2,0},{3,1},{4,6},{5,7},{6,4},{7,5},{8,10},{9,11},{10,... | collective-permute-start | bytes 98312 | tf_op jit(solution)/shard_map/ppermute | solution.py:605
  34.8 5.0 %collective-permute-start.7 = (bf16[64,1024]{1,0:T(8,128)(2,1)S(1)}, bf16[64,1024]{1,0:T(8,128)(2,1)S(1)}, u32[]{:S(2)}, u32[]{:S(2)}) collective-permute-start(bf16[64,1024]{1,0:T(8,128)(2,1)S(1)} %get-tuple-element.68), channel_id=1, source_target_pairs={{0,1},{1,0},{2,3},{3,2},{4,5},{5,4},{6,7},{7,6},{8,9},{9,8},{10,11... | collective-permute-start | bytes 393224 | tf_op jit(solution)/shard_map/ppermute | solution.py:605
  34.8 5.1 %collective-permute-start.8 = (bf16[64,1024]{1,0:T(8,128)(2,1)S(1)}, bf16[64,1024]{1,0:T(8,128)(2,1)S(1)}, u32[]{:S(2)}, u32[]{:S(2)}) collective-permute-start(bf16[64,1024]{1,0:T(8,128)(2,1)S(1)} %get-tuple-element.69), channel_id=1, source_target_pairs={{0,3},{1,2},{2,1},{3,0},{4,7},{5,6},{6,5},{7,4},{8,11},{9,10},{10,... | collective-permute-start | bytes 393224 | tf_op jit(solution)/shard_map/ppermute | solution.py:605
  41.5 10.7 %collective-permute-start.12 = (bf16[512,256]{1,0:T(8,128)(2,1)S(1)}, bf16[512,256]{1,0:T(8,128)(2,1)S(1)}, u32[]{:S(2)}, u32[]{:S(2)}) collective-permute-start(bf16[512,256]{1,0:T(8,128)(2,1)S(1)} %get-tuple-element.76), channel_id=1, source_target_pairs={{0,4},{4,0},{8,12},{12,8},{1,5},{5,1},{9,13},{13,9},{2,6},{6,2},{1... | collective-permute-start | bytes 786440 | tf_op jit(solution)/shard_map/ppermute | solution.py:678
  46.5 13.8 %collective-permute-start.10 = (bf16[512,256]{1,0:T(8,128)(2,1)S(1)}, bf16[512,256]{1,0:T(8,128)(2,1)S(1)}, u32[]{:S(2)}, u32[]{:S(2)}) collective-permute-start(bf16[512,256]{1,0:T(8,128)(2,1)S(1)} %get-tuple-element.72), channel_id=1, source_target_pairs={{0,4},{4,0},{8,12},{12,8},{1,5},{5,1},{9,13},{13,9},{2,6},{6,2},{1... | collective-permute-start | bytes 786440 | tf_op jit(solution)/shard_map/ppermute | solution.py:678
  52.2 9.0 %collective-permute-start.13 = (bf16[256,256]{1,0:T(8,128)(2,1)S(1)}, bf16[256,256]{1,0:T(8,128)(2,1)S(1)}, u32[]{:S(2)}, u32[]{:S(2)}) collective-permute-start(bf16[256,256]{1,0:T(8,128)(2,1)S(1)} %get-tuple-element.78), channel_id=1, source_target_pairs={{0,8},{4,12},{8,0},{12,4},{1,9},{5,13},{9,1},{13,5},{2,10},{6,14},... | collective-permute-start | bytes 393224 | tf_op jit(solution)/shard_map/ppermute | solution.py:678
  60.4 9.1 %collective-permute-start.11 = (bf16[256,256]{1,0:T(8,128)(2,1)S(1)}, bf16[256,256]{1,0:T(8,128)(2,1)S(1)}, u32[]{:S(2)}, u32[]{:S(2)}) collective-permute-start(bf16[256,256]{1,0:T(8,128)(2,1)S(1)} %get-tuple-element.74), channel_id=1, source_target_pairs={{0,8},{4,12},{8,0},{12,4},{1,9},{5,13},{9,1},{13,5},{2,10},{6,14},... | collective-permute-start | bytes 393224 | tf_op jit(solution)/shard_map/ppermute | solution.py:678

commit v10 on v9

--- a/solution.py
+++ b/solution.py
@@ -467,11 +467,11 @@
     first_rows(hots, whites[1::2], scale, later.at[1])
 
 
-def late_kernel(groups, n_pieces, n_dest, first_pair, early, first, hot, t_odd, t_even, *rest):
+def late_kernel(groups, n_pieces, n_dest, orders, first_pair, early, first, hot, t_odd, t_even, *rest):
     pieces = rest[:n_pieces]
-    send, keep = rest[n_pieces : n_pieces + 2]
-    incoming, second, x_odd, x_even = rest[n_pieces + 2 :]
-    pairs = send.shape[1]
+    outs = rest[n_pieces : n_pieces + len(orders)]
+    incoming, second, x_odd, x_even = rest[n_pieces + len(orders) :]
+    pairs = x_odd.shape[0]
     second_rows(groups, pieces, hot, first_pair, incoming, second)
 
     def group(i, carry):
@@ -490,7 +490,7 @@
     lag_rows = NL // n_dest
     me = lax.axis_index("tm")
     dims = (((1,), (1,)), ((), ()))
-    for out, order in ((send, range(1, n_dest, 2)), (keep, range(0, n_dest, 2))):
+    for out, order in zip(outs, orders):
         spots = [
             pl.ds(pl.multiple_of(jnp.bitwise_xor(me, r) * lag_rows, lag_rows), lag_rows) for r in order
         ]
@@ -509,13 +509,17 @@
         out[j * lag_rows : (j + 1) * lag_rows, :] = value.astype(out.dtype)
 
 
-def finish_kernel(*refs):
+def finish_kernel(counts, *refs):
     out = refs[-1]
     at = 0
-    for keep, received in zip(refs[0:-1:2], refs[1:-1:2]):
-        width = keep.shape[1]
-        out[:, at : at + width] = keep[...] + received[...].astype(F32)
-        at += width
+    refs = list(refs[:-1])
+    for n in counts:
+        total = refs[0][...]
+        for received in refs[1:n]:
+            total = total + received[...].astype(F32)
+        out[:, at : at + total.shape[1]] = total
+        at += total.shape[1]
+        refs = refs[n:]
 
 
 def in_vmem(*arrays):
@@ -651,51 +655,57 @@
     )(first_row, slot_row, *in_vmem(white0, white3, *whites, *early_in))
 
     lag_rows = NL // n_tm
-    n_half = 2
-    half = pairs // n_half
-    steps = [1 << k for k in range(n_tm.bit_length() - 1)]
-    done = []
-    parts = []
-    for h in range(n_half):
-        parts.append(
-            pl.pallas_call(
-                functools.partial(late_kernel, groups, len(buffers), n_tm, h * half),
-                out_shape=[pltpu.VMEM((NL // 2, half), BF16), pltpu.VMEM((NL // 2, half), F32)],
-                in_specs=[VMEM] * (5 + len(buffers)),
+    half = pairs // 2
+
+    def late(h, orders):
+        return pl.pallas_call(
+            functools.partial(late_kernel, groups, len(buffers), n_tm, orders, h * half),
+            out_shape=[
+                pltpu.VMEM((len(o) * lag_rows, half), F32 if 0 in o else BF16) for o in orders
+            ],
+            in_specs=[VMEM] * (5 + len(buffers)),
+            out_specs=[VMEM] * len(orders),
+            scratch_shapes=[
+                pltpu.VMEM((2, width, 2 * NF), BF16),
+                pltpu.VMEM((2, half, 2 * NF), F32),
+                pltpu.VMEM((half, NF), BF16),
+                pltpu.VMEM((half, NF), BF16),
+            ],
+            compiler_params=params(10),
+            cost_estimate=cost(2 * 2 * half * width * 2 * NF + 2 * NL * half * 2 * NF, 3 << 20),
+        )(*in_vmem(early, first, hot, t_odd, t_even, *late_in))
+
+    def swapped(x, r):
+        return lax.ppermute(x, "tm", [(i, i ^ r) for i in range(n_tm)])
+
+    def halving(h):
+        send, keep = late(h, [list(range(1, n_tm, 2)), list(range(0, n_tm, 2))])
+        step = 1
+        while True:
+            received = swapped(send, step)
+            if keep.shape[0] == lag_rows:
+                return [keep, received]
+            rows = keep.shape[0] // 2
+            send, keep = pl.pallas_call(
+                functools.partial(merge_kernel, lag_rows),
+                out_shape=[pltpu.VMEM((rows, half), BF16), pltpu.VMEM((rows, half), F32)],
+                in_specs=[VMEM] * 2,
                 out_specs=[VMEM] * 2,
-                scratch_shapes=[
-                    pltpu.VMEM((2, width, 2 * NF), BF16),
-                    pltpu.VMEM((2, half, 2 * NF), F32),
-                    pltpu.VMEM((half, NF), BF16),
-                    pltpu.VMEM((half, NF), BF16),
-                ],
-                compiler_params=params(10),
-                cost_estimate=cost(2 * 2 * half * width * 2 * NF + 2 * NL * half * 2 * NF, 3 << 20),
-            )(*in_vmem(early, first, hot, t_odd, t_even, *late_in))
-        )
-    for step in steps:
-        route = [(i, i ^ step) for i in range(n_tm)]
-        received = [lax.ppermute(send, "tm", route) for send, _ in parts]
-        if step == steps[-1]:
-            done = [x for (_, keep), got in zip(parts, received) for x in (keep, got)]
-            break
-        merged = []
-        for h in range(n_half):
-            keep = parts[h][1]
-            rows = keep.shape[0] // 2
-            merged.append(
-                pl.pallas_call(
-                    functools.partial(merge_kernel, lag_rows),
-                    out_shape=[pltpu.VMEM((rows, half), BF16), pltpu.VMEM((rows, half), F32)],
-                    in_specs=[VMEM] * 2,
-                    out_specs=[VMEM] * 2,
-                    compiler_params=params(1),
-                    cost_estimate=cost(rows * half, 1 << 20),
-                )(*in_vmem(keep, received[h]))
-            )
-        parts = merged
+                compiler_params=params(1),
+                cost_estimate=cost(rows * half, 1 << 20),
+            )(*in_vmem(keep, received))
+            step *= 2
+
+    def direct(h):
+        order = [r for r in (3, 2, 1, 0)]
+        outs = late(h, [[r] for r in order])
+        got = [swapped(x, r) for r, x in zip(order[:-1], outs)]
+        return [outs[-1]] + got
+
+    pieces = [halving(0), direct(1) if n_tm == 4 else halving(1)]
+    done = [x for piece in pieces for x in piece]
     return pl.pallas_call(
-        finish_kernel,
+        functools.partial(finish_kernel, tuple(len(piece) for piece in pieces)),
         out_shape=jax.ShapeDtypeStruct((lag_rows, pairs), F32),
         in_specs=[VMEM] * len(done),
         out_specs=VMEM,

time: 70.5 us -> 67.8 us (0.962)
  waiting for transfers between devices: 18.9 us -> 12.5 us
  starting transfers between devices: 20.8 us -> 24.4 us
    ppermute x4 -> x5, waiting for transfers between devices: 18.8 us -> 12.4 us  [swapped(): return lax.ppermute(x, 'tm', [(i, i ^ r) for i in range(n_tm)])]
    ppermute x4 -> x5, starting transfers between devices: 7.63 us -> 11.3 us  [swapped(): return lax.ppermute(x, 'tm', [(i, i ^ r) for i in range(n_tm)])]
    pallas_call x5 -> x4, Pallas kernels: 4.06 us -> 4.06 us  [the longest x2 3.15 us: late(): pl.pallas_call(functools.partial(late_kernel, groups, len(buffers), n_tm,...]
  transfers between devices with their start and end apart: 14 -> 15, of which waited for: 4 -> 5; matrix products, arithmetic and copies ran while one was open for 0% -> 0% of each run, Pallas kernels for 38% -> 39%
where the time goes in v10:
time: 67.8 us; the launch traced here: 67.7 us
  Pallas kernels  30.6 us (45%)
  starting transfers between devices  24.4 us (36%)
  waiting for transfers between devices  12.5 us (18%)
    ppermute x5, waiting for transfers between devices, swapped(): return lax.ppermute(x, 'tm', [(i, i ^ r) for i in range(n_tm)])  12.4 us
    ppermute x5, starting transfers between devices, swapped(): return lax.ppermute(x, 'tm', [(i, i ^ r) for i in range(n_tm)])  11.3 us
    pallas_call x2, Pallas kernels, on_device(): pl.pallas_call(functools.partial(rim_kernel, groups, sum(sizes[:i]), i, l...  9.81 us
    pallas_call x1, Pallas kernels, on_device(): pl.pallas_call(functools.partial(local_kernel, groups), out_shape=[table]...  9.66 us
    ppermute x4, starting transfers between devices, on_device(): got[swap] = lax.ppermute(packed[swap], 'tm', routes[swap])  8.71 us
    ppermute x6, starting transfers between devices, exchange(): got[i] = lax.ppermute(pieces[i], 'sta', route)  4.41 us
    pallas_call x1, Pallas kernels, on_device(): pl.pallas_call(functools.partial(early_kernel, groups, len(buffers), n_ch...  4.33 us
    pallas_call x2, Pallas kernels, late(): pl.pallas_call(functools.partial(late_kernel, groups, len(buffers), n_tm,...  3.15 us
  transfers between devices with their start and end apart: 15, of which 5 were waited for; matrix products, arithmetic and copies ran while one was open for 0% of the time, Pallas kernels for 39%

profile of v10, /device:TPU:0, one launch (start us, length us, event | category | flops | bytes accessed | tf_op | source)
XLA Modules:
  0.0 67.7 jit_solution(782954404466361504)
XLA Ops:
  0.0 1.5 %shard_map.82 = (bf16[336,1024]{1,0:T(8,128)(2,1)S(1)}, bf16[336,1024]{1,0:T(8,128)(2,1)S(1)}, s32[3]{0:T(128)S(4)}) custom-call(s32[3]{0:T(128)} %offsets.3, bf16[512,3072]{1,0:T(8,128)(2,1)} %main.9), custom_call_target="tpu_custom_call" | custom-call | bytes 2097152 | tf_op jit(solution)/shard_map/pallas_call | solution.py:562
  1.5 3.1 %collective-permute-start = (bf16[336,1024]{1,0:T(8,128)(2,1)S(1)}, bf16[336,1024]{1,0:T(8,128)(2,1)S(1)}, u32[]{:S(2)}, u32[]{:S(2)}) collective-permute-start(bf16[336,1024]{1,0:T(8,128)(2,1)S(1)} %get-tuple-element.49), channel_id=1, source_target_pairs={{0,4},{4,0},{8,12},{12,8},{1,5},{5,1},{9,13},{13,9},{2,6},{6,2},{1... | collective-permute-start | bytes 2064392 | tf_op jit(solution)/shard_map/ppermute | solution.py:579
  4.6 0.7 %collective-permute-start.1 = (bf16[336,1024]{1,0:T(8,128)(2,1)S(1)}, bf16[336,1024]{1,0:T(8,128)(2,1)S(1)}, u32[]{:S(2)}, u32[]{:S(2)}) collective-permute-start(bf16[336,1024]{1,0:T(8,128)(2,1)S(1)} %get-tuple-element.50), channel_id=1, source_target_pairs={{0,0},{4,8},{8,4},{12,12},{1,1},{5,9},{9,5},{13,13},{2,2},{6,10},{... | collective-permute-start | bytes 2064392 | tf_op jit(solution)/shard_map/ppermute | solution.py:579
  5.3 1.3 %shard_map.83 = (bf16[192,1024]{1,0:T(8,128)(2,1)S(1)}, bf16[192,1024]{1,0:T(8,128)(2,1)S(1)}, f32[64,512]{1,0:T(8,128)S(1)}, f32[64,512]{1,0:T(8,128)S(1)}, f32...) custom-call(s32[3]{0:T(128)} %offsets.3, bf16[512,3072]{1,0:T(8,128)(2,1)} %main.9, ...), custom_call_target="tpu_custom_call" | custom-call | bytes 2097152 | tf_op jit(solution)/shard_map/pallas_call | solution.py:562
  6.6 4.2 %collective-permute-start.2 = (bf16[192,1024]{1,0:T(8,128)(2,1)S(1)}, bf16[192,1024]{1,0:T(8,128)(2,1)S(1)}, u32[]{:S(2)}, u32[]{:S(2)}) collective-permute-start(bf16[192,1024]{1,0:T(8,128)(2,1)S(1)} %get-tuple-element.55), channel_id=1, source_target_pairs={{0,4},{4,0},{8,12},{12,8},{1,5},{5,1},{9,13},{13,9},{2,6},{6,2},{1... | collective-permute-start | bytes 1179656 | tf_op jit(solution)/shard_map/ppermute | solution.py:579
  10.8 0.7 collective-permute-start.3
  11.5 9.7 %local_windows.1 = (bf16[1024,512]{1,0:T(8,128)(2,1)S(1)}, bf16[1024,512]{1,0:T(8,128)(2,1)S(1)}, bf16[512,1024]{1,0:T(8,128)(2,1)S(1)}, bf16[512,1024]{1,0:T(8,...) custom-call(s32[3]{0:T(128)S(4)} %get-tuple-element.42.offsets, ...), custom_call_target="tpu_custom_call" | custom-call | flops 2147483648 | bytes 8388608 | tf_op jit(solution)/shard_map/local_windows/pallas_call | solution.py:592
  21.2 1.6 %collective-permute-start.6 = (bf16[16,1024]{1,0:T(8,128)(2,1)S(1)}, bf16[16,1024]{1,0:T(8,128)(2,1)S(1)}, u32[]{:S(2)}, u32[]{:S(2)}) collective-permute-start(bf16[16,1024]{1,0:T(8,128)(2,1)S(1)} %get-tuple-element.63), channel_id=1, source_target_pairs={{0,2},{1,3},{2,0},{3,1},{4,6},{5,7},{6,4},{7,5},{8,10},{9,11},{10,... | collective-permute-start | bytes 98312 | tf_op jit(solution)/shard_map/ppermute | solution.py:609
  22.7 0.0 collective-permute-done.rest_0_.rest_2_
  22.7 0.0 collective-permute-start.4
  22.7 0.0 collective-permute-done.1.rest_1_.rest_3_
  22.7 0.6 collective-permute-start.5
  23.4 6.2 %shard_map.84 = (bf16[320,1024]{1,0:T(8,128)(2,1)S(1)}, bf16[320,1024]{1,0:T(8,128)(2,1)S(1)}, f32[2,128,1024]{2,1,0:T(8,128)S(1)}) custom-call(s32[3]{0:T(128)S(4)} %get-tuple-element.42.offsets, bf16[512,3072]{1,0:T(8,128)(2,1)S(1)} %copy-done, bf16[336,1024]{1,0:T(8,128)(2,1)S(1)} %collective-permute-done.rest_0_.rest_2_, ...), custom_call_target="tpu_custom_call" | custom-call | flops 1342177280 | bytes 4194304 | tf_op jit(solution)/shard_map/pallas_call | solution.py:626
  29.5 0.0 collective-permute-done.3.rest_1_
  29.6 0.0 copy-start.1
  29.6 0.0 copy-start.2
  29.6 3.7 %shard_map.85 = (bf16[192,1024]{1,0:T(8,128)(2,1)S(1)}, bf16[192,1024]{1,0:T(8,128)(2,1)S(1)}, bf16[64,1024]{1,0:T(8,128)(2,1)S(1)}, bf16[64,1024]{1,0:T(8,128)(...) custom-call(s32[3]{0:T(128)S(4)} %get-tuple-element.42.offsets, bf16[512,3072]{1,0:T(8,128)(2,1)S(1)} %copy-done, ...), custom_call_target="tpu_custom_call" | custom-call | flops 805306368 | bytes 4194304 | tf_op jit(solution)/shard_map/pallas_call | solution.py:626
  33.2 1.5 %collective-permute-start.9 = (bf16[16,1024]{1,0:T(8,128)(2,1)S(1)}, bf16[16,1024]{1,0:T(8,128)(2,1)S(1)}, u32[]{:S(2)}, u32[]{:S(2)}) collective-permute-start(bf16[16,1024]{1,0:T(8,128)(2,1)S(1)} %get-tuple-element.70), channel_id=1, source_target_pairs={{0,2},{1,3},{2,0},{3,1},{4,6},{5,7},{6,4},{7,5},{8,10},{9,11},{10,... | collective-permute-start | bytes 98312 | tf_op jit(solution)/shard_map/ppermute | solution.py:609
  34.8 0.7 collective-permute-start.8
  35.5 4.3 %early_pairs.1 = (f32[512,1024]{1,0:T(8,128)S(1)}, f32[2,512,1024]{2,1,0:T(8,128)S(1)}, bf16[512,128]{1,0:T(8,128)(2,1)S(1)}) custom-call(s32[1,512]{1,0:T(1,128)S(1)} %bitcast.2, s32[1,512]{1,0:T(1,128)S(1)} %bitcast.3, bf16[512,1024]{1,0:T(8,128)(2,1)S(1)} %get-tuple-element.47.white0, bf16[512,1024]{1,0:T(8,128)(2,1)S(1)} %get-tuple-element.48.white3, ...), custom_call_target="tpu_custom_call" | custom-call | flops 2415919104 | bytes 4194304 | tf_op jit(solution)/shard_map/early_pairs/pallas_call | solution.py:642
  39.8 0.1 collective-permute-done.8.rest_2_
  39.9 1.6 %shard_map.86 = (bf16[512,256]{1,0:T(8,128)(2,1)S(1)}, f32[512,256]{1,0:T(8,128)S(1)}) custom-call(f32[512,1024]{1,0:T(8,128)S(1)} %get-tuple-element.64.early, f32[2,512,1024]{2,1,0:T(8,128)S(1)} %get-tuple-element.65.first, bf16[512,128]{1,0:T(8,128)(2,1)S(1)} %get-tuple-element.66.hot, bf16[1024,512]{1,0:T(8,128)(2,1)S(1)} %get-tuple-element.51.rest_3_.rest_5_.t_odd, ...), custom_call_target="tpu_custom_call" | custom-call | flops 671088640 | bytes 3145728 | tf_op jit(solution)/shard_map/pallas_call | solution.py:661
  41.5 3.5 %collective-permute-start.10 = (bf16[512,256]{1,0:T(8,128)(2,1)S(1)}, bf16[512,256]{1,0:T(8,128)(2,1)S(1)}, u32[]{:S(2)}, u32[]{:S(2)}) collective-permute-start(bf16[512,256]{1,0:T(8,128)(2,1)S(1)} %get-tuple-element.72), channel_id=1, source_target_pairs={{0,4},{4,0},{8,12},{12,8},{1,5},{5,1},{9,13},{13,9},{2,6},{6,2},{1... | collective-permute-start | bytes 786440 | tf_op jit(solution)/shard_map/ppermute | solution.py:679
  45.0 1.6 %shard_map.88 = (bf16[256,256]{1,0:T(8,128)(2,1)S(1)}, bf16[256,256]{1,0:T(8,128)(2,1)S(1)}, bf16[256,256]{1,0:T(8,128)(2,1)S(1)}, f32[256,256]{1,0:T(8,128)S(1)}) custom-call(f32[512,1024]{1,0:T(8,128)S(1)} %get-tuple-element.64.early, f32[2,512,1024]{2,1,0:T(8,128)S(1)} %get-tuple-element.65.first, bf16[512,128]{1,0:T(8,128)(2,1)S(1)} %get-tuple-element.66.hot, ...), custom_call_target="tpu_custom_call" | custom-call | flops 671088640 | bytes 3145728 | tf_op jit(solution)/shard_map/pallas_call | solution.py:661
  46.6 2.7 %collective-permute-start.12 = (bf16[256,256]{1,0:T(8,128)(2,1)S(1)}, bf16[256,256]{1,0:T(8,128)(2,1)S(1)}, u32[]{:S(2)}, u32[]{:S(2)}) collective-permute-start(bf16[256,256]{1,0:T(8,128)(2,1)S(1)} %get-tuple-element.76), channel_id=1, source_target_pairs={{0,12},{4,8},{8,4},{12,0},{1,13},{5,9},{9,5},{13,1},{2,14},{6,10},... | collective-permute-start | bytes 393224 | tf_op jit(solution)/shard_map/ppermute | solution.py:679
  49.3 1.7 %collective-permute-start.14 = (bf16[256,256]{1,0:T(8,128)(2,1)S(1)}, bf16[256,256]{1,0:T(8,128)(2,1)S(1)}, u32[]{:S(2)}, u32[]{:S(2)}) collective-permute-start(bf16[256,256]{1,0:T(8,128)(2,1)S(1)} %get-tuple-element.78), channel_id=1, source_target_pairs={{0,4},{4,0},{8,12},{12,8},{1,5},{5,1},{9,13},{13,9},{2,6},{6,2},{1... | collective-permute-start | bytes 393224 | tf_op jit(solution)/shard_map/ppermute | solution.py:679
  51.0 1.1 %collective-permute-done.10.received = bf16[512,256]{1,0:T(8,128)(2,1)S(1)} collective-permute-done((bf16[512,256]{1,0:T(8,128)(2,1)S(1)}, bf16[512,256]{1,0:T(8,128)(2,1)S(1)}, u32[]{:S(2)}, u32[]{:S(2)}) %collective-permute-start.10) | collective-permute-done | bytes 262176 | tf_op jit(solution)/shard_map/ppermute | solution.py:679
  52.2 3.3 %collective-permute-start.11 = (bf16[256,256]{1,0:T(8,128)(2,1)S(1)}, bf16[256,256]{1,0:T(8,128)(2,1)S(1)}, u32[]{:S(2)}, u32[]{:S(2)}) collective-permute-start(bf16[256,256]{1,0:T(8,128)(2,1)S(1)} %get-tuple-element.74), channel_id=1, source_target_pairs={{0,8},{4,12},{8,0},{12,4},{1,9},{5,13},{9,1},{13,5},{2,10},{6,14},... | collective-permute-start | bytes 393224 | tf_op jit(solution)/shard_map/ppermute | solution.py:679
  55.5 2.2 %collective-permute-done.12.refs_3_ = bf16[256,256]{1,0:T(8,128)(2,1)S(1)} collective-permute-done((bf16[256,256]{1,0:T(8,128)(2,1)S(1)}, bf16[256,256]{1,0:T(8,128)(2,1)S(1)}, u32[]{:S(2)}, u32[]{:S(2)}) %collective-permute-start.12) | collective-permute-done | bytes 131104 | tf_op jit(solution)/shard_map/ppermute | solution.py:679
  57.7 4.5 %collective-permute-done.13.refs_4_ = bf16[256,256]{1,0:T(8,128)(2,1)S(1)} collective-permute-done((bf16[256,256]{1,0:T(8,128)(2,1)S(1)}, bf16[256,256]{1,0:T(8,128)(2,1)S(1)}, u32[]{:S(2)}, u32[]{:S(2)}) %collective-permute-start.13) | collective-permute-done | bytes 131104 | tf_op jit(solution)/shard_map/ppermute | solution.py:679
  62.2 4.6 %collective-permute-done.11.refs_1_ = bf16[256,256]{1,0:T(8,128)(2,1)S(1)} collective-permute-done((bf16[256,256]{1,0:T(8,128)(2,1)S(1)}, bf16[256,256]{1,0:T(8,128)(2,1)S(1)}, u32[]{:S(2)}, u32[]{:S(2)}) %collective-permute-start.11) | collective-permute-done | bytes 131104 | tf_op jit(solution)/shard_map/ppermute | solution.py:679
  66.8 0.9 %finish.1 = f32[256,512]{1,0:T(8,128)} custom-call(f32[256,256]{1,0:T(8,128)S(1)} %get-tuple-element.73.refs_0_, bf16[256,256]{1,0:T(8,128)(2,1)S(1)} %collective-permute-done.11.refs_1_, f32[256,256]{1,0:T(8,128)S(1)} %get-tuple-element.75.refs_2_, bf16[256,256]{1,0:T(8,128)(2,1)S(1)} %collective-permute-done.12.refs_3_, ...), custom_call_target="tpu_custom_call" | custom-call | flops 131072 | bytes 1048576 | tf_op jit(solution)/shard_map/finish/pallas_call | solution.py:707
  (14 shorter events, 0.1 us)
Async XLA Ops:
  0.0 11.5 %copy-start = (bf16[512,3072]{1,0:T(8,128)(2,1)S(1)}, bf16[512,3072]{1,0:T(8,128)(2,1)}, u32[]{:S(2)}) copy-start(bf16[512,3072]{1,0:T(8,128)(2,1)} %main.9) | copy-start | bytes 9437188
  1.5 21.2 %collective-permute-start = (bf16[336,1024]{1,0:T(8,128)(2,1)S(1)}, bf16[336,1024]{1,0:T(8,128)(2,1)S(1)}, u32[]{:S(2)}, u32[]{:S(2)}) collective-permute-start(bf16[336,1024]{1,0:T(8,128)(2,1)S(1)} %get-tuple-element.49), channel_id=1, source_target_pairs={{0,4},{4,0},{8,12},{12,8},{1,5},{5,1},{9,13},{13,9},{2,6},{6,2},{1... | collective-permute-start | bytes 2064392 | tf_op jit(solution)/shard_map/ppermute | solution.py:579
  4.6 18.1 %collective-permute-start.1 = (bf16[336,1024]{1,0:T(8,128)(2,1)S(1)}, bf16[336,1024]{1,0:T(8,128)(2,1)S(1)}, u32[]{:S(2)}, u32[]{:S(2)}) collective-permute-start(bf16[336,1024]{1,0:T(8,128)(2,1)S(1)} %get-tuple-element.50), channel_id=1, source_target_pairs={{0,0},{4,8},{8,4},{12,12},{1,1},{5,9},{9,5},{13,13},{2,2},{6,10},{... | collective-permute-start | bytes 2064392 | tf_op jit(solution)/shard_map/ppermute | solution.py:579
  6.6 23.0 %collective-permute-start.2 = (bf16[192,1024]{1,0:T(8,128)(2,1)S(1)}, bf16[192,1024]{1,0:T(8,128)(2,1)S(1)}, u32[]{:S(2)}, u32[]{:S(2)}) collective-permute-start(bf16[192,1024]{1,0:T(8,128)(2,1)S(1)} %get-tuple-element.55), channel_id=1, source_target_pairs={{0,4},{4,0},{8,12},{12,8},{1,5},{5,1},{9,13},{13,9},{2,6},{6,2},{1... | collective-permute-start | bytes 1179656 | tf_op jit(solution)/shard_map/ppermute | solution.py:579
  10.8 18.7 %collective-permute-start.3 = (bf16[192,1024]{1,0:T(8,128)(2,1)S(1)}, bf16[192,1024]{1,0:T(8,128)(2,1)S(1)}, u32[]{:S(2)}, u32[]{:S(2)}) collective-permute-start(bf16[192,1024]{1,0:T(8,128)(2,1)S(1)} %get-tuple-element.56), channel_id=1, source_target_pairs={{0,0},{4,8},{8,4},{12,12},{1,1},{5,9},{9,5},{13,13},{2,2},{6,10},{... | collective-permute-start | bytes 1179656 | tf_op jit(solution)/shard_map/ppermute | solution.py:579
  21.2 13.6 %collective-permute-start.6 = (bf16[16,1024]{1,0:T(8,128)(2,1)S(1)}, bf16[16,1024]{1,0:T(8,128)(2,1)S(1)}, u32[]{:S(2)}, u32[]{:S(2)}) collective-permute-start(bf16[16,1024]{1,0:T(8,128)(2,1)S(1)} %get-tuple-element.63), channel_id=1, source_target_pairs={{0,2},{1,3},{2,0},{3,1},{4,6},{5,7},{6,4},{7,5},{8,10},{9,11},{10,... | collective-permute-start | bytes 98312 | tf_op jit(solution)/shard_map/ppermute | solution.py:609
  22.7 12.7 %collective-permute-start.4 = (bf16[64,1024]{1,0:T(8,128)(2,1)S(1)}, bf16[64,1024]{1,0:T(8,128)(2,1)S(1)}, u32[]{:S(2)}, u32[]{:S(2)}) collective-permute-start(bf16[64,1024]{1,0:T(8,128)(2,1)S(1)} %get-tuple-element.61), channel_id=1, source_target_pairs={{0,1},{1,0},{2,3},{3,2},{4,5},{5,4},{6,7},{7,6},{8,9},{9,8},{10,11... | collective-permute-start | bytes 393224 | tf_op jit(solution)/shard_map/ppermute | solution.py:609
  22.7 12.7 %collective-permute-start.5 = (bf16[64,1024]{1,0:T(8,128)(2,1)S(1)}, bf16[64,1024]{1,0:T(8,128)(2,1)S(1)}, u32[]{:S(2)}, u32[]{:S(2)}) collective-permute-start(bf16[64,1024]{1,0:T(8,128)(2,1)S(1)} %get-tuple-element.62), channel_id=1, source_target_pairs={{0,3},{1,2},{2,1},{3,0},{4,7},{5,6},{6,5},{7,4},{8,11},{9,10},{10,... | collective-permute-start | bytes 393224 | tf_op jit(solution)/shard_map/ppermute | solution.py:609
  29.6 5.9 %copy-start.1 = (s32[512]{0:T(512)S(1)}, s32[512]{0:T(512)}, u32[]{:S(2)}) copy-start(s32[512]{0:T(512)} %param.10) | copy-start | bytes 6148
  29.6 5.9 %copy-start.2 = (s32[512]{0:T(512)S(1)}, s32[512]{0:T(512)}, u32[]{:S(2)}) copy-start(s32[512]{0:T(512)} %param.11) | copy-start | bytes 6148
  33.2 6.6 %collective-permute-start.9 = (bf16[16,1024]{1,0:T(8,128)(2,1)S(1)}, bf16[16,1024]{1,0:T(8,128)(2,1)S(1)}, u32[]{:S(2)}, u32[]{:S(2)}) collective-permute-start(bf16[16,1024]{1,0:T(8,128)(2,1)S(1)} %get-tuple-element.70), channel_id=1, source_target_pairs={{0,2},{1,3},{2,0},{3,1},{4,6},{5,7},{6,4},{7,5},{8,10},{9,11},{10,... | collective-permute-start | bytes 98312 | tf_op jit(solution)/shard_map/ppermute | solution.py:609
  34.8 5.0 %collective-permute-start.7 = (bf16[64,1024]{1,0:T(8,128)(2,1)S(1)}, bf16[64,1024]{1,0:T(8,128)(2,1)S(1)}, u32[]{:S(2)}, u32[]{:S(2)}) collective-permute-start(bf16[64,1024]{1,0:T(8,128)(2,1)S(1)} %get-tuple-element.68), channel_id=1, source_target_pairs={{0,1},{1,0},{2,3},{3,2},{4,5},{5,4},{6,7},{7,6},{8,9},{9,8},{10,11... | collective-permute-start | bytes 393224 | tf_op jit(solution)/shard_map/ppermute | solution.py:609
  34.8 5.1 %collective-permute-start.8 = (bf16[64,1024]{1,0:T(8,128)(2,1)S(1)}, bf16[64,1024]{1,0:T(8,128)(2,1)S(1)}, u32[]{:S(2)}, u32[]{:S(2)}) collective-permute-start(bf16[64,1024]{1,0:T(8,128)(2,1)S(1)} %get-tuple-element.69), channel_id=1, source_target_pairs={{0,3},{1,2},{2,1},{3,0},{4,7},{5,6},{6,5},{7,4},{8,11},{9,10},{10,... | collective-permute-start | bytes 393224 | tf_op jit(solution)/shard_map/ppermute | solution.py:609
  41.5 10.6 %collective-permute-start.10 = (bf16[512,256]{1,0:T(8,128)(2,1)S(1)}, bf16[512,256]{1,0:T(8,128)(2,1)S(1)}, u32[]{:S(2)}, u32[]{:S(2)}) collective-permute-start(bf16[512,256]{1,0:T(8,128)(2,1)S(1)} %get-tuple-element.72), channel_id=1, source_target_pairs={{0,4},{4,0},{8,12},{12,8},{1,5},{5,1},{9,13},{13,9},{2,6},{6,2},{1... | collective-permute-start | bytes 786440 | tf_op jit(solution)/shard_map/ppermute | solution.py:679
  46.6 11.1 %collective-permute-start.12 = (bf16[256,256]{1,0:T(8,128)(2,1)S(1)}, bf16[256,256]{1,0:T(8,128)(2,1)S(1)}, u32[]{:S(2)}, u32[]{:S(2)}) collective-permute-start(bf16[256,256]{1,0:T(8,128)(2,1)S(1)} %get-tuple-element.76), channel_id=1, source_target_pairs={{0,12},{4,8},{8,4},{12,0},{1,13},{5,9},{9,5},{13,1},{2,14},{6,10},... | collective-permute-start | bytes 393224 | tf_op jit(solution)/shard_map/ppermute | solution.py:679
  49.3 12.9 %collective-permute-start.13 = (bf16[256,256]{1,0:T(8,128)(2,1)S(1)}, bf16[256,256]{1,0:T(8,128)(2,1)S(1)}, u32[]{:S(2)}, u32[]{:S(2)}) collective-permute-start(bf16[256,256]{1,0:T(8,128)(2,1)S(1)} %get-tuple-element.77), channel_id=1, source_target_pairs={{0,8},{4,12},{8,0},{12,4},{1,9},{5,13},{9,1},{13,5},{2,10},{6,14},... | collective-permute-start | bytes 393224 | tf_op jit(solution)/shard_map/ppermute | solution.py:679
  49.3 12.9 %collective-permute-start.14 = (bf16[256,256]{1,0:T(8,128)(2,1)S(1)}, bf16[256,256]{1,0:T(8,128)(2,1)S(1)}, u32[]{:S(2)}, u32[]{:S(2)}) collective-permute-start(bf16[256,256]{1,0:T(8,128)(2,1)S(1)} %get-tuple-element.78), channel_id=1, source_target_pairs={{0,4},{4,0},{8,12},{12,8},{1,5},{5,1},{9,13},{13,9},{2,6},{6,2},{1... | collective-permute-start | bytes 393224 | tf_op jit(solution)/shard_map/ppermute | solution.py:679
  52.2 14.7 %collective-permute-start.11 = (bf16[256,256]{1,0:T(8,128)(2,1)S(1)}, bf16[256,256]{1,0:T(8,128)(2,1)S(1)}, u32[]{:S(2)}, u32[]{:S(2)}) collective-permute-start(bf16[256,256]{1,0:T(8,128)(2,1)S(1)} %get-tuple-element.74), channel_id=1, source_target_pairs={{0,8},{4,12},{8,0},{12,4},{1,9},{5,13},{9,1},{13,5},{2,10},{6,14},... | collective-permute-start | bytes 393224 | tf_op jit(solution)/shard_map/ppermute | solution.py:679
